TPU v7x, 32 devices: a whole 2x2x4 slice. The times are simulated.
32 devices in a mesh: img: 8 (over z, x), seq: 4 (over y, core).
Axes of the slice: x: 2, y: 2, z: 4, core: 2. Of those that a mesh axis runs over, the one named last changes fastest.
Arguments:
- patches: bfloat16 [16, 1024, 1024], P('img', 'seq'), may hold values from -6 to 6
- cotangent: bfloat16 [16, 1024, 1024], P('img', 'seq'), may hold values from -6 to 6
- res_ids: int32 [16, 20], P('img'), may hold values from 0 to 384, as said below
- pos_table: float32 [49, 1024], replicated, may hold values from -3 to 3
- attn_in: float32 [1024, 3072], P(('img', 'seq')), may hold values from -0.1875 to 0.1875
- attn_out: float32 [1024, 1024], P(('img', 'seq')), may hold values from -0.5 to 0.5
- mlp_in: float32 [1024, 4096], P(('img', 'seq')), may hold values from -0.1875 to 0.1875
- mlp_out: float32 [4096, 1024], P(('img', 'seq')), may hold values from -0.09375 to 0.09375
- vectors: float32 [1024, 12], P(('img', 'seq')), may hold values from -1 to 1.75
- first_attn_in: float32 [1024, 3072], P(('img', 'seq')), may hold values from -0.0018 to 0.0018
- first_attn_out: float32 [1024, 1024], P(('img', 'seq')), may hold values from -0.0018 to 0.0018
- first_mlp_in: float32 [1024, 4096], P(('img', 'seq')), may hold values from -0.0018 to 0.0018
- first_mlp_out: float32 [4096, 1024], P(('img', 'seq')), may hold values from -0.0018 to 0.0018
- first_vectors: float32 [1024, 12], P(('img', 'seq')), may hold values from -0.0018 to 0.0018
- second_attn_in: float32 [1024, 3072], P(('img', 'seq')), may hold values from 3e-09 to 3e-07
- second_attn_out: float32 [1024, 1024], P(('img', 'seq')), may hold values from 3e-09 to 3e-07
- second_mlp_in: float32 [1024, 4096], P(('img', 'seq')), may hold values from 3e-09 to 3e-07
- second_mlp_out: float32 [4096, 1024], P(('img', 'seq')), may hold values from 3e-09 to 3e-07
- second_vectors: float32 [1024, 12], P(('img', 'seq')), may hold values from 3e-09 to 3e-07
Outputs:
- output: bfloat16 [16, 1024, 1024], P('img', 'seq')
- input_grad: bfloat16 [16, 1024, 1024], P('img', 'seq')
- table_grad: float32 [49, 1024], replicated
- grad_attn_in: float32 [1024, 3072], P(('img', 'seq'))
- grad_attn_out: float32 [1024, 1024], P(('img', 'seq'))
- grad_mlp_in: float32 [1024, 4096], P(('img', 'seq'))
- grad_mlp_out: float32 [4096, 1024], P(('img', 'seq'))
- grad_vectors: float32 [1024, 12], P(('img', 'seq'))
- update_attn_in: float32 [1024, 3072], P(('img', 'seq'))
- update_attn_out: float32 [1024, 1024], P(('img', 'seq'))
- update_mlp_in: float32 [1024, 4096], P(('img', 'seq'))
- update_mlp_out: float32 [4096, 1024], P(('img', 'seq'))
- update_vectors: float32 [1024, 12], P(('img', 'seq'))
- new_first_attn_in: float32 [1024, 3072], P(('img', 'seq'))
- new_first_attn_out: float32 [1024, 1024], P(('img', 'seq'))
- new_first_mlp_in: float32 [1024, 4096], P(('img', 'seq'))
- new_first_mlp_out: float32 [4096, 1024], P(('img', 'seq'))
- new_first_vectors: float32 [1024, 12], P(('img', 'seq'))
- new_second_attn_in: float32 [1024, 3072], P(('img', 'seq'))
- new_second_attn_out: float32 [1024, 1024], P(('img', 'seq'))
- new_second_mlp_in: float32 [1024, 4096], P(('img', 'seq'))
- new_second_mlp_out: float32 [4096, 1024], P(('img', 'seq'))
- new_second_vectors: float32 [1024, 12], P(('img', 'seq'))
Inputs may be any that keep to these rules, and one draw needn't show every extreme that they name: `res_ids`: each entry is 224, 384 or 0; a 0 is followed only by 0s in its row; a row's images fit within its 1024 tokens.
All inputs are finite; a program needn't handle non-finite values.
Results may differ from a plain program's by a relative error of at most 0.018.
Values may be sent and summed in bfloat16 or wider, within the bound.
No kernel may reach another device: no remote copies, remote signals or barrier semaphores. Data moves between devices by JAX's collectives and lax.ppermute only.
A program may use at most 256 MiB of HBM per device.

v0:
```python
import jax
import jax.numpy as jnp
from jax import lax
from jax.sharding import PartitionSpec as P

HEADS = 16
GRID = 7
GRID_HI = 12


PRECISE = lax.Precision.HIGHEST
FIRST_CORRECTION = 0.9999734386011124
SECOND_CORRECTION = 0.0952078528862911


def layout(res_ids, positions):
    grid_side = jnp.where(res_ids == 384, GRID_HI, jnp.where(res_ids == 224, GRID, 0)).astype(
        jnp.int32
    )
    lengths = grid_side * grid_side
    starts = jnp.cumsum(lengths, axis=1) - lengths
    places = positions[None, :, None]
    inside = ((places >= starts[:, None, :]) & (places < (starts + lengths)[:, None, :])).astype(
        jnp.int32
    )
    image_number = jnp.arange(res_ids.shape[1], dtype=jnp.int32)
    usable = jnp.sum(inside, axis=2)
    segment = jnp.sum(inside * image_number, axis=2) + (1 - usable) * res_ids.shape[1]
    start_of = jnp.sum(inside * starts[:, None, :], axis=2)
    side_of = jnp.sum(inside * grid_side[:, None, :], axis=2)
    patch_index = (positions[None, :] - start_of) * usable
    return (segment, side_of, patch_index, usable)


def axis_weights(coord, side_of):
    scaled = jnp.maximum((2 * coord + 1) * GRID - GRID_HI, 0)
    lower_fine = scaled // (2 * GRID_HI)
    fraction_fine = (scaled - lower_fine * 2 * GRID_HI).astype(jnp.float32) / (2.0 * GRID_HI)
    resized = side_of == GRID_HI
    lower_cell = jnp.where(resized, lower_fine, coord)
    fraction = jnp.where(resized, fraction_fine, jnp.zeros_like(fraction_fine))
    upper_cell = jnp.minimum(lower_cell + 1, GRID - 1)
    cell_index = jnp.arange(GRID, dtype=jnp.int32)
    below = (cell_index == lower_cell[..., None]).astype(jnp.float32)
    above = (cell_index == upper_cell[..., None]).astype(jnp.float32)
    return (1.0 - fraction)[..., None] * below + fraction[..., None] * above


def table_weights(side_of, patch_index, usable):
    safe_side = jnp.maximum(side_of, 1)
    row_coord = patch_index // safe_side
    column_coord = patch_index % safe_side
    outer = (
        axis_weights(row_coord, side_of)[..., :, None]
        * axis_weights(column_coord, side_of)[..., None, :]
    )
    outer = outer * usable.astype(jnp.float32)[..., None, None]
    return outer.reshape(side_of.shape + (GRID * GRID,))


def layer_norm(stream, gain, shift):
    center = jnp.mean(stream, axis=-1, keepdims=True)
    centered = stream - center
    spread = jnp.mean(centered * centered, axis=-1, keepdims=True)
    return centered * lax.rsqrt(spread + 1e-06) * gain + shift


def gelu_exact(values):
    return jax.nn.gelu(values, approximate=False)


def by_transpose(left, right):
    return lax.dot_general(
        left, right, (((1,), (1,)), ((), ())), preferred_element_type=jnp.float32
    )


def transpose_by(left, right):
    return lax.dot_general(
        left, right, (((0,), (0,)), ((), ())), preferred_element_type=jnp.float32
    )


def adam_update(weight, gradient, first_moment, second_moment, factor, decay):
    scaled = gradient * factor
    first_new = 0.9 * first_moment + 0.1 * scaled
    second_new = 0.999 * second_moment + 0.001 * scaled * scaled
    first_hat = first_new / FIRST_CORRECTION
    second_hat = second_new / SECOND_CORRECTION
    direction = first_hat / (jnp.sqrt(second_hat) + 1e-08) + decay * weight
    return (direction, first_new, second_new)


def masked_scores(query_heads, key_heads, allowed, score_scale):
    scores = (
        jnp.einsum("rqhe,rkhe->rhqk", query_heads, key_heads, preferred_element_type=jnp.float32)
        * score_scale
    )
    return jnp.where(allowed[:, None], scores, -1e30)


def per_device(
    patches,
    cotangent,
    res_ids,
    pos_table,
    attn_in,
    attn_out,
    mlp_in,
    mlp_out,
    vectors,
    first_attn_in,
    first_attn_out,
    first_mlp_in,
    first_mlp_out,
    first_vectors,
    second_attn_in,
    second_attn_out,
    second_mlp_in,
    second_mlp_out,
    second_vectors,
):
    row_count, local_len, model_width = patches.shape
    seq_count = lax.axis_size("seq")
    row_len = local_len * seq_count
    token_count = row_count * local_len
    head_count = HEADS
    head_size = model_width // head_count
    score_scale = head_size ** (-0.5)
    slot_total = row_count * lax.axis_size("img") * row_len
    all_positions = jnp.arange(row_len, dtype=jnp.int32)
    segment_all, side_all, patch_all, usable_all = layout(res_ids, all_positions)
    offset = lax.axis_index("seq") * local_len

    def local_part(array):
        return lax.dynamic_slice_in_dim(array, offset, local_len, 1)

    segment = local_part(segment_all)
    usable = local_part(usable_all)
    place = table_weights(local_part(side_all), local_part(patch_all), usable).reshape(
        token_count, GRID * GRID
    )
    usable_float = usable.reshape(token_count).astype(jnp.float32)[:, None]
    cast_in = attn_in.astype(jnp.bfloat16)
    cast_out = attn_out.astype(jnp.bfloat16)
    cast_up = mlp_in.astype(jnp.bfloat16)
    cast_down = mlp_out.astype(jnp.bfloat16)
    cast_vectors = vectors.astype(jnp.bfloat16)
    gathered = (
        lax.all_gather(cast_in, ("img", "seq"), axis=0, tiled=True),
        lax.all_gather(cast_out, ("img", "seq"), axis=0, tiled=True),
        lax.all_gather(cast_up, ("img", "seq"), axis=0, tiled=True),
        lax.all_gather(cast_down, ("img", "seq"), axis=0, tiled=True),
        lax.all_gather(cast_vectors, ("img", "seq"), axis=0, tiled=True),
    )
    in_matrix, out_matrix, up_matrix, down_matrix, vector_low = gathered
    vector_cols = vector_low.astype(jnp.float32)
    stream = patches.reshape(token_count, model_width).astype(jnp.float32) + jnp.dot(
        place, pos_table, precision=PRECISE, preferred_element_type=jnp.float32
    )
    normed_one = layer_norm(stream, vector_cols[:, 0], vector_cols[:, 1]).astype(jnp.bfloat16)
    projected = jnp.dot(normed_one, in_matrix, preferred_element_type=jnp.float32)
    query = (projected[:, :model_width] + vector_cols[:, 2]).astype(jnp.bfloat16)
    key_rows = (
        projected[:, model_width : 2 * model_width]
        .astype(jnp.bfloat16)
        .reshape(row_count, local_len, model_width)
    )
    value_rows = (
        (projected[:, 2 * model_width :] + vector_cols[:, 3])
        .astype(jnp.bfloat16)
        .reshape(row_count, local_len, model_width)
    )
    keys_all, values_all = (
        lax.all_gather(key_rows, "seq", axis=1, tiled=True),
        lax.all_gather(value_rows, "seq", axis=1, tiled=True),
    )
    key_len = keys_all.shape[1]
    query_heads = query.reshape(row_count, local_len, head_count, head_size)
    key_heads = keys_all.reshape(row_count, key_len, head_count, head_size)
    value_heads = values_all.reshape(row_count, key_len, head_count, head_size)
    allowed = segment[:, :, None] == segment_all[:, None, :]
    scores = masked_scores(query_heads, key_heads, allowed, score_scale)
    highest = jnp.max(scores, axis=-1, keepdims=True)
    exponent = jnp.exp(scores - highest)
    totals = jnp.sum(exponent, axis=-1, keepdims=True)
    probs = exponent / totals
    log_total = highest + jnp.log(totals)
    mixed = jnp.einsum(
        "rhqk,rkhe->rqhe",
        probs.astype(jnp.bfloat16),
        value_heads,
        preferred_element_type=jnp.float32,
    )
    attended = mixed.reshape(token_count, model_width).astype(jnp.bfloat16)
    branch = jnp.dot(attended, out_matrix, preferred_element_type=jnp.float32) + vector_cols[:, 4]
    stream_two = stream + branch
    normed_two = layer_norm(stream_two, vector_cols[:, 5], vector_cols[:, 6]).astype(jnp.bfloat16)
    hidden_pre = jnp.dot(normed_two, up_matrix, preferred_element_type=jnp.float32) + vector_cols[
        :, 8:
    ].reshape(-1)
    hidden = gelu_exact(hidden_pre).astype(jnp.bfloat16)
    last = jnp.dot(hidden, down_matrix, preferred_element_type=jnp.float32) + vector_cols[:, 7]
    output = (
        ((stream_two + last) * usable_float)
        .reshape(row_count, local_len, model_width)
        .astype(jnp.bfloat16)
    )
    grad_out_rows = cotangent.reshape(token_count, model_width).astype(jnp.float32) * usable_float
    grad_out_low = grad_out_rows.astype(jnp.bfloat16)
    grad_bias_down = jnp.sum(grad_out_low.astype(jnp.float32), axis=0)
    grad_down = transpose_by(hidden, grad_out_low)
    grad_hidden = by_transpose(grad_out_low, down_matrix)
    grad_pre = jax.vjp(gelu_exact, hidden_pre)[1](grad_hidden)[0]
    grad_pre_low = grad_pre.astype(jnp.bfloat16)
    grad_bias_up = jnp.sum(grad_pre_low.astype(jnp.float32), axis=0)
    grad_up = transpose_by(normed_two, grad_pre_low)
    grad_normed_two = by_transpose(grad_pre_low, up_matrix)
    norm_two_pull = jax.vjp(layer_norm, stream_two, vector_cols[:, 5], vector_cols[:, 6])[1]
    grad_stream_norm, grad_gain_two, grad_shift_two = norm_two_pull(grad_normed_two)
    grad_stream_two = grad_out_rows + grad_stream_norm
    grad_branch_low = grad_stream_two.astype(jnp.bfloat16)
    grad_bias_out = jnp.sum(grad_branch_low.astype(jnp.float32), axis=0)
    grad_out_matrix = transpose_by(attended, grad_branch_low)
    grad_mixed = by_transpose(grad_branch_low, out_matrix).astype(jnp.bfloat16)
    grad_mixed_heads = grad_mixed.reshape(row_count, local_len, head_count, head_size)
    scores_again = masked_scores(query_heads, key_heads, allowed, score_scale)
    probs_again = jnp.exp(scores_again - log_total)
    value_part = jnp.einsum(
        "rhqk,rqhe->rkhe",
        probs_again.astype(jnp.bfloat16),
        grad_mixed_heads,
        preferred_element_type=jnp.float32,
    )
    grad_probs = jnp.einsum(
        "rqhe,rkhe->rhqk", grad_mixed_heads, value_heads, preferred_element_type=jnp.float32
    )
    inner_sum = jnp.sum(grad_probs * probs_again, axis=-1, keepdims=True)
    grad_scores = (probs_again * (grad_probs - inner_sum)).astype(jnp.bfloat16)
    grad_query = (
        jnp.einsum("rhqk,rkhe->rqhe", grad_scores, key_heads, preferred_element_type=jnp.float32)
        * score_scale
    )
    key_part = (
        jnp.einsum("rhqk,rqhe->rkhe", grad_scores, query_heads, preferred_element_type=jnp.float32)
        * score_scale
    )
    key_part = key_part.reshape(row_count, key_len, model_width)
    value_part = value_part.reshape(row_count, key_len, model_width)
    grad_keys, grad_values = (
        lax.psum_scatter(
            key_part.astype(jnp.bfloat16), "seq", scatter_dimension=1, tiled=True
        ).astype(jnp.float32),
        lax.psum_scatter(
            value_part.astype(jnp.bfloat16), "seq", scatter_dimension=1, tiled=True
        ).astype(jnp.float32),
    )
    grad_query_low = grad_query.reshape(token_count, model_width).astype(jnp.bfloat16)
    grad_keys_low = grad_keys.reshape(token_count, model_width).astype(jnp.bfloat16)
    grad_values_low = grad_values.reshape(token_count, model_width).astype(jnp.bfloat16)
    grad_projected = jnp.concatenate([grad_query_low, grad_keys_low, grad_values_low], axis=1)
    grad_in_matrix = transpose_by(normed_one, grad_projected)
    grad_bias_query = jnp.sum(grad_query_low.astype(jnp.float32), axis=0)
    grad_bias_value = jnp.sum(grad_values_low.astype(jnp.float32), axis=0)
    grad_normed_one = by_transpose(grad_projected, in_matrix)
    norm_one_pull = jax.vjp(layer_norm, stream, vector_cols[:, 0], vector_cols[:, 1])[1]
    grad_stream_first, grad_gain_one, grad_shift_one = norm_one_pull(grad_normed_one)
    grad_stream = grad_stream_two + grad_stream_first
    input_grad = grad_stream.reshape(row_count, local_len, model_width).astype(jnp.bfloat16)
    table_part = lax.dot_general(
        place,
        grad_stream,
        (((0,), (0,)), ((), ())),
        precision=PRECISE,
        preferred_element_type=jnp.float32,
    )
    table_grad = lax.psum(table_part, ("img", "seq"))
    grad_vector_cols = jnp.concatenate(
        [
            jnp.stack(
                [
                    grad_gain_one,
                    grad_shift_one,
                    grad_bias_query,
                    grad_bias_value,
                    grad_bias_out,
                    grad_gain_two,
                    grad_shift_two,
                    grad_bias_down,
                ],
                axis=1,
            ),
            grad_bias_up.reshape(model_width, -1),
        ],
        axis=1,
    )
    shards = (
        lax.psum_scatter(grad_in_matrix, ("img", "seq"), scatter_dimension=0, tiled=True),
        lax.psum_scatter(grad_out_matrix, ("img", "seq"), scatter_dimension=0, tiled=True),
        lax.psum_scatter(grad_up, ("img", "seq"), scatter_dimension=0, tiled=True),
        lax.psum_scatter(grad_down, ("img", "seq"), scatter_dimension=0, tiled=True),
        lax.psum_scatter(grad_vector_cols, ("img", "seq"), scatter_dimension=0, tiled=True),
    )
    factor = jnp.float32(1.0 / slot_total)
    weights = (attn_in, attn_out, mlp_in, mlp_out, vectors)
    firsts = (first_attn_in, first_attn_out, first_mlp_in, first_mlp_out, first_vectors)
    seconds = (second_attn_in, second_attn_out, second_mlp_in, second_mlp_out, second_vectors)
    decays = (0.05, 0.05, 0.05, 0.05, 0.0)
    updated = [
        adam_update(
            weights[index], shards[index], firsts[index], seconds[index], factor, decays[index]
        )
        for index in range(5)
    ]
    return (
        output,
        input_grad,
        table_grad,
        shards[0],
        shards[1],
        shards[2],
        shards[3],
        shards[4],
        updated[0][0],
        updated[1][0],
        updated[2][0],
        updated[3][0],
        updated[4][0],
        updated[0][1],
        updated[1][1],
        updated[2][1],
        updated[3][1],
        updated[4][1],
        updated[0][2],
        updated[1][2],
        updated[2][2],
        updated[3][2],
        updated[4][2],
    )


def solution(mesh):
    return jax.shard_map(
        per_device,
        mesh=mesh,
        in_specs=(
            P("img", "seq", None),
            P("img", "seq", None),
            P("img", None),
            P(),
            P(("img", "seq"), None),
            P(("img", "seq"), None),
            P(("img", "seq"), None),
            P(("img", "seq"), None),
            P(("img", "seq"), None),
            P(("img", "seq"), None),
            P(("img", "seq"), None),
            P(("img", "seq"), None),
            P(("img", "seq"), None),
            P(("img", "seq"), None),
            P(("img", "seq"), None),
            P(("img", "seq"), None),
            P(("img", "seq"), None),
            P(("img", "seq"), None),
            P(("img", "seq"), None),
        ),
        out_specs=(
            P("img", "seq", None),
            P("img", "seq", None),
            P(),
            P(("img", "seq"), None),
            P(("img", "seq"), None),
            P(("img", "seq"), None),
            P(("img", "seq"), None),
            P(("img", "seq"), None),
            P(("img", "seq"), None),
            P(("img", "seq"), None),
            P(("img", "seq"), None),
            P(("img", "seq"), None),
            P(("img", "seq"), None),
            P(("img", "seq"), None),
            P(("img", "seq"), None),
            P(("img", "seq"), None),
            P(("img", "seq"), None),
            P(("img", "seq"), None),
            P(("img", "seq"), None),
            P(("img", "seq"), None),
            P(("img", "seq"), None),
            P(("img", "seq"), None),
            P(("img", "seq"), None),
        ),
        check_vma=False,
    )
```

profile of v0, /device:TPU:0, one launch (start us, length us, event | category | flops | bytes accessed | tf_op | source)
XLA Modules:
  0.0 1506.4 jit_solution(4276140562138739996)
XLA Ops:
  12.7 43.9 %all-gather = bf16[32,32,12]{1,2,0:T(8,128)(2,1)S(1)} all-gather(bf16[1,32,12]{1,2,0:T(8,128)(2,1)S(1)} %convert_bitcast_fusion), channel_id=1, replica_groups=mesh['img'=8,'seq'=4] {'img','seq'}, dimensions={0}, use_global_device_ids=true | all-gather | bytes 25344 | tf_op jit(solution)/shard_map/all_gather | solution.py:154
  61.3 22.6 %all-gather.8.cloned.1.call-done = bf16[1024,3072]{1,0:T(8,128)(2,1)} async-done(((bf16[32,3072]{1,0:T(8,128)(2,1)}), bf16[1024,3072]{1,0:T(8,128)(2,1)}) %all-gather.8.cloned.1.call-update) | async-done | bytes 6291472 | tf_op jit(solution)/shard_map/all_gather | solution.py:150
  114.4 12.3 all-gather.12.cloned.1.call-done
  126.7 6.2 copy.162
  132.9 30.4 %all-gather.10.cloned.1.call-done = bf16[2,1024,1024]{2,1,0:T(8,128)(2,1)} async-done(((bf16[2,256,1024]{2,1,0:T(8,128)(2,1)}), bf16[2,1024,1024]{2,1,0:T(8,128)(2,1)}) %all-gather.10.cloned.1.call-update) | async-done | bytes 4194320 | tf_op jit(solution)/shard_map/all_gather | solution.py:176
  169.5 16.1 %fusion.46 = (f32[2,16,256]{2,1,0:T(8,128)S(1)}, f32[2,16,256,1024]{3,2,1,0:T(8,128)}) fusion(bf16[2,256,16,64]{1,3,2,0:T(8,128)(2,1)S(1)} %copy.163, bf16[2,1024,16,64]{1,3,2,0:T(8,128)(2,1)} %bitcast.100, pred[2,256,1024]{2,1,0:T(8,128)(4,1)} %broadcast_compare_fusion), kind=kOutput, calls=%fused_computation.146 | convolution fusion | flops 1098899456 | bytes 39354368 | tf_op jit(solution)/shard_map/rqhe,rkhe->rhqk/dot_general | solution.py:96
  185.6 14.3 fusion
  200.0 15.5 %fusion.19 = bf16[2,256,16,64]{1,3,2,0:T(8,128)(2,1)S(1)} fusion(bf16[2,1024,16,64]{1,3,2,0:T(8,128)(2,1)} %bitcast.102, f32[2,16,256,1024]{3,2,1,0:T(8,128)} %get-tuple-element.135, f32[2,16,256]{2,1,0:T(8,128)S(1)} %fusion, f32[2,16,256]{2,1,0:T(8,128)S(1)} %get-tuple-element.134), kind=kOutput, calls=%fused_computation.62 | convolution fusion | flops 1099431936 | bytes 38862848 | tf_op jit(solution)/shard_map/rhqk,rkhe->rqhe/dot_general | solution.py:189
  227.7 75.0 %all-gather.16.cloned.1.call-done = bf16[1024,4096]{1,0:T(8,128)(2,1)} async-done(((bf16[32,4096]{1,0:T(8,128)(2,1)}), bf16[1024,4096]{1,0:T(8,128)(2,1)}) %all-gather.16.cloned.1.call-update) | async-done | bytes 8388624 | tf_op jit(solution)/shard_map/all_gather | solution.py:152
  302.8 12.0 fusion.38
  314.8 67.4 %all-gather.18.cloned.1.call-done = bf16[4096,1024]{1,0:T(8,128)(2,1)} async-done(((bf16[128,1024]{1,0:T(8,128)(2,1)}), bf16[4096,1024]{1,0:T(8,128)(2,1)}) %all-gather.18.cloned.1.call-update) | async-done | bytes 8388624 | tf_op jit(solution)/shard_map/all_gather | solution.py:153
  382.3 27.9 %convert_reduce_fusion = (f32[4096]{0:T(1024)S(1)}, bf16[512,4096]{1,0:T(8,128)(2,1)S(1)}, f32[512,4096]{1,0:T(8,128)}) fusion(f32[512,4096]{1,0:T(8,128)} %fusion.38, f32[4096]{0:T(1024)S(1)} %add.283, bf16[512,1024]{1,0:T(8,128)(2,1)S(1)} %copy-done.17, bf16[4096,1024]{1,0:T(8,128)(2,1)} %all-gather.18.cloned.1.call-done), kind=kOutput, calls=%fused_computation.13 | convolution fusion | flops 4452249600 | bytes 30441472 | tf_op jit(solution)/shard_map/dot_general | solution.py:73
  424.2 15.4 %fusion.12 = bf16[2,16,64,1024]{3,2,1,0:T(8,128)(2,1)} fusion(bf16[2,256,16,64]{1,3,2,0:T(8,128)(2,1)S(1)} %copy.167, f32[2,16,256,1024]{3,2,1,0:T(8,128)} %get-tuple-element.135, f32[2,16,256]{2,1,0:T(8,128)S(1)} %log_add_fusion), kind=kOutput, calls=%fused_computation.33 | convolution fusion | flops 1092616192 | bytes 38830080 | tf_op jit(solution)/shard_map/rhqk,rqhe->rkhe/dot_general | solution.py:229
  439.6 6.2 copy.172
  445.9 25.5 %multiply_reduce_fusion = (f32[2,16,256]{2,1,0:T(8,128)S(1)}, f32[2,16,256,1024]{3,2,1,0:T(8,128)}) fusion(f32[2,16,256,1024]{3,2,1,0:T(8,128)} %get-tuple-element.135, f32[2,16,256]{2,1,0:T(8,128)S(1)} %log_add_fusion, bf16[2,256,16,64]{1,3,2,0:T(8,128)(2,1)S(1)} %copy.167, bf16[2,1024,16,64]{1,3,2,0:T(8,128)(2,1)} %bitcast.103), kind=kOutput, calls=%fused_computation.1 | convolution fusion | flops 1098899456 | bytes 72417280 | tf_op jit(solution)/shard_map/rqhe,rkhe->rhqk/dot_general | solution.py:235
  471.4 28.1 %multiply_convert_fusion = bf16[2,16,256,1024]{3,2,1,0:T(8,128)(2,1)} fusion(f32[2,16,256,1024]{3,2,1,0:T(8,128)} %get-tuple-element.140, f32[2,16,256,1024]{3,2,1,0:T(8,128)} %get-tuple-element.135, f32[2,16,256]{2,1,0:T(8,128)S(1)} %get-tuple-element.139, f32[2,16,256]{2,1,0:T(8,128)S(1)} %log_add_fusion), kind=kLoop, calls=%fused_computation | loop fusion | flops 33554432 | bytes 83951616 | tf_op jit(solution)/shard_map/convert_element_type | solution.py:239
  499.5 10.8 multiply_convert_fusion.1
  510.3 6.2 copy.170
  522.9 10.7 convert_reduce_fusion.4
  538.3 20.9 %reduce-scatter.10.cloned.1.call-done = bf16[2,256,1024]{2,1,0:T(8,128)(2,1)} async-done(((bf16[2,1024,1024]{2,1,0:T(8,128)(2,1)}), bf16[2,256,1024]{2,1,0:T(8,128)(2,1)}) %reduce-scatter.10.cloned.1.call-update) | async-done | bytes 1048592 | tf_op jit(solution)/shard_map/reduce_scatter | solution.py:251
  562.9 9.0 multiply_reduce_fusion.2
  573.1 10.1 fusion.20
  583.9 13.3 fusion.37
  597.3 10.0 multiply_convert_fusion.2
  607.3 10.4 fusion.49
  618.4 10.8 multiply_convert_fusion.5
  634.5 68.5 %reduce-scatter.16.cloned.1.call-done = f32[32,1024]{1,0:T(8,128)} async-done(((f32[1024,1024]{1,0:T(8,128)}), f32[32,1024]{1,0:T(8,128)}) %reduce-scatter.16.cloned.1.call-update) | async-done | bytes 131088 | tf_op jit(solution)/shard_map/reduce_scatter | solution.py:299
  704.9 130.4 %reduce-scatter.22.cloned.1.call-done = f32[32,12]{1,0:T(8,128)} async-done(((f32[1024,12]{1,0:T(8,128)}), f32[32,12]{1,0:T(8,128)}) %reduce-scatter.22.cloned.1.call-update) | async-done | bytes 1552
  836.8 157.9 %reduce-scatter.14.cloned.1.call-done = f32[32,3072]{1,0:T(8,128)} async-done(((f32[1024,3072]{1,0:T(8,128)}), f32[32,3072]{1,0:T(8,128)}) %reduce-scatter.14.cloned.1.call-update) | async-done | bytes 393232 | tf_op jit(solution)/shard_map/reduce_scatter | solution.py:298
  997.1 182.4 %reduce-scatter.18.cloned.1.call-done = f32[32,4096]{1,0:T(8,128)} async-done(((f32[1024,4096]{1,0:T(8,128)}), f32[32,4096]{1,0:T(8,128)}) %reduce-scatter.18.cloned.1.call-update) | async-done | bytes 524304 | tf_op jit(solution)/shard_map/reduce_scatter | solution.py:300
  1181.9 185.1 %reduce-scatter.20.cloned.1.call-done = f32[128,1024]{1,0:T(8,128)} async-done(((f32[4096,1024]{1,0:T(8,128)}), f32[128,1024]{1,0:T(8,128)}) %reduce-scatter.20.cloned.1.call-update) | async-done | bytes 524304 | tf_op jit(solution)/shard_map/reduce_scatter | solution.py:301
  1369.5 128.1 %all-reduce.2.cloned.1.call-done = f32[49,1024]{1,0:T(8,128)} async-done(((f32[49,1024]{1,0:T(8,128)}), f32[49,1024]{1,0:T(8,128)}) %all-reduce.2.cloned.1.call-update) | async-done | bytes 200720 | tf_op jit(solution)/shard_map/psum | solution.py:277
  (219 shorter events, 107.5 us)
Async XLA Ops:
  7.2 76.7 %all-gather.8.cloned.1.call-start = ((), (), s32[]{:S(2)}) async-start(), calls=%async_computation.7 | async-start | bytes 6488064 | tf_op jit(solution)/shard_map/all_gather | solution.py:150
  9.0 117.6 %all-gather.12.cloned.1.call-start = ((), (), s32[]{:S(2)}) async-start(), calls=%async_computation.9 | async-start | bytes 5242880 | tf_op jit(solution)/shard_map/all_gather | solution.py:175
  11.4 93.6 %copy-start.28 = (s32[2,1024]{1,0:T(2,128)}, s32[2,1024]{1,0:T(2,128)S(1)}, u32[]{:S(2)}) copy-start(s32[2,1024]{1,0:T(2,128)S(1)} %get-tuple-element.76) | copy-start | bytes 24580
  11.5 94.8 %copy-start.29 = (f32[1,2,2,128]{3,1,2,0:T(2,128)}, f32[1,2,2,128]{3,1,2,0:T(2,128)S(1)}, u32[]{:S(2)}) copy-start(f32[1,2,2,128]{3,1,2,0:T(2,128)S(1)} %copy.183) | copy-start | bytes 6148
  12.0 77.7 %copy-start.21 = (f32[7,8,2,256]{3,1,2,0:T(8,128)}, f32[7,8,2,256]{3,1,2,0:T(8,128)S(1)}, u32[]{:S(2)}) copy-start(f32[7,8,2,256]{3,1,2,0:T(8,128)S(1)} %copy.182) | copy-start | bytes 344068
  60.0 163.1 %copy-start.2 = (f32[512,1024]{1,0:T(8,128)}, f32[512,1024]{1,0:T(8,128)S(1)}, u32[]{:S(2)}) copy-start(f32[512,1024]{1,0:T(8,128)S(1)} %get-tuple-element.133) | copy-start | bytes 6291460
  61.3 241.5 %copy-start.47 = (f32[1024,1]{0,1:T(1,128)}, f32[1024,1]{0,1:T(1,128)S(1)}, u32[]{:S(2)}) copy-start(f32[1024,1]{0,1:T(1,128)S(1)} %get-tuple-element.121) | copy-start | bytes 12292
  93.5 69.8 %all-gather.10.cloned.1.call-start = ((), (), s32[]{:S(2)}) async-start(), calls=%async_computation.8 | async-start | bytes 5242880 | tf_op jit(solution)/shard_map/all_gather | solution.py:176
  97.8 125.2 %all-gather.14.cloned.1.call-start = ((), (), s32[]{:S(2)}) async-start(), calls=%async_computation.10 | async-start | bytes 2162688 | tf_op jit(solution)/shard_map/all_gather | solution.py:151
  98.6 204.2 %all-gather.16.cloned.1.call-start = ((), (), s32[]{:S(2)}) async-start(), calls=%async_computation.11 | async-start | bytes 8650752 | tf_op jit(solution)/shard_map/all_gather | solution.py:152
  100.5 281.8 %all-gather.18.cloned.1.call-start = ((), (), s32[]{:S(2)}) async-start(), calls=%async_computation.12 | async-start | bytes 8650752 | tf_op jit(solution)/shard_map/all_gather | solution.py:153
  102.5 433.5 %reduce-scatter.12.cloned.1.call-start = ((), (), s32[]{:S(2)}) async-start(), calls=%async_computation.14 | async-start | bytes 5242880 | tf_op jit(solution)/shard_map/reduce_scatter | solution.py:254
  302.8 79.5 %copy-start.17 = (bf16[512,1024]{1,0:T(8,128)(2,1)S(1)}, bf16[512,1024]{1,0:T(8,128)(2,1)}, u32[]{:S(2)}) copy-start(bf16[512,1024]{1,0:T(8,128)(2,1)} %fusion.17) | copy-start | bytes 3145732
  314.8 95.4 %copy-start.11 = (f32[512,1024]{1,0:T(8,128)S(1)}, f32[512,1024]{1,0:T(8,128)}, u32[]{:S(2)}) copy-start(f32[512,1024]{1,0:T(8,128)} %copy-done.10) | copy-start | bytes 6291460
  445.9 113.3 %reduce-scatter.10.cloned.1.call-start = ((), (), s32[]{:S(2)}) async-start(), calls=%async_computation.13 | async-start | bytes 5242880 | tf_op jit(solution)/shard_map/reduce_scatter | solution.py:251
  516.6 186.5 %reduce-scatter.16.cloned.1.call-start = ((), (), s32[]{:S(2)}) async-start(), calls=%async_computation.17 | async-start | bytes 4325376 | tf_op jit(solution)/shard_map/reduce_scatter | solution.py:299
  521.1 314.2 %reduce-scatter.22.cloned.1.call-start = ((), (), s32[]{:S(2)}) async-start(), calls=%async_computation.20 | async-start | bytes 540672
  573.0 421.6 %reduce-scatter.14.cloned.1.call-start = ((), (), s32[]{:S(2)}) async-start(), calls=%async_computation.16 | async-start | bytes 12976128 | tf_op jit(solution)/shard_map/reduce_scatter | solution.py:298
  583.2 596.3 %reduce-scatter.18.cloned.1.call-start = ((), (), s32[]{:S(2)}) async-start(), calls=%async_computation.18 | async-start | bytes 17301504 | tf_op jit(solution)/shard_map/reduce_scatter | solution.py:300
  597.2 769.7 %reduce-scatter.20.cloned.1.call-start = ((), (), s32[]{:S(2)}) async-start(), calls=%async_computation.19 | async-start | bytes 17301504 | tf_op jit(solution)/shard_map/reduce_scatter | solution.py:301
  617.8 879.9 %all-reduce.2.cloned.1.call-start = ((), (), s32[]{:S(2)}) async-start(), calls=%async_computation.15 | async-start | bytes 458752 | tf_op jit(solution)/shard_map/psum | solution.py:277
  630.9 205.2 %copy-start.33 = (f32[32,12]{0,1:T(8,128)S(1)}, f32[32,12]{0,1:T(8,128)}, u32[]{:S(2)}) copy-start(f32[32,12]{0,1:T(8,128)} %param.27) | copy-start | bytes 4612
  630.9 205.2 %copy-start.44 = (f32[32,12]{0,1:T(8,128)S(1)}, f32[32,12]{0,1:T(8,128)}, u32[]{:S(2)}) copy-start(f32[32,12]{0,1:T(8,128)} %param.32) | copy-start | bytes 4612
  630.9 205.2 %copy-start.45 = (f32[32,12]{0,1:T(8,128)S(1)}, f32[32,12]{0,1:T(8,128)}, u32[]{:S(2)}) copy-start(f32[32,12]{0,1:T(8,128)} %param.37) | copy-start | bytes 4612
  630.9 363.7 %copy-start.16 = (f32[32,3072]{1,0:T(8,128)S(1)}, f32[32,3072]{1,0:T(8,128)}, u32[]{:S(2)}) copy-start(f32[32,3072]{1,0:T(8,128)} %param.23) | copy-start | bytes 1179652
  632.4 547.1 %copy-start.13 = (f32[32,4096]{1,0:T(8,128)S(1)}, f32[32,4096]{1,0:T(8,128)}, u32[]{:S(2)}) copy-start(f32[32,4096]{1,0:T(8,128)} %param.25) | copy-start | bytes 1572868
  632.4 547.1 %copy-start.23 = (f32[32,4096]{1,0:T(8,128)S(1)}, f32[32,4096]{1,0:T(8,128)}, u32[]{:S(2)}) copy-start(f32[32,4096]{1,0:T(8,128)} %param.30) | copy-start | bytes 1572868
  632.4 547.1 %copy-start.24 = (f32[32,4096]{1,0:T(8,128)S(1)}, f32[32,4096]{1,0:T(8,128)}, u32[]{:S(2)}) copy-start(f32[32,4096]{1,0:T(8,128)} %param.35) | copy-start | bytes 1572868
  634.5 732.4 %copy-start.14 = (f32[128,1024]{1,0:T(8,128)S(1)}, f32[128,1024]{1,0:T(8,128)}, u32[]{:S(2)}) copy-start(f32[128,1024]{1,0:T(8,128)} %param.26) | copy-start | bytes 1572868
  634.5 732.4 %copy-start.25 = (f32[128,1024]{1,0:T(8,128)S(1)}, f32[128,1024]{1,0:T(8,128)}, u32[]{:S(2)}) copy-start(f32[128,1024]{1,0:T(8,128)} %param.31) | copy-start | bytes 1572868
  836.1 533.4 %copy-start.32 = (f32[32,12]{0,1:T(8,128)}, f32[32,12]{0,1:T(8,128)S(1)}, u32[]{:S(2)}) copy-start(f32[32,12]{0,1:T(8,128)S(1)} %copy.177) | copy-start | bytes 4612
  994.6 504.7 %copy-start.1 = (f32[49,1024]{1,0:T(8,128)S(1)}, f32[49,1024]{1,0:T(8,128)}, u32[]{:S(2)}) copy-start(f32[49,1024]{1,0:T(8,128)} %param.22) | copy-start | bytes 602116
  (36 other events, 586.8 us)
Sparse Core Ops, SparseCore 0:
  11.5 72.3 all-gather.7
  93.6 32.9 all-gather.11
  128.8 34.4 all-gather.9
  166.6 56.3 all-gather.13
  226.3 76.4 all-gather.15
  306.1 76.1 all-gather.17
  446.0 43.0 reduce-scatter.11
  516.7 42.4 reduce-scatter.9
  562.0 140.9 reduce-scatter.15
  705.7 129.5 reduce-scatter.21
  843.0 151.6 reduce-scatter.13
  997.3 182.0 reduce-scatter.17
  1182.3 184.5 reduce-scatter.19
  1372.9 124.7 all-reduce.1
where the time goes:
time: 1510 us
  waiting for transfers between devices  1090 us (72%)
  matrix products  211 us (14%)
  other arithmetic  84.7 us (6%)
  local copies, waits for them, and re-layouts  62.5 us (4%)
  blocking collectives  43.9 us (3%)
  between operations  15.1 us (1%)
    reduce_scatter x1, waiting for transfers between devices, per_device(): lax.psum_scatter(grad_down, ('img', 'seq'), scatter_dimension=0, tiled=True)  185 us
    reduce_scatter x1, waiting for transfers between devices, per_device(): lax.psum_scatter(grad_up, ('img', 'seq'), scatter_dimension=0, tiled=True)  182 us
    reduce_scatter x1, waiting for transfers between devices, per_device(): lax.psum_scatter(grad_in_matrix, ('img', 'seq'), scatter_dimension=0, til...  158 us
    unnamed x15, waiting for transfers between devices  131 us
    psum x1, waiting for transfers between devices, per_device(): table_grad = lax.psum(table_part, ('img', 'seq'))  128 us
    all_gather x1, waiting for transfers between devices, per_device(): lax.all_gather(cast_up, ('img', 'seq'), axis=0, tiled=True)  75 us
    reduce_scatter x1, waiting for transfers between devices, per_device(): lax.psum_scatter(grad_out_matrix, ('img', 'seq'), scatter_dimension=0, ti...  68.5 us
    all_gather x1, waiting for transfers between devices, per_device(): lax.all_gather(cast_down, ('img', 'seq'), axis=0, tiled=True)  67.4 us
  transfers between devices with their start and end apart: 14, of which 13 were waited for; matrix products, arithmetic and copies ran while one was open for 18% of the time, Pallas kernels for 0%

commit v1 on v0

v1 whole, which is shorter than its diff:
```python
import functools
import math

import jax
import jax.numpy as jnp
from jax import lax
from jax.experimental import pallas as pl
from jax.experimental.pallas import tpu as pltpu
from jax.sharding import Mesh
from jax.sharding import PartitionSpec as P

HEADS = 16
GRID = 7
GRID_HI = 12
TILE = 128

PRECISE = lax.Precision.HIGHEST
FIRST_CORRECTION = 0.9999734386011124
SECOND_CORRECTION = 0.0952078528862911
EPS = 1e-06

F32 = jnp.float32
BF16 = jnp.bfloat16


def image_spans(res_row):
    side = jnp.where(res_row == 384, GRID_HI, jnp.where(res_row == 224, GRID, 0)).astype(jnp.int32)
    lengths = side * side
    slots = res_row.shape[0]
    order = jnp.arange(slots, dtype=jnp.int32)
    earlier = order[None, :] < order[:, None]
    starts = jnp.sum(jnp.where(earlier, lengths[None, :], 0), axis=1)
    return side, lengths, starts


def layout(res_row, positions):
    side, lengths, starts = image_spans(res_row)
    slots = res_row.shape[0]
    places = positions[:, None]
    inside = ((places >= starts[None, :]) & (places < (starts + lengths)[None, :])).astype(jnp.int32)
    usable = jnp.sum(inside, axis=1)
    image_number = jnp.arange(slots, dtype=jnp.int32)
    segment = jnp.sum(inside * image_number, axis=1) + (1 - usable) * slots
    start_of = jnp.sum(inside * starts[None, :], axis=1)
    side_of = jnp.sum(inside * side[None, :], axis=1)
    patch_index = (positions - start_of) * usable
    return segment, side_of, patch_index, usable


def key_bounds(res_row, row_len):
    _, lengths, starts = image_spans(res_row)
    total = jnp.sum(lengths)
    firsts = jnp.arange(row_len // TILE, dtype=jnp.int32) * TILE

    def span(positions):
        places = positions[:, None]
        inside = (places >= starts[None, :]) & (places < (starts + lengths)[None, :])
        found = positions < total
        begin = jnp.sum(jnp.where(inside, starts[None, :], 0), axis=1)
        end = jnp.sum(jnp.where(inside, (starts + lengths)[None, :], 0), axis=1)
        return jnp.where(found, begin, total), jnp.where(found, end, row_len)

    begin, _ = span(firsts)
    _, end = span(firsts + (TILE - 1))
    return begin // TILE, (end + TILE - 1) // TILE


def axis_weights(coord, side_of):
    scaled = jnp.maximum((2 * coord + 1) * GRID - GRID_HI, 0)
    lower_fine = scaled // (2 * GRID_HI)
    fraction_fine = (scaled - lower_fine * 2 * GRID_HI).astype(F32) / (2.0 * GRID_HI)
    resized = side_of == GRID_HI
    lower_cell = jnp.where(resized, lower_fine, coord)
    fraction = jnp.where(resized, fraction_fine, jnp.zeros_like(fraction_fine))
    upper_cell = jnp.minimum(lower_cell + 1, GRID - 1)
    cell_index = jnp.arange(GRID, dtype=jnp.int32)
    below = (cell_index == lower_cell[..., None]).astype(F32)
    above = (cell_index == upper_cell[..., None]).astype(F32)
    return (1.0 - fraction)[..., None] * below + fraction[..., None] * above


def table_weights(side_of, patch_index, usable):
    safe_side = jnp.maximum(side_of, 1)
    row_coord = patch_index // safe_side
    column_coord = patch_index % safe_side
    outer = axis_weights(row_coord, side_of)[:, :, None] * axis_weights(column_coord, side_of)[:, None, :]
    outer = outer * usable.astype(F32)[:, None, None]
    return outer.reshape(side_of.shape[0], GRID * GRID)


def place_of(block, own_y, own_c, per):
    quarter = block // per
    core = (quarter % 2 + own_c) % 2
    half = (quarter // 2 + own_y) % 2
    return (core * 2 + half) * per + block % per


def split_heads(pair):
    lane = lax.broadcasted_iota(jnp.int32, pair.shape, 1)
    zero = jnp.zeros_like(pair)
    low = lane < pair.shape[1] // 2
    return jnp.concatenate([jnp.where(low, pair, zero), jnp.where(low, zero, pair)], axis=0)


def join_heads(stacked):
    half = stacked.shape[0] // 2
    lane = lax.broadcasted_iota(jnp.int32, (half, stacked.shape[1]), 1)
    return jnp.where(lane < stacked.shape[1] // 2, stacked[:half], stacked[half:])


def down_lanes(row):
    return jnp.transpose(jnp.broadcast_to(row, (TILE, TILE)))


def nt(left, right):
    return lax.dot_general(left, right, (((1,), (1,)), ((), ())), preferred_element_type=F32)


def tn(left, right):
    return lax.dot_general(left, right, (((0,), (0,)), ((), ())), preferred_element_type=F32)


def nn(left, right):
    return jnp.dot(left, right, preferred_element_type=F32)


def attend_kernel(pairs, width, per, scale, info, qkv, seg, out, log_sum, scores, high, total, mixed):
    tile = pl.program_id(0)
    own_y, own_c = info[0], info[1]
    first, last = info[2 + tile], info[2 + pl.num_programs(0) + tile]
    q_at = pl.multiple_of(place_of(tile, own_y, own_c, per) * TILE, TILE)
    seg_q = down_lanes(seg[0:1, pl.ds(pl.multiple_of(tile * TILE, TILE), TILE)])
    high[...] = jnp.full_like(high, -1e30)
    total[...] = jnp.zeros_like(total)
    mixed[...] = jnp.zeros_like(mixed)
    queries = []
    for j in range(pairs):
        queries.append(split_heads(qkv[pl.ds(q_at, TILE), j * TILE : (j + 1) * TILE] * jnp.asarray(scale, BF16)))

    def score(block, carry):
        k_at = pl.multiple_of(place_of(block, own_y, own_c, per) * TILE, TILE)
        seg_k = seg[0:1, pl.ds(pl.multiple_of(block * TILE, TILE), TILE)]
        same = seg_q == seg_k
        same = jnp.concatenate([same, same], axis=0)
        for j in range(pairs):
            keys = qkv[pl.ds(k_at, TILE), width + j * TILE : width + (j + 1) * TILE]
            s = jnp.where(same, nt(queries[j], keys), -1e30)
            scores[j, block] = s
            high[j] = jnp.maximum(high[j], s)
        return carry

    lax.fori_loop(first, last, score, 0)
    tops = [jnp.max(high[j], axis=1, keepdims=True) for j in range(pairs)]

    def mix(block, carry):
        k_at = pl.multiple_of(place_of(block, own_y, own_c, per) * TILE, TILE)
        for j in range(pairs):
            values = qkv[pl.ds(k_at, TILE), 2 * width + j * TILE : 2 * width + (j + 1) * TILE]
            p = jnp.exp(scores[j, block] - tops[j])
            total[j] += p
            mixed[j] += nn(p.astype(BF16), values)
        return carry

    lax.fori_loop(first, last, mix, 0)
    lane = lax.broadcasted_iota(jnp.int32, (TILE, TILE), 1)
    logs = jnp.zeros((TILE, TILE), F32)
    for j in range(pairs):
        sums = jnp.sum(total[j], axis=1, keepdims=True)
        out[:, j * TILE : (j + 1) * TILE] = join_heads(mixed[j] / sums).astype(BF16)
        log_total = tops[j] + jnp.log(sums)
        logs = jnp.where(lane == 2 * j, log_total[:TILE], logs)
        logs = jnp.where(lane == 2 * j + 1, log_total[TILE:], logs)
    log_sum[...] = jnp.transpose(logs)[: 2 * pairs]


def attend_back_kernel(
    pairs, width, per, scale, info, qkv, mixed, grad, seg, log_sum, out, grad_keys, grad_values, grad_query
):
    tile = pl.program_id(0)
    own_y, own_c = info[0], info[1]
    first, last = info[2 + tile], info[2 + pl.num_programs(0) + tile]
    q_at = pl.multiple_of(place_of(tile, own_y, own_c, per) * TILE, TILE)
    q_from = pl.multiple_of(tile * TILE, TILE)
    seg_q = seg[0:1, pl.ds(q_from, TILE)]

    @pl.when(tile == 0)
    def _():
        grad_keys[...] = jnp.zeros_like(grad_keys)
        grad_values[...] = jnp.zeros_like(grad_values)

    grad_query[...] = jnp.zeros_like(grad_query)
    queries, grads, logs, inner = [], [], [], []
    for j in range(pairs):
        columns = slice(j * TILE, (j + 1) * TILE)
        queries.append(split_heads(qkv[pl.ds(q_at, TILE), columns] * jnp.asarray(scale, BF16)))
        g = grad[pl.ds(q_at, TILE), columns]
        grads.append(split_heads(g))
        both = jnp.transpose(g.astype(F32) * mixed[pl.ds(q_at, TILE), columns].astype(F32))
        low = jnp.sum(both[: TILE // 2], axis=0, keepdims=True)
        high = jnp.sum(both[TILE // 2 :], axis=0, keepdims=True)
        inner.append(jnp.concatenate([low, high], axis=1))
        here = log_sum[2 * j : 2 * j + 2, pl.ds(q_from, TILE)]
        logs.append(jnp.concatenate([here[0:1], here[1:2]], axis=1))

    def step(block, carry):
        at = place_of(block, own_y, own_c, per) * TILE
        k_at = pl.multiple_of(at, TILE)
        seg_k = down_lanes(seg[0:1, pl.ds(pl.multiple_of(block * TILE, TILE), TILE)])
        same = seg_k == seg_q
        same = jnp.concatenate([same, same], axis=1)
        for j in range(pairs):
            columns = slice(j * TILE, (j + 1) * TILE)
            keys = qkv[pl.ds(k_at, TILE), width + j * TILE : width + (j + 1) * TILE]
            values = qkv[pl.ds(k_at, TILE), 2 * width + j * TILE : 2 * width + (j + 1) * TILE]
            s = jnp.where(same, nt(keys, queries[j]), -1e30)
            p = jnp.exp(s - logs[j])
            grad_values[pl.ds(k_at, TILE), columns] += nn(p.astype(BF16), grads[j])
            ds = (p * (nt(values, grads[j]) - inner[j])).astype(BF16)
            grad_keys[pl.ds(k_at, TILE), columns] += nn(ds, queries[j])
            grad_query[j] += tn(ds, keys)
        return carry

    lax.fori_loop(first, last, step, 0)
    for j in range(pairs):
        out[pl.ds(q_at, TILE), j * TILE : (j + 1) * TILE] = (join_heads(grad_query[j]) * scale).astype(BF16)

    @pl.when(tile == pl.num_programs(0) - 1)
    def _():
        out[:, width : 2 * width] = grad_keys[...].astype(BF16)
        out[:, 2 * width :] = grad_values[...].astype(BF16)


def attention(qkv, seg, info, per, head_size):
    length, width = qkv.shape[0], qkv.shape[1] // 3
    pairs, tiles = width // TILE, length // TILE
    scale = head_size ** (-0.5)

    def place(i, info):
        return place_of(i, info[0], info[1], per)

    return pl.pallas_call(
        functools.partial(attend_kernel, pairs, width, per, scale),
        name="attend",
        out_shape=(
            jax.ShapeDtypeStruct((length, width), BF16),
            jax.ShapeDtypeStruct((2 * pairs, length), F32),
        ),
        grid_spec=pltpu.PrefetchScalarGridSpec(
            num_scalar_prefetch=1,
            grid=(tiles,),
            in_specs=[
                pl.BlockSpec(qkv.shape, lambda i, info: (0, 0), pipeline_mode=pl.Buffered(1)),
                pl.BlockSpec(seg.shape, lambda i, info: (0, 0), pipeline_mode=pl.Buffered(1)),
            ],
            out_specs=[
                pl.BlockSpec((TILE, width), lambda i, info: (place(i, info), 0)),
                pl.BlockSpec((2 * pairs, TILE), lambda i, info: (0, i)),
            ],
            scratch_shapes=[
                pltpu.VMEM((pairs, tiles, 2 * TILE, TILE), F32),
                pltpu.VMEM((pairs, 2 * TILE, TILE), F32),
                pltpu.VMEM((pairs, 2 * TILE, TILE), F32),
                pltpu.VMEM((pairs, 2 * TILE, TILE), F32),
            ],
        ),
        compiler_params=pltpu.CompilerParams(
            dimension_semantics=("arbitrary",), vmem_limit_bytes=40 << 20
        ),
        cost_estimate=pl.CostEstimate(
            flops=length * length * width * 2, bytes_accessed=4 * length * width * 2, transcendentals=0
        ),
    )(info, qkv, seg)


def attention_back(qkv, mixed, grad, seg, log_sum, info, per, head_size):
    length, width = qkv.shape[0], qkv.shape[1] // 3
    pairs, tiles = width // TILE, length // TILE
    scale = head_size ** (-0.5)

    def whole(array):
        return pl.BlockSpec(array.shape, lambda i, info: (0, 0), pipeline_mode=pl.Buffered(1))

    return pl.pallas_call(
        functools.partial(attend_back_kernel, pairs, width, per, scale),
        name="attend_back",
        out_shape=jax.ShapeDtypeStruct(qkv.shape, BF16),
        grid_spec=pltpu.PrefetchScalarGridSpec(
            num_scalar_prefetch=1,
            grid=(tiles,),
            in_specs=[whole(qkv), whole(mixed), whole(grad), whole(seg), whole(log_sum)],
            out_specs=pl.BlockSpec(qkv.shape, lambda i, info: (0, 0)),
            scratch_shapes=[
                pltpu.VMEM((length, width), F32),
                pltpu.VMEM((length, width), F32),
                pltpu.VMEM((pairs, 2 * TILE, TILE), F32),
            ],
        ),
        compiler_params=pltpu.CompilerParams(
            dimension_semantics=("arbitrary",), vmem_limit_bytes=48 << 20
        ),
        cost_estimate=pl.CostEstimate(
            flops=length * length * width * 5, bytes_accessed=8 * length * width * 2, transcendentals=0
        ),
    )(info, qkv, mixed, grad, seg, log_sum)


SWAP = [(0, 1), (1, 0)]


def swap_core(array):
    return lax.ppermute(array, "sc", SWAP)


def swap_chip(array):
    return lax.ppermute(array, "sy", SWAP)


def swap_bit(array, bit):
    if bit == 0:
        return swap_chip(array)
    count = lax.axis_size("img")
    return lax.ppermute(array, "img", [(i, i ^ (1 << (bit - 1))) for i in range(count)])


def own_bit(bit):
    if bit == 0:
        return lax.axis_index("sy")
    return (lax.axis_index("img") >> (bit - 1)) & 1


def bit_orders():
    bits = int(math.log2(lax.axis_size("img"))) + 1
    rest = list(range(2, bits))
    return rest + [1, 0], rest + [0, 1]


def axis_of(bit, done):
    return sum(1 for other in done if other > bit)


def pick(index, low, high):
    return jnp.where(index == 0, low, high)


def gather_chips(block, order):
    held, done = block, []
    for bit in order:
        came = swap_bit(held, bit)
        mine = own_bit(bit)
        held = jnp.stack([pick(mine, held, came), pick(mine, came, held)], axis=axis_of(bit, done))
        done.append(bit)
    return held.reshape(-1, block.shape[1])


def scatter_chips(total, order):
    rows, columns = total.shape
    bits = sorted(order, reverse=True)
    held = total.astype(BF16).reshape((2,) * len(bits) + (rows >> len(bits), columns))
    for bit in reversed(order):
        axis = bits.index(bit)
        mine = own_bit(bit)
        away = lax.dynamic_index_in_dim(held, 1 - mine, axis, keepdims=False)
        keep = lax.dynamic_index_in_dim(held, mine, axis, keepdims=False)
        held = keep.astype(F32) + swap_bit(away, bit).astype(F32)
        bits.remove(bit)
        if bits:
            held = held.astype(BF16)
    return held


def gather_halves(block):
    first, second = bit_orders()
    half = block.shape[1] // 2
    return gather_chips(block[:, :half], first), gather_chips(block[:, half:], second)


def gather_all(block):
    return jnp.concatenate(gather_halves(block), axis=1)


def scatter_all(total):
    first, second = bit_orders()
    half = total.shape[1] // 2
    return jnp.concatenate(
        [scatter_chips(total[:, :half], first), scatter_chips(total[:, half:], second)], axis=1
    )


def normalize(stream):
    center = jnp.mean(stream, axis=-1, keepdims=True)
    centered = stream - center
    spread = jnp.mean(centered * centered, axis=-1, keepdims=True)
    inverse = lax.rsqrt(spread + EPS)
    return centered * inverse, inverse


def normalize_back(normed, inverse, gain, grad):
    scaled = grad * gain
    middle = jnp.mean(scaled, axis=-1, keepdims=True)
    along = jnp.mean(scaled * normed, axis=-1, keepdims=True)
    return (
        inverse * (scaled - middle - normed * along),
        jnp.sum(grad * normed, axis=0),
        jnp.sum(grad, axis=0),
    )


def gelu_and_slope(values):
    cdf = 0.5 * (1.0 + lax.erf(values * (0.5**0.5)))
    density = jnp.exp(-0.5 * values * values) * (1.0 / math.sqrt(2.0 * math.pi))
    return values * cdf, cdf + values * density


def adam_update(weight, gradient, first_moment, second_moment, factor, decay):
    scaled = gradient * factor
    first_new = 0.9 * first_moment + 0.1 * scaled
    second_new = 0.999 * second_moment + 0.001 * scaled * scaled
    first_hat = first_new / FIRST_CORRECTION
    second_hat = second_new / SECOND_CORRECTION
    direction = first_hat / (jnp.sqrt(second_hat) + 1e-08) + decay * weight
    return (direction, first_new, second_new)


def per_device(
    patches,
    cotangent,
    res_ids,
    pos_table,
    attn_in,
    attn_out,
    mlp_in,
    mlp_out,
    vectors,
    first_attn_in,
    first_attn_out,
    first_mlp_in,
    first_mlp_out,
    first_vectors,
    second_attn_in,
    second_attn_out,
    second_mlp_in,
    second_mlp_out,
    second_vectors,
):
    row_count, local_len, width = patches.shape
    img_count, halves = lax.axis_size("img"), lax.axis_size("sy")
    chips = img_count * halves
    row_len = local_len * halves * 2
    slot_total = row_count * img_count * row_len
    head_size = width // HEADS
    own_y, own_c = lax.axis_index("sy"), lax.axis_index("sc")
    rows = attn_in.shape[0]
    half = width // 2
    ff_rows = mlp_out.shape[0]
    ff_half = chips * ff_rows
    table_size = GRID * GRID
    vector_count = vectors.shape[1]

    def to_row(array):
        mine = lax.dynamic_index_in_dim(array, own_y, 0, keepdims=False)
        other = lax.dynamic_index_in_dim(array, 1 - own_y, 0, keepdims=False)
        return jnp.concatenate([mine, swap_chip(other)], axis=0)

    def from_row(array):
        mine, other = array[:local_len], swap_chip(array[local_len:])
        return jnp.stack([pick(own_y, mine, other), pick(own_y, other, mine)], axis=0)

    res_row = lax.dynamic_index_in_dim(res_ids, own_y, 0, keepdims=False)
    all_positions = jnp.arange(row_len, dtype=jnp.int32)
    segment_all, _, _, _ = layout(res_row, all_positions)
    seg = jnp.broadcast_to(segment_all.astype(F32)[None, :], (8, row_len))
    begin, end = key_bounds(res_row, row_len)
    info = jnp.concatenate([jnp.stack([own_y, own_c]).astype(jnp.int32), begin, end])
    near = jnp.arange(local_len, dtype=jnp.int32)
    positions = jnp.concatenate(
        [(2 * own_y + own_c) * local_len + near, (2 * (1 - own_y) + own_c) * local_len + near]
    )
    _, side_of, patch_index, usable = layout(res_row, positions)
    place = table_weights(side_of, patch_index, usable)
    usable = usable.astype(F32)[:, None]

    def by_core(array, blocks):
        split = array.reshape(rows, blocks, 2, -1)
        low, high = split[:, :, 0].reshape(rows, -1), split[:, :, 1].reshape(rows, -1)
        return pick(own_c, low, high), pick(own_c, high, low)

    vector_pad = jnp.pad(vectors, ((0, 0), (0, TILE - vector_count))).astype(BF16)
    mine_in, away_in = by_core(attn_in.astype(BF16), 3)
    mine_out, away_out = by_core(attn_out.astype(BF16), 1)
    mine_up, away_up = by_core(mlp_in.astype(BF16), chips)
    came = swap_core(jnp.concatenate([away_in, vector_pad, away_out, away_up], axis=1))
    mine = jnp.concatenate([mine_in, vector_pad, mine_out, mine_up], axis=1)
    shard = jnp.concatenate([pick(own_c, mine, came), pick(own_c, came, mine)], axis=0)
    in_width = 3 * half
    head_end = in_width + TILE
    attn_part = gather_all(shard[:, : head_end + half])
    in_matrix = attn_part[:, :in_width]
    vector_cols = attn_part[:, in_width : in_width + vector_count].astype(F32)
    out_columns = attn_part[:, head_end:]
    up_matrix = gather_all(shard[:, head_end + half :])
    down_matrix = gather_all(mlp_out.astype(BF16))
    keep_out = lax.dynamic_slice_in_dim(out_columns, own_c * half, half, 0)
    came_out = swap_core(lax.dynamic_slice_in_dim(out_columns, (1 - own_c) * half, half, 0))
    out_matrix = jnp.concatenate([pick(own_c, keep_out, came_out), pick(own_c, came_out, keep_out)], axis=1)

    gain_one, shift_one = vector_cols[:, 0], vector_cols[:, 1]
    bias_query = lax.dynamic_slice_in_dim(vector_cols[:, 2], own_c * half, half, 0)
    bias_value = lax.dynamic_slice_in_dim(vector_cols[:, 3], own_c * half, half, 0)
    bias_out, gain_two, shift_two, bias_down = (vector_cols[:, i] for i in (4, 5, 6, 7))
    bias_up = lax.dynamic_index_in_dim(
        vector_cols[:, 8:].reshape(chips, 2, ff_rows), own_c, 1, keepdims=False
    ).reshape(-1)

    own = local_len * row_count

    def with_core(array):
        return jnp.concatenate([array, swap_core(array)], axis=0)

    def sum_core(left, weights, product):
        away = product(left[own:], weights).astype(BF16)
        came = swap_core(away)
        return product(left[:own], weights) + came.astype(F32)

    stream = to_row(patches).astype(F32) + jnp.dot(
        place, pos_table, precision=PRECISE, preferred_element_type=F32
    )
    hat_one, inverse_one = normalize(stream)
    normed_one = with_core((hat_one * gain_one + shift_one).astype(BF16))
    bias_qkv = jnp.concatenate([bias_query, jnp.zeros_like(bias_query), bias_value])
    qkv = (nn(normed_one, in_matrix) + bias_qkv).astype(BF16)
    per = local_len // TILE
    mixed, log_sum = attention(qkv, seg, info, per, head_size)
    stream_two = stream + sum_core(mixed, out_matrix, nn) + bias_out
    hat_two, inverse_two = normalize(stream_two)
    normed_two = with_core((hat_two * gain_two + shift_two).astype(BF16))
    hidden_pre = nn(normed_two, up_matrix) + bias_up
    hidden, slope = gelu_and_slope(hidden_pre)
    hidden = hidden.astype(BF16)
    last = sum_core(hidden, down_matrix, nn) + bias_down
    output = from_row(((stream_two + last) * usable).astype(BF16))

    grad_own = to_row(cotangent).astype(F32) * usable
    grad_last = with_core(grad_own.astype(BF16))
    grad_bias_down = jnp.sum(grad_own, axis=0)
    grad_down = tn(hidden, grad_last)
    shard_down = scatter_all(grad_down)
    grad_pre = (nt(grad_last, down_matrix) * slope).astype(BF16)
    grad_bias_up = jnp.sum(grad_pre.astype(F32), axis=0)
    grad_up = tn(normed_two, grad_pre)
    shard_up = scatter_all(grad_up)
    grad_normed_two = sum_core(grad_pre, up_matrix, nt)
    back_two, grad_gain_two, grad_shift_two = normalize_back(hat_two, inverse_two, gain_two, grad_normed_two)
    grad_two = grad_own + back_two
    grad_branch = grad_two.astype(BF16)
    grad_bias_out = jnp.sum(grad_branch.astype(F32), axis=0)
    grad_branch = with_core(grad_branch)
    grad_out_rows = tn(mixed, grad_branch).astype(BF16)
    keep_rows = lax.dynamic_slice_in_dim(grad_out_rows, own_c * half, half, 1)
    came_rows = swap_core(lax.dynamic_slice_in_dim(grad_out_rows, (1 - own_c) * half, half, 1))
    shard_out = scatter_all(
        jnp.concatenate([pick(own_c, keep_rows, came_rows), pick(own_c, came_rows, keep_rows)], axis=0)
    )
    grad_mixed = nt(grad_branch, out_matrix).astype(BF16)
    grad_qkv = attention_back(qkv, mixed, grad_mixed, seg, log_sum, info, per, head_size)
    grad_bias_qkv = jnp.sum(grad_qkv.astype(F32), axis=0)
    grad_in = tn(normed_one, grad_qkv)
    grad_normed_one = sum_core(grad_qkv, in_matrix, nt)
    back_one, grad_gain_one, grad_shift_one = normalize_back(hat_one, inverse_one, gain_one, grad_normed_one)
    grad_stream = grad_two + back_one
    input_grad = from_row(grad_stream.astype(BF16))
    table_part = lax.dot_general(
        grad_stream, place, (((0,), (0,)), ((), ())), precision=PRECISE, preferred_element_type=F32
    )

    def widen(array, blocks):
        array = array.reshape(blocks, -1)
        zero = jnp.zeros_like(array)
        return jnp.stack([pick(own_c, array, zero), pick(own_c, zero, array)], axis=1).reshape(-1)

    narrow = jnp.stack(
        [
            grad_gain_one,
            grad_shift_one,
            widen(grad_bias_qkv[:half], 1),
            widen(grad_bias_qkv[2 * half :], 1),
            grad_bias_out,
            grad_gain_two,
            grad_shift_two,
            grad_bias_down,
        ],
        axis=1,
    )
    narrow = jnp.concatenate(
        [
            narrow,
            widen(grad_bias_up, chips).reshape(width, -1),
            table_part,
            jnp.zeros((width, TILE - vector_count - table_size), F32),
        ],
        axis=1,
    )
    shard_in = scatter_all(jnp.concatenate([grad_in, narrow], axis=1))

    def rows_of(array, core):
        return lax.dynamic_slice_in_dim(array, core * rows, rows, 0)

    def trade(array, blocks):
        away, keep = rows_of(array, 1 - own_c), rows_of(array, own_c)
        came = swap_core(away).reshape(rows, blocks, -1)
        keep = keep.reshape(rows, blocks, -1)
        both = jnp.stack([pick(own_c, keep, came), pick(own_c, came, keep)], axis=2)
        return both.reshape(rows, -1)

    grad_up_shard = trade(shard_up, chips)
    grad_out_shard = trade(shard_out, 1)
    grad_in_shard = trade(shard_in[:, :in_width], 3)
    narrow_shard = shard_in[:, in_width:]
    narrow_shard = rows_of(narrow_shard, own_c) + swap_core(rows_of(narrow_shard, 1 - own_c))
    grad_vectors_shard = narrow_shard[:, :vector_count]
    both = jnp.stack(
        [
            pick(own_c, narrow_shard, swap_core(narrow_shard)),
            pick(own_c, swap_core(narrow_shard), narrow_shard),
        ],
        axis=0,
    ).reshape(2 * rows, TILE)
    table_grad = gather_chips(both, bit_orders()[0])[:, vector_count : vector_count + table_size].T

    factor = jnp.float32(1.0 / slot_total)
    shards = (grad_in_shard, grad_out_shard, grad_up_shard, shard_down, grad_vectors_shard)
    weights = (attn_in, attn_out, mlp_in, mlp_out, vectors)
    firsts = (first_attn_in, first_attn_out, first_mlp_in, first_mlp_out, first_vectors)
    seconds = (second_attn_in, second_attn_out, second_mlp_in, second_mlp_out, second_vectors)
    decays = (0.05, 0.05, 0.05, 0.05, 0.0)
    updated = [
        adam_update(weights[i], shards[i], firsts[i], seconds[i], factor, decays[i]) for i in range(5)
    ]
    return (
        output,
        input_grad,
        table_grad,
        *shards,
        *(updated[i][0] for i in range(5)),
        *(updated[i][1] for i in range(5)),
        *(updated[i][2] for i in range(5)),
    )


def solution(mesh):
    img, seq = mesh.shape["img"], mesh.shape["seq"]
    inner = Mesh(mesh.devices.reshape(img, seq // 2, 2), ("img", "sy", "sc"))
    tokens = P("img", ("sy", "sc"), None)
    shard = P(("img", "sy", "sc"), None)
    return jax.shard_map(
        per_device,
        mesh=inner,
        in_specs=(tokens, tokens, P("img", None), P()) + (shard,) * 15,
        out_specs=(tokens, tokens, P()) + (shard,) * 20,
        check_vma=False,
    )
```

time: 1510 us -> 687 us (0.45)
  waiting for transfers between devices: 1090 us -> 343 us
  matrix products: 211 us -> 74.6 us
  starting transfers between devices: 1.3 us -> 64.7 us
  Pallas kernels: 0 us -> 50.5 us
  blocking collectives: 43.9 us -> 0 us
  other arithmetic: 84.7 us -> 60.6 us
  local copies, waits for them, and re-layouts: 62.5 us -> 79.2 us
    reduce_scatter x6 -> x0, waiting for transfers between devices: 615 us -> none  [the longest x1 185 us: per_device(): lax.psum_scatter(grad_down, ('img', 'seq'), scatter_dimension=0, tiled=True)]
    ppermute x0 -> x80, waiting for transfers between devices: none -> 343 us  [the longest x45 259 us: swap_bit(): lax.ppermute(array, 'img', [(i, i ^ 1 << bit - 1) for i in range(count)])]
    all_gather x6 -> x0, waiting for transfers between devices: 214 us -> none  [the longest x1 75 us: per_device(): lax.all_gather(cast_up, ('img', 'seq'), axis=0, tiled=True)]
    dot_general x20 -> x18, matrix products: 211 us -> 74.6 us  [the longest x6 25.4 us: nt(): lax.dot_general(left, right, (((1,), (1,)), ((), ())), preferred_element_...]
    unnamed x15 -> x0, waiting for transfers between devices: 131 us -> none
    psum x1 -> x0, waiting for transfers between devices: 128 us -> none  [per_device(): table_grad = lax.psum(table_part, ('img', 'seq'))]
    ppermute x0 -> x80, starting transfers between devices: none -> 64.7 us  [the longest x45 36.8 us: swap_bit(): lax.ppermute(array, 'img', [(i, i ^ 1 << bit - 1) for i in range(count)])]
    pallas_call x0 -> x2, Pallas kernels: none -> 50.5 us  [the longest x1 32.4 us: attention_back(): pl.pallas_call(functools.partial(attend_back_kernel, pairs, width, per, s...]
  transfers between devices with their start and end apart: 14 -> 80, of which waited for: 13 -> 43; matrix products, arithmetic and copies ran while one was open for 18% -> 27% of each run, Pallas kernels for 0% -> 7%
where the time goes in v1:
time: 687 us; the launch traced here: 676 us
  waiting for transfers between devices  343 us (50%)
  local copies, waits for them, and re-layouts  79.2 us (12%)
  matrix products  74.6 us (11%)
  starting transfers between devices  64.7 us (9%)
  other arithmetic  60.6 us (9%)
  Pallas kernels  50.5 us (7%)
    ppermute x45, waiting for transfers between devices, swap_bit(): lax.ppermute(array, 'img', [(i, i ^ 1 << bit - 1) for i in range(count)])  259 us
    ppermute x19, waiting for transfers between devices, swap_chip(): return lax.ppermute(array, 'sy', SWAP)  81.2 us
    ppermute x45, starting transfers between devices, swap_bit(): lax.ppermute(array, 'img', [(i, i ^ 1 << bit - 1) for i in range(count)])  36.8 us
    pallas_call x1, Pallas kernels, attention_back(): pl.pallas_call(functools.partial(attend_back_kernel, pairs, width, per, s...  32.4 us
    dot_general x6, matrix products, nt(): lax.dot_general(left, right, (((1,), (1,)), ((), ())), preferred_element_...  25.4 us
    ppermute x19, starting transfers between devices, swap_chip(): return lax.ppermute(array, 'sy', SWAP)  24.2 us
    dot_general x6, matrix products, nn(): return jnp.dot(left, right, preferred_element_type=F32)  24 us
    dot_general x4, matrix products, tn(): lax.dot_general(left, right, (((0,), (0,)), ((), ())), preferred_element_...  20.6 us
  transfers between devices with their start and end apart: 80, of which 43 were waited for; matrix products, arithmetic and copies ran while one was open for 27% of the time, Pallas kernels for 7%

profile of v1, /device:TPU:0, one launch (start us, length us, event | category | flops | bytes accessed | tf_op | source)
XLA Modules:
  0.0 676.1 jit_solution(5970118827503853844)
XLA Ops:
  22.4 6.3 collective-permute-done.14
  38.5 35.5 %collective-permute-done.3 = bf16[2,64,1088]{2,1,0:T(8,128)(2,1)S(1)} collective-permute-done((bf16[2,64,1088]{2,1,0:T(8,128)(2,1)S(1)}, bf16[2,64,1088]{2,1,0:T(8,128)(2,1)S(1)}, u32[]{:S(2)}, u32[]{:S(2)}) %collective-permute-start.3) | collective-permute-done | bytes 278560 | tf_op jit(solution)/shard_map/ppermute | solution.py:322
  80.9 6.7 collective-permute-done.4
  97.6 23.6 %collective-permute-done.5 = bf16[2,2,2,64,1088]{4,3,1,0,2:T(8,128)(2,1)S(1)} collective-permute-done((bf16[2,2,2,64,1088]{4,3,1,0,2:T(8,128)(2,1)S(1)}, bf16[2,2,2,64,1088]{4,3,1,0,2:T(8,128)(2,1)S(1)}, u32[]{:S(2)}, u32[]{:S(2)}) %collective-permute-start.5) | collective-permute-done | bytes 1114144 | tf_op jit(solution)/shard_map/ppermute | solution.py:322
  132.9 18.1 %attend.1 = (bf16[1024,512]{1,0:T(8,128)(2,1)S(1)}, f32[8,1024]{1,0:T(8,128)S(1)}) custom-call(s32[18]{0:T(128)S(1)} %pad_add_fusion.1.info, bf16[1024,1536]{1,0:T(8,128)(2,1)S(1)} %add_convert_fusion.qkv, f32[8,1024]{1,0:T(8,128)S(1)} %broadcast_in_dim.76.seg), custom_call_target="tpu_custom_call" | custom-call | flops 1073741824 | bytes 4194304 | tf_op jit(solution)/shard_map/attend/pallas_call | solution.py:241
  159.6 19.5 %collective-permute-done.21 = bf16[2,2,2,64,1024]{4,3,1,0,2:T(8,128)(2,1)S(1)} collective-permute-done((bf16[2,2,2,64,1024]{4,3,1,0,2:T(8,128)(2,1)S(1)}, bf16[2,2,2,64,1024]{4,3,1,0,2:T(8,128)(2,1)S(1)}, u32[]{:S(2)}, u32[]{:S(2)}) %collective-permute-start.21) | collective-permute-done | bytes 1048608 | tf_op jit(solution)/shard_map/ppermute | solution.py:322
  184.4 9.8 %multiply_convert_fusion = (bf16[1024,2048]{1,0:T(8,128)(2,1)S(1)}, f32[1024,2048]{1,0:T(8,128)}) fusion(f32[2048]{0:T(1024)S(1)} %bitcast.465, bf16[1024,1024]{1,0:T(8,128)(2,1)S(1)} %bitcast.425, bf16[1024,1024]{1,0:T(8,128)(2,1)} %bitcast.428, bf16[512,1024]{1,0:T(8,128)(2,1)} %collective-permute-done.13, bf16[512,1024]{1,0:T(8,128)(2,1)} %add_convert_fusion.1), kind=kOutput, calls=%fused_computation.8 | convolution fusion | flops 4320133120 | bytes 18882560 | tf_op jit(solution)/shard_map/dot_general | solution.py:124
  194.2 8.1 %convolution_convert_fusion.1 = bf16[2048,1024]{1,0:T(8,128)(2,1)S(1)} fusion(bf16[1024,2048]{1,0:T(8,128)(2,1)S(1)} %get-tuple-element.395, bf16[512,1024]{1,0:T(8,128)(2,1)} %collective-permute-done.33, bf16[512,1024]{1,0:T(8,128)(2,1)} %get-tuple-element.308), kind=kOutput, calls=%fused_computation.15 | convolution fusion | flops 4301258752 | bytes 10485760 | tf_op jit(solution)/shard_map/dot_general | solution.py:120
  205.7 21.7 %collective-permute-done.76 = bf16[2,2,2,128,512]{4,3,1,0,2:T(8,128)(2,1)S(1)} collective-permute-done((bf16[2,2,2,128,512]{4,3,1,0,2:T(8,128)(2,1)S(1)}, bf16[2,2,2,128,512]{4,3,1,0,2:T(8,128)(2,1)S(1)}, u32[]{:S(2)}, u32[]{:S(2)}) %collective-permute-start.76) | collective-permute-done | bytes 1048608 | tf_op jit(solution)/shard_map/ppermute | solution.py:322
  232.1 9.0 %collective-permute-done.77 = bf16[2,2,128,512]{3,2,1,0:T(8,128)(2,1)} collective-permute-done((bf16[2,2,128,512]{3,2,1,0:T(8,128)(2,1)}, bf16[2,2,128,512]{3,2,1,0:T(8,128)(2,1)}, u32[]{:S(2)}, u32[]{:S(2)}) %collective-permute-start.77) | collective-permute-done | bytes 524320 | tf_op jit(solution)/shard_map/ppermute | solution.py:315
  246.7 15.4 %collective-permute-done.78 = bf16[2,128,512]{2,1,0:T(8,128)(2,1)S(1)} collective-permute-done((bf16[2,128,512]{2,1,0:T(8,128)(2,1)S(1)}, bf16[2,128,512]{2,1,0:T(8,128)(2,1)S(1)}, u32[]{:S(2)}, u32[]{:S(2)}) %collective-permute-start.78) | collective-permute-done | bytes 262176 | tf_op jit(solution)/shard_map/ppermute | solution.py:322
  273.1 5.0 collective-permute-done.22
  284.4 14.2 %collective-permute-done.23 = bf16[2,128,512]{2,1,0:T(8,128)(2,1)S(1)} collective-permute-done((bf16[2,128,512]{2,1,0:T(8,128)(2,1)S(1)}, bf16[2,128,512]{2,1,0:T(8,128)(2,1)S(1)}, u32[]{:S(2)}, u32[]{:S(2)}) %collective-permute-start.23) | collective-permute-done | bytes 262176 | tf_op jit(solution)/shard_map/ppermute | solution.py:322
  303.1 5.4 collective-permute-done.24
  310.9 6.3 collective-permute-done.28
  319.9 16.8 %collective-permute-done.25 = bf16[2,2,2,128,512]{4,3,2,1,0:T(8,128)(2,1)} collective-permute-done((bf16[2,2,2,128,512]{4,3,2,1,0:T(8,128)(2,1)}, bf16[2,2,2,128,512]{4,3,2,1,0:T(8,128)(2,1)}, u32[]{:S(2)}, u32[]{:S(2)}) %collective-permute-start.25) | collective-permute-done | bytes 1048608 | tf_op jit(solution)/shard_map/ppermute | solution.py:315
  347.3 9.3 %convert_reduce_fusion = (bf16[2048]{0:T(1024)(128)(2,1)S(1)}, bf16[1024,2048]{1,0:T(8,128)(2,1)S(1)}) fusion(f32[1024,2048]{1,0:T(8,128)S(1)} %bitcast.469, f32[2048]{0:T(1024)S(1)} %bitcast.466, bf16[2048,512]{1,0:T(8,128)(2,1)S(1)} %bitcast.435, bf16[2048,512]{1,0:T(8,128)(2,1)S(1)} %bitcast.432, bf16[512,1024]{1,0:T(8,128)(2,1)} %collective-permute-done.33, ...), kind=kOutput, calls=%fused_computation.7 | convolution fusion | flops 4334811136 | bytes 18886656 | tf_op jit(solution)/shard_map/dot_general | solution.py:116
  360.4 6.4 convolution_convert_fusion.2
  376.4 5.1 multiply_convert_fusion.1
  381.9 15.3 %collective-permute-done.63 = bf16[2,2,2,64,1024]{4,3,1,0,2:T(8,128)(2,1)} collective-permute-done((bf16[2,2,2,64,1024]{4,3,1,0,2:T(8,128)(2,1)}, bf16[2,2,2,64,1024]{4,3,1,0,2:T(8,128)(2,1)}, u32[]{:S(2)}, u32[]{:S(2)}) %collective-permute-start.63) | collective-permute-done | bytes 1048608 | tf_op jit(solution)/shard_map/ppermute | solution.py:315
  412.3 6.3 collective-permute-done.68
  420.1 12.7 %collective-permute-done.65 = bf16[2,64,1024]{2,1,0:T(8,128)(2,1)S(1)} collective-permute-done((bf16[2,64,1024]{2,1,0:T(8,128)(2,1)S(1)}, bf16[2,64,1024]{2,1,0:T(8,128)(2,1)S(1)}, u32[]{:S(2)}, u32[]{:S(2)}) %collective-permute-start.65) | collective-permute-done | bytes 262176 | tf_op jit(solution)/shard_map/ppermute | solution.py:322
  432.9 5.5 collective-permute-done.69
  446.2 32.4 %attend_back.1 = bf16[1024,1536]{1,0:T(8,128)(2,1)S(1)} custom-call(s32[18]{0:T(128)S(1)} %pad_add_fusion.1.info, bf16[1024,1536]{1,0:T(8,128)(2,1)} %copy-done.4, bf16[1024,512]{1,0:T(8,128)(2,1)S(1)} %copy-done.3, bf16[1024,512]{1,0:T(8,128)(2,1)S(1)} %convolution_convert_fusion.4.grad, f32[8,1024]{1,0:T(8,128)S(1)} %broadcast_in_dim.76.seg, ...), custom_call_target="tpu_custom_call" | custom-call | flops 2684354560 | bytes 8388608 | tf_op jit(solution)/shard_map/attend_back/pallas_call | solution.py:283
  484.8 4.9 convolution_convert_fusion
  507.7 15.3 %collective-permute-done.54 = bf16[2,2,2,64,256]{4,3,1,0,2:T(8,128)(2,1)S(1)} collective-permute-done((bf16[2,2,2,64,256]{4,3,1,0,2:T(8,128)(2,1)S(1)}, bf16[2,2,2,64,256]{4,3,1,0,2:T(8,128)(2,1)S(1)}, u32[]{:S(2)}, u32[]{:S(2)}) %collective-permute-start.54) | collective-permute-done | bytes 262176 | tf_op jit(solution)/shard_map/ppermute | solution.py:315
  552.3 7.4 %concatenate.108 = bf16[1024,1664]{1,0:T(8,128)(2,1)} concatenate(bf16[1024,1536]{1,0:T(8,128)(2,1)S(1)} %copy-done.11, bf16[1024,1]{1,0:T(8,128)(2,1)} %stack.471, bf16[1024,1]{1,0:T(8,128)(2,1)} %stack.472, bf16[1024,1]{1,0:T(8,128)(2,1)} %bitcast.441, bf16[1024,1]{1,0:T(8,128)(2,1)} %bitcast.442, bf16[1024,1]{1,0:T(8,128)(2,1)} %stack.473, bf16[1024,1]{1,0:T(8,128)(2,1)} %stack.474, ...), dimensions={1} | concatenate | bytes 6815744 | tf_op jit(solution)/shard_map/concatenate | solution.py:602
  574.4 12.7 %collective-permute-done.38 = bf16[2,2,2,64,832]{4,3,2,1,0:T(8,128)(2,1)} collective-permute-done((bf16[2,2,2,64,832]{4,3,2,1,0:T(8,128)(2,1)}, bf16[2,2,2,64,832]{4,3,2,1,0:T(8,128)(2,1)}, u32[]{:S(2)}, u32[]{:S(2)}) %collective-permute-start.38) | collective-permute-done | bytes 852000 | tf_op jit(solution)/shard_map/ppermute | solution.py:322
  612.0 19.3 %collective-permute-done.50 = bf16[2,64,832]{1,2,0:T(8,128)(2,1)} collective-permute-done((bf16[2,64,832]{1,2,0:T(8,128)(2,1)}, bf16[2,64,832]{1,2,0:T(8,128)(2,1)}, u32[]{:S(2)}, u32[]{:S(2)}) %collective-permute-start.50) | collective-permute-done | bytes 213024 | tf_op jit(solution)/shard_map/ppermute | solution.py:322
  632.6 7.0 %collective-permute-done.40 = bf16[2,64,832]{1,2,0:T(8,128)(2,1)S(1)} collective-permute-done((bf16[2,64,832]{1,2,0:T(8,128)(2,1)S(1)}, bf16[2,64,832]{1,2,0:T(8,128)(2,1)S(1)}, u32[]{:S(2)}, u32[]{:S(2)}) %collective-permute-start.40) | collective-permute-done | bytes 213024 | tf_op jit(solution)/shard_map/ppermute | solution.py:322
  639.9 8.7 %collective-permute-done.41 = bf16[64,832]{0,1:T(8,128)(2,1)S(1)} collective-permute-done((bf16[64,832]{0,1:T(8,128)(2,1)S(1)}, bf16[64,832]{0,1:T(8,128)(2,1)S(1)}, u32[]{:S(2)}, u32[]{:S(2)}) %collective-permute-start.41) | collective-permute-done | bytes 106528 | tf_op jit(solution)/shard_map/ppermute | solution.py:322
  669.5 4.9 collective-permute-done.47
  (598 shorter events, 277.8 us)
Async XLA Ops:
  5.6 29.2 %collective-permute-start = (bf16[256,1024]{1,0:T(8,128)(2,1)}, bf16[256,1024]{1,0:T(8,128)(2,1)}, u32[]{:S(2)}, u32[]{:S(2)}) collective-permute-start(bf16[256,1024]{1,0:T(8,128)(2,1)} %get-tuple-element.322), channel_id=1, source_target_pairs={{0,2},{2,0},{1,3},{3,1},{4,6},{6,4},{5,7},{7,5},{8,10},{10,8},{9,1... | collective-permute-start | bytes 1572872 | tf_op jit(solution)/shard_map/ppermute | solution.py:315
  10.2 141.8 %collective-permute-start.32 = (bf16[256,1024]{1,0:T(8,128)(2,1)}, bf16[256,1024]{1,0:T(8,128)(2,1)S(1)}, u32[]{:S(2)}, u32[]{:S(2)}) collective-permute-start(bf16[256,1024]{1,0:T(8,128)(2,1)} %get-tuple-element.312), channel_id=1, source_target_pairs={{0,2},{2,0},{1,3},{3,1},{4,6},{6,4},{5,7},{7,5},{8,10},{10,8},{9,1... | collective-permute-start | bytes 1572872 | tf_op jit(solution)/shard_map/ppermute | solution.py:315
  28.7 60.4 %collective-permute-start.19 = (bf16[2,64,1024]{2,1,0:T(8,128)(2,1)S(1)}, bf16[2,64,1024]{2,1,0:T(8,128)(2,1)S(1)}, u32[]{:S(2)}, u32[]{:S(2)}) collective-permute-start(bf16[2,64,1024]{2,1,0:T(8,128)(2,1)S(1)} %pad_maximum_fusion.60), channel_id=1, source_target_pairs={{0,16},{4,20},{8,24},{12,28},{16,0},{20,4},{24,8},{28,12},{1,17},{... | collective-permute-start | bytes 786440 | tf_op jit(solution)/shard_map/ppermute | solution.py:322
  31.5 57.6 %collective-permute-start.15 = (bf16[2,64,1024]{2,1,0:T(8,128)(2,1)S(1)}, bf16[2,64,1024]{2,1,0:T(8,128)(2,1)S(1)}, u32[]{:S(2)}, u32[]{:S(2)}) collective-permute-start(bf16[2,64,1024]{2,1,0:T(8,128)(2,1)S(1)} %pad_maximum_fusion.59), channel_id=1, source_target_pairs={{0,16},{4,20},{8,24},{12,28},{16,0},{20,4},{24,8},{28,12},{1,17},{... | collective-permute-start | bytes 786440 | tf_op jit(solution)/shard_map/ppermute | solution.py:322
  31.9 42.2 %collective-permute-start.3 = (bf16[2,64,1088]{2,1,0:T(8,128)(2,1)S(1)}, bf16[2,64,1088]{2,1,0:T(8,128)(2,1)S(1)}, u32[]{:S(2)}, u32[]{:S(2)}) collective-permute-start(bf16[2,64,1088]{2,1,0:T(8,128)(2,1)S(1)} %pad_maximum_fusion.55), channel_id=1, source_target_pairs={{0,16},{4,20},{8,24},{12,28},{16,0},{20,4},{24,8},{28,12},{1,17},{... | collective-permute-start | bytes 835592 | tf_op jit(solution)/shard_map/ppermute | solution.py:322
  34.8 44.6 %collective-permute-start.8 = (bf16[2,64,1088]{2,1,0:T(8,128)(2,1)S(1)}, bf16[2,64,1088]{2,1,0:T(8,128)(2,1)S(1)}, u32[]{:S(2)}, u32[]{:S(2)}) collective-permute-start(bf16[2,64,1088]{2,1,0:T(8,128)(2,1)S(1)} %pad_maximum_fusion.56), channel_id=1, source_target_pairs={{0,16},{4,20},{8,24},{12,28},{16,0},{20,4},{24,8},{28,12},{1,17},{... | collective-permute-start | bytes 835592 | tf_op jit(solution)/shard_map/ppermute | solution.py:322
  87.9 33.2 %collective-permute-start.5 = (bf16[2,2,2,64,1088]{4,3,1,0,2:T(8,128)(2,1)S(1)}, bf16[2,2,2,64,1088]{4,3,1,0,2:T(8,128)(2,1)S(1)}, u32[]{:S(2)}, u32[]{:S(2)}) collective-permute-start(bf16[2,2,2,64,1088]{4,3,1,0,2:T(8,128)(2,1)S(1)} %pad_maximum_fusion.31), channel_id=1, source_target_pairs={{0,4},{4,0},{8,12},{12,8},{16,20},{20,16},{24,28},{28,24},{1,5},{5... | collective-permute-start | bytes 3342344 | tf_op jit(solution)/shard_map/ppermute | solution.py:322
  89.3 64.3 %collective-permute-start.20 = (bf16[2,2,64,1024]{3,2,1,0:T(8,128)(2,1)S(1)}, bf16[2,2,64,1024]{3,2,1,0:T(8,128)(2,1)S(1)}, u32[]{:S(2)}, u32[]{:S(2)}) collective-permute-start(bf16[2,2,64,1024]{3,2,1,0:T(8,128)(2,1)S(1)} %pad_maximum_fusion.45), channel_id=1, source_target_pairs={{0,2},{2,0},{1,3},{3,1},{4,6},{6,4},{5,7},{7,5},{8,10},{10,8},{9,1... | collective-permute-start | bytes 1572872 | tf_op jit(solution)/shard_map/ppermute | solution.py:315
  90.9 63.2 %collective-permute-start.16 = (bf16[2,2,64,1024]{3,2,1,0:T(8,128)(2,1)S(1)}, bf16[2,2,64,1024]{3,2,1,0:T(8,128)(2,1)S(1)}, u32[]{:S(2)}, u32[]{:S(2)}) collective-permute-start(bf16[2,2,64,1024]{3,2,1,0:T(8,128)(2,1)S(1)} %pad_maximum_fusion.44), channel_id=1, source_target_pairs={{0,4},{4,0},{8,12},{12,8},{16,20},{20,16},{24,28},{28,24},{1,5},{5... | collective-permute-start | bytes 1572872 | tf_op jit(solution)/shard_map/ppermute | solution.py:322
  96.1 28.9 %collective-permute-start.10 = (bf16[2,2,2,64,1088]{4,3,1,0,2:T(8,128)(2,1)S(1)}, bf16[2,2,2,64,1088]{4,3,1,0,2:T(8,128)(2,1)S(1)}, u32[]{:S(2)}, u32[]{:S(2)}) collective-permute-start(bf16[2,2,2,64,1088]{4,3,1,0,2:T(8,128)(2,1)S(1)} %pad_maximum_fusion.32), channel_id=1, source_target_pairs={{0,2},{2,0},{1,3},{3,1},{4,6},{6,4},{5,7},{7,5},{8,10},{10,8},{9,1... | collective-permute-start | bytes 3342344 | tf_op jit(solution)/shard_map/ppermute | solution.py:315
  153.2 41.0 %collective-permute-start.33 = (bf16[512,1024]{1,0:T(8,128)(2,1)}, bf16[512,1024]{1,0:T(8,128)(2,1)}, u32[]{:S(2)}, u32[]{:S(2)}) collective-permute-start(bf16[512,1024]{1,0:T(8,128)(2,1)} %get-tuple-element.308), channel_id=1, source_target_pairs={{0,1},{1,0},{2,3},{3,2},{4,5},{5,4},{6,7},{7,6},{8,9},{9,8},{10,11... | collective-permute-start | bytes 3145736 | tf_op jit(solution)/shard_map/ppermute | solution.py:311
  153.7 25.3 %collective-permute-start.21 = (bf16[2,2,2,64,1024]{4,3,1,0,2:T(8,128)(2,1)S(1)}, bf16[2,2,2,64,1024]{4,3,1,0,2:T(8,128)(2,1)S(1)}, u32[]{:S(2)}, u32[]{:S(2)}) collective-permute-start(bf16[2,2,2,64,1024]{4,3,1,0,2:T(8,128)(2,1)S(1)} %pad_maximum_fusion.35), channel_id=1, source_target_pairs={{0,4},{4,0},{8,12},{12,8},{16,20},{20,16},{24,28},{28,24},{1,5},{5... | collective-permute-start | bytes 3145736 | tf_op jit(solution)/shard_map/ppermute | solution.py:322
  154.2 25.9 %collective-permute-start.17 = (bf16[2,2,2,64,1024]{4,3,1,0,2:T(8,128)(2,1)S(1)}, bf16[2,2,2,64,1024]{4,3,1,0,2:T(8,128)(2,1)S(1)}, u32[]{:S(2)}, u32[]{:S(2)}) collective-permute-start(bf16[2,2,2,64,1024]{4,3,1,0,2:T(8,128)(2,1)S(1)} %pad_maximum_fusion.34), channel_id=1, source_target_pairs={{0,2},{2,0},{1,3},{3,1},{4,6},{6,4},{5,7},{7,5},{8,10},{10,8},{9,1... | collective-permute-start | bytes 3145736 | tf_op jit(solution)/shard_map/ppermute | solution.py:315
  159.6 24.8 %collective-permute-start.13 = (bf16[512,1024]{1,0:T(8,128)(2,1)}, bf16[512,1024]{1,0:T(8,128)(2,1)}, u32[]{:S(2)}, u32[]{:S(2)}) collective-permute-start(bf16[512,1024]{1,0:T(8,128)(2,1)} %add_convert_fusion.1), channel_id=1, source_target_pairs={{0,1},{1,0},{2,3},{3,2},{4,5},{5,4},{6,7},{7,6},{8,9},{9,8},{10,11... | collective-permute-start | bytes 3145736 | tf_op jit(solution)/shard_map/ppermute | solution.py:311
  202.9 24.5 %collective-permute-start.76 = (bf16[2,2,2,128,512]{4,3,1,0,2:T(8,128)(2,1)S(1)}, bf16[2,2,2,128,512]{4,3,1,0,2:T(8,128)(2,1)S(1)}, u32[]{:S(2)}, u32[]{:S(2)}) collective-permute-start(bf16[2,2,2,128,512]{4,3,1,0,2:T(8,128)(2,1)S(1)} %bitcast.444), channel_id=1, source_target_pairs={{0,4},{4,0},{8,12},{12,8},{16,20},{20,16},{24,28},{28,24},{1,5},{5... | collective-permute-start | bytes 3145736 | tf_op jit(solution)/shard_map/ppermute | solution.py:322
  204.2 25.8 %collective-permute-start.72 = (bf16[2,2,2,128,512]{4,3,1,0,2:T(8,128)(2,1)S(1)}, bf16[2,2,2,128,512]{4,3,1,0,2:T(8,128)(2,1)S(1)}, u32[]{:S(2)}, u32[]{:S(2)}) collective-permute-start(bf16[2,2,2,128,512]{4,3,1,0,2:T(8,128)(2,1)S(1)} %bitcast.443), channel_id=1, source_target_pairs={{0,2},{2,0},{1,3},{3,1},{4,6},{6,4},{5,7},{7,5},{8,10},{10,8},{9,1... | collective-permute-start | bytes 3145736 | tf_op jit(solution)/shard_map/ppermute | solution.py:315
  309.7 27.1 %collective-permute-start.25 = (bf16[2,2,2,128,512]{4,3,2,1,0:T(8,128)(2,1)}, bf16[2,2,2,128,512]{4,3,2,1,0:T(8,128)(2,1)}, u32[]{:S(2)}, u32[]{:S(2)}) collective-permute-start(bf16[2,2,2,128,512]{4,3,2,1,0:T(8,128)(2,1)} %pad_maximum_fusion.36), channel_id=1, source_target_pairs={{0,2},{2,0},{1,3},{3,1},{4,6},{6,4},{5,7},{7,5},{8,10},{10,8},{9,1... | collective-permute-start | bytes 3145736 | tf_op jit(solution)/shard_map/ppermute | solution.py:315
  347.2 29.2 %collective-permute-start.30 = (bf16[512,1024]{1,0:T(8,128)(2,1)}, bf16[512,1024]{1,0:T(8,128)(2,1)}, u32[]{:S(2)}, u32[]{:S(2)}) collective-permute-start(bf16[512,1024]{1,0:T(8,128)(2,1)} %fusion.33), channel_id=1, source_target_pairs={{0,1},{1,0},{2,3},{3,2},{4,5},{5,4},{6,7},{7,6},{8,9},{9,8},{10,11... | collective-permute-start | bytes 3145736 | tf_op jit(solution)/shard_map/ppermute | solution.py:311
  359.9 40.0 %collective-permute-start.34 = (bf16[512,1024]{1,0:T(8,128)(2,1)}, bf16[512,1024]{1,0:T(8,128)(2,1)}, u32[]{:S(2)}, u32[]{:S(2)}) collective-permute-start(bf16[512,1024]{1,0:T(8,128)(2,1)} %fusion.36), channel_id=1, source_target_pairs={{0,1},{1,0},{2,3},{3,2},{4,5},{5,4},{6,7},{7,6},{8,9},{9,8},{10,11... | collective-permute-start | bytes 3145736 | tf_op jit(solution)/shard_map/ppermute | solution.py:311
  370.8 26.3 %collective-permute-start.63 = (bf16[2,2,2,64,1024]{4,3,1,0,2:T(8,128)(2,1)}, bf16[2,2,2,64,1024]{4,3,1,0,2:T(8,128)(2,1)}, u32[]{:S(2)}, u32[]{:S(2)}) collective-permute-start(bf16[2,2,2,64,1024]{4,3,1,0,2:T(8,128)(2,1)} %bitcast.402), channel_id=1, source_target_pairs={{0,2},{2,0},{1,3},{3,1},{4,6},{6,4},{5,7},{7,5},{8,10},{10,8},{9,1... | collective-permute-start | bytes 3145736 | tf_op jit(solution)/shard_map/ppermute | solution.py:315
  374.7 29.5 %collective-permute-start.67 = (bf16[2,2,2,64,1024]{4,3,2,1,0:T(8,128)(2,1)S(1)}, bf16[2,2,2,64,1024]{4,3,2,1,0:T(8,128)(2,1)S(1)}, u32[]{:S(2)}, u32[]{:S(2)}) collective-permute-start(bf16[2,2,2,64,1024]{4,3,2,1,0:T(8,128)(2,1)S(1)} %dynamic-slice_bitcast_fusion), channel_id=1, source_target_pairs={{0,4},{4,0},{8,12},{12,8},{16,20},{20,16},{24,28},{28,24},{1,5},{5... | collective-permute-start | bytes 3145736 | tf_op jit(solution)/shard_map/ppermute | solution.py:322
  381.6 37.3 %collective-permute-start.31 = (bf16[256,1024]{1,0:T(8,128)(2,1)S(1)}, bf16[256,1024]{1,0:T(8,128)(2,1)S(1)}, u32[]{:S(2)}, u32[]{:S(2)}) collective-permute-start(bf16[256,1024]{1,0:T(8,128)(2,1)S(1)} %slice.240), channel_id=1, source_target_pairs={{0,2},{2,0},{1,3},{3,1},{4,6},{6,4},{5,7},{7,5},{8,10},{10,8},{9,1... | collective-permute-start | bytes 1572872 | tf_op jit(solution)/shard_map/ppermute | solution.py:315
  409.2 35.7 %collective-permute-start.35 = (bf16[512,1024]{1,0:T(8,128)(2,1)S(1)}, bf16[512,1024]{1,0:T(8,128)(2,1)S(1)}, u32[]{:S(2)}, u32[]{:S(2)}) collective-permute-start(bf16[512,1024]{1,0:T(8,128)(2,1)S(1)} %get-tuple-element.250), channel_id=1, source_target_pairs={{0,1},{1,0},{2,3},{3,2},{4,5},{5,4},{6,7},{7,6},{8,9},{9,8},{10,11... | collective-permute-start | bytes 3145736 | tf_op jit(solution)/shard_map/ppermute | solution.py:311
  444.8 52.4 %collective-permute-start.71 = (f32[32,2048]{1,0:T(8,128)}, f32[32,2048]{1,0:T(8,128)}, u32[]{:S(2)}, u32[]{:S(2)}) collective-permute-start(f32[32,2048]{1,0:T(8,128)} %fusion.63), channel_id=1, source_target_pairs={{0,1},{1,0},{2,3},{3,2},{4,5},{5,4},{6,7},{7,6},{8,9},{9,8},{10,11... | collective-permute-start | bytes 786440 | tf_op jit(solution)/shard_map/ppermute | solution.py:311
  482.0 59.3 %collective-permute-start.36 = (bf16[512,1024]{1,0:T(8,128)(2,1)}, bf16[512,1024]{1,0:T(8,128)(2,1)}, u32[]{:S(2)}, u32[]{:S(2)}) collective-permute-start(bf16[512,1024]{1,0:T(8,128)(2,1)} %fusion.30), channel_id=1, source_target_pairs={{0,1},{1,0},{2,3},{3,2},{4,5},{5,4},{6,7},{7,6},{8,9},{9,8},{10,11... | collective-permute-start | bytes 3145736 | tf_op jit(solution)/shard_map/ppermute | solution.py:311
  494.4 30.8 %collective-permute-start.48 = (bf16[2,2,2,64,832]{4,3,2,1,0:T(8,128)(2,1)}, bf16[2,2,2,64,832]{4,3,2,1,0:T(8,128)(2,1)}, u32[]{:S(2)}, u32[]{:S(2)}) collective-permute-start(bf16[2,2,2,64,832]{4,3,2,1,0:T(8,128)(2,1)} %get-tuple-element.290), channel_id=1, source_target_pairs={{0,2},{2,0},{1,3},{3,1},{4,6},{6,4},{5,7},{7,5},{8,10},{10,8},{9,1... | collective-permute-start | bytes 2555912 | tf_op jit(solution)/shard_map/ppermute | solution.py:315
  538.5 26.9 %collective-permute-start.57 = (bf16[64,256]{1,0:T(8,128)(2,1)S(1)}, bf16[64,256]{1,0:T(8,128)(2,1)}, u32[]{:S(2)}, u32[]{:S(2)}) collective-permute-start(bf16[64,256]{1,0:T(8,128)(2,1)S(1)} %dynamic-slice_bitcast_fusion.29), channel_id=1, source_target_pairs={{0,8},{4,12},{8,0},{12,4},{16,24},{20,28},{24,16},{28,20},{1,9},{5... | collective-permute-start | bytes 98312 | tf_op jit(solution)/shard_map/ppermute | solution.py:322
  540.5 25.7 %collective-permute-start.61 = (bf16[64,256]{1,0:T(8,128)(2,1)}, bf16[64,256]{1,0:T(8,128)(2,1)}, u32[]{:S(2)}, u32[]{:S(2)}) collective-permute-start(bf16[64,256]{1,0:T(8,128)(2,1)} %dynamic-slice_bitcast_fusion.28), channel_id=1, source_target_pairs={{0,8},{4,12},{8,0},{12,4},{16,24},{20,28},{24,16},{28,20},{1,9},{5... | collective-permute-start | bytes 98312 | tf_op jit(solution)/shard_map/ppermute | solution.py:322
  568.3 31.6 %collective-permute-start.49 = (bf16[2,2,64,832]{3,2,1,0:T(8,128)(2,1)}, bf16[2,2,64,832]{3,2,1,0:T(8,128)(2,1)}, u32[]{:S(2)}, u32[]{:S(2)}) collective-permute-start(bf16[2,2,64,832]{3,2,1,0:T(8,128)(2,1)} %bitcast.99), channel_id=1, source_target_pairs={{0,4},{4,0},{8,12},{12,8},{16,20},{20,16},{24,28},{28,24},{1,5},{5... | collective-permute-start | bytes 1277960 | tf_op jit(solution)/shard_map/ppermute | solution.py:322
  569.3 70.5 %collective-permute-start.37 = (bf16[256,1024]{1,0:T(8,128)(2,1)}, bf16[256,1024]{1,0:T(8,128)(2,1)S(1)}, u32[]{:S(2)}, u32[]{:S(2)}) collective-permute-start(bf16[256,1024]{1,0:T(8,128)(2,1)} %slice.246), channel_id=1, source_target_pairs={{0,2},{2,0},{1,3},{3,1},{4,6},{6,4},{5,7},{7,5},{8,10},{10,8},{9,1... | collective-permute-start | bytes 1572872 | tf_op jit(solution)/shard_map/ppermute | solution.py:315
  605.2 26.1 %collective-permute-start.50 = (bf16[2,64,832]{1,2,0:T(8,128)(2,1)}, bf16[2,64,832]{1,2,0:T(8,128)(2,1)}, u32[]{:S(2)}, u32[]{:S(2)}) collective-permute-start(bf16[2,64,832]{1,2,0:T(8,128)(2,1)} %dynamic-slice_bitcast_fusion.11), channel_id=1, source_target_pairs={{0,16},{4,20},{8,24},{12,28},{16,0},{20,4},{24,8},{28,12},{1,17},{... | collective-permute-start | bytes 638984 | tf_op jit(solution)/shard_map/ppermute | solution.py:322
  609.9 29.7 %collective-permute-start.40 = (bf16[2,64,832]{1,2,0:T(8,128)(2,1)S(1)}, bf16[2,64,832]{1,2,0:T(8,128)(2,1)S(1)}, u32[]{:S(2)}, u32[]{:S(2)}) collective-permute-start(bf16[2,64,832]{1,2,0:T(8,128)(2,1)S(1)} %dynamic-slice_bitcast_fusion.12), channel_id=1, source_target_pairs={{0,16},{4,20},{8,24},{12,28},{16,0},{20,4},{24,8},{28,12},{1,17},{... | collective-permute-start | bytes 638984 | tf_op jit(solution)/shard_map/ppermute | solution.py:322
  (131 other events, 1531.9 us)

commit v2 on v1

v2 whole, which is shorter than its diff:
```python
import functools
import math

import jax
import jax.numpy as jnp
from jax import lax
from jax.experimental import pallas as pl
from jax.experimental.pallas import tpu as pltpu
from jax.sharding import Mesh
from jax.sharding import PartitionSpec as P

HEADS = 16
GRID = 7
GRID_HI = 12
TILE = 128

PRECISE = lax.Precision.HIGHEST
FIRST_CORRECTION = 0.9999734386011124
SECOND_CORRECTION = 0.0952078528862911
EPS = 1e-06

F32 = jnp.float32
BF16 = jnp.bfloat16


def image_spans(res_row):
    side = jnp.where(res_row == 384, GRID_HI, jnp.where(res_row == 224, GRID, 0)).astype(jnp.int32)
    lengths = side * side
    slots = res_row.shape[0]
    order = jnp.arange(slots, dtype=jnp.int32)
    earlier = order[None, :] < order[:, None]
    starts = jnp.sum(jnp.where(earlier, lengths[None, :], 0), axis=1)
    return side, lengths, starts


def layout(res_row, positions):
    side, lengths, starts = image_spans(res_row)
    slots = res_row.shape[0]
    places = positions[:, None]
    inside = ((places >= starts[None, :]) & (places < (starts + lengths)[None, :])).astype(jnp.int32)
    usable = jnp.sum(inside, axis=1)
    image_number = jnp.arange(slots, dtype=jnp.int32)
    segment = jnp.sum(inside * image_number, axis=1) + (1 - usable) * slots
    start_of = jnp.sum(inside * starts[None, :], axis=1)
    side_of = jnp.sum(inside * side[None, :], axis=1)
    patch_index = (positions - start_of) * usable
    return segment, side_of, patch_index, usable


def key_bounds(res_row, row_len):
    _, lengths, starts = image_spans(res_row)
    total = jnp.sum(lengths)
    firsts = jnp.arange(row_len // TILE, dtype=jnp.int32) * TILE

    def span(positions):
        places = positions[:, None]
        inside = (places >= starts[None, :]) & (places < (starts + lengths)[None, :])
        found = positions < total
        begin = jnp.sum(jnp.where(inside, starts[None, :], 0), axis=1)
        end = jnp.sum(jnp.where(inside, (starts + lengths)[None, :], 0), axis=1)
        return jnp.where(found, begin, total), jnp.where(found, end, row_len)

    begin, _ = span(firsts)
    _, end = span(firsts + (TILE - 1))
    return begin // TILE, (end + TILE - 1) // TILE


def axis_weights(coord, side_of):
    scaled = jnp.maximum((2 * coord + 1) * GRID - GRID_HI, 0)
    lower_fine = scaled // (2 * GRID_HI)
    fraction_fine = (scaled - lower_fine * 2 * GRID_HI).astype(F32) / (2.0 * GRID_HI)
    resized = side_of == GRID_HI
    lower_cell = jnp.where(resized, lower_fine, coord)
    fraction = jnp.where(resized, fraction_fine, jnp.zeros_like(fraction_fine))
    upper_cell = jnp.minimum(lower_cell + 1, GRID - 1)
    cell_index = jnp.arange(GRID, dtype=jnp.int32)
    below = (cell_index == lower_cell[..., None]).astype(F32)
    above = (cell_index == upper_cell[..., None]).astype(F32)
    return (1.0 - fraction)[..., None] * below + fraction[..., None] * above


def table_weights(side_of, patch_index, usable):
    safe_side = jnp.maximum(side_of, 1)
    row_coord = patch_index // safe_side
    column_coord = patch_index % safe_side
    outer = axis_weights(row_coord, side_of)[:, :, None] * axis_weights(column_coord, side_of)[:, None, :]
    outer = outer * usable.astype(F32)[:, None, None]
    return outer.reshape(side_of.shape[0], GRID * GRID)


def place_of(block, own_y, own_c, per):
    quarter = block // per
    core = (quarter % 2 + own_c) % 2
    half = (quarter // 2 + own_y) % 2
    return (core * 2 + half) * per + block % per


def split_heads(pair):
    lane = lax.broadcasted_iota(jnp.int32, pair.shape, 1)
    zero = jnp.zeros_like(pair)
    low = lane < pair.shape[1] // 2
    return jnp.concatenate([jnp.where(low, pair, zero), jnp.where(low, zero, pair)], axis=0)


def join_heads(stacked):
    half = stacked.shape[0] // 2
    lane = lax.broadcasted_iota(jnp.int32, (half, stacked.shape[1]), 1)
    return jnp.where(lane < stacked.shape[1] // 2, stacked[:half], stacked[half:])


def down_lanes(row):
    return jnp.transpose(jnp.broadcast_to(row, (TILE, TILE)))


def nt(left, right):
    return lax.dot_general(left, right, (((1,), (1,)), ((), ())), preferred_element_type=F32)


def tn(left, right):
    return lax.dot_general(left, right, (((0,), (0,)), ((), ())), preferred_element_type=F32)


def nn(left, right):
    return jnp.dot(left, right, preferred_element_type=F32)


def fold(array, over):
    parts = array.reshape(array.shape[0] // 8, 8, array.shape[1])
    return jnp.max(parts, axis=0) if over == "max" else jnp.sum(parts, axis=0)


def same_segment(seg_down, chunk, seg_q):
    same = seg_down[chunk] == seg_q
    return jnp.concatenate([same, same], axis=1)


def fill_segments(seg, seg_down):
    chunks, span, _ = seg_down.shape
    for chunk in range(chunks):
        row = seg[0:1, chunk * span : (chunk + 1) * span]
        seg_down[chunk] = jnp.transpose(jnp.broadcast_to(row, (TILE, span)))


def join_turned(turned):
    half = turned.shape[1] // 2
    row = lax.broadcasted_iota(jnp.int32, (turned.shape[0], half), 0)
    return jnp.transpose(jnp.where(row < turned.shape[0] // 2, turned[:, :half], turned[:, half:]))


def columns_of(base, j):
    return slice(base + j * TILE, base + (j + 1) * TILE)


def attend_kernel(pairs, width, per, scale, info, qkv, seg, out, log_sum, scores, turned, seg_down):
    tile = pl.program_id(0)
    chunks, span, _ = seg_down.shape
    own_y, own_c = info[0], info[1]
    ratio = span // TILE
    first = info[2 + tile] // ratio
    last = (info[2 + pl.num_programs(0) + tile] + ratio - 1) // ratio

    def at(chunk):
        return pl.multiple_of(place_of(chunk * ratio, own_y, own_c, per) * TILE, TILE)

    @pl.when(tile == 0)
    def _():
        fill_segments(seg, seg_down)
        for chunk in range(chunks):
            for j in range(pairs):
                turned[chunk, j] = jnp.transpose(qkv[pl.ds(at(chunk), span), columns_of(2 * width, j)])

    q_at = pl.multiple_of(place_of(tile, own_y, own_c, per) * TILE, TILE)
    seg_q = seg[0:1, pl.ds(pl.multiple_of(tile * TILE, TILE), TILE)]
    queries = [
        split_heads(qkv[pl.ds(q_at, TILE), columns_of(0, j)] * jnp.asarray(scale, BF16)) for j in range(pairs)
    ]

    def score(chunk, high):
        same = same_segment(seg_down, chunk, seg_q)
        products = [nt(qkv[pl.ds(at(chunk), span), columns_of(width, j)], queries[j]) for j in range(pairs)]
        made = []
        for j in range(pairs):
            s = jnp.where(same, products[j], -1e30)
            scores[j, chunk] = s
            made.append(jnp.maximum(high[j], fold(s, "max")))
        return tuple(made)

    high = lax.fori_loop(first, last, score, (jnp.full((8, 2 * TILE), -1e30, F32),) * pairs)
    tops = [jnp.max(high[j], axis=0, keepdims=True) for j in range(pairs)]

    def mix(chunk, carry):
        total, mixed = carry
        powers = [jnp.exp(scores[j, chunk] - tops[j]) for j in range(pairs)]
        return (
            tuple(total[j] + fold(powers[j], "sum") for j in range(pairs)),
            tuple(mixed[j] + nn(turned[chunk, j], powers[j].astype(BF16)) for j in range(pairs)),
        )

    total, mixed = lax.fori_loop(
        first,
        last,
        mix,
        ((jnp.zeros((8, 2 * TILE), F32),) * pairs, (jnp.zeros((TILE, 2 * TILE), F32),) * pairs),
    )
    for j in range(pairs):
        sums = jnp.sum(total[j], axis=0, keepdims=True)
        out[:, columns_of(0, j)] = join_turned(mixed[j] / sums).astype(BF16)
        log_total = tops[j] + jnp.log(sums)
        log_sum[2 * j : 2 * j + 1] = log_total[:, :TILE]
        log_sum[2 * j + 1 : 2 * j + 2] = log_total[:, TILE:]


def attend_back_kernel(
    start, pairs, width, per, scale, info, qkv, mixed, grad, seg, log_sum, out, grad_keys, grad_values, turned, seg_down
):
    tile = pl.program_id(0)
    chunks, span, _ = seg_down.shape
    own_y, own_c = info[0], info[1]
    ratio = span // TILE
    first = info[2 + tile] // ratio
    last = (info[2 + pl.num_programs(0) + tile] + ratio - 1) // ratio
    heads = range(start, start + pairs)

    def at(chunk):
        return pl.multiple_of(place_of(chunk * ratio, own_y, own_c, per) * TILE, TILE)

    @pl.when(tile == 0)
    def _():
        fill_segments(seg, seg_down)
        grad_keys[...] = jnp.zeros_like(grad_keys)
        grad_values[...] = jnp.zeros_like(grad_values)
        for chunk in range(chunks):
            for i, j in enumerate(heads):
                turned[chunk, i] = jnp.transpose(qkv[pl.ds(at(chunk), span), columns_of(width, j)])

    q_at = pl.multiple_of(place_of(tile, own_y, own_c, per) * TILE, TILE)
    q_from = pl.multiple_of(tile * TILE, TILE)
    seg_q = seg[0:1, pl.ds(q_from, TILE)]
    queries, grads, logs, inner = [], [], [], []
    for j in heads:
        queries.append(split_heads(qkv[pl.ds(q_at, TILE), columns_of(0, j)] * jnp.asarray(scale, BF16)))
        g = grad[pl.ds(q_at, TILE), columns_of(0, j)]
        grads.append(split_heads(g))
        both = jnp.transpose(g.astype(F32) * mixed[pl.ds(q_at, TILE), columns_of(0, j)].astype(F32))
        low = jnp.sum(both[: TILE // 2], axis=0, keepdims=True)
        high = jnp.sum(both[TILE // 2 :], axis=0, keepdims=True)
        inner.append(jnp.concatenate([low, high], axis=1))
        here = log_sum[2 * j : 2 * j + 2, pl.ds(q_from, TILE)]
        logs.append(jnp.concatenate([here[0:1], here[1:2]], axis=1))

    def step(chunk, carry):
        k_at = at(chunk)
        same = same_segment(seg_down, chunk, seg_q)
        scores = [nt(qkv[pl.ds(k_at, span), columns_of(width, j)], queries[i]) for i, j in enumerate(heads)]
        slopes = [nt(qkv[pl.ds(k_at, span), columns_of(2 * width, j)], grads[i]) for i, j in enumerate(heads)]
        powers = [jnp.exp(jnp.where(same, scores[i], -1e30) - logs[i]) for i in range(pairs)]
        changes = [(powers[i] * (slopes[i] - inner[i])).astype(BF16) for i in range(pairs)]
        to_values = [nn(powers[i].astype(BF16), grads[i]) for i in range(pairs)]
        to_keys = [nn(changes[i], queries[i]) for i in range(pairs)]
        to_query = tuple(carry[i] + nn(turned[chunk, i], changes[i]) for i in range(pairs))
        for i in range(pairs):
            grad_values[chunk, :, columns_of(0, i)] += to_values[i]
            grad_keys[chunk, :, columns_of(0, i)] += to_keys[i]
        return to_query

    grad_query = lax.fori_loop(first, last, step, (jnp.zeros((TILE, 2 * TILE), F32),) * pairs)
    for i in range(pairs):
        out[pl.ds(q_at, TILE), columns_of(0, i)] = (join_turned(grad_query[i]) * scale).astype(BF16)

    @pl.when(tile == pl.num_programs(0) - 1)
    def _():
        all_heads = pairs * TILE
        for chunk in range(chunks):
            out[pl.ds(at(chunk), span), all_heads : 2 * all_heads] = grad_keys[chunk].astype(BF16)
            out[pl.ds(at(chunk), span), 2 * all_heads :] = grad_values[chunk].astype(BF16)


def attention(qkv, seg, info, per, head_size):
    length, width = qkv.shape[0], qkv.shape[1] // 3
    pairs, tiles = width // TILE, length // TILE
    span = per * TILE
    chunks = length // span
    scale = head_size ** (-0.5)

    def place(i, info):
        return place_of(i, info[0], info[1], per)

    return pl.pallas_call(
        functools.partial(attend_kernel, pairs, width, per, scale),
        name="attend",
        out_shape=(
            jax.ShapeDtypeStruct((length, width), BF16),
            jax.ShapeDtypeStruct((2 * pairs, length), F32),
        ),
        grid_spec=pltpu.PrefetchScalarGridSpec(
            num_scalar_prefetch=1,
            grid=(tiles,),
            in_specs=[
                pl.BlockSpec(qkv.shape, lambda i, info: (0, 0), pipeline_mode=pl.Buffered(1)),
                pl.BlockSpec(seg.shape, lambda i, info: (0, 0), pipeline_mode=pl.Buffered(1)),
            ],
            out_specs=[
                pl.BlockSpec((TILE, width), lambda i, info: (place(i, info), 0)),
                pl.BlockSpec((2 * pairs, TILE), lambda i, info: (0, i)),
            ],
            scratch_shapes=[
                pltpu.VMEM((pairs, chunks, span, 2 * TILE), F32),
                pltpu.VMEM((chunks, pairs, TILE, span), BF16),
                pltpu.VMEM((chunks, span, TILE), F32),
            ],
        ),
        compiler_params=pltpu.CompilerParams(
            dimension_semantics=("arbitrary",), vmem_limit_bytes=40 << 20
        ),
        cost_estimate=pl.CostEstimate(
            flops=length * length * width * 2, bytes_accessed=4 * length * width * 2, transcendentals=0
        ),
    )(info, qkv, seg)


def attention_back(part, parts, qkv, mixed, grad, seg, log_sum, info, per, head_size):
    length, width = qkv.shape[0], qkv.shape[1] // 3
    pairs, tiles = width // TILE // parts, length // TILE
    span = per * TILE
    chunks = length // span
    out = jax.ShapeDtypeStruct((length, 3 * pairs * TILE), BF16)
    scale = head_size ** (-0.5)

    def whole(array):
        return pl.BlockSpec(array.shape, lambda i, info: (0, 0), pipeline_mode=pl.Buffered(1))

    return pl.pallas_call(
        functools.partial(attend_back_kernel, part * pairs, pairs, width, per, scale),
        name="attend_back",
        out_shape=out,
        grid_spec=pltpu.PrefetchScalarGridSpec(
            num_scalar_prefetch=1,
            grid=(tiles,),
            in_specs=[whole(qkv), whole(mixed), whole(grad), whole(seg), whole(log_sum)],
            out_specs=pl.BlockSpec(out.shape, lambda i, info: (0, 0)),
            scratch_shapes=[
                pltpu.VMEM((chunks, span, pairs * TILE), F32),
                pltpu.VMEM((chunks, span, pairs * TILE), F32),
                pltpu.VMEM((chunks, pairs, TILE, span), BF16),
                pltpu.VMEM((chunks, span, TILE), F32),
            ],
        ),
        compiler_params=pltpu.CompilerParams(
            dimension_semantics=("arbitrary",), vmem_limit_bytes=48 << 20
        ),
        cost_estimate=pl.CostEstimate(
            flops=length * length * width * 5 // parts,
            bytes_accessed=8 * length * width * 2 // parts,
            transcendentals=0,
        ),
    )(info, qkv, mixed, grad, seg, log_sum)


SWAP = [(0, 1), (1, 0)]


def swap_core(array):
    return lax.ppermute(array, "sc", SWAP)


def swap_chip(array):
    return lax.ppermute(array, "sy", SWAP)


def swap_bit(array, bit):
    if bit == 0:
        return swap_chip(array)
    count = lax.axis_size("img")
    return lax.ppermute(array, "img", [(i, i ^ (1 << (bit - 1))) for i in range(count)])


def own_bit(bit):
    if bit == 0:
        return lax.axis_index("sy")
    return (lax.axis_index("img") >> (bit - 1)) & 1


def fence(*values):
    return lax.optimization_barrier(values)


def axis_of(bit, done):
    return sum(1 for other in done if other > bit)


def pick(index, low, high):
    return jnp.where(index == 0, low, high)


def far_bits():
    return list(range(2, int(math.log2(lax.axis_size("img"))) + 1))


def join(first, second, axis):
    shape = list(first.shape)
    shape[axis] += second.shape[axis]
    held = lax.dynamic_update_slice_in_dim(jnp.zeros(shape, first.dtype), first, 0, axis)
    return lax.dynamic_update_slice_in_dim(held, second, first.shape[axis], axis)


class Gather:
    def __init__(self, block, cut):
        self.rows, self.width, self.cut = block.shape[0], block.shape[1], cut
        self.steps = [*[(bit,) for bit in reversed(far_bits())], (1, 0), (0, 1)]
        self.held, self.done = [block], [[]]

    def send(self):
        bits = self.steps[0]
        if len(bits) > len(self.held):
            whole = self.held[0]
            self.held = [whole[..., : self.cut], whole[..., self.cut :]]
            self.done = [list(self.done[0]), list(self.done[0])]
        return [swap_bit(array, bit) for array, bit in zip(self.held, bits)]

    def take(self, came):
        bits = self.steps.pop(0)
        for i, bit in enumerate(bits):
            mine = own_bit(bit)
            low, high = pick(mine, self.held[i], came[i]), pick(mine, came[i], self.held[i])
            self.held[i] = jnp.stack([low, high], axis=axis_of(bit, self.done[i]))
            self.done[i].append(bit)

    def result(self):
        flat = [array.reshape(-1, array.shape[-1]) for array in self.held]
        return flat[0] if len(flat) == 1 else join(*flat, axis=1)


class Scatter:
    def __init__(self, left, right):
        far = far_bits()
        self.bits = [sorted([0, 1, *far], reverse=True) for _ in range(2)]
        count = len(self.bits[0])
        self.held = [
            array.astype(BF16).reshape((2,) * count + (array.shape[0] >> count, array.shape[1]))
            for array in (left, right)
        ]
        self.steps = [(0, 1), (1, 0), *[(bit,) for bit in far]]

    def send(self):
        bits = self.steps[0]
        if len(bits) < len(self.held):
            self.held = [join(*self.held, axis=self.held[0].ndim - 1)]
        return [
            swap_bit(lax.dynamic_index_in_dim(array, 1 - own_bit(bit), self.bits[i].index(bit), keepdims=False), bit)
            for i, (array, bit) in enumerate(zip(self.held, bits))
        ]

    def take(self, came):
        bits = self.steps.pop(0)
        for i, bit in enumerate(bits):
            keep = lax.dynamic_index_in_dim(self.held[i], own_bit(bit), self.bits[i].index(bit), keepdims=False)
            total = keep.astype(F32) + came[i].astype(F32)
            self.held[i] = total.astype(BF16) if self.steps else total
            self.bits[i].remove(bit)

    def result(self):
        return self.held[0]


def add_over(array, *bits):
    for bit in bits:
        own = array.astype(BF16)
        array = own.astype(F32) + (swap_core(own) if bit == "core" else swap_bit(own, bit)).astype(F32)
    return array


def phase(moves, work, *values):
    moves = [move if isinstance(move, tuple) else (move, 1) for move in moves]
    moves = [(move, min(count, len(move.steps))) for move, count in moves if move.steps]
    held, values = fence([move.held for move, _ in moves], values)
    came = []
    for (move, count), arrays in zip(moves, held):
        move.held = list(arrays)
        for _ in range(count - 1):
            move.take(move.send())
        came.append(move.send())
    made = work(*values) if work else ()
    came, made = fence(came, made)
    for (move, _), arrays in zip(moves, came):
        move.take(arrays)
    return made


def normalize(stream):
    center = jnp.mean(stream, axis=-1, keepdims=True)
    centered = stream - center
    spread = jnp.mean(centered * centered, axis=-1, keepdims=True)
    inverse = lax.rsqrt(spread + EPS)
    return centered * inverse, inverse


def normalize_back(normed, inverse, gain, grad):
    scaled = grad * gain
    middle = jnp.mean(scaled, axis=-1, keepdims=True)
    along = jnp.mean(scaled * normed, axis=-1, keepdims=True)
    return (
        inverse * (scaled - middle - normed * along),
        jnp.sum(grad * normed, axis=0, keepdims=True),
        jnp.sum(grad, axis=0, keepdims=True),
    )


def rows_from(columns, count):
    one_hot = (jnp.arange(16)[:, None] == jnp.arange(TILE)[None, :]).astype(BF16)
    rows = nt(one_hot, columns)
    return [rows[i : i + 1] for i in range(count)]


def column_choice(rows, columns):
    row, lane = jnp.arange(rows)[:, None], jnp.arange(TILE)[None, :]
    return (row == 8 + lane % columns).astype(F32)


def own_place(width, columns):
    per_run = TILE // columns
    row, lane = jnp.arange(width)[:, None], jnp.arange(TILE)[None, :]
    return row % per_run == lane // columns


def unroll_bias(columns, own_c, ff_rows):
    width, extra = columns.shape[0], 4
    spread = nn(columns, column_choice(TILE, extra).astype(BF16))
    runs = jnp.where(own_place(width, extra), spread, 0.0).reshape(-1, TILE // extra, TILE).sum(axis=1)
    runs = runs.reshape(-1, 2, ff_rows)
    return pick(own_c, runs[:, 0], runs[:, 1]).reshape(1, -1)


def roll_bias(sums, own_c, width, rows, ff_rows):
    extra = 4
    runs = sums.reshape(-1, ff_rows)
    zero = jnp.zeros_like(runs)
    runs = jnp.stack([pick(own_c, runs, zero), pick(own_c, zero, runs)], axis=1).reshape(-1, 1, TILE)
    spread = jnp.broadcast_to(runs, (runs.shape[0], TILE // extra, TILE)).reshape(width, TILE)
    spread = jnp.where(own_place(width, extra), spread, 0.0)
    return lax.dot_general(
        column_choice(rows, extra), spread, (((1,), (1,)), ((), ())), precision=PRECISE, preferred_element_type=F32
    )


def token_sums(array):
    return nn(jnp.ones((8, array.shape[0]), BF16), array)[:1]


def gelu_and_slope(values):
    cdf = 0.5 * (1.0 + lax.erf(values * (0.5**0.5)))
    density = jnp.exp(-0.5 * values * values) * (1.0 / math.sqrt(2.0 * math.pi))
    return values * cdf, cdf + values * density


def adam_update(weight, gradient, first_moment, second_moment, factor, decay):
    scaled = gradient * factor
    first_new = 0.9 * first_moment + 0.1 * scaled
    second_new = 0.999 * second_moment + 0.001 * scaled * scaled
    first_hat = first_new / FIRST_CORRECTION
    second_hat = second_new / SECOND_CORRECTION
    direction = first_hat / (jnp.sqrt(second_hat) + 1e-08) + decay * weight
    return (direction, first_new, second_new)


def per_device(
    patches,
    cotangent,
    res_ids,
    pos_table,
    attn_in,
    attn_out,
    mlp_in,
    mlp_out,
    vectors,
    first_attn_in,
    first_attn_out,
    first_mlp_in,
    first_mlp_out,
    first_vectors,
    second_attn_in,
    second_attn_out,
    second_mlp_in,
    second_mlp_out,
    second_vectors,
):
    row_count, local_len, width = patches.shape
    img_count, halves = lax.axis_size("img"), lax.axis_size("sy")
    chips = img_count * halves
    row_len = local_len * halves * 2
    slot_total = row_count * img_count * row_len
    head_size = width // HEADS
    own_y, own_c = lax.axis_index("sy"), lax.axis_index("sc")
    rows = attn_in.shape[0]
    half = width // 2
    ff_rows = mlp_out.shape[0]
    ff_half = chips * ff_rows
    table_size = GRID * GRID
    vector_count = vectors.shape[1]

    def to_rows(*arrays):
        mine = [lax.dynamic_index_in_dim(array, own_y, 0, keepdims=False) for array in arrays]
        other = [lax.dynamic_index_in_dim(array, 1 - own_y, 0, keepdims=False) for array in arrays]
        came = swap_chip(jnp.stack(other))
        return [join(mine[i], came[i], 0) for i in range(len(arrays))]

    def from_row(array):
        mine, other = array[:local_len], swap_chip(array[local_len:])
        return jnp.stack([pick(own_y, mine, other), pick(own_y, other, mine)], axis=0)

    res_row = lax.dynamic_index_in_dim(res_ids, own_y, 0, keepdims=False)
    all_positions = jnp.arange(row_len, dtype=jnp.int32)
    segment_all, _, _, _ = layout(res_row, all_positions)
    seg = jnp.broadcast_to(segment_all.astype(F32)[None, :], (8, row_len))
    begin, end = key_bounds(res_row, row_len)
    info = jnp.concatenate([jnp.stack([own_y, own_c]).astype(jnp.int32), begin, end])
    near = jnp.arange(local_len, dtype=jnp.int32)
    positions = jnp.concatenate(
        [(2 * own_y + own_c) * local_len + near, (2 * (1 - own_y) + own_c) * local_len + near]
    )
    _, side_of, patch_index, usable = layout(res_row, positions)
    place = table_weights(side_of, patch_index, usable)
    usable = usable.astype(F32)[:, None]

    def by_core(array, blocks):
        split = array.reshape(rows, blocks, 2, -1)
        low, high = split[:, :, 0].reshape(rows, -1), split[:, :, 1].reshape(rows, -1)
        return pick(own_c, low, high), pick(own_c, high, low)

    vector_pad = jnp.pad(vectors, ((0, 0), (0, TILE - vector_count))).astype(BF16)
    mine_in, away_in = by_core(attn_in.astype(BF16), 3)
    mine_out, away_out = by_core(attn_out.astype(BF16), 1)
    mine_up, away_up = by_core(mlp_in.astype(BF16), chips)
    came = swap_core(jnp.concatenate([away_in, vector_pad, away_out, away_up], axis=1))
    mine = jnp.concatenate([mine_in, vector_pad, mine_out, mine_up], axis=1)
    shard = jnp.concatenate([pick(own_c, mine, came), pick(own_c, came, mine)], axis=0)
    in_width = 3 * half
    head_end = in_width + TILE
    own = local_len * row_count
    per = local_len // TILE

    def cut_of(columns):
        return columns // (2 * TILE) * TILE

    def with_core(array):
        return join(array, swap_core(array), 0)

    def sum_core(left, weights, product):
        away = product(left[own:], weights).astype(BF16)
        came = swap_core(away)
        return product(left[:own], weights) + came.astype(F32)

    gather_in = Gather(shard[:, :head_end], cut_of(head_end))
    gather_up = Gather(shard[:, head_end:], cut_of(half + ff_half))
    gather_down = Gather(mlp_out.astype(BF16), cut_of(width))

    def first(patches, cotangent):
        patches, cotangent = to_rows(patches, cotangent)
        stream = patches.astype(F32) + jnp.dot(
            place, pos_table, precision=PRECISE, preferred_element_type=F32
        )
        hat_one, inverse_one = normalize(stream)
        grad_own = cotangent.astype(F32) * usable
        return stream, hat_one, inverse_one, grad_own, with_core(grad_own.astype(BF16))

    stream, hat_one, inverse_one, grad_own, grad_last = phase(
        [(gather_in, len(far_bits()))], first, patches, cotangent
    )
    phase([gather_in, gather_up], None)
    phase([gather_in, gather_up], None)
    attn_part = gather_in.result()
    in_matrix = attn_part[:, :in_width]
    vector_part = attn_part[:, in_width:]
    gain_one, shift_one, bias_query, bias_value, bias_out, gain_two, shift_two, bias_down = (
        rows_from(vector_part, 8)
    )
    bias_query = pick(own_c, bias_query[:, :half], bias_query[:, half:])
    bias_value = pick(own_c, bias_value[:, :half], bias_value[:, half:])
    bias_up = unroll_bias(vector_part, own_c, ff_rows)
    bias_qkv = jnp.concatenate([bias_query, jnp.zeros_like(bias_query), bias_value], axis=1)

    def project(hat_one, in_matrix):
        normed_one = with_core((hat_one * gain_one + shift_one).astype(BF16))
        return normed_one, (nn(normed_one, in_matrix) + bias_qkv).astype(BF16)

    normed_one, qkv = phase([gather_up, gather_down], project, hat_one, in_matrix)
    mixed, log_sum = phase(
        [gather_up, gather_down],
        lambda qkv: attention(qkv, seg, info, per, head_size),
        qkv,
    )
    while gather_up.steps:
        phase([gather_up, gather_down], None)
    up_part = gather_up.result()
    out_columns, up_matrix = up_part[:, :half], up_part[:, half:]

    def project_out(stream, mixed, out_columns):
        low, high = out_columns[:half], out_columns[half:]
        keep_out, came_out = pick(own_c, low, high), swap_core(pick(own_c, high, low))
        out_matrix = jnp.concatenate(
            [pick(own_c, keep_out, came_out), pick(own_c, came_out, keep_out)], axis=1
        )
        stream_two = stream + sum_core(mixed, out_matrix, nn) + bias_out
        hat_two, inverse_two = normalize(stream_two)
        normed_two = with_core((hat_two * gain_two + shift_two).astype(BF16))
        return out_matrix, stream_two, hat_two, inverse_two, normed_two

    out_matrix, stream_two, hat_two, inverse_two, normed_two = phase(
        [gather_down], project_out, stream, mixed, out_columns
    )

    def expand(normed_two, up_matrix, grad_last):
        hidden_pre = nn(normed_two, up_matrix) + bias_up
        hidden, slope = gelu_and_slope(hidden_pre)
        hidden = hidden.astype(BF16)
        cut = cut_of(width)
        return hidden, slope, tn(hidden, grad_last[:, :cut]).astype(BF16), tn(hidden, grad_last[:, cut:]).astype(BF16)

    hidden, slope, *grad_down = phase([gather_down], expand, normed_two, up_matrix, grad_last)
    while gather_down.steps:
        phase([gather_down], None)
    down_matrix = gather_down.result()

    scatter_down = Scatter(*grad_down)

    def hidden_back(grad_last, down_matrix, slope, normed_two):
        grad_pre = (nt(grad_last, down_matrix) * slope).astype(BF16)
        cut = cut_of(ff_half + half)
        return (
            grad_pre,
            tn(normed_two, grad_pre[:, :cut]).astype(BF16),
            tn(normed_two, grad_pre[:, cut:]).astype(BF16),
        )

    grad_pre, *grad_up = phase([scatter_down], hidden_back, grad_last, down_matrix, slope, normed_two)
    def norm_two_back(grad_pre, up_matrix, hat_two, inverse_two, grad_own):
        grad_normed_two = sum_core(grad_pre, up_matrix, nt)
        back_two, grad_gain_two, grad_shift_two = normalize_back(
            hat_two, inverse_two, gain_two, grad_normed_two
        )
        grad_two = grad_own + back_two
        grad_branch = grad_two.astype(BF16)
        return grad_two, with_core(grad_branch), grad_gain_two, grad_shift_two

    def finish_output(hidden, stream_two, down_matrix):
        last = sum_core(hidden, down_matrix, nn) + bias_down
        return ((stream_two + last) * usable).astype(BF16)

    (grad_two, grad_branch, grad_gain_two, grad_shift_two), output = phase(
        [scatter_down],
        lambda values, others: (norm_two_back(*values), finish_output(*others)),
        (grad_pre, up_matrix, hat_two, inverse_two, grad_own),
        (hidden, stream_two, down_matrix),
    )

    grad_rows = tn(mixed, grad_branch).astype(BF16)
    low, high = grad_rows[:, :half], grad_rows[:, half:]
    keep_rows, came_rows = pick(own_c, low, high), swap_core(pick(own_c, high, low))
    grad_out = join(pick(own_c, keep_rows, came_rows), pick(own_c, came_rows, keep_rows), 0)
    scatter_up = Scatter(grad_up[0], join(grad_up[1], grad_out, 1))

    def attention_grads(grad_branch, out_matrix, qkv, mixed, log_sum, normed_one):
        grad_mixed = nt(grad_branch, out_matrix).astype(BF16)
        grad_qkv = attention_back(0, 1, qkv, mixed, grad_mixed, seg, log_sum, info, per, head_size)
        cut = cut_of(in_width)
        return (
            grad_qkv,
            tn(normed_one, grad_qkv[:, :cut]).astype(BF16),
            tn(normed_one, grad_qkv[:, cut:]).astype(BF16),
        )

    grad_qkv, *grad_in = phase(
        [scatter_up, (scatter_down, 9)], attention_grads, grad_branch, out_matrix, qkv, mixed, log_sum, normed_one
    )
    scatter_in = Scatter(*grad_in)

    def widen(row):
        zero = jnp.zeros_like(row)
        return jnp.concatenate([pick(own_c, row, zero), pick(own_c, zero, row)], axis=1)

    narrow_rows = vector_count + table_size
    narrow_rows += -narrow_rows % 16

    def norm_one_back(grad_qkv, in_matrix, hat_one, inverse_one, grad_two, grad_pre, grad_branch, grad_last):
        grad_normed_one = sum_core(grad_qkv, in_matrix, nt)
        back_one, grad_gain_one, grad_shift_one = normalize_back(
            hat_one, inverse_one, gain_one, grad_normed_one
        )
        grad_stream = grad_two + back_one
        wide_place = jnp.pad(place, ((0, 0), (vector_count, narrow_rows - vector_count - table_size)))
        narrow = lax.dot_general(
            wide_place, grad_stream, (((0,), (0,)), ((), ())), precision=PRECISE, preferred_element_type=F32
        ) + roll_bias(token_sums(grad_pre), own_c, width, narrow_rows, ff_rows)
        sums = token_sums(grad_qkv)
        rows_of_sums = [
            grad_gain_one,
            grad_shift_one,
            widen(sums[:, :half]),
            widen(sums[:, 2 * half :]),
            token_sums(grad_branch[:own]),
            grad_gain_two,
            grad_shift_two,
            token_sums(grad_last[:own]),
        ]
        row = jnp.arange(narrow_rows)[:, None]
        for i, values in enumerate(rows_of_sums):
            narrow = jnp.where(row == i, values, narrow)
        return grad_stream, narrow

    scatters = [scatter_in, scatter_up]
    grad_stream, narrow = phase(
        scatters, norm_one_back, grad_qkv, in_matrix, hat_one, inverse_one, grad_two, grad_pre, grad_branch, grad_last
    )
    far = far_bits()
    (narrow,) = phase(scatters, lambda narrow: (add_over(narrow, "core", *far[1:]),), narrow)

    def send_back(narrow, output, grad_stream):
        return add_over(narrow, 0, 1), from_row(output), from_row(grad_stream.astype(BF16))

    narrow, output, input_grad = phase(scatters, send_back, narrow, output, grad_stream)
    (narrow,) = phase(scatters, lambda narrow: (add_over(narrow, *far[:1]),), narrow)
    while any(move.steps for move in scatters):
        phase(scatters, None)
    shard_down, shard_in = scatter_down.result(), scatter_in.result()
    shard_up, shard_out = scatter_up.result()[:, :ff_half], scatter_up.result()[:, ff_half:]

    def rows_of(array, core):
        return lax.dynamic_slice_in_dim(array, core * rows, rows, 0)

    def trade(array, blocks):
        away, keep = rows_of(array, 1 - own_c), rows_of(array, own_c)
        came = swap_core(away).reshape(rows, blocks, -1)
        keep = keep.reshape(rows, blocks, -1)
        both = jnp.stack([pick(own_c, keep, came), pick(own_c, came, keep)], axis=2)
        return both.reshape(rows, -1)

    grad_up_shard = trade(shard_up, chips)
    grad_out_shard = trade(shard_out, 1)
    grad_in_shard = trade(shard_in, 3)
    device = (lax.axis_index("img") * halves + own_y) * 2 + own_c
    grad_vectors_shard = lax.dynamic_slice_in_dim(narrow[:vector_count], device * rows, rows, 1).T
    table_grad = narrow[vector_count : vector_count + table_size]

    factor = jnp.float32(1.0 / slot_total)
    shards = (grad_in_shard, grad_out_shard, grad_up_shard, shard_down, grad_vectors_shard)
    weights = (attn_in, attn_out, mlp_in, mlp_out, vectors)
    firsts = (first_attn_in, first_attn_out, first_mlp_in, first_mlp_out, first_vectors)
    seconds = (second_attn_in, second_attn_out, second_mlp_in, second_mlp_out, second_vectors)
    decays = (0.05, 0.05, 0.05, 0.05, 0.0)
    updated = [
        adam_update(weights[i], shards[i], firsts[i], seconds[i], factor, decays[i]) for i in range(5)
    ]
    return (
        output,
        input_grad,
        table_grad,
        *shards,
        *(updated[i][0] for i in range(5)),
        *(updated[i][1] for i in range(5)),
        *(updated[i][2] for i in range(5)),
    )


def solution(mesh):
    img, seq = mesh.shape["img"], mesh.shape["seq"]
    inner = Mesh(mesh.devices.reshape(img, seq // 2, 2), ("img", "sy", "sc"))
    tokens = P("img", ("sy", "sc"), None)
    shard = P(("img", "sy", "sc"), None)
    return jax.shard_map(
        per_device,
        mesh=inner,
        in_specs=(tokens, tokens, P("img", None), P()) + (shard,) * 15,
        out_specs=(tokens, tokens, P()) + (shard,) * 20,
        check_vma=False,
    )
```

time: 687 us -> 449 us (0.65)
  waiting for transfers between devices: 343 us -> 201 us
  local copies, waits for them, and re-layouts: 79.2 us -> 25.8 us
  Pallas kernels: 50.5 us -> 31.8 us
  starting transfers between devices: 64.7 us -> 56.5 us
  matrix products: 74.6 us -> 67.5 us
    ppermute x45 -> x27, waiting for transfers between devices: 259 us -> 131 us  [swap_bit(): lax.ppermute(array, 'img', [(i, i ^ 1 << bit - 1) for i in range(count)])]
    ppermute x19 -> x16, waiting for transfers between devices: 81.2 us -> 66.6 us  [swap_chip(): return lax.ppermute(array, 'sy', SWAP)]
    pallas_call x1, Pallas kernels: 32.4 us -> 19 us  [attention_back(): pl.pallas_call(functools.partial(attend_back_kernel, part * pairs, pairs,...]
    dynamic_slice x18 -> x0, local copies, waits for them, and re-layouts: 11.3 us -> none  [the longest x8 5.7 us: scatter_chips(): away = lax.dynamic_index_in_dim(held, 1 - mine, axis, keepdims=False)]
    ppermute x5 -> x0, local copies, waits for them, and re-layouts: 10.1 us -> none  [the longest x2 5.04 us: swap_bit(): lax.ppermute(array, 'img', [(i, i ^ 1 << bit - 1) for i in range(count)])]
    another operation x22 -> x6, local copies, waits for them, and re-layouts: 10.1 us -> 0.81 us  [the longest x5 0.81 us: take(): self.held[i] = jnp.stack([low, high], axis=axis_of(bit, self.done[i]))]
    concatenate x1 -> x0, local copies, waits for them, and re-layouts: 7.44 us -> none  [per_device(): shard_in = scatter_all(jnp.concatenate([grad_in, narrow], axis=1))]
    dynamic_update_slice x0 -> x8, other arithmetic: none -> 7.17 us  [join(): lax.dynamic_update_slice_in_dim(held, second, first.shape[axis], axis)]
  transfers between devices with their start and end apart: 80 -> 58, of which waited for: 43 -> 31; matrix products, arithmetic and copies ran while one was open for 27% -> 21% of each run, Pallas kernels for 7% -> 7%
where the time goes in v2:
time: 449 us; the launch traced here: 441 us
  waiting for transfers between devices  201 us (45%)
  matrix products  67.5 us (15%)
  starting transfers between devices  56.5 us (13%)
  other arithmetic  55.1 us (12%)
  Pallas kernels  31.8 us (7%)
  local copies, waits for them, and re-layouts  25.8 us (6%)
    ppermute x27, waiting for transfers between devices, swap_bit(): lax.ppermute(array, 'img', [(i, i ^ 1 << bit - 1) for i in range(count)])  131 us
    ppermute x16, waiting for transfers between devices, swap_chip(): return lax.ppermute(array, 'sy', SWAP)  66.6 us
    ppermute x27, starting transfers between devices, swap_bit(): lax.ppermute(array, 'img', [(i, i ^ 1 << bit - 1) for i in range(count)])  36.1 us
    dot_general x11, matrix products, nn(): return jnp.dot(left, right, preferred_element_type=F32)  26.7 us
    dot_general x7, matrix products, nt(): lax.dot_general(left, right, (((1,), (1,)), ((), ())), preferred_element_...  19.2 us
    pallas_call x1, Pallas kernels, attention_back(): pl.pallas_call(functools.partial(attend_back_kernel, part * pairs, pairs,...  19 us
    ppermute x16, starting transfers between devices, swap_chip(): return lax.ppermute(array, 'sy', SWAP)  17.8 us
    dot_general x7, matrix products, tn(): lax.dot_general(left, right, (((0,), (0,)), ((), ())), preferred_element_...  17.5 us
  transfers between devices with their start and end apart: 58, of which 31 were waited for; matrix products, arithmetic and copies ran while one was open for 21% of the time, Pallas kernels for 7%

profile of v2, /device:TPU:0, one launch (start us, length us, event | category | flops | bytes accessed | tf_op | source)
XLA Modules:
  0.0 441.1 jit_solution(5138920312779618486)
XLA Ops:
  6.0 2.6 collective-permute-start.3
  8.6 2.6 collective-permute-start.1
  12.0 9.5 %collective-permute-done.1 = bf16[64,1664]{1,0:T(8,128)(2,1)S(1)} collective-permute-done((bf16[64,1664]{1,0:T(8,128)(2,1)S(1)}, bf16[64,1664]{1,0:T(8,128)(2,1)S(1)}, u32[]{:S(2)}, u32[]{:S(2)}) %collective-permute-start.1) | collective-permute-done | bytes 213024 | tf_op jit(solution)/shard_map/ppermute | solution.py:374
  22.3 10.1 %collective-permute-done.3 = bf16[2,256,1024]{2,1,0:T(8,128)(2,1)S(1)} collective-permute-done((bf16[2,256,1024]{2,1,0:T(8,128)(2,1)S(1)}, bf16[2,256,1024]{2,1,0:T(8,128)(2,1)S(1)}, u32[]{:S(2)}, u32[]{:S(2)}) %collective-permute-start.3) | collective-permute-done | bytes 1048608 | tf_op jit(solution)/shard_map/ppermute | solution.py:367
  47.3 15.2 %collective-permute-done.7 = bf16[64,2560]{1,0:T(8,128)(2,1)} collective-permute-done((bf16[64,2560]{1,0:T(8,128)(2,1)}, bf16[64,2560]{1,0:T(8,128)(2,1)}, u32[]{:S(2)}, u32[]{:S(2)}) %collective-permute-start.7) | collective-permute-done | bytes 327712 | tf_op jit(solution)/shard_map/ppermute | solution.py:374
  67.9 14.6 %collective-permute-done.10 = bf16[2,64,2560]{2,1,0:T(8,128)(2,1)S(1)} collective-permute-done((bf16[2,64,2560]{2,1,0:T(8,128)(2,1)S(1)}, bf16[2,64,2560]{2,1,0:T(8,128)(2,1)S(1)}, u32[]{:S(2)}, u32[]{:S(2)}) %collective-permute-start.10) | collective-permute-done | bytes 655392 | tf_op jit(solution)/shard_map/ppermute | solution.py:374
  95.3 4.7 %add_convert_fusion.qkv = bf16[1024,1536]{1,0:T(8,128)(2,1)S(1)} fusion(bf16[1024,1536]{1,0:T(8,128)(2,1)S(1)} %pad_maximum_fusion.2, f32[1536]{0:T(1024)S(1)} %maximum_reduce_fusion, bf16[512,1024]{1,0:T(8,128)(2,1)S(1)} %collective-permute-done.14, bf16[512,1024]{1,0:T(8,128)(2,1)S(1)} %add_convert_fusion.2), kind=kOutput, calls=%fused_computation.8 | convolution fusion | flops 3228565504 | bytes 8394752 | tf_op jit(solution)/shard_map/dot_general | solution.py:124
  101.7 6.9 %collective-permute-done.13 = bf16[128,1024]{1,0:T(8,128)(2,1)S(1)} collective-permute-done((bf16[128,1024]{1,0:T(8,128)(2,1)S(1)}, bf16[128,1024]{1,0:T(8,128)(2,1)S(1)}, u32[]{:S(2)}, u32[]{:S(2)}) %collective-permute-start.13) | collective-permute-done | bytes 262176 | tf_op jit(solution)/shard_map/ppermute | solution.py:374
  115.6 12.8 %attend.1 = (bf16[1024,512]{1,0:T(8,128)(2,1)S(1)}, f32[8,1024]{1,0:T(8,128)S(1)}) custom-call(s32[18]{0:T(128)S(1)} %pad_add_fusion.1.info, bf16[1024,1536]{1,0:T(8,128)(2,1)S(1)} %add_convert_fusion.qkv, f32[8,1024]{1,0:T(8,128)S(1)} %broadcast_in_dim.266.seg), custom_call_target="tpu_custom_call" | custom-call | flops 1073741824 | bytes 4194304 | tf_op jit(solution)/shard_map/attend/pallas_call | solution.py:288
  128.4 12.6 %collective-permute-done.15 = bf16[2,2,2,64,1280]{4,3,0,1,2:T(8,128)(2,1)S(1)} collective-permute-done((bf16[2,2,2,64,1280]{4,3,0,1,2:T(8,128)(2,1)S(1)}, bf16[2,2,2,64,1280]{4,3,0,1,2:T(8,128)(2,1)S(1)}, u32[]{:S(2)}, u32[]{:S(2)}) %collective-permute-start.15) | collective-permute-done | bytes 1310752 | tf_op jit(solution)/shard_map/ppermute | solution.py:367
  163.3 9.2 %collective-permute-done.18 = bf16[2,2,128,512]{3,2,1,0:T(8,128)(2,1)S(1)} collective-permute-done((bf16[2,2,128,512]{3,2,1,0:T(8,128)(2,1)S(1)}, bf16[2,2,128,512]{3,2,1,0:T(8,128)(2,1)S(1)}, u32[]{:S(2)}, u32[]{:S(2)}) %collective-permute-start.18) | collective-permute-done | bytes 524320 | tf_op jit(solution)/shard_map/ppermute | solution.py:374
  176.2 9.4 %fusion.3 = (f32[1024,2048]{1,0:T(8,128)}, bf16[1024,2048]{1,0:T(8,128)(2,1)S(1)}) fusion(f32[2048]{0:T(1024)S(1)} %bitcast.367, bf16[1024,1024]{1,0:T(8,128)(2,1)S(1)} %pad_maximum_fusion.7, bf16[1024,2048]{1,0:T(8,128)(2,1)S(1)} %pad_maximum_fusion), kind=kOutput, calls=%fused_computation.4 | convolution fusion | flops 4318035968 | bytes 18882560 | tf_op jit(solution)/shard_map/dot_general | solution.py:124
  190.6 7.5 %collective-permute-done.23 = bf16[2,2,2,128,512]{4,3,2,1,0:T(8,128)(2,1)S(1)} collective-permute-done((bf16[2,2,2,128,512]{4,3,2,1,0:T(8,128)(2,1)S(1)}, bf16[2,2,2,128,512]{4,3,2,1,0:T(8,128)(2,1)S(1)}, u32[]{:S(2)}, u32[]{:S(2)}) %collective-permute-start.23) | collective-permute-done | bytes 1048608 | tf_op jit(solution)/shard_map/ppermute | solution.py:367
  200.4 2.6 pad_maximum_fusion.1
  206.4 8.3 %multiply_convert_fusion = bf16[1024,2048]{1,0:T(8,128)(2,1)S(1)} fusion(f32[1024,2048]{1,0:T(8,128)} %get-tuple-element.228, bf16[1024,1024]{1,0:T(8,128)(2,1)S(1)} %copy-done.14, bf16[2048,1024]{1,0:T(8,128)(2,1)} %pad_maximum_fusion.1), kind=kOutput, calls=%fused_computation.5 | convolution fusion | flops 4299161600 | bytes 18874368 | tf_op jit(solution)/shard_map/dot_general | solution.py:116
  214.7 3.1 convolution_convert_fusion.5
  217.7 4.5 %convolution_convert_fusion = bf16[1024,1280]{1,0:T(8,128)(2,1)} fusion(bf16[1024,1024]{1,0:T(8,128)(2,1)S(1)} %copy-done.37, bf16[1024,2048]{1,0:T(8,128)(2,1)S(1)} %multiply_convert_fusion), kind=kOutput, calls=%fused_computation.11 | convolution fusion | flops 2685665280 | bytes 7340032 | tf_op jit(solution)/shard_map/dot_general | solution.py:120
  222.3 5.0 %collective-permute-done.26 = bf16[2,2,2,128,512]{4,3,0,1,2:T(8,128)(2,1)} collective-permute-done((bf16[2,2,2,128,512]{4,3,0,1,2:T(8,128)(2,1)}, bf16[2,2,2,128,512]{4,3,0,1,2:T(8,128)(2,1)}, u32[]{:S(2)}, u32[]{:S(2)}) %collective-permute-start.26) | collective-permute-done | bytes 1048608 | tf_op jit(solution)/shard_map/ppermute | solution.py:374
  238.4 3.0 multiply_reduce_fusion.2
  246.1 3.5 multiply_convert_fusion.2
  249.8 8.0 %collective-permute-done.28 = bf16[2,2,128,512]{3,2,0,1:T(8,128)(2,1)S(1)} collective-permute-done((bf16[2,2,128,512]{3,2,0,1:T(8,128)(2,1)S(1)}, bf16[2,2,128,512]{3,2,0,1:T(8,128)(2,1)S(1)}, u32[]{:S(2)}, u32[]{:S(2)}) %collective-permute-start.28) | collective-permute-done | bytes 524320 | tf_op jit(solution)/shard_map/ppermute | solution.py:367
  274.3 19.0 %attend_back.1 = bf16[1024,1536]{1,0:T(8,128)(2,1)S(1)} custom-call(s32[18]{0:T(128)S(1)} %pad_add_fusion.1.info, bf16[1024,1536]{1,0:T(8,128)(2,1)} %copy-done.2, bf16[1024,512]{1,0:T(8,128)(2,1)S(1)} %get-tuple-element.261.mixed, bf16[1024,512]{1,0:T(8,128)(2,1)S(1)} %convolution_convert_fusion.6.grad, f32[8,1024]{1,0:T(8,128)S(1)} %broadcast_in_dim.266.seg, ...), custom_call_target="tpu_custom_call" | custom-call | flops 2684354560 | bytes 8388608 | tf_op jit(solution)/shard_map/attend_back/pallas_call | solution.py:332
  296.5 2.6 collective-permute-start.36
  301.0 9.9 %collective-permute-done.36 = bf16[128,1024]{1,0:T(8,128)(2,1)S(1)} collective-permute-done((bf16[128,1024]{1,0:T(8,128)(2,1)S(1)}, bf16[128,1024]{1,0:T(8,128)(2,1)S(1)}, u32[]{:S(2)}, u32[]{:S(2)}) %collective-permute-start.36) | collective-permute-done | bytes 262176 | tf_op jit(solution)/shard_map/ppermute | solution.py:374
  330.2 21.9 %collective-permute-done.39 = bf16[2,2,64,1280]{3,2,1,0:T(8,128)(2,1)S(1)} collective-permute-done((bf16[2,2,64,1280]{3,2,1,0:T(8,128)(2,1)S(1)}, bf16[2,2,64,1280]{3,2,1,0:T(8,128)(2,1)S(1)}, u32[]{:S(2)}, u32[]{:S(2)}) %collective-permute-start.39) | collective-permute-done | bytes 655392 | tf_op jit(solution)/shard_map/ppermute | solution.py:374
  355.9 3.2 collective-permute-start.46
  360.6 11.1 %collective-permute-done.46 = bf16[64,1024]{1,0:T(8,128)(2,1)S(1)} collective-permute-done((bf16[64,1024]{1,0:T(8,128)(2,1)S(1)}, bf16[64,1024]{1,0:T(8,128)(2,1)S(1)}, u32[]{:S(2)}, u32[]{:S(2)}) %collective-permute-start.46) | collective-permute-done | bytes 131104 | tf_op jit(solution)/shard_map/ppermute | solution.py:374
  379.3 22.8 %collective-permute-done.49 = bf16[64,1024]{1,0:T(8,128)(2,1)S(1)} collective-permute-done((bf16[64,1024]{1,0:T(8,128)(2,1)S(1)}, bf16[64,1024]{1,0:T(8,128)(2,1)S(1)}, u32[]{:S(2)}, u32[]{:S(2)}) %collective-permute-start.49) | collective-permute-done | bytes 131104 | tf_op jit(solution)/shard_map/ppermute | solution.py:367
  409.6 10.1 %collective-permute-done.48 = bf16[64,2560]{1,0:T(8,128)(2,1)S(1)} collective-permute-done((bf16[64,2560]{1,0:T(8,128)(2,1)S(1)}, bf16[64,2560]{1,0:T(8,128)(2,1)S(1)}, u32[]{:S(2)}, u32[]{:S(2)}) %collective-permute-start.48) | collective-permute-done | bytes 327712 | tf_op jit(solution)/shard_map/ppermute | solution.py:374
  420.8 3.0 collective-permute-start.53
  424.8 3.8 collective-permute-done.54
  428.7 4.2 collective-permute-done.53
  (474 shorter events, 170.5 us)
Async XLA Ops:
  6.0 26.4 %collective-permute-start.3 = (bf16[2,256,1024]{2,1,0:T(8,128)(2,1)S(1)}, bf16[2,256,1024]{2,1,0:T(8,128)(2,1)S(1)}, u32[]{:S(2)}, u32[]{:S(2)}) collective-permute-start(bf16[2,256,1024]{2,1,0:T(8,128)(2,1)S(1)} %pad_maximum_fusion.16), channel_id=1, source_target_pairs={{0,2},{2,0},{1,3},{3,1},{4,6},{6,4},{5,7},{7,5},{8,10},{10,8},{9,1... | collective-permute-start | bytes 3145736 | tf_op jit(solution)/shard_map/ppermute | solution.py:367
  21.5 18.2 %collective-permute-start.2 = (bf16[2,64,1664]{2,1,0:T(8,128)(2,1)S(1)}, bf16[2,64,1664]{2,1,0:T(8,128)(2,1)S(1)}, u32[]{:S(2)}, u32[]{:S(2)}) collective-permute-start(bf16[2,64,1664]{2,1,0:T(8,128)(2,1)S(1)} %pad_maximum_fusion.30), channel_id=1, source_target_pairs={{0,8},{4,12},{8,0},{12,4},{16,24},{20,28},{24,16},{28,20},{1,9},{5... | collective-permute-start | bytes 1277960 | tf_op jit(solution)/shard_map/ppermute | solution.py:374
  40.7 21.8 %collective-permute-start.6 = (bf16[2,2,64,896]{3,2,0,1:T(8,128)(2,1)}, bf16[2,2,64,896]{3,2,0,1:T(8,128)(2,1)}, u32[]{:S(2)}, u32[]{:S(2)}) collective-permute-start(bf16[2,2,64,896]{3,2,0,1:T(8,128)(2,1)} %slice.217), channel_id=1, source_target_pairs={{0,2},{2,0},{1,3},{3,1},{4,6},{6,4},{5,7},{7,5},{8,10},{10,8},{9,1... | collective-permute-start | bytes 1376264 | tf_op jit(solution)/shard_map/ppermute | solution.py:367
  43.2 19.3 %collective-permute-start.5 = (bf16[2,2,64,768]{3,2,0,1:T(8,128)(2,1)}, bf16[2,2,64,768]{3,2,0,1:T(8,128)(2,1)}, u32[]{:S(2)}, u32[]{:S(2)}) collective-permute-start(bf16[2,2,64,768]{3,2,0,1:T(8,128)(2,1)} %slice.216), channel_id=1, source_target_pairs={{0,4},{4,0},{8,12},{12,8},{16,20},{20,16},{24,28},{28,24},{1,5},{5... | collective-permute-start | bytes 1179656 | tf_op jit(solution)/shard_map/ppermute | solution.py:374
  44.7 17.8 %collective-permute-start.7 = (bf16[64,2560]{1,0:T(8,128)(2,1)}, bf16[64,2560]{1,0:T(8,128)(2,1)}, u32[]{:S(2)}, u32[]{:S(2)}) collective-permute-start(bf16[64,2560]{1,0:T(8,128)(2,1)} %pad_maximum_fusion.31), channel_id=1, source_target_pairs={{0,16},{4,20},{8,24},{12,28},{16,0},{20,4},{24,8},{28,12},{1,17},{... | collective-permute-start | bytes 983048 | tf_op jit(solution)/shard_map/ppermute | solution.py:374
  66.1 21.4 %collective-permute-start.9 = (bf16[2,2,2,64,896]{4,3,0,1,2:T(8,128)(2,1)S(1)}, bf16[2,2,2,64,896]{4,3,0,1,2:T(8,128)(2,1)S(1)}, u32[]{:S(2)}, u32[]{:S(2)}) collective-permute-start(bf16[2,2,2,64,896]{4,3,0,1,2:T(8,128)(2,1)S(1)} %pad_maximum_fusion.23), channel_id=1, source_target_pairs={{0,4},{4,0},{8,12},{12,8},{16,20},{20,16},{24,28},{28,24},{1,5},{5... | collective-permute-start | bytes 2752520 | tf_op jit(solution)/shard_map/ppermute | solution.py:374
  66.7 18.3 %collective-permute-start.8 = (bf16[2,2,2,64,768]{4,3,0,1,2:T(8,128)(2,1)S(1)}, bf16[2,2,2,64,768]{4,3,0,1,2:T(8,128)(2,1)S(1)}, u32[]{:S(2)}, u32[]{:S(2)}) collective-permute-start(bf16[2,2,2,64,768]{4,3,0,1,2:T(8,128)(2,1)S(1)} %pad_maximum_fusion.25), channel_id=1, source_target_pairs={{0,2},{2,0},{1,3},{3,1},{4,6},{6,4},{5,7},{7,5},{8,10},{10,8},{9,1... | collective-permute-start | bytes 2359304 | tf_op jit(solution)/shard_map/ppermute | solution.py:367
  67.2 15.4 %collective-permute-start.10 = (bf16[2,64,2560]{2,1,0:T(8,128)(2,1)S(1)}, bf16[2,64,2560]{2,1,0:T(8,128)(2,1)S(1)}, u32[]{:S(2)}, u32[]{:S(2)}) collective-permute-start(bf16[2,64,2560]{2,1,0:T(8,128)(2,1)S(1)} %pad_maximum_fusion.26), channel_id=1, source_target_pairs={{0,8},{4,12},{8,0},{12,4},{16,24},{20,28},{24,16},{28,20},{1,9},{5... | collective-permute-start | bytes 1966088 | tf_op jit(solution)/shard_map/ppermute | solution.py:374
  92.7 17.2 %collective-permute-start.11 = (bf16[2,2,64,1280]{3,2,0,1:T(8,128)(2,1)S(1)}, bf16[2,2,64,1280]{3,2,0,1:T(8,128)(2,1)S(1)}, u32[]{:S(2)}, u32[]{:S(2)}) collective-permute-start(bf16[2,2,64,1280]{3,2,0,1:T(8,128)(2,1)S(1)} %get-tuple-element.403), channel_id=1, source_target_pairs={{0,4},{4,0},{8,12},{12,8},{16,20},{20,16},{24,28},{28,24},{1,5},{5... | collective-permute-start | bytes 1966088 | tf_op jit(solution)/shard_map/ppermute | solution.py:374
  93.4 16.9 %collective-permute-start.12 = (bf16[2,2,64,1280]{3,2,0,1:T(8,128)(2,1)S(1)}, bf16[2,2,64,1280]{3,2,0,1:T(8,128)(2,1)S(1)}, u32[]{:S(2)}, u32[]{:S(2)}) collective-permute-start(bf16[2,2,64,1280]{3,2,0,1:T(8,128)(2,1)S(1)} %get-tuple-element.402), channel_id=1, source_target_pairs={{0,2},{2,0},{1,3},{3,1},{4,6},{6,4},{5,7},{7,5},{8,10},{10,8},{9,1... | collective-permute-start | bytes 1966088 | tf_op jit(solution)/shard_map/ppermute | solution.py:367
  110.8 30.2 %collective-permute-start.15 = (bf16[2,2,2,64,1280]{4,3,0,1,2:T(8,128)(2,1)S(1)}, bf16[2,2,2,64,1280]{4,3,0,1,2:T(8,128)(2,1)S(1)}, u32[]{:S(2)}, u32[]{:S(2)}) collective-permute-start(bf16[2,2,2,64,1280]{4,3,0,1,2:T(8,128)(2,1)S(1)} %pad_maximum_fusion.14), channel_id=1, source_target_pairs={{0,2},{2,0},{1,3},{3,1},{4,6},{6,4},{5,7},{7,5},{8,10},{10,8},{9,1... | collective-permute-start | bytes 3932168 | tf_op jit(solution)/shard_map/ppermute | solution.py:367
  111.5 29.8 %collective-permute-start.16 = (bf16[2,2,2,64,1280]{4,3,0,1,2:T(8,128)(2,1)S(1)}, bf16[2,2,2,64,1280]{4,3,0,1,2:T(8,128)(2,1)S(1)}, u32[]{:S(2)}, u32[]{:S(2)}) collective-permute-start(bf16[2,2,2,64,1280]{4,3,0,1,2:T(8,128)(2,1)S(1)} %pad_maximum_fusion.15), channel_id=1, source_target_pairs={{0,4},{4,0},{8,12},{12,8},{16,20},{20,16},{24,28},{28,24},{1,5},{5... | collective-permute-start | bytes 3932168 | tf_op jit(solution)/shard_map/ppermute | solution.py:374
  174.0 24.1 %collective-permute-start.23 = (bf16[2,2,2,128,512]{4,3,2,1,0:T(8,128)(2,1)S(1)}, bf16[2,2,2,128,512]{4,3,2,1,0:T(8,128)(2,1)S(1)}, u32[]{:S(2)}, u32[]{:S(2)}) collective-permute-start(bf16[2,2,2,128,512]{4,3,2,1,0:T(8,128)(2,1)S(1)} %pad_maximum_fusion.19), channel_id=1, source_target_pairs={{0,2},{2,0},{1,3},{3,1},{4,6},{6,4},{5,7},{7,5},{8,10},{10,8},{9,1... | collective-permute-start | bytes 3145736 | tf_op jit(solution)/shard_map/ppermute | solution.py:367
  175.6 23.8 %collective-permute-start.24 = (bf16[2,2,2,128,512]{4,3,1,0,2:T(8,128)(2,1)S(1)}, bf16[2,2,2,128,512]{4,3,1,0,2:T(8,128)(2,1)S(1)}, u32[]{:S(2)}, u32[]{:S(2)}) collective-permute-start(bf16[2,2,2,128,512]{4,3,1,0,2:T(8,128)(2,1)S(1)} %pad_maximum_fusion.20), channel_id=1, source_target_pairs={{0,4},{4,0},{8,12},{12,8},{16,20},{20,16},{24,28},{28,24},{1,5},{5... | collective-permute-start | bytes 3145736 | tf_op jit(solution)/shard_map/ppermute | solution.py:374
  204.1 23.2 %collective-permute-start.26 = (bf16[2,2,2,128,512]{4,3,0,1,2:T(8,128)(2,1)}, bf16[2,2,2,128,512]{4,3,0,1,2:T(8,128)(2,1)}, u32[]{:S(2)}, u32[]{:S(2)}) collective-permute-start(bf16[2,2,2,128,512]{4,3,0,1,2:T(8,128)(2,1)} %copy_bitcast_fusion.1), channel_id=1, source_target_pairs={{0,4},{4,0},{8,12},{12,8},{16,20},{20,16},{24,28},{28,24},{1,5},{5... | collective-permute-start | bytes 3145736 | tf_op jit(solution)/shard_map/ppermute | solution.py:374
  205.8 22.9 %collective-permute-start.25 = (bf16[2,2,2,128,512]{4,3,0,1,2:T(8,128)(2,1)}, bf16[2,2,2,128,512]{4,3,0,1,2:T(8,128)(2,1)}, u32[]{:S(2)}, u32[]{:S(2)}) collective-permute-start(bf16[2,2,2,128,512]{4,3,0,1,2:T(8,128)(2,1)} %copy_bitcast_fusion.2), channel_id=1, source_target_pairs={{0,2},{2,0},{1,3},{3,1},{4,6},{6,4},{5,7},{7,5},{8,10},{10,8},{9,1... | collective-permute-start | bytes 3145736 | tf_op jit(solution)/shard_map/ppermute | solution.py:367
  265.8 29.4 %collective-permute-start.35 = (bf16[2,128,1024]{2,1,0:T(8,128)(2,1)S(1)}, bf16[2,128,1024]{2,1,0:T(8,128)(2,1)}, u32[]{:S(2)}, u32[]{:S(2)}) collective-permute-start(bf16[2,128,1024]{2,1,0:T(8,128)(2,1)S(1)} %dynamic-slice_bitcast_fusion.4), channel_id=1, source_target_pairs={{0,8},{4,12},{8,0},{12,4},{16,24},{20,28},{24,16},{28,20},{1,9},{5... | collective-permute-start | bytes 1572872 | tf_op jit(solution)/shard_map/ppermute | solution.py:374
  268.9 42.0 %collective-permute-start.34 = (bf16[2,2,2,64,1280]{4,3,1,0,2:T(8,128)(2,1)}, bf16[2,2,2,64,1280]{4,3,1,0,2:T(8,128)(2,1)}, u32[]{:S(2)}, u32[]{:S(2)}) collective-permute-start(bf16[2,2,2,64,1280]{4,3,1,0,2:T(8,128)(2,1)} %copy_bitcast_fusion), channel_id=1, source_target_pairs={{0,4},{4,0},{8,12},{12,8},{16,20},{20,16},{24,28},{28,24},{1,5},{5... | collective-permute-start | bytes 3932168 | tf_op jit(solution)/shard_map/ppermute | solution.py:374
  271.6 39.3 %collective-permute-start.33 = (bf16[2,2,2,64,1280]{4,3,2,1,0:T(8,128)(2,1)}, bf16[2,2,2,64,1280]{4,3,2,1,0:T(8,128)(2,1)}, u32[]{:S(2)}, u32[]{:S(2)}) collective-permute-start(bf16[2,2,2,64,1280]{4,3,2,1,0:T(8,128)(2,1)} %dynamic-slice_bitcast_fusion), channel_id=1, source_target_pairs={{0,2},{2,0},{1,3},{3,1},{4,6},{6,4},{5,7},{7,5},{8,10},{10,8},{9,1... | collective-permute-start | bytes 3932168 | tf_op jit(solution)/shard_map/ppermute | solution.py:367
  318.1 34.5 %collective-permute-start.38 = (bf16[2,2,2,64,768]{4,3,0,1,2:T(8,128)(2,1)S(1)}, bf16[2,2,2,64,768]{4,3,0,1,2:T(8,128)(2,1)S(1)}, u32[]{:S(2)}, u32[]{:S(2)}) collective-permute-start(bf16[2,2,2,64,768]{4,3,0,1,2:T(8,128)(2,1)S(1)} %copy_bitcast_fusion.3), channel_id=1, source_target_pairs={{0,4},{4,0},{8,12},{12,8},{16,20},{20,16},{24,28},{28,24},{1,5},{5... | collective-permute-start | bytes 2359304 | tf_op jit(solution)/shard_map/ppermute | solution.py:374
  318.8 33.8 %collective-permute-start.37 = (bf16[2,2,2,64,768]{4,3,0,1,2:T(8,128)(2,1)S(1)}, bf16[2,2,2,64,768]{4,3,0,1,2:T(8,128)(2,1)S(1)}, u32[]{:S(2)}, u32[]{:S(2)}) collective-permute-start(bf16[2,2,2,64,768]{4,3,0,1,2:T(8,128)(2,1)S(1)} %copy_bitcast_fusion.4), channel_id=1, source_target_pairs={{0,2},{2,0},{1,3},{3,1},{4,6},{6,4},{5,7},{7,5},{8,10},{10,8},{9,1... | collective-permute-start | bytes 2359304 | tf_op jit(solution)/shard_map/ppermute | solution.py:367
  319.5 32.6 %collective-permute-start.39 = (bf16[2,2,64,1280]{3,2,1,0:T(8,128)(2,1)S(1)}, bf16[2,2,64,1280]{3,2,1,0:T(8,128)(2,1)S(1)}, u32[]{:S(2)}, u32[]{:S(2)}) collective-permute-start(bf16[2,2,64,1280]{3,2,1,0:T(8,128)(2,1)S(1)} %dynamic-slice_bitcast_fusion.3), channel_id=1, source_target_pairs={{0,4},{4,0},{8,12},{12,8},{16,20},{20,16},{24,28},{28,24},{1,5},{5... | collective-permute-start | bytes 1966088 | tf_op jit(solution)/shard_map/ppermute | solution.py:374
  320.7 31.8 %collective-permute-start.40 = (bf16[2,2,64,1280]{3,2,1,0:T(8,128)(2,1)S(1)}, bf16[2,2,64,1280]{3,2,1,0:T(8,128)(2,1)S(1)}, u32[]{:S(2)}, u32[]{:S(2)}) collective-permute-start(bf16[2,2,64,1280]{3,2,1,0:T(8,128)(2,1)S(1)} %dynamic-slice_bitcast_fusion.2), channel_id=1, source_target_pairs={{0,2},{2,0},{1,3},{3,1},{4,6},{6,4},{5,7},{7,5},{8,10},{10,8},{9,1... | collective-permute-start | bytes 1966088 | tf_op jit(solution)/shard_map/ppermute | solution.py:367
  353.8 20.0 %collective-permute-start.44 = (bf16[2,64,2560]{2,1,0:T(8,128)(2,1)S(1)}, bf16[2,64,2560]{2,1,0:T(8,128)(2,1)S(1)}, u32[]{:S(2)}, u32[]{:S(2)}) collective-permute-start(bf16[2,64,2560]{2,1,0:T(8,128)(2,1)S(1)} %dynamic-slice_bitcast_fusion.1), channel_id=1, source_target_pairs={{0,8},{4,12},{8,0},{12,4},{16,24},{20,28},{24,16},{28,20},{1,9},{5... | collective-permute-start | bytes 1966088 | tf_op jit(solution)/shard_map/ppermute | solution.py:374
  354.0 17.7 %collective-permute-start.43 = (bf16[2,2,64,768]{3,2,0,1:T(8,128)(2,1)S(1)}, bf16[2,2,64,768]{3,2,0,1:T(8,128)(2,1)S(1)}, u32[]{:S(2)}, u32[]{:S(2)}) collective-permute-start(bf16[2,2,64,768]{3,2,0,1:T(8,128)(2,1)S(1)} %dynamic-slice_bitcast_fusion.10), channel_id=1, source_target_pairs={{0,2},{2,0},{1,3},{3,1},{4,6},{6,4},{5,7},{7,5},{8,10},{10,8},{9,1... | collective-permute-start | bytes 1179656 | tf_op jit(solution)/shard_map/ppermute | solution.py:367
  354.7 17.0 %collective-permute-start.42 = (bf16[2,2,64,768]{3,2,0,1:T(8,128)(2,1)S(1)}, bf16[2,2,64,768]{3,2,0,1:T(8,128)(2,1)S(1)}, u32[]{:S(2)}, u32[]{:S(2)}) collective-permute-start(bf16[2,2,64,768]{3,2,0,1:T(8,128)(2,1)S(1)} %dynamic-slice_bitcast_fusion.11), channel_id=1, source_target_pairs={{0,4},{4,0},{8,12},{12,8},{16,20},{20,16},{24,28},{28,24},{1,5},{5... | collective-permute-start | bytes 1179656 | tf_op jit(solution)/shard_map/ppermute | solution.py:374
  355.9 15.8 %collective-permute-start.46 = (bf16[64,1024]{1,0:T(8,128)(2,1)S(1)}, bf16[64,1024]{1,0:T(8,128)(2,1)S(1)}, u32[]{:S(2)}, u32[]{:S(2)}) collective-permute-start(bf16[64,1024]{1,0:T(8,128)(2,1)S(1)} %add_convert_fusion.4), channel_id=1, source_target_pairs={{0,16},{4,20},{8,24},{12,28},{16,0},{20,4},{24,8},{28,12},{1,17},{... | collective-permute-start | bytes 393224 | tf_op jit(solution)/shard_map/ppermute | solution.py:374
  374.4 32.8 %collective-permute-start.52 = (bf16[256,1024]{1,0:T(8,128)(2,1)S(1)}, bf16[256,1024]{1,0:T(8,128)(2,1)S(1)}, u32[]{:S(2)}, u32[]{:S(2)}) collective-permute-start(bf16[256,1024]{1,0:T(8,128)(2,1)S(1)} %slice.308), channel_id=1, source_target_pairs={{0,2},{2,0},{1,3},{3,1},{4,6},{6,4},{5,7},{7,5},{8,10},{10,8},{9,1... | collective-permute-start | bytes 1572872 | tf_op jit(solution)/shard_map/ppermute | solution.py:367
  375.5 31.9 %collective-permute-start.51 = (bf16[256,1024]{1,0:T(8,128)(2,1)S(1)}, bf16[256,1024]{1,0:T(8,128)(2,1)S(1)}, u32[]{:S(2)}, u32[]{:S(2)}) collective-permute-start(bf16[256,1024]{1,0:T(8,128)(2,1)S(1)} %slice.264), channel_id=1, source_target_pairs={{0,2},{2,0},{1,3},{3,1},{4,6},{6,4},{5,7},{7,5},{8,10},{10,8},{9,1... | collective-permute-start | bytes 1572872 | tf_op jit(solution)/shard_map/ppermute | solution.py:367
  376.7 25.4 %collective-permute-start.49 = (bf16[64,1024]{1,0:T(8,128)(2,1)S(1)}, bf16[64,1024]{1,0:T(8,128)(2,1)S(1)}, u32[]{:S(2)}, u32[]{:S(2)}) collective-permute-start(bf16[64,1024]{1,0:T(8,128)(2,1)S(1)} %convert_add_fusion.23), channel_id=1, source_target_pairs={{0,2},{2,0},{1,3},{3,1},{4,6},{6,4},{5,7},{7,5},{8,10},{10,8},{9,1... | collective-permute-start | bytes 393224 | tf_op jit(solution)/shard_map/ppermute | solution.py:367
  377.7 42.1 %collective-permute-start.47 = (bf16[2,64,1536]{2,1,0:T(8,128)(2,1)S(1)}, bf16[2,64,1536]{2,1,0:T(8,128)(2,1)S(1)}, u32[]{:S(2)}, u32[]{:S(2)}) collective-permute-start(bf16[2,64,1536]{2,1,0:T(8,128)(2,1)S(1)} %dynamic-slice_bitcast_fusion.9), channel_id=1, source_target_pairs={{0,8},{4,12},{8,0},{12,4},{16,24},{20,28},{24,16},{28,20},{1,9},{5... | collective-permute-start | bytes 1179656 | tf_op jit(solution)/shard_map/ppermute | solution.py:374
  403.6 16.1 %collective-permute-start.48 = (bf16[64,2560]{1,0:T(8,128)(2,1)S(1)}, bf16[64,2560]{1,0:T(8,128)(2,1)S(1)}, u32[]{:S(2)}, u32[]{:S(2)}) collective-permute-start(bf16[64,2560]{1,0:T(8,128)(2,1)S(1)} %dynamic-slice_bitcast_fusion.12), channel_id=1, source_target_pairs={{0,16},{4,20},{8,24},{12,28},{16,0},{20,4},{24,8},{28,12},{1,17},{... | collective-permute-start | bytes 983048 | tf_op jit(solution)/shard_map/ppermute | solution.py:374
  (96 other events, 614.0 us)

commit v3 on v2

--- a/solution.py
+++ b/solution.py
@@ -310,11 +310,9 @@
             ],
         ),
         compiler_params=pltpu.CompilerParams(
-            dimension_semantics=("arbitrary",), vmem_limit_bytes=40 << 20
+            dimension_semantics=("arbitrary",), vmem_limit_bytes=20 << 20
         ),
-        cost_estimate=pl.CostEstimate(
-            flops=length * length * width * 2, bytes_accessed=4 * length * width * 2, transcendentals=0
-        ),
+        cost_estimate=pl.CostEstimate(flops=0, bytes_accessed=0, transcendentals=0),
     )(info, qkv, seg)
 
 
@@ -346,12 +344,10 @@
             ],
         ),
         compiler_params=pltpu.CompilerParams(
-            dimension_semantics=("arbitrary",), vmem_limit_bytes=48 << 20
+            dimension_semantics=("arbitrary",), vmem_limit_bytes=28 << 20
         ),
         cost_estimate=pl.CostEstimate(
-            flops=length * length * width * 5 // parts,
-            bytes_accessed=8 * length * width * 2 // parts,
-            transcendentals=0,
+            flops=32 * length * length * width, bytes_accessed=8 * length * width * 2, transcendentals=0
         ),
     )(info, qkv, mixed, grad, seg, log_sum)
 
@@ -403,87 +399,386 @@
     return lax.dynamic_update_slice_in_dim(held, second, first.shape[axis], axis)
 
 
+class Turn:
+    def __init__(self):
+        self.arrays, self.shapes, self.jobs = [], [], []
+
+    def read(self, array):
+        for i, other in enumerate(self.arrays):
+            if other is array:
+                return i
+        self.arrays.append(array)
+        return len(self.arrays) - 1
+
+    def write(self, shape, dtype):
+        self.shapes.append(jax.ShapeDtypeStruct(shape, dtype))
+        return len(self.shapes) - 1
+
+    def run(self, bits):
+        count = len(self.arrays)
+
+        def kernel(own, *refs):
+            mine = [own[i] for i in range(bits.shape[0])]
+            for job in self.jobs:
+                job(mine, refs[:count], refs[count:])
+
+        spent = sum(a.size * jnp.dtype(a.dtype).itemsize for a in [*self.arrays, *self.shapes])
+        return pl.pallas_call(
+            kernel,
+            name="turn",
+            out_shape=tuple(self.shapes),
+            in_specs=[pl.BlockSpec(memory_space=pltpu.SMEM)] + [pl.BlockSpec(memory_space=pltpu.VMEM)] * count,
+            out_specs=tuple(pl.BlockSpec(memory_space=pltpu.VMEM) for _ in self.shapes),
+            compiler_params=pltpu.CompilerParams(vmem_limit_bytes=spent + (2 << 20)),
+            cost_estimate=pl.CostEstimate(flops=0, bytes_accessed=0, transcendentals=0),
+        )(bits, *self.arrays)
+
+
+def combinations(bits):
+    made = [{}]
+    for bit in bits:
+        made = [{**choice, bit: value} for choice in made for value in (0, 1)]
+    return made
+
+
+def flat_index(choice, bits):
+    at = 0
+    for bit in sorted(bits, reverse=True):
+        at = at * 2 + choice[bit]
+    return at
+
+
+def block_of(at, rows, base=0):
+    start = at * rows + base
+    if isinstance(start, int):
+        return pl.ds(start, rows)
+    return pl.ds(pl.multiple_of(start, math.gcd(rows, base) if base else rows), rows)
+
+
+class Piece:
+    def __init__(self, array, rows, bits, order, stride=None, base=0):
+        self.held, self.rows, self.bits = (array, base), rows, list(bits)
+        self.fixed, self.order, self.came = [], list(order), None
+        self.stride, self.source = stride or rows, bool(bits)
+
+
 class Gather:
-    def __init__(self, block, cut):
-        self.rows, self.width, self.cut = block.shape[0], block.shape[1], cut
-        self.steps = [*[(bit,) for bit in reversed(far_bits())], (1, 0), (0, 1)]
-        self.held, self.done = [block], [[]]
-
-    def send(self):
-        bits = self.steps[0]
-        if len(bits) > len(self.held):
-            whole = self.held[0]
-            self.held = [whole[..., : self.cut], whole[..., self.cut :]]
-            self.done = [list(self.done[0]), list(self.done[0])]
-        return [swap_bit(array, bit) for array, bit in zip(self.held, bits)]
-
-    def take(self, came):
-        bits = self.steps.pop(0)
-        for i, bit in enumerate(bits):
-            mine = own_bit(bit)
-            low, high = pick(mine, self.held[i], came[i]), pick(mine, came[i], self.held[i])
-            self.held[i] = jnp.stack([low, high], axis=axis_of(bit, self.done[i]))
-            self.done[i].append(bit)
+    def __init__(self, first, second):
+        far = list(reversed(far_bits()))
+        self.pieces = [
+            Piece(array, array.shape[0], [], [*far, *last])
+            for array, last in ((first, (1, 0)), (second, (0, 1)))
+        ]
+
+    def wants(self):
+        return [(p.order[0], p.rows << (len(p.bits) + (p.came is not None))) for p in self.pieces]
+
+    def turn(self, turn, places):
+        for p, (out, base) in zip(self.pieces, places):
+            if p.came is None:
+                turn.jobs.append(copy_rows(turn.read(p.held[0]), p.held[1], out, base, p.rows << len(p.bits)))
+            else:
+                bit = p.sent
+                absorb_gather(turn, p, bit, lambda choice, p=p, out=out, base=base: [(out, choice, base)])
+            p.sent = p.order.pop(0)
+            p.next_held = (out, base)
+
+    def settle(self, outs, came):
+        for p, where in zip(self.pieces, came):
+            if p.came is not None:
+                p.bits.append(p.last)
+            p.held, p.came, p.last = (outs[p.next_held[0]], p.next_held[1]), where, p.sent
+
+    def arrays(self):
+        return [a for p in self.pieces for a in ([p.held[0]] + ([p.came[0]] if p.came else []))]
+
+    def relabel(self, swap):
+        for p in self.pieces:
+            p.held = (swap(p.held[0]), p.held[1])
+            if p.came:
+                p.came = (swap(p.came[0]), p.came[1])
+
+    def left(self):
+        return len(self.pieces[0].order)
+
+    def result(self, bits, outs):
+        turn = Turn()
+        made = [turn.write(shape, BF16) for shape, _ in outs]
+        for i, p in enumerate(self.pieces):
+            held, came = turn.read(p.held[0]), turn.read(p.came[0])
+            moves = [(out, move) for out, (_, moves) in zip(made, outs) for move in moves[i]]
+
+            def job(mine, ins, refs, p=p, held=held, came=came, moves=moves):
+                everyone = [*p.bits, p.last]
+                for choice in combinations(p.bits):
+                    at = flat_index(choice, p.bits)
+                    for source, base, value in (
+                        (ins[held], p.held[1], mine[p.last]),
+                        (ins[came], p.came[1], 1 - mine[p.last]),
+                    ):
+                        chip = flat_index({**choice, p.last: value}, everyone)
+                        for out, ((low, high), (left, right), stride, row, column) in moves:
+                            start = pl.multiple_of(chip * stride + row, math.gcd(stride, row) if row else stride)
+                            refs[out][pl.ds(start, high - low), column : column + right - left] = source[
+                                pl.ds(base + at * p.rows + low, high - low), left:right
+                            ]
+
+            turn.jobs.append(job)
+        return turn.run(bits)
+
+
+class Spread:
+    def __init__(self, array):
+        self.pieces = [Piece(array, array.shape[0], [], [*reversed(far_bits()), 0, 1])]
+
+    def wants(self):
+        return [(self.pieces[0].order[0], self.pieces[0].rows)]
+
+    def turn(self, turn, places):
+        [p], [(out, base)] = self.pieces, places
+        p.order.pop(0)
+        p.next_held = (out, base)
+        if p.came is None:
+            turn.jobs.append(copy_rows(turn.read(p.held[0]), p.held[1], out, base, p.rows))
+            return
+        held, came, held_base, came_base, rows = turn.read(p.held[0]), turn.read(p.came[0]), p.held[1], p.came[1], p.rows
+
+        def job(mine, ins, refs):
+            refs[out][base : base + rows] = (
+                ins[held][held_base : held_base + rows] + ins[came][came_base : came_base + rows]
+            )
+
+        turn.jobs.append(job)
+
+    def settle(self, outs, came):
+        [p] = self.pieces
+        p.held, p.came = (outs[p.next_held[0]], p.next_held[1]), came[0]
+
+    arrays, relabel, left = Gather.arrays, Gather.relabel, Gather.left
 
     def result(self):
-        flat = [array.reshape(-1, array.shape[-1]) for array in self.held]
-        return flat[0] if len(flat) == 1 else join(*flat, axis=1)
+        [p] = self.pieces
+        return sum(array[base : base + p.rows] for array, base in (p.held, p.came))
+
+
+class Rider:
+    def __init__(self, array, bit):
+        self.pieces = [Piece(array, array.shape[0], [], [bit])]
+
+    wants, turn, settle = Spread.wants, Spread.turn, Spread.settle
+    arrays, relabel, left = Gather.arrays, Gather.relabel, Gather.left
+
+    def result(self):
+        [p] = self.pieces
+        return p.came[0][p.came[1] : p.came[1] + p.rows]
+
+
+def copy_rows(source, source_base, out, base, rows):
+    def job(mine, ins, refs):
+        refs[out][base : base + rows] = ins[source][source_base : source_base + rows]
+
+    return job
+
+
+def absorb_gather(turn, p, bit, targets):
+    held, came = turn.read(p.held[0]), turn.read(p.came[0])
+    last = p.last
+    known = list(p.bits)
+    held_base, came_base, rows = p.held[1], p.came[1], p.rows
+    [(out, _, base)] = targets(None)
+
+    def job(mine, ins, refs):
+        for choice in combinations(known):
+            at = flat_index(choice, known)
+            for source, start, value in ((held, held_base, mine[last]), (came, came_base, 1 - mine[last])):
+                to = flat_index({**choice, last: value}, [*known, last])
+                refs[out][block_of(to, rows, base)] = ins[source][block_of(at, rows, start)]
+
+    turn.jobs.append(job)
 
 
 class Scatter:
-    def __init__(self, left, right):
+    def __init__(self, first, second=None):
         far = far_bits()
-        self.bits = [sorted([0, 1, *far], reverse=True) for _ in range(2)]
-        count = len(self.bits[0])
-        self.held = [
-            array.astype(BF16).reshape((2,) * count + (array.shape[0] >> count, array.shape[1]))
-            for array in (left, right)
-        ]
-        self.steps = [(0, 1), (1, 0), *[(bit,) for bit in far]]
-
-    def send(self):
-        bits = self.steps[0]
-        if len(bits) < len(self.held):
-            self.held = [join(*self.held, axis=self.held[0].ndim - 1)]
-        return [
-            swap_bit(lax.dynamic_index_in_dim(array, 1 - own_bit(bit), self.bits[i].index(bit), keepdims=False), bit)
-            for i, (array, bit) in enumerate(zip(self.held, bits))
-        ]
-
-    def take(self, came):
-        bits = self.steps.pop(0)
-        for i, bit in enumerate(bits):
-            keep = lax.dynamic_index_in_dim(self.held[i], own_bit(bit), self.bits[i].index(bit), keepdims=False)
-            total = keep.astype(F32) + came[i].astype(F32)
-            self.held[i] = total.astype(BF16) if self.steps else total
-            self.bits[i].remove(bit)
-
-    def result(self):
-        return self.held[0]
-
-
-def add_over(array, *bits):
-    for bit in bits:
-        own = array.astype(BF16)
-        array = own.astype(F32) + (swap_core(own) if bit == "core" else swap_bit(own, bit)).astype(F32)
-    return array
-
-
-def phase(moves, work, *values):
-    moves = [move if isinstance(move, tuple) else (move, 1) for move in moves]
-    moves = [(move, min(count, len(move.steps))) for move, count in moves if move.steps]
-    held, values = fence([move.held for move, _ in moves], values)
-    came = []
-    for (move, count), arrays in zip(moves, held):
-        move.held = list(arrays)
+        bits = sorted([0, 1, *far], reverse=True)
+        rows = first.shape[0] >> len(bits)
+        if second is None:
+            half = rows // 2
+            self.pieces = [
+                Piece(first, half, bits, [*near, *far], rows, base) for near, base in (((0, 1), 0), ((1, 0), half))
+            ]
+        else:
+            self.pieces = [
+                Piece(array, rows, bits, [*near, *far]) for array, near in ((first, (0, 1)), (second, (1, 0)))
+            ]
+
+    def wants(self):
+        return [(p.order[0], p.rows << (len(p.bits) - len(p.fixed) - 1)) for p in self.pieces]
+
+    def turn(self, turn, places):
+        for p, (out, base) in zip(self.pieces, places):
+            bit = p.order.pop(0)
+            free = [b for b in p.bits if b not in p.fixed and b != bit]
+            rows, bits, fixed = p.rows, list(p.bits), list(p.fixed)
+            held = turn.read(p.held[0])
+            stride, first = p.stride, p.held[1]
+
+            def block(choice, bits=bits, stride=stride, first=first, rows=rows):
+                start = flat_index(choice, bits) * stride + first
+                return pl.ds(pl.multiple_of(start, math.gcd(stride, first) if first else stride), rows)
+
+            if p.came is None:
+                p.next = None
+
+                def job(mine, ins, refs, held=held, rows=rows, free=free, bit=bit, out=out, base=base, block=block):
+                    for choice in combinations(free):
+                        refs[out][block_of(flat_index(choice, free), rows, base)] = ins[held][
+                            block({**choice, bit: 1 - mine[bit]})
+                        ]
+
+            else:
+                came, came_base = turn.read(p.came[0]), p.came[1]
+                keep = turn.write((rows << len(free), p.held[0].shape[1]), BF16)
+                p.next = keep
+
+                def job(
+                    mine, ins, refs, held=held, rows=rows, fixed=fixed, free=free, bit=bit, out=out, base=base,
+                    came=came, came_base=came_base, keep=keep, block=block,
+                ):
+                    settled = {b: mine[b] for b in fixed}
+                    for choice in combinations(free):
+                        for value, target, start in ((1 - mine[bit], out, base), (mine[bit], keep, 0)):
+                            now = {**choice, bit: value}
+                            total = ins[held][block({**now, **settled})].astype(F32) + ins[came][
+                                block_of(flat_index(now, [*free, bit]), rows, came_base)
+                            ].astype(F32)
+                            refs[target][block_of(flat_index(choice, free), rows, start)] = total.astype(BF16)
+
+            turn.jobs.append(job)
+            p.sent, p.free = bit, free
+
+    def settle(self, outs, came):
+        for p, where in zip(self.pieces, came):
+            if p.next is None:
+                p.fixed = [p.sent]
+            else:
+                p.held, p.bits, p.fixed = (outs[p.next], 0), list(p.free), []
+                p.stride, p.source = p.rows, False
+            p.came = where
+
+    arrays, relabel, left = Gather.arrays, Gather.relabel, Gather.left
+
+    def result(self, bits):
+        turn = Turn()
+        for p in self.pieces:
+            held, came, base, rows = turn.read(p.held[0]), turn.read(p.came[0]), p.came[1], p.rows
+            out = turn.write((rows, p.held[0].shape[1]), F32)
+
+            def job(mine, ins, refs, held=held, came=came, base=base, rows=rows, out=out):
+                refs[out][...] = ins[held][...].astype(F32) + ins[came][base : base + rows].astype(F32)
+
+            turn.jobs.append(job)
+        return turn.run(bits)
+
+
+def swap_rows(moves, bits):
+    wants = [move.wants() for move in moves]
+    sizes, places = {}, []
+    for bit, rows in (want for group in wants for want in group):
+        places.append((bit, sizes.get(bit, 0)))
+        sizes[bit] = sizes.get(bit, 0) + rows
+    turn = Turn()
+    width = moves[0].pieces[0].held[0].shape[1]
+    outs = {bit: turn.write((rows, width), BF16) for bit, rows in sizes.items()}
+    located = [(outs[bit], base) for bit, base in places]
+    starts = [0]
+    for move in moves:
+        starts.append(starts[-1] + len(move.pieces))
+    for i, move in enumerate(moves):
+        move.turn(turn, located[starts[i] : starts[i + 1]])
+    made = turn.run(bits)
+    got = {bit: swap_bit(made[out], bit) for bit, out in outs.items()}
+    came = [(got[bit], base) for bit, base in places]
+    for i, move in enumerate(moves):
+        move.settle(made, came[starts[i] : starts[i + 1]])
+
+
+def add_came(own, came):
+    return own.astype(BF16).astype(F32) + came.astype(F32)
+
+
+def add_hop(array, bit):
+    return add_came(array, swap_bit(array.astype(BF16), bit))
+
+
+def phase(bits, moves, work, *values):
+    chains = [move if isinstance(move, tuple) else (move, 1) for move in moves]
+    chains = [
+        ([move for move in chain[:-1] if move.left()], min(chain[-1], chain[0].left())) for chain in chains
+    ]
+    moves = [move for chain, _ in chains for move in chain]
+
+    def tie(extra):
+        arrays = [a for move in moves for a in move.arrays()]
+        held, extra = fence(arrays, extra)
+        table = list(zip(arrays, held))
+        for move in moves:
+            move.relabel(lambda array: next(new for old, new in table if old is array))
+        return extra
+
+    values = tie(values)
+    if moves:
+        swap_rows(moves, bits)
+    for chain, count in chains:
         for _ in range(count - 1):
-            move.take(move.send())
-        came.append(move.send())
+            swap_rows(chain, bits)
     made = work(*values) if work else ()
-    came, made = fence(came, made)
-    for (move, _), arrays in zip(moves, came):
-        move.take(arrays)
-    return made
+    return tie(made)
+
+
+def by_rows(body, rows, whole, outs, sums=0, tile=TILE, name="rows"):
+    rows = [array if isinstance(array, tuple) else (array, 0, array.shape[0]) for array in rows]
+    length = rows[0][2]
+    width = outs[0][0]
+
+    def kernel(*refs):
+        ins, results = refs[: len(rows) + len(whole)], refs[len(rows) + len(whole) :]
+        made = body(*(ref[...] for ref in ins))
+        for ref, value in zip(results, made):
+            if ref.shape[0] == 1:
+
+                @pl.when(pl.program_id(0) == 0)
+                def _(ref=ref):
+                    ref[...] = jnp.zeros_like(ref)
+
+                ref[...] += value
+            else:
+                ref[...] = value.astype(ref.dtype)
+
+    spent = sum(array.size * array.dtype.itemsize for array in whole)
+    for columns, kind in [*outs, *((array.shape[1], array.dtype) for array, _, _ in rows)]:
+        spent += 2 * tile * columns * jnp.dtype(kind).itemsize
+
+    def steps(columns, first=0):
+        return pl.BlockSpec((tile, columns), lambda i: (i + first // tile, 0))
+
+    def fixed(shape, **how):
+        return pl.BlockSpec(shape, lambda i: (0,) * len(shape), **how)
+
+    return pl.pallas_call(
+        kernel,
+        name=name,
+        grid=(length // tile,),
+        out_shape=[jax.ShapeDtypeStruct((length, columns), dtype) for columns, dtype in outs]
+        + [jax.ShapeDtypeStruct((1, width), F32)] * sums,
+        in_specs=[steps(array.shape[1], first) for array, first, _ in rows]
+        + [fixed(array.shape, pipeline_mode=pl.Buffered(1)) for array in whole],
+        out_specs=[steps(columns) for columns, _ in outs] + [fixed((1, width))] * sums,
+        compiler_params=pltpu.CompilerParams(
+            dimension_semantics=("arbitrary",), vmem_limit_bytes=spent + (12 << 20)
+        ),
+        cost_estimate=pl.CostEstimate(flops=0, bytes_accessed=0, transcendentals=0),
+    )(*(array for array, _, _ in rows), *whole)
 
 
 def normalize(stream):
@@ -499,7 +794,7 @@
     middle = jnp.mean(scaled, axis=-1, keepdims=True)
     along = jnp.mean(scaled * normed, axis=-1, keepdims=True)
     return (
-        inverse * (scaled - middle - normed * along),
+        inverse[:, :1] * (scaled - middle - normed * along),
         jnp.sum(grad * normed, axis=0, keepdims=True),
         jnp.sum(grad, axis=0, keepdims=True),
     )
@@ -597,17 +892,14 @@
     table_size = GRID * GRID
     vector_count = vectors.shape[1]
 
-    def to_rows(*arrays):
-        mine = [lax.dynamic_index_in_dim(array, own_y, 0, keepdims=False) for array in arrays]
-        other = [lax.dynamic_index_in_dim(array, 1 - own_y, 0, keepdims=False) for array in arrays]
-        came = swap_chip(jnp.stack(other))
-        return [join(mine[i], came[i], 0) for i in range(len(arrays))]
-
-    def from_row(array):
-        mine, other = array[:local_len], swap_chip(array[local_len:])
-        return jnp.stack([pick(own_y, mine, other), pick(own_y, other, mine)], axis=0)
-
-    res_row = lax.dynamic_index_in_dim(res_ids, own_y, 0, keepdims=False)
+    bits = jnp.stack([own_bit(bit) for bit in [0, 1, *far_bits()]]).astype(jnp.int32)
+
+    def to_rows(array):
+        mine = lax.dynamic_index_in_dim(array, own_y, 0, keepdims=False)
+        other = lax.dynamic_index_in_dim(array, 1 - own_y, 0, keepdims=False)
+        return join(mine, swap_chip(other), 0)
+
+    res_row = pick(own_y, res_ids[0], res_ids[1])
     all_positions = jnp.arange(row_len, dtype=jnp.int32)
     segment_all, _, _, _ = layout(res_row, all_positions)
     seg = jnp.broadcast_to(segment_all.astype(F32)[None, :], (8, row_len))
@@ -630,16 +922,19 @@
     mine_in, away_in = by_core(attn_in.astype(BF16), 3)
     mine_out, away_out = by_core(attn_out.astype(BF16), 1)
     mine_up, away_up = by_core(mlp_in.astype(BF16), chips)
-    came = swap_core(jnp.concatenate([away_in, vector_pad, away_out, away_up], axis=1))
-    mine = jnp.concatenate([mine_in, vector_pad, mine_out, mine_up], axis=1)
+    mine = jnp.concatenate([mine_in, mine_out, mine_up], axis=1)
+    away = jnp.concatenate([away_in, away_out, away_up], axis=1)
+    came, came_vector = swap_core(away), swap_core(vector_pad)
     shard = jnp.concatenate([pick(own_c, mine, came), pick(own_c, came, mine)], axis=0)
+    vector_shard = jnp.concatenate(
+        [pick(own_c, vector_pad, came_vector), pick(own_c, came_vector, vector_pad)], axis=0
+    )[:, :16].reshape(1, -1)
+    vector_row = jnp.pad(vector_shard, ((0, 0), (0, width - vector_shard.shape[1])))
+    chip = lax.axis_index("img") * halves + own_y
+    vector_rows = jnp.where(jnp.arange(chips)[:, None] == chip, vector_row, jnp.zeros_like(vector_row))
     in_width = 3 * half
-    head_end = in_width + TILE
     own = local_len * row_count
     per = local_len // TILE
-
-    def cut_of(columns):
-        return columns // (2 * TILE) * TILE
 
     def with_core(array):
         return join(array, swap_core(array), 0)
@@ -649,27 +944,61 @@
         came = swap_core(away)
         return product(left[:own], weights) + came.astype(F32)
 
-    gather_in = Gather(shard[:, :head_end], cut_of(head_end))
-    gather_up = Gather(shard[:, head_end:], cut_of(half + ff_half))
-    gather_down = Gather(mlp_out.astype(BF16), cut_of(width))
+    low_down, high_down = jnp.split(mlp_out.astype(BF16), 2)
+    gather_in = Gather(shard[:, :width], shard[:, width : 2 * width])
+    gather_vectors = Spread(vector_rows)
+    gather_up = Gather(shard[:, 2 * width : 2 * width + half * 2], shard[:, 2 * width + half * 2 :])
+    gather_down = Gather(low_down, high_down)
+
+    patches, cotangent = phase(
+        bits,
+        [(gather_in, gather_vectors, len(far_bits()))],
+        lambda *arrays: [to_rows(array) for array in arrays],
+        patches,
+        cotangent,
+    )
+
+    wide_place = jnp.pad(place, ((0, 0), (0, TILE - table_size)))
+    wide_table = jnp.pad(pos_table, ((0, TILE - table_size), (0, 0)))
+    wide_usable = jnp.broadcast_to(usable, (own, TILE))
+    small = TILE
 
     def first(patches, cotangent):
-        patches, cotangent = to_rows(patches, cotangent)
-        stream = patches.astype(F32) + jnp.dot(
-            place, pos_table, precision=PRECISE, preferred_element_type=F32
+        def body(patches, place, cotangent, usable, table):
+            stream = patches.astype(F32) + jnp.dot(place, table, precision=PRECISE, preferred_element_type=F32)
+            normed, inverse = normalize(stream)
+            grad = cotangent.astype(F32) * usable[:, :1]
+            return stream, normed, jnp.broadcast_to(inverse, (stream.shape[0], TILE)), grad
+
+        stream, hat_one, inverse_one, grad_own = by_rows(
+            body,
+            [patches, wide_place, cotangent, wide_usable],
+            [wide_table],
+            [(width, F32), (width, F32), (TILE, F32), (width, BF16)],
+            name="first",
         )
-        hat_one, inverse_one = normalize(stream)
-        grad_own = cotangent.astype(F32) * usable
-        return stream, hat_one, inverse_one, grad_own, with_core(grad_own.astype(BF16))
-
-    stream, hat_one, inverse_one, grad_own, grad_last = phase(
-        [(gather_in, len(far_bits()))], first, patches, cotangent
-    )
-    phase([gather_in, gather_up], None)
-    phase([gather_in, gather_up], None)
-    attn_part = gather_in.result()
-    in_matrix = attn_part[:, :in_width]
-    vector_part = attn_part[:, in_width:]
+        return stream, hat_one, inverse_one, grad_own
+
+    far = far_bits()
+    stream, hat_one, inverse_one, grad_own = phase(
+        bits, [gather_in, gather_vectors, gather_up], first, patches, cotangent
+    )
+    phase(bits, [gather_in, gather_vectors, (gather_up, len(far) - 1), gather_down], None)
+    block = 2 * rows
+    spare = in_width - width
+    in_matrix, out_columns = gather_in.result(
+        bits,
+        [
+            (
+                (width, in_width),
+                ([((0, block), (0, width), block, 0, 0)], [((0, block), (0, spare), block, 0, width)]),
+            ),
+            ((width, width - spare), ([], [((0, block), (spare, width), block, 0, 0)])),
+        ],
+    )
+    vector_part = jnp.pad(
+        gather_vectors.result()[:, : block * 16].reshape(-1, 16), ((0, 0), (0, TILE - 16))
+    )
     gain_one, shift_one, bias_query, bias_value, bias_out, gain_two, shift_two, bias_down = (
         rows_from(vector_part, 8)
     )
@@ -678,100 +1007,155 @@
     bias_up = unroll_bias(vector_part, own_c, ff_rows)
     bias_qkv = jnp.concatenate([bias_query, jnp.zeros_like(bias_query), bias_value], axis=1)
 
-    def project(hat_one, in_matrix):
+    def project(hat_one, in_matrix, out_columns):
         normed_one = with_core((hat_one * gain_one + shift_one).astype(BF16))
-        return normed_one, (nn(normed_one, in_matrix) + bias_qkv).astype(BF16)
-
-    normed_one, qkv = phase([gather_up, gather_down], project, hat_one, in_matrix)
-    mixed, log_sum = phase(
-        [gather_up, gather_down],
-        lambda qkv: attention(qkv, seg, info, per, head_size),
-        qkv,
-    )
-    while gather_up.steps:
-        phase([gather_up, gather_down], None)
-    up_part = gather_up.result()
-    out_columns, up_matrix = up_part[:, :half], up_part[:, half:]
-
-    def project_out(stream, mixed, out_columns):
         low, high = out_columns[:half], out_columns[half:]
         keep_out, came_out = pick(own_c, low, high), swap_core(pick(own_c, high, low))
-        out_matrix = jnp.concatenate(
-            [pick(own_c, keep_out, came_out), pick(own_c, came_out, keep_out)], axis=1
+        out_matrix = join(pick(own_c, keep_out, came_out), pick(own_c, came_out, keep_out), 1)
+        return normed_one, out_matrix, (nn(normed_one, in_matrix) + bias_qkv).astype(BF16)
+
+    normed_one, out_matrix, qkv = phase(
+        bits,
+        [gather_up, (gather_down, len(far) - 1)], project, hat_one, in_matrix, out_columns
+    )
+
+    def matmul_rows(left, right, product, name):
+        return product(left[own:], right).astype(BF16)
+
+    def attend(qkv, out_matrix, grad_own):
+        mixed, log_sum = attention(qkv, seg, info, per, head_size)
+        return mixed, log_sum, matmul_rows(mixed, out_matrix, nn, "out_away"), with_core(grad_own)
+
+    mixed, log_sum, out_away, grad_last = phase(bits, [gather_up], attend, qkv, out_matrix, grad_own)
+
+    def project_out(stream, mixed, out_away, out_matrix):
+        def body(stream, mixed, came, matrix, bias, gain, shift):
+            stream_two = stream + nn(mixed, matrix) + came.astype(F32) + bias
+            normed, inverse = normalize(stream_two)
+            return stream_two, normed, jnp.broadcast_to(inverse, (stream.shape[0], TILE)), normed * gain + shift
+
+        return by_rows(
+            body,
+            [(stream, 0, own), mixed, swap_core(out_away)],
+            [out_matrix, bias_out, gain_two, shift_two],
+            [(width, F32), (width, F32), (TILE, F32), (width, BF16)],
+            name="out_norm",
+            tile=own // 2,
         )
-        stream_two = stream + sum_core(mixed, out_matrix, nn) + bias_out
-        hat_two, inverse_two = normalize(stream_two)
-        normed_two = with_core((hat_two * gain_two + shift_two).astype(BF16))
-        return out_matrix, stream_two, hat_two, inverse_two, normed_two
-
-    out_matrix, stream_two, hat_two, inverse_two, normed_two = phase(
-        [gather_down], project_out, stream, mixed, out_columns
+
+    stream_two, hat_two, inverse_two, normed_two = phase(
+        bits, [gather_down], project_out, stream, mixed, out_away, out_matrix
+    )
+    (up_matrix,) = gather_up.result(
+        bits,
+        [
+            (
+                (width, ff_half),
+                ([((0, block), (0, width), block, 0, 0)], [((0, block), (0, width), block, 0, width)]),
+            )
+        ],
     )
 
     def expand(normed_two, up_matrix, grad_last):
+        normed_two = with_core(normed_two)
         hidden_pre = nn(normed_two, up_matrix) + bias_up
         hidden, slope = gelu_and_slope(hidden_pre)
         hidden = hidden.astype(BF16)
-        cut = cut_of(width)
-        return hidden, slope, tn(hidden, grad_last[:, :cut]).astype(BF16), tn(hidden, grad_last[:, cut:]).astype(BF16)
-
-    hidden, slope, *grad_down = phase([gather_down], expand, normed_two, up_matrix, grad_last)
-    while gather_down.steps:
-        phase([gather_down], None)
-    down_matrix = gather_down.result()
-
-    scatter_down = Scatter(*grad_down)
-
-    def hidden_back(grad_last, down_matrix, slope, normed_two):
+        return normed_two, hidden, slope, tn(hidden, grad_last).astype(BF16)
+
+    normed_two, hidden, slope, grad_down = phase(bits, [gather_down], expand, normed_two, up_matrix, grad_last)
+    part_rows = ff_rows // 2
+    (down_matrix,) = gather_down.result(
+        bits,
+        [
+            (
+                (ff_half, width),
+                (
+                    [((0, part_rows), (0, width), ff_rows, 0, 0)],
+                    [((0, part_rows), (0, width), ff_rows, part_rows, 0)],
+                ),
+            )
+        ],
+    )
+
+    scatter_down = Scatter(grad_down)
+
+    def hidden_back(grad_last, down_matrix, slope, normed_two, up_matrix):
         grad_pre = (nt(grad_last, down_matrix) * slope).astype(BF16)
-        cut = cut_of(ff_half + half)
         return (
             grad_pre,
-            tn(normed_two, grad_pre[:, :cut]).astype(BF16),
-            tn(normed_two, grad_pre[:, cut:]).astype(BF16),
+            matmul_rows(grad_pre, up_matrix, nt, "norm_two_away"),
+            tn(normed_two, grad_pre[:, :width]).astype(BF16),
+            tn(normed_two, grad_pre[:, width:]).astype(BF16),
         )
 
-    grad_pre, *grad_up = phase([scatter_down], hidden_back, grad_last, down_matrix, slope, normed_two)
-    def norm_two_back(grad_pre, up_matrix, hat_two, inverse_two, grad_own):
-        grad_normed_two = sum_core(grad_pre, up_matrix, nt)
-        back_two, grad_gain_two, grad_shift_two = normalize_back(
-            hat_two, inverse_two, gain_two, grad_normed_two
+    grad_pre, two_away, *grad_up = phase(
+        bits, [scatter_down], hidden_back, grad_last, down_matrix, slope, normed_two, up_matrix
+    )
+    scatter_up = Scatter(*grad_up)
+
+    def norm_back(grad, away, matrix, hat, inverse, added, gain, name):
+        def body(grad, came, hat, inverse, added, matrix, gain):
+            back, gain_sum, shift_sum = normalize_back(hat, inverse, gain, nt(grad, matrix) + came.astype(F32))
+            total = added.astype(F32) + back
+            return total, total, gain_sum, shift_sum
+
+        return by_rows(
+            body,
+            [(grad, 0, own), swap_core(away), hat, inverse, added],
+            [matrix, gain],
+            [(width, F32), (width, BF16)],
+            sums=2,
+            name=name,
+            tile=own // 2,
         )
-        grad_two = grad_own + back_two
-        grad_branch = grad_two.astype(BF16)
-        return grad_two, with_core(grad_branch), grad_gain_two, grad_shift_two
-
-    def finish_output(hidden, stream_two, down_matrix):
-        last = sum_core(hidden, down_matrix, nn) + bias_down
-        return ((stream_two + last) * usable).astype(BF16)
-
-    (grad_two, grad_branch, grad_gain_two, grad_shift_two), output = phase(
+
+    def middle(values, hidden, down_matrix):
+        return norm_back(*values, "norm_two_back"), matmul_rows(hidden, down_matrix, nn, "output_away")
+
+    (grad_two, grad_branch, grad_gain_two, grad_shift_two), output_away = phase(
+        bits,
         [scatter_down],
-        lambda values, others: (norm_two_back(*values), finish_output(*others)),
-        (grad_pre, up_matrix, hat_two, inverse_two, grad_own),
-        (hidden, stream_two, down_matrix),
-    )
-
-    grad_rows = tn(mixed, grad_branch).astype(BF16)
-    low, high = grad_rows[:, :half], grad_rows[:, half:]
-    keep_rows, came_rows = pick(own_c, low, high), swap_core(pick(own_c, high, low))
-    grad_out = join(pick(own_c, keep_rows, came_rows), pick(own_c, came_rows, keep_rows), 0)
-    scatter_up = Scatter(grad_up[0], join(grad_up[1], grad_out, 1))
-
-    def attention_grads(grad_branch, out_matrix, qkv, mixed, log_sum, normed_one):
+        middle,
+        (grad_pre, two_away, up_matrix, hat_two, inverse_two, grad_own, gain_two),
+        hidden,
+        down_matrix,
+    )
+
+    def attention_grads(grad_branch, out_matrix, qkv, mixed, log_sum, output_away):
+        grad_branch = with_core(grad_branch)
         grad_mixed = nt(grad_branch, out_matrix).astype(BF16)
         grad_qkv = attention_back(0, 1, qkv, mixed, grad_mixed, seg, log_sum, info, per, head_size)
-        cut = cut_of(in_width)
+        return grad_branch, swap_core(output_away), grad_qkv
+
+    grad_branch, came_output, grad_qkv = phase(
+        bits,
+        [scatter_up, scatter_down],
+        attention_grads,
+        grad_branch,
+        out_matrix,
+        qkv,
+        mixed,
+        log_sum,
+        output_away,
+    )
+
+    def in_grads(mixed, grad_branch, normed_one, grad_qkv, in_matrix):
+        grad_rows = tn(mixed, grad_branch).astype(BF16)
+        low, high = grad_rows[:, :half], grad_rows[:, half:]
+        keep_rows, came_rows = pick(own_c, low, high), swap_core(pick(own_c, high, low))
+        grad_out = join(pick(own_c, keep_rows, came_rows), pick(own_c, came_rows, keep_rows), 0)
         return (
-            grad_qkv,
-            tn(normed_one, grad_qkv[:, :cut]).astype(BF16),
-            tn(normed_one, grad_qkv[:, cut:]).astype(BF16),
+            matmul_rows(grad_qkv, in_matrix, nt, "norm_one_away"),
+            tn(normed_one, grad_qkv[:, :width]).astype(BF16),
+            tn(normed_one, grad_qkv[:, width:]).astype(BF16),
+            grad_out,
         )
 
-    grad_qkv, *grad_in = phase(
-        [scatter_up, (scatter_down, 9)], attention_grads, grad_branch, out_matrix, qkv, mixed, log_sum, normed_one
-    )
-    scatter_in = Scatter(*grad_in)
+    one_away, left, right, grad_out = phase(
+        bits, [scatter_up, scatter_down], in_grads, mixed, grad_branch, normed_one, grad_qkv, in_matrix
+    )
+    scatter_in = Scatter(left, join(right, grad_out, 1))
 
     def widen(row):
         zero = jnp.zeros_like(row)
@@ -780,12 +1164,10 @@
     narrow_rows = vector_count + table_size
     narrow_rows += -narrow_rows % 16
 
-    def norm_one_back(grad_qkv, in_matrix, hat_one, inverse_one, grad_two, grad_pre, grad_branch, grad_last):
-        grad_normed_one = sum_core(grad_qkv, in_matrix, nt)
-        back_one, grad_gain_one, grad_shift_one = normalize_back(
-            hat_one, inverse_one, gain_one, grad_normed_one
+    def norm_one_back(grad_qkv, one_away, in_matrix, hat_one, inverse_one, grad_two, grad_pre, grad_branch, grad_last):
+        grad_stream, grad_low, grad_gain_one, grad_shift_one = norm_back(
+            grad_qkv, one_away, in_matrix, hat_one, inverse_one, grad_two, gain_one, "norm_one_back"
         )
-        grad_stream = grad_two + back_one
         wide_place = jnp.pad(place, ((0, 0), (vector_count, narrow_rows - vector_count - table_size)))
         narrow = lax.dot_general(
             wide_place, grad_stream, (((0,), (0,)), ((), ())), precision=PRECISE, preferred_element_type=F32
@@ -804,24 +1186,55 @@
         row = jnp.arange(narrow_rows)[:, None]
         for i, values in enumerate(rows_of_sums):
             narrow = jnp.where(row == i, values, narrow)
-        return grad_stream, narrow
+        return grad_low, add_came(narrow, swap_core(narrow.astype(BF16)))
+
+    def finish_output(hidden, came, stream_two, down_matrix):
+        def body(hidden, came, stream_two, usable, matrix, bias):
+            return ((stream_two + nn(hidden, matrix) + came.astype(F32) + bias) * usable[:, :1],)
+
+        return by_rows(
+            body,
+            [(hidden, 0, own), came, stream_two, wide_usable],
+            [down_matrix, bias_down],
+            [(width, BF16)],
+            name="output",
+            tile=own // 2,
+        )
+
+    (grad_low, narrow), (output,) = phase(
+        bits,
+        [scatter_in, scatter_up, (scatter_down, len(far) - 1)],
+        lambda values, others: (norm_one_back(*values), finish_output(*others)),
+        (grad_qkv, one_away, in_matrix, hat_one, inverse_one, grad_two, grad_pre, grad_branch, grad_last),
+        (hidden, came_output, stream_two, down_matrix),
+    )
+
+    def ride(narrow, bit):
+        return Rider(narrow.astype(BF16), bit)
 
     scatters = [scatter_in, scatter_up]
-    grad_stream, narrow = phase(
-        scatters, norm_one_back, grad_qkv, in_matrix, hat_one, inverse_one, grad_two, grad_pre, grad_branch, grad_last
-    )
-    far = far_bits()
-    (narrow,) = phase(scatters, lambda narrow: (add_over(narrow, "core", *far[1:]),), narrow)
-
-    def send_back(narrow, output, grad_stream):
-        return add_over(narrow, 0, 1), from_row(output), from_row(grad_stream.astype(BF16))
-
-    narrow, output, input_grad = phase(scatters, send_back, narrow, output, grad_stream)
-    (narrow,) = phase(scatters, lambda narrow: (add_over(narrow, *far[:1]),), narrow)
-    while any(move.steps for move in scatters):
-        phase(scatters, None)
-    shard_down, shard_in = scatter_down.result(), scatter_in.result()
-    shard_up, shard_out = scatter_up.result()[:, :ff_half], scatter_up.result()[:, ff_half:]
+    rider = ride(narrow, 0)
+    phase(bits, [*scatters, rider], None)
+    narrow = add_came(narrow, rider.result())
+    sent = [Rider(output[local_len:], 0), Rider(grad_low[local_len:], 0)]
+    for step, bit in enumerate(far):
+        rider = ride(narrow, bit)
+        phase(bits, [*scatters, rider, *sent[step : step + 1]], None)
+        narrow = add_came(narrow, rider.result())
+    while any(move.left() for move in [*scatters, *sent]):
+        phase(bits, [*scatters, *sent], None)
+    narrow = add_hop(narrow, 1)
+    came_output, came_grad = (rider.result() for rider in sent)
+
+    def back_to_rows(array, other):
+        mine = array[:local_len]
+        return jnp.stack([pick(own_y, mine, other), pick(own_y, other, mine)], axis=0)
+
+    output, input_grad = back_to_rows(output, came_output), back_to_rows(grad_low, came_grad)
+    shard_down = jnp.concatenate(scatter_down.result(bits), axis=0)
+    shard_up = jnp.concatenate(scatter_up.result(bits), axis=1)
+    shard_in = jnp.concatenate(scatter_in.result(bits), axis=1)
+    shard_in, shard_out = shard_in[:, :in_width], shard_in[:, in_width:]
 
     def rows_of(array, core):
         return lax.dynamic_slice_in_dim(array, core * rows, rows, 0)
@@ -840,15 +1253,24 @@
     grad_vectors_shard = lax.dynamic_slice_in_dim(narrow[:vector_count], device * rows, rows, 1).T
     table_grad = narrow[vector_count : vector_count + table_size]
 
-    factor = jnp.float32(1.0 / slot_total)
+    factor = 1.0 / slot_total
     shards = (grad_in_shard, grad_out_shard, grad_up_shard, shard_down, grad_vectors_shard)
     weights = (attn_in, attn_out, mlp_in, mlp_out, vectors)
     firsts = (first_attn_in, first_attn_out, first_mlp_in, first_mlp_out, first_vectors)
     seconds = (second_attn_in, second_attn_out, second_mlp_in, second_mlp_out, second_vectors)
     decays = (0.05, 0.05, 0.05, 0.05, 0.0)
     updated = [
-        adam_update(weights[i], shards[i], firsts[i], seconds[i], factor, decays[i]) for i in range(5)
+        by_rows(
+            lambda w, g, m, v, decay=decays[i]: adam_update(w, g, m, v, factor, decay),
+            [weights[i], shards[i], firsts[i], seconds[i]],
+            [],
+            [(weights[i].shape[1], F32)] * 3,
+            name="adam",
+            tile=weights[i].shape[0],
+        )
+        for i in range(4)
     ]
+    updated.append(adam_update(vectors, grad_vectors_shard, first_vectors, second_vectors, factor, 0.0))
     return (
         output,
         input_grad,

time: 449 us -> 377 us (0.84)
  waiting for transfers between devices: 201 us -> 140 us
  Pallas kernels: 31.8 us -> 71.6 us
  other arithmetic: 55.1 us -> 17.5 us
  matrix products: 67.5 us -> 52 us
  local copies, waits for them, and re-layouts: 25.8 us -> 33.9 us
    ppermute x27 -> x25, waiting for transfers between devices: 131 us -> 82.4 us  [swap_bit(): lax.ppermute(array, 'img', [(i, i ^ 1 << bit - 1) for i in range(count)])]
    pallas_call x0 -> x31, Pallas kernels: none -> 43.1 us  [the longest x22 24.1 us: run(): pl.pallas_call(kernel, name='turn', out_shape=tuple(self.shapes), in_spec...]
    convert_element_type x22 -> x4, other arithmetic: 16.5 us -> 0.13 us  [the longest x2 0.07 us: ride(): return Rider(narrow.astype(BF16), bit)]
    unnamed x153 -> x189, local copies, waits for them, and re-layouts: 13.9 us -> 24.6 us
    ppermute x16, waiting for transfers between devices: 66.6 us -> 56.5 us  [swap_chip(): return lax.ppermute(array, 'sy', SWAP)]
    dot_general x11 -> x9, matrix products: 26.7 us -> 18.6 us  [nn(): return jnp.dot(left, right, preferred_element_type=F32)]
    another operation x40 -> x6, other arithmetic: 12.7 us -> 5.19 us  [the longest x4 4.35 us: back_to_rows(): jnp.stack([pick(own_y, mine, other), pick(own_y, other, mine)], axis=0)]
    add x5 -> x1, other arithmetic: 5.57 us -> 0.7 us  [adam_update(): direction = first_hat / (jnp.sqrt(second_hat) + 1e-08) + decay * weight]
  transfers between devices with their start and end apart: 58 -> 57, of which waited for: 31 -> 36; matrix products, arithmetic and copies ran while one was open for 21% -> 19% of each run, Pallas kernels for 7% -> 15%
where the time goes in v3:
time: 377 us; the launch traced here: 372 us
  waiting for transfers between devices  140 us (37%)
  Pallas kernels  71.6 us (19%)
  starting transfers between devices  54.4 us (14%)
  matrix products  52 us (14%)
  local copies, waits for them, and re-layouts  33.9 us (9%)
  other arithmetic  17.5 us (5%)
    ppermute x25, waiting for transfers between devices, swap_bit(): lax.ppermute(array, 'img', [(i, i ^ 1 << bit - 1) for i in range(count)])  82.4 us
    ppermute x16, waiting for transfers between devices, swap_chip(): return lax.ppermute(array, 'sy', SWAP)  56.5 us
    ppermute x25, starting transfers between devices, swap_bit(): lax.ppermute(array, 'img', [(i, i ^ 1 << bit - 1) for i in range(count)])  36.8 us
    unnamed x189, local copies, waits for them, and re-layouts  24.6 us
    pallas_call x22, Pallas kernels, run(): pl.pallas_call(kernel, name='turn', out_shape=tuple(self.shapes), in_spec...  24.1 us
    pallas_call x9, Pallas kernels, by_rows(): pl.pallas_call(kernel, name=name, grid=(length // tile,), out_shape=[jax....  19.1 us
    dot_general x9, matrix products, nn(): return jnp.dot(left, right, preferred_element_type=F32)  18.6 us
    dot_general x6, matrix products, tn(): lax.dot_general(left, right, (((0,), (0,)), ((), ())), preferred_element_...  16.9 us
  transfers between devices with their start and end apart: 57, of which 36 were waited for; matrix products, arithmetic and copies ran while one was open for 19% of the time, Pallas kernels for 15%

profile of v3, /device:TPU:0, one launch (start us, length us, event | category | flops | bytes accessed | tf_op | source)
XLA Modules:
  0.0 372.5 jit_solution(16158080485988857704)
XLA Ops:
  8.0 4.1 %collective-permute-start.2 = (bf16[144,1024]{1,0:T(8,128)(2,1)S(1)}, bf16[144,1024]{1,0:T(8,128)(2,1)S(1)}, u32[]{:S(2)}, u32[]{:S(2)}) collective-permute-start(bf16[144,1024]{1,0:T(8,128)(2,1)S(1)} %turn.22.refs_0_), channel_id=1, source_target_pairs={{0,16},{4,20},{8,24},{12,28},{16,0},{20,4},{24,8},{28,12},{1,17},{... | collective-permute-start | bytes 884744 | tf_op jit(solution)/shard_map/ppermute | solution.py:370
  15.6 10.0 %collective-permute-done.2.refs_1_ = bf16[144,1024]{1,0:T(8,128)(2,1)S(1)} collective-permute-done((bf16[144,1024]{1,0:T(8,128)(2,1)S(1)}, bf16[144,1024]{1,0:T(8,128)(2,1)S(1)}, u32[]{:S(2)}, u32[]{:S(2)}) %collective-permute-start.2) | collective-permute-done | bytes 294944 | tf_op jit(solution)/shard_map/ppermute | solution.py:370
  27.2 9.9 %collective-permute-done.5 = bf16[256,1024]{1,0:T(8,128)(2,1)S(1)} collective-permute-done((bf16[256,1024]{1,0:T(8,128)(2,1)S(1)}, bf16[256,1024]{1,0:T(8,128)(2,1)S(1)}, u32[]{:S(2)}, u32[]{:S(2)}) %collective-permute-start.5) | collective-permute-done | bytes 524320 | tf_op jit(solution)/shard_map/ppermute | solution.py:363
  45.0 3.2 collective-permute-start.8
  50.4 3.3 first.1
  54.7 4.7 %collective-permute-done.8.refs_5_ = bf16[128,1024]{1,0:T(8,128)(2,1)S(1)} collective-permute-done((bf16[128,1024]{1,0:T(8,128)(2,1)}, bf16[128,1024]{1,0:T(8,128)(2,1)S(1)}, u32[]{:S(2)}, u32[]{:S(2)}) %collective-permute-start.8) | collective-permute-done | bytes 262176 | tf_op jit(solution)/shard_map/ppermute | solution.py:370
  63.9 3.3 collective-permute-start.12
  67.9 11.6 %collective-permute-done.12.refs_3_ = bf16[128,1024]{1,0:T(8,128)(2,1)S(1)} collective-permute-done((bf16[128,1024]{1,0:T(8,128)(2,1)S(1)}, bf16[128,1024]{1,0:T(8,128)(2,1)S(1)}, u32[]{:S(2)}, u32[]{:S(2)}) %collective-permute-start.12) | collective-permute-done | bytes 262176 | tf_op jit(solution)/shard_map/ppermute | solution.py:370
  80.3 5.4 %collective-permute-done.9.refs_1_ = bf16[512,1024]{1,0:T(8,128)(2,1)S(1)} collective-permute-done((bf16[512,1024]{1,0:T(8,128)(2,1)S(1)}, bf16[512,1024]{1,0:T(8,128)(2,1)S(1)}, u32[]{:S(2)}, u32[]{:S(2)}) %collective-permute-start.9) | collective-permute-done | bytes 1048608 | tf_op jit(solution)/shard_map/ppermute | solution.py:363
  99.4 4.5 %add_convert_fusion.qkv = bf16[1024,1536]{1,0:T(8,128)(2,1)S(1)} fusion(bf16[1024,1536]{1,0:T(8,128)(2,1)S(1)} %copy-done.13, f32[1536]{0:T(1024)S(1)} %maximum_reduce_fusion, bf16[512,1024]{1,0:T(8,128)(2,1)S(1)} %collective-permute-done.16, bf16[512,1024]{1,0:T(8,128)(2,1)S(1)} %add_convert_fusion.1), kind=kOutput, calls=%fused_computation.8 | convolution fusion | flops 3228565504 | bytes 8394752 | tf_op jit(solution)/shard_map/dot_general | solution.py:124
  103.9 2.5 collective-permute-done.13.refs_1_
  111.8 12.1 %attend.1 = (bf16[1024,512]{1,0:T(8,128)(2,1)S(1)}, f32[8,1024]{1,0:T(8,128)S(1)}) custom-call(s32[18]{0:T(128)S(1)} %pad_add_fusion.2.info, bf16[1024,1536]{1,0:T(8,128)(2,1)S(1)} %add_convert_fusion.qkv, f32[8,1024]{1,0:T(8,128)S(1)} %broadcast_in_dim.285.seg), custom_call_target="tpu_custom_call" | custom-call | tf_op jit(solution)/shard_map/attend/pallas_call | solution.py:288
  124.9 9.1 %collective-permute-done.18.refs_1_ = bf16[512,1024]{1,0:T(8,128)(2,1)S(1)} collective-permute-done((bf16[512,1024]{1,0:T(8,128)(2,1)S(1)}, bf16[512,1024]{1,0:T(8,128)(2,1)S(1)}, u32[]{:S(2)}, u32[]{:S(2)}) %collective-permute-start.18) | collective-permute-done | bytes 1048608 | tf_op jit(solution)/shard_map/ppermute | solution.py:363
  140.1 10.2 %collective-permute-done.21.refs_1_ = bf16[256,1024]{1,0:T(8,128)(2,1)S(1)} collective-permute-done((bf16[256,1024]{1,0:T(8,128)(2,1)S(1)}, bf16[256,1024]{1,0:T(8,128)(2,1)S(1)}, u32[]{:S(2)}, u32[]{:S(2)}) %collective-permute-start.21) | collective-permute-done | bytes 524320 | tf_op jit(solution)/shard_map/ppermute | solution.py:370
  153.8 9.1 %fusion.3 = (f32[1024,2048]{1,0:T(8,128)}, bf16[1024,2048]{1,0:T(8,128)(2,1)S(1)}) fusion(f32[2048]{0:T(1024)S(1)} %bitcast.154, bf16[1024,1024]{1,0:T(8,128)(2,1)S(1)} %constant_dynamic-update-slice_fusion, bf16[1024,2048]{1,0:T(8,128)(2,1)S(1)} %turn.30.refs_5_), kind=kOutput, calls=%fused_computation.4 | convolution fusion | flops 4318035968 | bytes 18882560 | tf_op jit(solution)/shard_map/dot_general | solution.py:124
  162.9 5.3 %convolution_convert_fusion.refs_0_ = bf16[2048,1024]{1,0:T(8,128)(2,1)S(1)} fusion(bf16[1024,2048]{1,0:T(8,128)(2,1)S(1)} %get-tuple-element.609.refs_0_, bf16[1024,1024]{1,0:T(8,128)(2,1)S(1)} %pad_maximum_fusion.1), kind=kOutput, calls=%fused_computation.9 | convolution fusion | flops 4297064448 | bytes 10485760 | tf_op jit(solution)/shard_map/dot_general | solution.py:120
  168.2 9.3 %collective-permute-done.24.refs_1_ = bf16[512,1024]{1,0:T(8,128)(2,1)S(1)} collective-permute-done((bf16[512,1024]{1,0:T(8,128)(2,1)S(1)}, bf16[512,1024]{1,0:T(8,128)(2,1)S(1)}, u32[]{:S(2)}, u32[]{:S(2)}) %collective-permute-start.24) | collective-permute-done | bytes 1048608 | tf_op jit(solution)/shard_map/ppermute | solution.py:363
  183.2 7.7 %multiply_convert_fusion.refs_0_ = bf16[1024,2048]{1,0:T(8,128)(2,1)S(1)} fusion(f32[1024,2048]{1,0:T(8,128)} %get-tuple-element.485, bf16[1024,1024]{1,0:T(8,128)(2,1)} %copy-done.73, bf16[2048,1024]{1,0:T(8,128)(2,1)S(1)} %turn.32.refs_4_), kind=kOutput, calls=%fused_computation.5 | convolution fusion | flops 4299161600 | bytes 18874368 | tf_op jit(solution)/shard_map/dot_general | solution.py:116
  190.9 4.1 %fusion.20.refs_1_.refs_2_ = bf16[1024,1024]{1,0:T(8,128)(2,1)S(1)} fusion(bf16[1024,1024]{1,0:T(8,128)(2,1)} %copy-done.82, bf16[1024,2048]{1,0:T(8,128)(2,1)S(1)} %multiply_convert_fusion.refs_0_), kind=kOutput, calls=%fused_computation.26 | convolution fusion | flops 2148532224 | bytes 6291456 | tf_op jit(solution)/shard_map/dot_general | solution.py:120
  199.9 5.6 %collective-permute-done.27.refs_1_ = bf16[512,1024]{1,0:T(8,128)(2,1)} collective-permute-done((bf16[512,1024]{1,0:T(8,128)(2,1)}, bf16[512,1024]{1,0:T(8,128)(2,1)}, u32[]{:S(2)}, u32[]{:S(2)}) %collective-permute-start.27) | collective-permute-done | bytes 1048608 | tf_op jit(solution)/shard_map/ppermute | solution.py:363
  212.8 3.8 %norm_two_back.1 = (f32[512,1024]{1,0:T(8,128)S(1)}, bf16[512,1024]{1,0:T(8,128)(2,1)S(1)}, f32[1,1024]{1,0:T(1,128)S(1)}, f32[1,1024]{1,0:T(1,128)S(1)}) custom-call(bf16[1024,2048]{1,0:T(8,128)(2,1)S(1)} %multiply_convert_fusion.refs_0_, bf16[512,1024]{1,0:T(8,128)(2,1)S(1)} %collective-permute-done.31.refs_1_, f32[512,1024]{1,0:T(8,128)S(1)} %copy-done.25, ...), custom_call_target="tpu_custom_call" | custom-call | tf_op jit(solution)/shard_map/norm_two_back/pallas_call | solution.py:768
  216.6 6.5 %collective-permute-done.29.refs_3_ = bf16[256,1024]{1,0:T(8,128)(2,1)S(1)} collective-permute-done((bf16[256,1024]{1,0:T(8,128)(2,1)S(1)}, bf16[256,1024]{1,0:T(8,128)(2,1)S(1)}, u32[]{:S(2)}, u32[]{:S(2)}) %collective-permute-start.29) | collective-permute-done | bytes 524320 | tf_op jit(solution)/shard_map/ppermute | solution.py:370
  231.4 16.3 %attend_back.1.refs_0_ = bf16[1024,1536]{1,0:T(8,128)(2,1)S(1)} custom-call(s32[18]{0:T(128)S(1)} %pad_add_fusion.2.info, bf16[1024,1536]{1,0:T(8,128)(2,1)S(1)} %copy-done.11, bf16[1024,512]{1,0:T(8,128)(2,1)S(1)} %copy-done.9, bf16[1024,512]{1,0:T(8,128)(2,1)S(1)} %convolution_convert_fusion.3.grad, f32[8,1024]{1,0:T(8,128)S(1)} %broadcast_in_dim.285.seg, ...), custom_call_target="tpu_custom_call" | custom-call | flops 17179869184 | bytes 8388608 | tf_op jit(solution)/shard_map/attend_back/pallas_call | solution.py:330
  247.7 4.2 %collective-permute-done.32.refs_1_ = bf16[512,1024]{1,0:T(8,128)(2,1)S(1)} collective-permute-done((bf16[512,1024]{1,0:T(8,128)(2,1)S(1)}, bf16[512,1024]{1,0:T(8,128)(2,1)S(1)}, u32[]{:S(2)}, u32[]{:S(2)}) %collective-permute-start.32) | collective-permute-done | bytes 1048608 | tf_op jit(solution)/shard_map/ppermute | solution.py:363
  253.4 3.3 collective-permute-start.39
  260.5 2.4 fusion.14.refs_0_
  278.1 2.9 norm_one_back.1
  283.8 2.9 output.1
  286.7 9.2 %collective-permute-done.41.refs_1_ = bf16[512,1024]{1,0:T(8,128)(2,1)S(1)} collective-permute-done((bf16[512,1024]{1,0:T(8,128)(2,1)S(1)}, bf16[512,1024]{1,0:T(8,128)(2,1)S(1)}, u32[]{:S(2)}, u32[]{:S(2)}) %collective-permute-start.41) | collective-permute-done | bytes 1048608 | tf_op jit(solution)/shard_map/ppermute | solution.py:363
  303.6 9.2 %collective-permute-done.48.refs_1_ = bf16[128,1024]{1,0:T(8,128)(2,1)} collective-permute-done((bf16[128,1024]{1,0:T(8,128)(2,1)}, bf16[128,1024]{1,0:T(8,128)(2,1)}, u32[]{:S(2)}, u32[]{:S(2)}) %collective-permute-start.48) | collective-permute-done | bytes 262176 | tf_op jit(solution)/shard_map/ppermute | solution.py:370
  332.7 3.8 %collective-permute-done.49.refs_1_ = bf16[320,1024]{1,0:T(8,128)(2,1)S(1)} collective-permute-done((bf16[320,1024]{1,0:T(8,128)(2,1)}, bf16[320,1024]{1,0:T(8,128)(2,1)S(1)}, u32[]{:S(2)}, u32[]{:S(2)}) %collective-permute-start.49) | collective-permute-done | bytes 655392 | tf_op jit(solution)/shard_map/ppermute | solution.py:370
  348.8 13.0 %collective-permute-done.51.refs_1_ = bf16[192,1024]{1,0:T(8,128)(2,1)S(1)} collective-permute-done((bf16[192,1024]{1,0:T(8,128)(2,1)S(1)}, bf16[192,1024]{1,0:T(8,128)(2,1)S(1)}, u32[]{:S(2)}, u32[]{:S(2)}) %collective-permute-start.51) | collective-permute-done | bytes 393248 | tf_op jit(solution)/shard_map/ppermute | solution.py:370
  (446 shorter events, 157.2 us)
Async XLA Ops:
  8.0 17.7 %collective-permute-start.2 = (bf16[144,1024]{1,0:T(8,128)(2,1)S(1)}, bf16[144,1024]{1,0:T(8,128)(2,1)S(1)}, u32[]{:S(2)}, u32[]{:S(2)}) collective-permute-start(bf16[144,1024]{1,0:T(8,128)(2,1)S(1)} %turn.22.refs_0_), channel_id=1, source_target_pairs={{0,16},{4,20},{8,24},{12,28},{16,0},{20,4},{24,8},{28,12},{1,17},{... | collective-permute-start | bytes 884744 | tf_op jit(solution)/shard_map/ppermute | solution.py:370
  12.2 14.9 %collective-permute-start.4 = (bf16[256,1024]{1,0:T(8,128)(2,1)S(1)}, bf16[256,1024]{1,0:T(8,128)(2,1)S(1)}, u32[]{:S(2)}, u32[]{:S(2)}) collective-permute-start(bf16[256,1024]{1,0:T(8,128)(2,1)S(1)} %get-tuple-element.730), channel_id=1, source_target_pairs={{0,2},{2,0},{1,3},{3,1},{4,6},{6,4},{5,7},{7,5},{8,10},{10,8},{9,1... | collective-permute-start | bytes 1572872 | tf_op jit(solution)/shard_map/ppermute | solution.py:363
  15.1 22.0 %collective-permute-start.5 = (bf16[256,1024]{1,0:T(8,128)(2,1)S(1)}, bf16[256,1024]{1,0:T(8,128)(2,1)S(1)}, u32[]{:S(2)}, u32[]{:S(2)}) collective-permute-start(bf16[256,1024]{1,0:T(8,128)(2,1)S(1)} %get-tuple-element.728), channel_id=1, source_target_pairs={{0,2},{2,0},{1,3},{3,1},{4,6},{6,4},{5,7},{7,5},{8,10},{10,8},{9,1... | collective-permute-start | bytes 1572872 | tf_op jit(solution)/shard_map/ppermute | solution.py:363
  26.2 14.1 %collective-permute-start.3 = (bf16[272,1024]{1,0:T(8,128)(2,1)S(1)}, bf16[272,1024]{1,0:T(8,128)(2,1)S(1)}, u32[]{:S(2)}, u32[]{:S(2)}) collective-permute-start(bf16[272,1024]{1,0:T(8,128)(2,1)S(1)} %turn.23.refs_0_), channel_id=1, source_target_pairs={{0,8},{4,12},{8,0},{12,4},{16,24},{20,28},{24,16},{28,20},{1,9},{5... | collective-permute-start | bytes 1671176 | tf_op jit(solution)/shard_map/ppermute | solution.py:370
  42.0 17.4 %collective-permute-start.6 = (bf16[256,1024]{1,0:T(8,128)(2,1)}, bf16[256,1024]{1,0:T(8,128)(2,1)}, u32[]{:S(2)}, u32[]{:S(2)}) collective-permute-start(bf16[256,1024]{1,0:T(8,128)(2,1)} %get-tuple-element.386.refs_0_), channel_id=1, source_target_pairs={{0,4},{4,0},{8,12},{12,8},{16,20},{20,16},{24,28},{28,24},{1,5},{5... | collective-permute-start | bytes 1572872 | tf_op jit(solution)/shard_map/ppermute | solution.py:370
  43.3 16.1 %collective-permute-start.7 = (bf16[272,1024]{1,0:T(8,128)(2,1)}, bf16[272,1024]{1,0:T(8,128)(2,1)}, u32[]{:S(2)}, u32[]{:S(2)}) collective-permute-start(bf16[272,1024]{1,0:T(8,128)(2,1)} %get-tuple-element.388.refs_2_), channel_id=1, source_target_pairs={{0,2},{2,0},{1,3},{3,1},{4,6},{6,4},{5,7},{7,5},{8,10},{10,8},{9,1... | collective-permute-start | bytes 1671176 | tf_op jit(solution)/shard_map/ppermute | solution.py:363
  45.0 14.4 %collective-permute-start.8 = (bf16[128,1024]{1,0:T(8,128)(2,1)}, bf16[128,1024]{1,0:T(8,128)(2,1)S(1)}, u32[]{:S(2)}, u32[]{:S(2)}) collective-permute-start(bf16[128,1024]{1,0:T(8,128)(2,1)} %get-tuple-element.390.refs_4_), channel_id=1, source_target_pairs={{0,16},{4,20},{8,24},{12,28},{16,0},{20,4},{24,8},{28,12},{1,17},{... | collective-permute-start | bytes 786440 | tf_op jit(solution)/shard_map/ppermute | solution.py:370
  61.2 24.9 %collective-permute-start.10 = (bf16[528,1024]{1,0:T(8,128)(2,1)S(1)}, bf16[528,1024]{1,0:T(8,128)(2,1)S(1)}, u32[]{:S(2)}, u32[]{:S(2)}) collective-permute-start(bf16[528,1024]{1,0:T(8,128)(2,1)S(1)} %get-tuple-element.405.refs_2_), channel_id=1, source_target_pairs={{0,4},{4,0},{8,12},{12,8},{16,20},{20,16},{24,28},{28,24},{1,5},{5... | collective-permute-start | bytes 3244040 | tf_op jit(solution)/shard_map/ppermute | solution.py:370
  61.8 23.9 %collective-permute-start.9 = (bf16[512,1024]{1,0:T(8,128)(2,1)S(1)}, bf16[512,1024]{1,0:T(8,128)(2,1)S(1)}, u32[]{:S(2)}, u32[]{:S(2)}) collective-permute-start(bf16[512,1024]{1,0:T(8,128)(2,1)S(1)} %get-tuple-element.403.refs_0_), channel_id=1, source_target_pairs={{0,2},{2,0},{1,3},{3,1},{4,6},{6,4},{5,7},{7,5},{8,10},{10,8},{9,1... | collective-permute-start | bytes 3145736 | tf_op jit(solution)/shard_map/ppermute | solution.py:363
  62.3 18.0 %collective-permute-start.11 = (bf16[256,1024]{1,0:T(8,128)(2,1)S(1)}, bf16[256,1024]{1,0:T(8,128)(2,1)S(1)}, u32[]{:S(2)}, u32[]{:S(2)}) collective-permute-start(bf16[256,1024]{1,0:T(8,128)(2,1)S(1)} %get-tuple-element.409.refs_0_), channel_id=1, source_target_pairs={{0,8},{4,12},{8,0},{12,4},{16,24},{20,28},{24,16},{28,20},{1,9},{5... | collective-permute-start | bytes 1572872 | tf_op jit(solution)/shard_map/ppermute | solution.py:370
  63.9 15.6 %collective-permute-start.12 = (bf16[128,1024]{1,0:T(8,128)(2,1)S(1)}, bf16[128,1024]{1,0:T(8,128)(2,1)S(1)}, u32[]{:S(2)}, u32[]{:S(2)}) collective-permute-start(bf16[128,1024]{1,0:T(8,128)(2,1)S(1)} %get-tuple-element.411.refs_2_), channel_id=1, source_target_pairs={{0,16},{4,20},{8,24},{12,28},{16,0},{20,4},{24,8},{28,12},{1,17},{... | collective-permute-start | bytes 786440 | tf_op jit(solution)/shard_map/ppermute | solution.py:370
  107.4 17.3 %collective-permute-start.20 = (bf16[512,1024]{1,0:T(8,128)(2,1)S(1)}, bf16[512,1024]{1,0:T(8,128)(2,1)S(1)}, u32[]{:S(2)}, u32[]{:S(2)}) collective-permute-start(bf16[512,1024]{1,0:T(8,128)(2,1)S(1)} %copy-done.5), channel_id=1, source_target_pairs={{0,1},{1,0},{2,3},{3,2},{4,5},{5,4},{6,7},{7,6},{8,9},{9,8},{10,11... | collective-permute-start | bytes 3145736 | tf_op jit(solution)/shard_map/ppermute | solution.py:359
  108.3 25.6 %collective-permute-start.18 = (bf16[512,1024]{1,0:T(8,128)(2,1)S(1)}, bf16[512,1024]{1,0:T(8,128)(2,1)S(1)}, u32[]{:S(2)}, u32[]{:S(2)}) collective-permute-start(bf16[512,1024]{1,0:T(8,128)(2,1)S(1)} %get-tuple-element.459.refs_0_), channel_id=1, source_target_pairs={{0,2},{2,0},{1,3},{3,1},{4,6},{6,4},{5,7},{7,5},{8,10},{10,8},{9,1... | collective-permute-start | bytes 3145736 | tf_op jit(solution)/shard_map/ppermute | solution.py:363
  109.9 25.3 %collective-permute-start.19 = (bf16[512,1024]{1,0:T(8,128)(2,1)S(1)}, bf16[512,1024]{1,0:T(8,128)(2,1)S(1)}, u32[]{:S(2)}, u32[]{:S(2)}) collective-permute-start(bf16[512,1024]{1,0:T(8,128)(2,1)S(1)} %get-tuple-element.461.refs_2_), channel_id=1, source_target_pairs={{0,4},{4,0},{8,12},{12,8},{16,20},{20,16},{24,28},{28,24},{1,5},{5... | collective-permute-start | bytes 3145736 | tf_op jit(solution)/shard_map/ppermute | solution.py:370
  135.8 14.4 %collective-permute-start.21 = (bf16[256,1024]{1,0:T(8,128)(2,1)S(1)}, bf16[256,1024]{1,0:T(8,128)(2,1)S(1)}, u32[]{:S(2)}, u32[]{:S(2)}) collective-permute-start(bf16[256,1024]{1,0:T(8,128)(2,1)S(1)} %get-tuple-element.464.refs_0_), channel_id=1, source_target_pairs={{0,4},{4,0},{8,12},{12,8},{16,20},{20,16},{24,28},{28,24},{1,5},{5... | collective-permute-start | bytes 1572872 | tf_op jit(solution)/shard_map/ppermute | solution.py:370
  136.9 14.1 %collective-permute-start.22 = (bf16[256,1024]{1,0:T(8,128)(2,1)S(1)}, bf16[256,1024]{1,0:T(8,128)(2,1)S(1)}, u32[]{:S(2)}, u32[]{:S(2)}) collective-permute-start(bf16[256,1024]{1,0:T(8,128)(2,1)S(1)} %get-tuple-element.466.refs_2_), channel_id=1, source_target_pairs={{0,2},{2,0},{1,3},{3,1},{4,6},{6,4},{5,7},{7,5},{8,10},{10,8},{9,1... | collective-permute-start | bytes 1572872 | tf_op jit(solution)/shard_map/ppermute | solution.py:363
  151.9 25.6 %collective-permute-start.24 = (bf16[512,1024]{1,0:T(8,128)(2,1)S(1)}, bf16[512,1024]{1,0:T(8,128)(2,1)S(1)}, u32[]{:S(2)}, u32[]{:S(2)}) collective-permute-start(bf16[512,1024]{1,0:T(8,128)(2,1)S(1)} %get-tuple-element.474.refs_0_), channel_id=1, source_target_pairs={{0,2},{2,0},{1,3},{3,1},{4,6},{6,4},{5,7},{7,5},{8,10},{10,8},{9,1... | collective-permute-start | bytes 3145736 | tf_op jit(solution)/shard_map/ppermute | solution.py:363
  152.5 25.3 %collective-permute-start.25 = (bf16[512,1024]{1,0:T(8,128)(2,1)S(1)}, bf16[512,1024]{1,0:T(8,128)(2,1)S(1)}, u32[]{:S(2)}, u32[]{:S(2)}) collective-permute-start(bf16[512,1024]{1,0:T(8,128)(2,1)S(1)} %get-tuple-element.476.refs_2_), channel_id=1, source_target_pairs={{0,4},{4,0},{8,12},{12,8},{16,20},{20,16},{24,28},{28,24},{1,5},{5... | collective-permute-start | bytes 3145736 | tf_op jit(solution)/shard_map/ppermute | solution.py:370
  180.6 24.9 %collective-permute-start.27 = (bf16[512,1024]{1,0:T(8,128)(2,1)}, bf16[512,1024]{1,0:T(8,128)(2,1)}, u32[]{:S(2)}, u32[]{:S(2)}) collective-permute-start(bf16[512,1024]{1,0:T(8,128)(2,1)} %get-tuple-element.481), channel_id=1, source_target_pairs={{0,2},{2,0},{1,3},{3,1},{4,6},{6,4},{5,7},{7,5},{8,10},{10,8},{9,1... | collective-permute-start | bytes 3145736 | tf_op jit(solution)/shard_map/ppermute | solution.py:363
  182.1 24.5 %collective-permute-start.28 = (bf16[512,1024]{1,0:T(8,128)(2,1)}, bf16[512,1024]{1,0:T(8,128)(2,1)}, u32[]{:S(2)}, u32[]{:S(2)}) collective-permute-start(bf16[512,1024]{1,0:T(8,128)(2,1)} %get-tuple-element.482), channel_id=1, source_target_pairs={{0,4},{4,0},{8,12},{12,8},{16,20},{20,16},{24,28},{28,24},{1,5},{5... | collective-permute-start | bytes 3145736 | tf_op jit(solution)/shard_map/ppermute | solution.py:370
  208.7 14.4 %collective-permute-start.29 = (bf16[256,1024]{1,0:T(8,128)(2,1)S(1)}, bf16[256,1024]{1,0:T(8,128)(2,1)S(1)}, u32[]{:S(2)}, u32[]{:S(2)}) collective-permute-start(bf16[256,1024]{1,0:T(8,128)(2,1)S(1)} %get-tuple-element.502), channel_id=1, source_target_pairs={{0,4},{4,0},{8,12},{12,8},{16,20},{20,16},{24,28},{28,24},{1,5},{5... | collective-permute-start | bytes 1572872 | tf_op jit(solution)/shard_map/ppermute | solution.py:370
  224.8 22.8 %collective-permute-start.34 = (bf16[256,1024]{1,0:T(8,128)(2,1)S(1)}, bf16[256,1024]{1,0:T(8,128)(2,1)S(1)}, u32[]{:S(2)}, u32[]{:S(2)}) collective-permute-start(bf16[256,1024]{1,0:T(8,128)(2,1)S(1)} %get-tuple-element.534), channel_id=1, source_target_pairs={{0,8},{4,12},{8,0},{12,4},{16,24},{20,28},{24,16},{28,20},{1,9},{5... | collective-permute-start | bytes 1572872 | tf_op jit(solution)/shard_map/ppermute | solution.py:370
  226.6 25.3 %collective-permute-start.32 = (bf16[512,1024]{1,0:T(8,128)(2,1)S(1)}, bf16[512,1024]{1,0:T(8,128)(2,1)S(1)}, u32[]{:S(2)}, u32[]{:S(2)}) collective-permute-start(bf16[512,1024]{1,0:T(8,128)(2,1)S(1)} %get-tuple-element.531), channel_id=1, source_target_pairs={{0,2},{2,0},{1,3},{3,1},{4,6},{6,4},{5,7},{7,5},{8,10},{10,8},{9,1... | collective-permute-start | bytes 3145736 | tf_op jit(solution)/shard_map/ppermute | solution.py:363
  227.2 25.0 %collective-permute-start.33 = (bf16[512,1024]{1,0:T(8,128)(2,1)S(1)}, bf16[512,1024]{1,0:T(8,128)(2,1)S(1)}, u32[]{:S(2)}, u32[]{:S(2)}) collective-permute-start(bf16[512,1024]{1,0:T(8,128)(2,1)S(1)} %get-tuple-element.532), channel_id=1, source_target_pairs={{0,4},{4,0},{8,12},{12,8},{16,20},{20,16},{24,28},{28,24},{1,5},{5... | collective-permute-start | bytes 3145736 | tf_op jit(solution)/shard_map/ppermute | solution.py:370
  228.1 24.0 %collective-permute-start.36 = (bf16[512,1024]{1,0:T(8,128)(2,1)S(1)}, bf16[512,1024]{1,0:T(8,128)(2,1)S(1)}, u32[]{:S(2)}, u32[]{:S(2)}) collective-permute-start(bf16[512,1024]{1,0:T(8,128)(2,1)S(1)} %fusion.28), channel_id=1, source_target_pairs={{0,1},{1,0},{2,3},{3,2},{4,5},{5,4},{6,7},{7,6},{8,9},{9,8},{10,11... | collective-permute-start | bytes 3145736 | tf_op jit(solution)/shard_map/ppermute | solution.py:359
  253.4 14.4 %collective-permute-start.39 = (bf16[128,1024]{1,0:T(8,128)(2,1)S(1)}, bf16[128,1024]{1,0:T(8,128)(2,1)S(1)}, u32[]{:S(2)}, u32[]{:S(2)}) collective-permute-start(bf16[128,1024]{1,0:T(8,128)(2,1)S(1)} %get-tuple-element.564), channel_id=1, source_target_pairs={{0,16},{4,20},{8,24},{12,28},{16,0},{20,4},{24,8},{28,12},{1,17},{... | collective-permute-start | bytes 786440 | tf_op jit(solution)/shard_map/ppermute | solution.py:370
  272.5 14.2 %collective-permute-start.43 = (bf16[256,1024]{1,0:T(8,128)(2,1)S(1)}, bf16[256,1024]{1,0:T(8,128)(2,1)S(1)}, u32[]{:S(2)}, u32[]{:S(2)}) collective-permute-start(bf16[256,1024]{1,0:T(8,128)(2,1)S(1)} %get-tuple-element.592), channel_id=1, source_target_pairs={{0,8},{4,12},{8,0},{12,4},{16,24},{20,28},{24,16},{28,20},{1,9},{5... | collective-permute-start | bytes 1572872 | tf_op jit(solution)/shard_map/ppermute | solution.py:370
  273.0 22.9 %collective-permute-start.41 = (bf16[512,1024]{1,0:T(8,128)(2,1)S(1)}, bf16[512,1024]{1,0:T(8,128)(2,1)S(1)}, u32[]{:S(2)}, u32[]{:S(2)}) collective-permute-start(bf16[512,1024]{1,0:T(8,128)(2,1)S(1)} %get-tuple-element.589), channel_id=1, source_target_pairs={{0,2},{2,0},{1,3},{3,1},{4,6},{6,4},{5,7},{7,5},{8,10},{10,8},{9,1... | collective-permute-start | bytes 3145736 | tf_op jit(solution)/shard_map/ppermute | solution.py:363
  274.4 22.6 %collective-permute-start.42 = (bf16[512,1024]{1,0:T(8,128)(2,1)S(1)}, bf16[512,1024]{1,0:T(8,128)(2,1)S(1)}, u32[]{:S(2)}, u32[]{:S(2)}) collective-permute-start(bf16[512,1024]{1,0:T(8,128)(2,1)S(1)} %get-tuple-element.590), channel_id=1, source_target_pairs={{0,4},{4,0},{8,12},{12,8},{16,20},{20,16},{24,28},{28,24},{1,5},{5... | collective-permute-start | bytes 3145736 | tf_op jit(solution)/shard_map/ppermute | solution.py:370
  322.1 14.5 %collective-permute-start.49 = (bf16[320,1024]{1,0:T(8,128)(2,1)}, bf16[320,1024]{1,0:T(8,128)(2,1)S(1)}, u32[]{:S(2)}, u32[]{:S(2)}) collective-permute-start(bf16[320,1024]{1,0:T(8,128)(2,1)} %get-tuple-element.648), channel_id=1, source_target_pairs={{0,8},{4,12},{8,0},{12,4},{16,24},{20,28},{24,16},{28,20},{1,9},{5... | collective-permute-start | bytes 1966088 | tf_op jit(solution)/shard_map/ppermute | solution.py:370
  339.5 22.3 %collective-permute-start.52 = (bf16[256,1024]{1,0:T(8,128)(2,1)}, bf16[256,1024]{1,0:T(8,128)(2,1)}, u32[]{:S(2)}, u32[]{:S(2)}) collective-permute-start(bf16[256,1024]{1,0:T(8,128)(2,1)} %get-tuple-element.664), channel_id=1, source_target_pairs={{0,2},{2,0},{1,3},{3,1},{4,6},{6,4},{5,7},{7,5},{8,10},{10,8},{9,1... | collective-permute-start | bytes 1572872 | tf_op jit(solution)/shard_map/ppermute | solution.py:363
  345.3 16.6 %collective-permute-start.51 = (bf16[192,1024]{1,0:T(8,128)(2,1)S(1)}, bf16[192,1024]{1,0:T(8,128)(2,1)S(1)}, u32[]{:S(2)}, u32[]{:S(2)}) collective-permute-start(bf16[192,1024]{1,0:T(8,128)(2,1)S(1)} %copy-done.70), channel_id=1, source_target_pairs={{0,16},{4,20},{8,24},{12,28},{16,0},{20,4},{24,8},{28,12},{1,17},{... | collective-permute-start | bytes 1179656 | tf_op jit(solution)/shard_map/ppermute | solution.py:370
  (114 other events, 731.0 us)

commit v4 on v3

--- a/solution.py
+++ b/solution.py
@@ -402,6 +402,14 @@
 class Turn:
     def __init__(self):
         self.arrays, self.shapes, self.jobs = [], [], []
+        self.kept = None
+
+    def keep(self, rows, columns):
+        if self.kept is None:
+            self.kept = self.write((0, columns), BF16)
+        before = self.shapes[self.kept].shape[0]
+        self.shapes[self.kept] = jax.ShapeDtypeStruct((before + rows, columns), BF16)
+        return self.kept, before
 
     def read(self, array):
         for i, other in enumerate(self.arrays):
@@ -463,12 +471,12 @@
 
 
 class Gather:
-    def __init__(self, first, second):
-        far = list(reversed(far_bits()))
-        self.pieces = [
-            Piece(array, array.shape[0], [], [*far, *last])
-            for array, last in ((first, (1, 0)), (second, (0, 1)))
-        ]
+    def __init__(self, *parts):
+        self.pieces = []
+        for array, first, rows, order in parts:
+            piece = Piece(array, rows, [], order)
+            piece.held = (array, first)
+            self.pieces.append(piece)
 
     def wants(self):
         return [(p.order[0], p.rows << (len(p.bits) + (p.came is not None))) for p in self.pieces]
@@ -501,30 +509,31 @@
     def left(self):
         return len(self.pieces[0].order)
 
-    def result(self, bits, outs):
-        turn = Turn()
-        made = [turn.write(shape, BF16) for shape, _ in outs]
-        for i, p in enumerate(self.pieces):
-            held, came = turn.read(p.held[0]), turn.read(p.came[0])
-            moves = [(out, move) for out, (_, moves) in zip(made, outs) for move in moves[i]]
-
-            def job(mine, ins, refs, p=p, held=held, came=came, moves=moves):
-                everyone = [*p.bits, p.last]
-                for choice in combinations(p.bits):
-                    at = flat_index(choice, p.bits)
-                    for source, base, value in (
-                        (ins[held], p.held[1], mine[p.last]),
-                        (ins[came], p.came[1], 1 - mine[p.last]),
-                    ):
-                        chip = flat_index({**choice, p.last: value}, everyone)
-                        for out, ((low, high), (left, right), stride, row, column) in moves:
-                            start = pl.multiple_of(chip * stride + row, math.gcd(stride, row) if row else stride)
-                            refs[out][pl.ds(start, high - low), column : column + right - left] = source[
-                                pl.ds(base + at * p.rows + low, high - low), left:right
-                            ]
-
-            turn.jobs.append(job)
-        return turn.run(bits)
+
+def gathered(pieces, bits, outs):
+    turn = Turn()
+    made = [turn.write(shape, BF16) for shape, _ in outs]
+    for i, p in enumerate(pieces):
+        held, came = turn.read(p.held[0]), turn.read(p.came[0])
+        moves = [(out, move) for out, (_, moves) in zip(made, outs) for move in moves[i]]
+
+        def job(mine, ins, refs, p=p, held=held, came=came, moves=moves):
+            everyone = [*p.bits, p.last]
+            for choice in combinations(p.bits):
+                at = flat_index(choice, p.bits)
+                for source, base, value in (
+                    (ins[held], p.held[1], mine[p.last]),
+                    (ins[came], p.came[1], 1 - mine[p.last]),
+                ):
+                    chip = flat_index({**choice, p.last: value}, everyone)
+                    for out, ((low, high), (left, right), stride, row, column) in moves:
+                        start = pl.multiple_of(chip * stride + row, math.gcd(stride, row) if row else stride)
+                        refs[out][pl.ds(start, high - low), column : column + right - left] = source[
+                            pl.ds(base + at * p.rows + low, high - low), left:right
+                        ]
+
+        turn.jobs.append(job)
+    return turn.run(bits)
 
 
 class Spread:
@@ -562,8 +571,9 @@
 
 
 class Rider:
-    def __init__(self, array, bit):
-        self.pieces = [Piece(array, array.shape[0], [], [bit])]
+    def __init__(self, array, bit, first, rows):
+        self.pieces = [Piece(array, rows, [], [bit])]
+        self.pieces[0].held = (array, first)
 
     wants, turn, settle = Spread.wants, Spread.turn, Spread.settle
     arrays, relabel, left = Gather.arrays, Gather.relabel, Gather.left
@@ -571,6 +581,40 @@
     def result(self):
         [p] = self.pieces
         return p.came[0][p.came[1] : p.came[1] + p.rows]
+
+
+class Total:
+    def __init__(self, array, order):
+        self.pieces = [Piece(array, array.shape[0], [], order)]
+
+    wants, arrays, relabel, left = Spread.wants, Gather.arrays, Gather.relabel, Gather.left
+
+    def turn(self, turn, places):
+        [p], [(out, base)] = self.pieces, places
+        p.order.pop(0)
+        held, rows = turn.read(p.held[0]), p.rows
+        came, came_base = (None, 0) if p.came is None else (turn.read(p.came[0]), p.came[1])
+        p.next = None if came is None else turn.write(p.held[0].shape, F32)
+
+        def job(mine, ins, refs, keep=p.next):
+            own = ins[held][...].astype(BF16)
+            if came is not None:
+                total = own.astype(F32) + ins[came][came_base : came_base + rows].astype(F32)
+                refs[keep][...] = total
+                own = total.astype(BF16)
+            refs[out][base : base + rows] = own
+
+        turn.jobs.append(job)
+
+    def settle(self, outs, came):
+        [p] = self.pieces
+        if p.next is not None:
+            p.held = (outs[p.next], 0)
+        p.came = came[0]
+
+    def result(self):
+        [p] = self.pieces
+        return add_came(p.held[0], p.came[0][p.came[1] : p.came[1] + p.rows])
 
 
 def copy_rows(source, source_base, out, base, rows):
@@ -598,19 +642,13 @@
 
 
 class Scatter:
-    def __init__(self, first, second=None):
+    def __init__(self, *parts):
         far = far_bits()
         bits = sorted([0, 1, *far], reverse=True)
-        rows = first.shape[0] >> len(bits)
-        if second is None:
-            half = rows // 2
-            self.pieces = [
-                Piece(first, half, bits, [*near, *far], rows, base) for near, base in (((0, 1), 0), ((1, 0), half))
-            ]
-        else:
-            self.pieces = [
-                Piece(array, rows, bits, [*near, *far]) for array, near in ((first, (0, 1)), (second, (1, 0)))
-            ]
+        self.pieces = [
+            Piece(array, rows, bits, [*((1, 0) if turned else (0, 1)), *far], stride, first)
+            for array, rows, stride, first, turned in parts
+        ]
 
     def wants(self):
         return [(p.order[0], p.rows << (len(p.bits) - len(p.fixed) - 1)) for p in self.pieces]
@@ -638,16 +676,16 @@
 
             else:
                 came, came_base = turn.read(p.came[0]), p.came[1]
-                keep = turn.write((rows << len(free), p.held[0].shape[1]), BF16)
-                p.next = keep
+                keep, keep_base = turn.keep(rows << len(free), p.held[0].shape[1])
+                p.next = (keep, keep_base)
 
                 def job(
                     mine, ins, refs, held=held, rows=rows, fixed=fixed, free=free, bit=bit, out=out, base=base,
-                    came=came, came_base=came_base, keep=keep, block=block,
+                    came=came, came_base=came_base, keep=keep, keep_base=keep_base, block=block,
                 ):
                     settled = {b: mine[b] for b in fixed}
                     for choice in combinations(free):
-                        for value, target, start in ((1 - mine[bit], out, base), (mine[bit], keep, 0)):
+                        for value, target, start in ((1 - mine[bit], out, base), (mine[bit], keep, keep_base)):
                             now = {**choice, bit: value}
                             total = ins[held][block({**now, **settled})].astype(F32) + ins[came][
                                 block_of(flat_index(now, [*free, bit]), rows, came_base)
@@ -662,7 +700,7 @@
             if p.next is None:
                 p.fixed = [p.sent]
             else:
-                p.held, p.bits, p.fixed = (outs[p.next], 0), list(p.free), []
+                p.held, p.bits, p.fixed = (outs[p.next[0]], p.next[1]), list(p.free), []
                 p.stride, p.source = p.rows, False
             p.came = where
 
@@ -671,11 +709,11 @@
     def result(self, bits):
         turn = Turn()
         for p in self.pieces:
-            held, came, base, rows = turn.read(p.held[0]), turn.read(p.came[0]), p.came[1], p.rows
+            held, came, base, rows, first = turn.read(p.held[0]), turn.read(p.came[0]), p.came[1], p.rows, p.held[1]
             out = turn.write((rows, p.held[0].shape[1]), F32)
 
-            def job(mine, ins, refs, held=held, came=came, base=base, rows=rows, out=out):
-                refs[out][...] = ins[held][...].astype(F32) + ins[came][base : base + rows].astype(F32)
+            def job(mine, ins, refs, held=held, came=came, base=base, rows=rows, out=out, first=first):
+                refs[out][...] = ins[held][first : first + rows].astype(F32) + ins[came][base : base + rows].astype(F32)
 
             turn.jobs.append(job)
         return turn.run(bits)
@@ -711,7 +749,7 @@
     return add_came(array, swap_bit(array.astype(BF16), bit))
 
 
-def phase(bits, moves, work, *values):
+def phase(bits, moves, work, *values, also=()):
     chains = [move if isinstance(move, tuple) else (move, 1) for move in moves]
     chains = [
         ([move for move in chain[:-1] if move.left()], min(chain[-1], chain[0].left())) for chain in chains
@@ -719,10 +757,13 @@
     moves = [move for chain, _ in chains for move in chain]
 
     def tie(extra):
-        arrays = [a for move in moves for a in move.arrays()]
+        arrays = []
+        for array in (a for move in [*moves, *also] for a in move.arrays()):
+            if not any(array is other for other in arrays):
+                arrays.append(array)
         held, extra = fence(arrays, extra)
         table = list(zip(arrays, held))
-        for move in moves:
+        for move in [*moves, *also]:
             move.relabel(lambda array: next(new for old, new in table if old is array))
         return extra
 
@@ -945,10 +986,22 @@
         return product(left[:own], weights) + came.astype(F32)
 
     low_down, high_down = jnp.split(mlp_out.astype(BF16), 2)
-    gather_in = Gather(shard[:, :width], shard[:, width : 2 * width])
+    ahead = list(reversed(far_bits()))
+    one_way, other_way = [*ahead, 1, 0], [*ahead, 0, 1]
+    block = 2 * rows
+    gather_in = Gather(
+        (shard[:, :width], 0, block, one_way), (shard[:, width : 2 * width], 0, block, other_way)
+    )
     gather_vectors = Spread(vector_rows)
-    gather_up = Gather(shard[:, 2 * width : 2 * width + half * 2], shard[:, 2 * width + half * 2 :])
-    gather_down = Gather(low_down, high_down)
+    gather_up = Gather(
+        (shard[:, 2 * width : 2 * width + half * 2], 0, block, one_way),
+        (shard[:, 2 * width + half * 2 :], 0, block, other_way),
+    )
+    low_down = mlp_out.astype(BF16)
+    side = 3 * ff_rows // 8 if ff_rows % 128 == 0 else ff_rows // 2
+    rest_rows = ff_rows - 2 * side
+    gather_down = Gather((low_down, 0, side, one_way), (low_down, side, side, other_way))
+    gather_rest = [Gather((low_down, 2 * side, rest_rows, [1, 0, *ahead]))] if rest_rows else []
 
     patches, cotangent = phase(
         bits,
@@ -981,12 +1034,12 @@
 
     far = far_bits()
     stream, hat_one, inverse_one, grad_own = phase(
-        bits, [gather_in, gather_vectors, gather_up], first, patches, cotangent
+        bits, [gather_in, gather_vectors, gather_up, *gather_rest], first, patches, cotangent
     )
     phase(bits, [gather_in, gather_vectors, (gather_up, len(far) - 1), gather_down], None)
-    block = 2 * rows
     spare = in_width - width
-    in_matrix, out_columns = gather_in.result(
+    in_matrix, out_columns = gathered(
+        gather_in.pieces,
         bits,
         [
             (
@@ -1007,26 +1060,29 @@
     bias_up = unroll_bias(vector_part, own_c, ff_rows)
     bias_qkv = jnp.concatenate([bias_query, jnp.zeros_like(bias_query), bias_value], axis=1)
 
-    def project(hat_one, in_matrix, out_columns):
-        normed_one = with_core((hat_one * gain_one + shift_one).astype(BF16))
+    def project(hat_one, out_columns):
         low, high = out_columns[:half], out_columns[half:]
         keep_out, came_out = pick(own_c, low, high), swap_core(pick(own_c, high, low))
         out_matrix = join(pick(own_c, keep_out, came_out), pick(own_c, came_out, keep_out), 1)
-        return normed_one, out_matrix, (nn(normed_one, in_matrix) + bias_qkv).astype(BF16)
-
-    normed_one, out_matrix, qkv = phase(
-        bits,
-        [gather_up, (gather_down, len(far) - 1)], project, hat_one, in_matrix, out_columns
+        return out_matrix, (hat_one * gain_one + shift_one).astype(BF16)
+
+    out_matrix, normed_one = phase(
+        bits, [gather_up, (gather_down, len(far) - 1), *gather_rest], project, hat_one, out_columns
     )
 
     def matmul_rows(left, right, product, name):
         return product(left[own:], right).astype(BF16)
 
-    def attend(qkv, out_matrix, grad_own):
+    def attend(normed_one, in_matrix, out_matrix, grad_own):
+        normed_one = with_core(normed_one)
+        qkv = (nn(normed_one, in_matrix) + bias_qkv).astype(BF16)
         mixed, log_sum = attention(qkv, seg, info, per, head_size)
-        return mixed, log_sum, matmul_rows(mixed, out_matrix, nn, "out_away"), with_core(grad_own)
-
-    mixed, log_sum, out_away, grad_last = phase(bits, [gather_up], attend, qkv, out_matrix, grad_own)
+        away = matmul_rows(mixed, out_matrix, nn, "out_away")
+        return normed_one, qkv, mixed, log_sum, away, with_core(grad_own)
+
+    normed_one, qkv, mixed, log_sum, out_away, grad_last = phase(
+        bits, [gather_up, *gather_rest], attend, normed_one, in_matrix, out_matrix, grad_own
+    )
 
     def project_out(stream, mixed, out_away, out_matrix):
         def body(stream, mixed, came, matrix, bias, gain, shift):
@@ -1046,7 +1102,8 @@
     stream_two, hat_two, inverse_two, normed_two = phase(
         bits, [gather_down], project_out, stream, mixed, out_away, out_matrix
     )
-    (up_matrix,) = gather_up.result(
+    (up_matrix,) = gathered(
+        gather_up.pieces,
         bits,
         [
             (
@@ -1063,22 +1120,25 @@
         hidden = hidden.astype(BF16)
         return normed_two, hidden, slope, tn(hidden, grad_last).astype(BF16)
 
-    normed_two, hidden, slope, grad_down = phase(bits, [gather_down], expand, normed_two, up_matrix, grad_last)
+    normed_two, hidden, slope, grad_down = phase(
+        bits, [gather_down, *((move, 9) for move in gather_rest)], expand, normed_two, up_matrix, grad_last
+    )
     part_rows = ff_rows // 2
-    (down_matrix,) = gather_down.result(
+    down_pieces = [piece for move in [gather_down, *gather_rest] for piece in move.pieces]
+    (down_matrix,) = gathered(
+        down_pieces,
         bits,
         [
             (
                 (ff_half, width),
-                (
-                    [((0, part_rows), (0, width), ff_rows, 0, 0)],
-                    [((0, part_rows), (0, width), ff_rows, part_rows, 0)],
-                ),
+                [[((0, piece.rows), (0, width), ff_rows, i * side, 0)] for i, piece in enumerate(down_pieces)],
             )
         ],
     )
 
-    scatter_down = Scatter(grad_down)
+    scatter_down = Scatter(
+        (grad_down, part_rows, ff_rows, 0, False), (grad_down, part_rows, ff_rows, part_rows, True)
+    )
 
     def hidden_back(grad_last, down_matrix, slope, normed_two, up_matrix):
         grad_pre = (nt(grad_last, down_matrix) * slope).astype(BF16)
@@ -1092,7 +1152,7 @@
     grad_pre, two_away, *grad_up = phase(
         bits, [scatter_down], hidden_back, grad_last, down_matrix, slope, normed_two, up_matrix
     )
-    scatter_up = Scatter(*grad_up)
+    scatter_up = Scatter((grad_up[0], block, block, 0, False), (grad_up[1], block, block, 0, True))
 
     def norm_back(grad, away, matrix, hat, inverse, added, gain, name):
         def body(grad, came, hat, inverse, added, matrix, gain):
@@ -1122,13 +1182,27 @@
         down_matrix,
     )
 
+    paired = block % 64 == 0
+
+    def pair(array):
+        blocks = array.reshape(chips, 2, -1, array.shape[1])
+        return jnp.concatenate([blocks[:, 0], blocks[:, 1]], axis=2).reshape(-1, 2 * array.shape[1])
+
+    def part(array):
+        columns = array.shape[1] // 2
+        return jnp.concatenate([array[:, :columns], array[:, columns:]], axis=0)
+
     def attention_grads(grad_branch, out_matrix, qkv, mixed, log_sum, output_away):
         grad_branch = with_core(grad_branch)
         grad_mixed = nt(grad_branch, out_matrix).astype(BF16)
         grad_qkv = attention_back(0, 1, qkv, mixed, grad_mixed, seg, log_sum, info, per, head_size)
-        return grad_branch, swap_core(output_away), grad_qkv
-
-    grad_branch, came_output, grad_qkv = phase(
+        grad_rows = tn(mixed, grad_branch).astype(BF16)
+        low, high = grad_rows[:, :half], grad_rows[:, half:]
+        keep_rows, came_rows = pick(own_c, low, high), swap_core(pick(own_c, high, low))
+        grad_out = join(pick(own_c, keep_rows, came_rows), pick(own_c, came_rows, keep_rows), 0)
+        return grad_branch, swap_core(output_away), grad_qkv, pair(grad_out) if paired else grad_out
+
+    grad_branch, came_output, grad_qkv, grad_out = phase(
         bits,
         [scatter_up, scatter_down],
         attention_grads,
@@ -1139,23 +1213,34 @@
         log_sum,
         output_away,
     )
-
-    def in_grads(mixed, grad_branch, normed_one, grad_qkv, in_matrix):
-        grad_rows = tn(mixed, grad_branch).astype(BF16)
-        low, high = grad_rows[:, :half], grad_rows[:, half:]
-        keep_rows, came_rows = pick(own_c, low, high), swap_core(pick(own_c, high, low))
-        grad_out = join(pick(own_c, keep_rows, came_rows), pick(own_c, came_rows, keep_rows), 0)
+    quarter = block // 4
+    scatter_out = []
+    if paired:
+        scatter_out = [
+            Scatter(
+                (grad_out, quarter, 2 * quarter, 0, False), (grad_out, quarter, 2 * quarter, quarter, True)
+            )
+        ]
+
+    def in_grads(normed_one, grad_qkv, in_matrix):
+        right = tn(normed_one, grad_qkv[:, width:]).astype(BF16)
         return (
             matmul_rows(grad_qkv, in_matrix, nt, "norm_one_away"),
             tn(normed_one, grad_qkv[:, :width]).astype(BF16),
-            tn(normed_one, grad_qkv[:, width:]).astype(BF16),
-            grad_out,
+            pair(right) if paired else right,
         )
 
-    one_away, left, right, grad_out = phase(
-        bits, [scatter_up, scatter_down], in_grads, mixed, grad_branch, normed_one, grad_qkv, in_matrix
-    )
-    scatter_in = Scatter(left, join(right, grad_out, 1))
+    one_away, left, right = phase(
+        bits, [scatter_up, *scatter_out, scatter_down], in_grads, normed_one, grad_qkv, in_matrix
+    )
+    if paired:
+        scatter_in = Scatter(
+            (left, 3 * quarter, block, 0, False),
+            (left, quarter, block, 3 * quarter, True),
+            (right, 2 * quarter, 2 * quarter, 0, True),
+        )
+    else:
+        scatter_in = Scatter((left, block, block, 0, False), (join(right, grad_out, 1), block, block, 0, True))
 
     def widen(row):
         zero = jnp.zeros_like(row)
@@ -1169,9 +1254,10 @@
             grad_qkv, one_away, in_matrix, hat_one, inverse_one, grad_two, gain_one, "norm_one_back"
         )
         wide_place = jnp.pad(place, ((0, 0), (vector_count, narrow_rows - vector_count - table_size)))
-        narrow = lax.dot_general(
+        table_part = lax.dot_general(
             wide_place, grad_stream, (((0,), (0,)), ((), ())), precision=PRECISE, preferred_element_type=F32
-        ) + roll_bias(token_sums(grad_pre), own_c, width, narrow_rows, ff_rows)
+        )
+        bias_part = roll_bias(token_sums(grad_pre), own_c, width, narrow_rows, ff_rows)
         sums = token_sums(grad_qkv)
         rows_of_sums = [
             grad_gain_one,
@@ -1183,9 +1269,19 @@
             grad_shift_two,
             token_sums(grad_last[:own]),
         ]
-        row = jnp.arange(narrow_rows)[:, None]
-        for i, values in enumerate(rows_of_sums):
-            narrow = jnp.where(row == i, values, narrow)
+
+        def stack(*refs):
+            refs[-1][...] = refs[0][...] + refs[1][...]
+            for i in range(len(rows_of_sums)):
+                refs[-1][i : i + 1] = refs[2 + i][...]
+
+        narrow = pl.pallas_call(
+            stack,
+            name="narrow",
+            out_shape=jax.ShapeDtypeStruct((narrow_rows, width), F32),
+            compiler_params=pltpu.CompilerParams(vmem_limit_bytes=4 << 20),
+            cost_estimate=pl.CostEstimate(flops=0, bytes_accessed=0, transcendentals=0),
+        )(table_part, bias_part, *rows_of_sums)
         return grad_low, add_came(narrow, swap_core(narrow.astype(BF16)))
 
     def finish_output(hidden, came, stream_two, down_matrix):
@@ -1203,38 +1299,11 @@
 
     (grad_low, narrow), (output,) = phase(
         bits,
-        [scatter_in, scatter_up, (scatter_down, len(far) - 1)],
+        [scatter_in, *scatter_out, scatter_up, (scatter_down, len(far) - 1)],
         lambda values, others: (norm_one_back(*values), finish_output(*others)),
         (grad_qkv, one_away, in_matrix, hat_one, inverse_one, grad_two, grad_pre, grad_branch, grad_last),
         (hidden, came_output, stream_two, down_matrix),
     )
-
-    def ride(narrow, bit):
-        return Rider(narrow.astype(BF16), bit)
-
-    scatters = [scatter_in, scatter_up]
-    rider = ride(narrow, 0)
-    phase(bits, [*scatters, rider], None)
-    narrow = add_came(narrow, rider.result())
-    sent = [Rider(output[local_len:], 0), Rider(grad_low[local_len:], 0)]
-    for step, bit in enumerate(far):
-        rider = ride(narrow, bit)
-        phase(bits, [*scatters, rider, *sent[step : step + 1]], None)
-        narrow = add_came(narrow, rider.result())
-    while any(move.left() for move in [*scatters, *sent]):
-        phase(bits, [*scatters, *sent], None)
-    narrow = add_hop(narrow, 1)
-    came_output, came_grad = (rider.result() for rider in sent)
-
-    def back_to_rows(array, other):
-        mine = array[:local_len]
-        return jnp.stack([pick(own_y, mine, other), pick(own_y, other, mine)], axis=0)
-
-    output, input_grad = back_to_rows(output, came_output), back_to_rows(grad_low, came_grad)
-    shard_down = jnp.concatenate(scatter_down.result(bits), axis=0)
-    shard_up = jnp.concatenate(scatter_up.result(bits), axis=1)
-    shard_in = jnp.concatenate(scatter_in.result(bits), axis=1)
-    shard_in, shard_out = shard_in[:, :in_width], shard_in[:, in_width:]
 
     def rows_of(array, core):
         return lax.dynamic_slice_in_dim(array, core * rows, rows, 0)
@@ -1246,30 +1315,150 @@
         both = jnp.stack([pick(own_c, keep, came), pick(own_c, came, keep)], axis=2)
         return both.reshape(rows, -1)
 
-    grad_up_shard = trade(shard_up, chips)
-    grad_out_shard = trade(shard_out, 1)
-    grad_in_shard = trade(shard_in, 3)
+    factor = 1.0 / slot_total
+
+    def adam(weight, gradient, first_moment, second_moment):
+        return by_rows(
+            lambda w, g, m, v: adam_update(w, g, m, v, factor, 0.05),
+            [weight, gradient, first_moment, second_moment],
+            [],
+            [(weight.shape[1], F32)] * 3,
+            name="adam",
+            tile=weight.shape[0],
+        )
+
+    scatters = [scatter_in, *scatter_out, scatter_up]
+    total = Total(narrow, [0, *ahead, 1])
+    phase(bits, [*scatters, total], None)
+    core = own_c.astype(jnp.int32).reshape(1)
+
+    def split_rows(pieces, columns, rule):
+        arrays = []
+        for p in pieces:
+            arrays += [p.held[0], p.came[0]]
+
+        def kernel(own, *refs):
+            away, keep = refs[-2:]
+            for here in (0, 1):
+
+                @pl.when(own[0] == here)
+                def _(here=here):
+                    for out, which in ((keep, here), (away, 1 - here)):
+                        for i, (low, high), (left, right), row, column in rule(which):
+                            p = pieces[i]
+                            at, came = p.held[1] + low, p.came[1] + low
+                            out[row : row + high - low, column : column + right - left] = refs[2 * i][
+                                at : at + high - low, left:right
+                            ].astype(F32) + refs[2 * i + 1][came : came + high - low, left:right].astype(F32)
+
+        size = sum(a.size * jnp.dtype(a.dtype).itemsize for a in arrays) + 8 * rows * columns
+        return pl.pallas_call(
+            kernel,
+            name="split_rows",
+            out_shape=[jax.ShapeDtypeStruct((rows, columns), F32)] * 2,
+            in_specs=[pl.BlockSpec(memory_space=pltpu.SMEM)]
+            + [pl.BlockSpec(memory_space=pltpu.VMEM)] * len(arrays),
+            compiler_params=pltpu.CompilerParams(vmem_limit_bytes=size + (2 << 20)),
+            cost_estimate=pl.CostEstimate(flops=0, bytes_accessed=0, transcendentals=0),
+        )(core, *arrays)
+
+    def adam_joined(keep, came, blocks, weight, first_moment, second_moment):
+        span = keep.shape[1] // blocks
+
+        def kernel(own, keep, came, weight, first, second, *outs):
+            low_is_own = own[0] == 0
+            for i in range(blocks):
+                mine, other = keep[:, i * span : (i + 1) * span], came[:, i * span : (i + 1) * span]
+                for j, values in enumerate(
+                    (jnp.where(low_is_own, mine, other), jnp.where(low_is_own, other, mine))
+                ):
+                    at = slice((2 * i + j) * span, (2 * i + j + 1) * span)
+                    made = adam_update(weight[:, at], values, first[:, at], second[:, at], factor, 0.05)
+                    for out, value in zip(outs, (values, *made)):
+                        out[:, at] = value
+
+        size = 4 * (2 * keep.size + 7 * weight.size)
+        gradient, *updated = pl.pallas_call(
+            kernel,
+            name="adam_joined",
+            out_shape=[jax.ShapeDtypeStruct(weight.shape, F32)] * 4,
+            in_specs=[pl.BlockSpec(memory_space=pltpu.SMEM)] + [pl.BlockSpec(memory_space=pltpu.VMEM)] * 5,
+            compiler_params=pltpu.CompilerParams(vmem_limit_bytes=size + (2 << 20)),
+            cost_estimate=pl.CostEstimate(flops=0, bytes_accessed=0, transcendentals=0),
+        )(core, keep, came, weight, first_moment, second_moment)
+        return gradient, updated
+
+    def finish_up():
+        away, keep = split_rows(
+            scatter_up.pieces,
+            ff_half,
+            lambda c: [(i, (c * rows, (c + 1) * rows), (0, width), 0, i * width) for i in (0, 1)],
+        )
+        return adam_joined(keep, swap_core(away), chips, mlp_in, first_mlp_in, second_mlp_in)
+
+    def finish_mlp():
+        shard_down = jnp.concatenate(scatter_down.result(bits), axis=0)
+        if paired:
+            shard_up, adam_up = finish_up()
+        else:
+            shard_up = trade(jnp.concatenate(scatter_up.result(bits), axis=1), chips)
+            adam_up = adam(mlp_in, shard_up, first_mlp_in, second_mlp_in)
+        return shard_up, shard_down, adam_up, adam(mlp_out, shard_down, first_mlp_out, second_mlp_out)
+
+    send_output = Rider(output, 0, local_len, local_len)
+    send_grad = Rider(grad_low, 0, local_len, local_len)
+    rest = [scatter_in, *scatter_out, total]
+    if scatter_up.left():
+        phase(bits, [*rest, (scatter_up, 9)], None)
+    grad_up_shard, shard_down, adam_up, adam_down = phase(
+        bits, [*rest, send_output], finish_mlp, also=[scatter_up, scatter_down]
+    )
+
+    def back_to_rows(array, other):
+        mine = array[:local_len]
+        return jnp.stack([pick(own_y, mine, other), pick(own_y, other, mine)], axis=0)
+
+    output = phase(bits, [*rest, send_grad], back_to_rows, output, send_output.result())
+    while scatter_in.left():
+        phase(bits, rest, None)
+    while total.left() > 1:
+        phase(bits, [total], None)
+    if total.left():
+        phase(bits, [total], None)
+    input_grad = back_to_rows(grad_low, send_grad.result())
+    narrow = total.result()
+    if paired:
+
+        def in_rule(c):
+            left = [(0, (0, rows), (0, width), 0, 0)]
+            if c == 1:
+                left = [
+                    (0, (rows, 3 * quarter), (0, width), 0, 0),
+                    (1, (0, quarter), (0, width), 3 * quarter - rows, 0),
+                ]
+            return [*left, (2, (0, rows), (c * half, (c + 1) * half), 0, width)]
+
+        away, keep = split_rows(scatter_in.pieces, in_width, in_rule)
+        grad_in_shard, adam_in = adam_joined(keep, swap_core(away), 3, attn_in, first_attn_in, second_attn_in)
+        away, keep = split_rows(
+            scatter_out[0].pieces,
+            half,
+            lambda c: [(i, (0, quarter), (c * half, (c + 1) * half), i * quarter, 0) for i in (0, 1)],
+        )
+        grad_out_shard, adam_out = adam_joined(
+            keep, swap_core(away), 1, attn_out, first_attn_out, second_attn_out
+        )
+    else:
+        shard_in = jnp.concatenate(scatter_in.result(bits), axis=1)
+        grad_out_shard, grad_in_shard = trade(shard_in[:, in_width:], 1), trade(shard_in[:, :in_width], 3)
+        adam_in = adam(attn_in, grad_in_shard, first_attn_in, second_attn_in)
+        adam_out = adam(attn_out, grad_out_shard, first_attn_out, second_attn_out)
+    updated = [adam_in, adam_out, adam_up, adam_down]
     device = (lax.axis_index("img") * halves + own_y) * 2 + own_c
     grad_vectors_shard = lax.dynamic_slice_in_dim(narrow[:vector_count], device * rows, rows, 1).T
     table_grad = narrow[vector_count : vector_count + table_size]
 
-    factor = 1.0 / slot_total
     shards = (grad_in_shard, grad_out_shard, grad_up_shard, shard_down, grad_vectors_shard)
-    weights = (attn_in, attn_out, mlp_in, mlp_out, vectors)
-    firsts = (first_attn_in, first_attn_out, first_mlp_in, first_mlp_out, first_vectors)
-    seconds = (second_attn_in, second_attn_out, second_mlp_in, second_mlp_out, second_vectors)
-    decays = (0.05, 0.05, 0.05, 0.05, 0.0)
-    updated = [
-        by_rows(
-            lambda w, g, m, v, decay=decays[i]: adam_update(w, g, m, v, factor, decay),
-            [weights[i], shards[i], firsts[i], seconds[i]],
-            [],
-            [(weights[i].shape[1], F32)] * 3,
-            name="adam",
-            tile=weights[i].shape[0],
-        )
-        for i in range(4)
-    ]
     updated.append(adam_update(vectors, grad_vectors_shard, first_vectors, second_vectors, factor, 0.0))
     return (
         output,

time: 377 us -> 357 us (0.947)
  local copies, waits for them, and re-layouts: 33.9 us -> 16.4 us
  starting transfers between devices: 54.4 us -> 64.5 us
  waiting for transfers between devices: 140 us -> 135 us
  other arithmetic: 17.5 us -> 13.4 us
    unnamed x189 -> x166, local copies, waits for them, and re-layouts: 24.6 us -> 9.57 us
    ppermute x25 -> x30, starting transfers between devices: 36.8 us -> 46 us  [swap_bit(): lax.ppermute(array, 'img', [(i, i ^ 1 << bit - 1) for i in range(count)])]
    ppermute x16, waiting for transfers between devices: 56.5 us -> 49.7 us  [swap_chip(): return lax.ppermute(array, 'sy', SWAP)]
    pallas_call x0 -> x7, Pallas kernels: none -> 4.16 us  [the longest x3 4 us: adam_joined(): pl.pallas_call(kernel, name='adam_joined', out_shape=[jax.ShapeDtypeStruc...]
    pallas_call x9 -> x6, Pallas kernels: 19.1 us -> 15.8 us  [by_rows(): pl.pallas_call(kernel, name=name, grid=(length // tile,), out_shape=[jax....]
    pallas_call x22 -> x21, Pallas kernels: 24.1 us -> 21.6 us  [run(): pl.pallas_call(kernel, name='turn', out_shape=tuple(self.shapes), in_spec...]
    ppermute x25 -> x30, waiting for transfers between devices: 82.4 us -> 83.5 us  [swap_bit(): lax.ppermute(array, 'img', [(i, i ^ 1 << bit - 1) for i in range(count)])]
  transfers between devices with their start and end apart: 57 -> 62, of which waited for: 36 -> 37; matrix products, arithmetic and copies ran while one was open for 19% -> 19% of each run, Pallas kernels for 15% -> 15%
where the time goes in v4:
time: 357 us; the launch traced here: 353 us
  waiting for transfers between devices  135 us (38%)
  Pallas kernels  70.1 us (20%)
  starting transfers between devices  64.5 us (18%)
  matrix products  51.4 us (14%)
  local copies, waits for them, and re-layouts  16.4 us (5%)
  other arithmetic  13.4 us (4%)
    ppermute x30, waiting for transfers between devices, swap_bit(): lax.ppermute(array, 'img', [(i, i ^ 1 << bit - 1) for i in range(count)])  83.5 us
    ppermute x16, waiting for transfers between devices, swap_chip(): return lax.ppermute(array, 'sy', SWAP)  49.7 us
    ppermute x30, starting transfers between devices, swap_bit(): lax.ppermute(array, 'img', [(i, i ^ 1 << bit - 1) for i in range(count)])  46 us
    pallas_call x21, Pallas kernels, run(): pl.pallas_call(kernel, name='turn', out_shape=tuple(self.shapes), in_spec...  21.6 us
    dot_general x9, matrix products, nn(): return jnp.dot(left, right, preferred_element_type=F32)  18.7 us
    dot_general x6, matrix products, tn(): lax.dot_general(left, right, (((0,), (0,)), ((), ())), preferred_element_...  17 us
    pallas_call x1, Pallas kernels, attention_back(): pl.pallas_call(functools.partial(attend_back_kernel, part * pairs, pairs,...  16.3 us
    ppermute x16, starting transfers between devices, swap_chip(): return lax.ppermute(array, 'sy', SWAP)  16.3 us
  transfers between devices with their start and end apart: 62, of which 37 were waited for; matrix products, arithmetic and copies ran while one was open for 19% of the time, Pallas kernels for 15%

profile of v4, /device:TPU:0, one launch (start us, length us, event | category | flops | bytes accessed | tf_op | source)
XLA Modules:
  0.0 353.1 jit_solution(15127078276271549132)
XLA Ops:
  7.8 4.1 %collective-permute-start.2 = (bf16[144,1024]{1,0:T(8,128)(2,1)S(1)}, bf16[144,1024]{1,0:T(8,128)(2,1)S(1)}, u32[]{:S(2)}, u32[]{:S(2)}) collective-permute-start(bf16[144,1024]{1,0:T(8,128)(2,1)S(1)} %turn.21.refs_0_), channel_id=1, source_target_pairs={{0,16},{4,20},{8,24},{12,28},{16,0},{20,4},{24,8},{28,12},{1,17},{... | collective-permute-start | bytes 884744 | tf_op jit(solution)/shard_map/ppermute | solution.py:370
  16.8 8.7 %collective-permute-done.2.refs_1_ = bf16[144,1024]{1,0:T(8,128)(2,1)S(1)} collective-permute-done((bf16[144,1024]{1,0:T(8,128)(2,1)S(1)}, bf16[144,1024]{1,0:T(8,128)(2,1)S(1)}, u32[]{:S(2)}, u32[]{:S(2)}) %collective-permute-start.2) | collective-permute-done | bytes 294944 | tf_op jit(solution)/shard_map/ppermute | solution.py:370
  28.3 9.9 %collective-permute-done.5 = bf16[256,1024]{1,0:T(8,128)(2,1)S(1)} collective-permute-done((bf16[256,1024]{1,0:T(8,128)(2,1)S(1)}, bf16[256,1024]{1,0:T(8,128)(2,1)S(1)}, u32[]{:S(2)}, u32[]{:S(2)}) %collective-permute-start.5) | collective-permute-done | bytes 524320 | tf_op jit(solution)/shard_map/ppermute | solution.py:363
  50.3 3.3 first.4
  55.3 4.0 %collective-permute-done.8.refs_5_ = bf16[128,1024]{1,0:T(8,128)(2,1)} collective-permute-done((bf16[128,1024]{1,0:T(8,128)(2,1)}, bf16[128,1024]{1,0:T(8,128)(2,1)}, u32[]{:S(2)}, u32[]{:S(2)}) %collective-permute-start.8) | collective-permute-done | bytes 262176 | tf_op jit(solution)/shard_map/ppermute | solution.py:370
  63.1 3.4 collective-permute-start.12
  66.5 11.4 %collective-permute-done.12.refs_3_ = bf16[96,1024]{1,0:T(8,128)(2,1)S(1)} collective-permute-done((bf16[96,1024]{1,0:T(8,128)(2,1)S(1)}, bf16[96,1024]{1,0:T(8,128)(2,1)S(1)}, u32[]{:S(2)}, u32[]{:S(2)}) %collective-permute-start.12) | collective-permute-done | bytes 196640 | tf_op jit(solution)/shard_map/ppermute | solution.py:370
  78.9 6.8 %collective-permute-done.9.refs_1_ = bf16[512,1024]{1,0:T(8,128)(2,1)S(1)} collective-permute-done((bf16[512,1024]{1,0:T(8,128)(2,1)S(1)}, bf16[512,1024]{1,0:T(8,128)(2,1)S(1)}, u32[]{:S(2)}, u32[]{:S(2)}) %collective-permute-start.9) | collective-permute-done | bytes 1048608 | tf_op jit(solution)/shard_map/ppermute | solution.py:363
  99.6 5.5 %collective-permute-done.15.refs_1_ = bf16[192,1024]{1,0:T(8,128)(2,1)S(1)} collective-permute-done((bf16[192,1024]{1,0:T(8,128)(2,1)S(1)}, bf16[192,1024]{1,0:T(8,128)(2,1)S(1)}, u32[]{:S(2)}, u32[]{:S(2)}) %collective-permute-start.15) | collective-permute-done | bytes 393248 | tf_op jit(solution)/shard_map/ppermute | solution.py:370
  105.1 6.1 %collective-permute-done.13.refs_1_ = bf16[256,1024]{1,0:T(8,128)(2,1)S(1)} collective-permute-done((bf16[256,1024]{1,0:T(8,128)(2,1)S(1)}, bf16[256,1024]{1,0:T(8,128)(2,1)S(1)}, u32[]{:S(2)}, u32[]{:S(2)}) %collective-permute-start.13) | collective-permute-done | bytes 524320 | tf_op jit(solution)/shard_map/ppermute | solution.py:370
  111.2 3.6 %collective-permute-done.14.refs_3_ = bf16[320,1024]{1,0:T(8,128)(2,1)S(1)} collective-permute-done((bf16[320,1024]{1,0:T(8,128)(2,1)S(1)}, bf16[320,1024]{1,0:T(8,128)(2,1)S(1)}, u32[]{:S(2)}, u32[]{:S(2)}) %collective-permute-start.14) | collective-permute-done | bytes 655392 | tf_op jit(solution)/shard_map/ppermute | solution.py:363
  117.3 3.4 collective-permute-start.19
  122.3 3.6 %add_convert_fusion.qkv = bf16[1024,1536]{1,0:T(8,128)(2,1)S(1)} fusion(bf16[1024,1024]{1,0:T(8,128)(2,1)S(1)} %constant_dynamic-update-slice_fusion, bf16[1024,1536]{1,0:T(8,128)(2,1)S(1)} %copy-done.14, f32[1536]{0:T(1024)S(1)} %maximum_reduce_fusion), kind=kOutput, calls=%fused_computation.8 | convolution fusion | flops 3224371200 | bytes 8394752 | tf_op jit(solution)/shard_map/dot_general | solution.py:124
  126.0 12.1 %attend.1 = (bf16[1024,512]{1,0:T(8,128)(2,1)S(1)}, f32[8,1024]{1,0:T(8,128)S(1)}) custom-call(s32[18]{0:T(128)S(1)} %pad_add_fusion.2.info, bf16[1024,1536]{1,0:T(8,128)(2,1)S(1)} %add_convert_fusion.qkv, f32[8,1024]{1,0:T(8,128)S(1)} %broadcast_in_dim.182.seg), custom_call_target="tpu_custom_call" | custom-call | tf_op jit(solution)/shard_map/attend/pallas_call | solution.py:288
  139.5 6.1 %collective-permute-done.17.refs_1_ = bf16[512,1024]{1,0:T(8,128)(2,1)S(1)} collective-permute-done((bf16[512,1024]{1,0:T(8,128)(2,1)S(1)}, bf16[512,1024]{1,0:T(8,128)(2,1)S(1)}, u32[]{:S(2)}, u32[]{:S(2)}) %collective-permute-start.17) | collective-permute-done | bytes 1048608 | tf_op jit(solution)/shard_map/ppermute | solution.py:363
  151.4 6.5 %collective-permute-done.22.refs_1_ = bf16[192,1024]{1,0:T(8,128)(2,1)S(1)} collective-permute-done((bf16[192,1024]{1,0:T(8,128)(2,1)S(1)}, bf16[192,1024]{1,0:T(8,128)(2,1)S(1)}, u32[]{:S(2)}, u32[]{:S(2)}) %collective-permute-start.22) | collective-permute-done | bytes 393248 | tf_op jit(solution)/shard_map/ppermute | solution.py:370
  162.6 9.1 %fusion.3 = (f32[1024,2048]{1,0:T(8,128)}, bf16[1024,2048]{1,0:T(8,128)(2,1)S(1)}) fusion(f32[2048]{0:T(1024)S(1)} %bitcast.132, bf16[1024,1024]{1,0:T(8,128)(2,1)S(1)} %constant_dynamic-update-slice_fusion.2, bf16[1024,2048]{1,0:T(8,128)(2,1)S(1)} %turn.29.refs_5_), kind=kOutput, calls=%fused_computation.4 | convolution fusion | flops 4318035968 | bytes 18882560 | tf_op jit(solution)/shard_map/dot_general | solution.py:124
  171.8 5.4 %convolution_convert_fusion.refs_0_ = bf16[2048,1024]{1,0:T(8,128)(2,1)S(1)} fusion(bf16[1024,2048]{1,0:T(8,128)(2,1)S(1)} %get-tuple-element.631.refs_0_, bf16[1024,1024]{1,0:T(8,128)(2,1)S(1)} %pad_maximum_fusion), kind=kOutput, calls=%fused_computation.9 | convolution fusion | flops 4297064448 | bytes 10485760 | tf_op jit(solution)/shard_map/dot_general | solution.py:120
  185.4 7.0 %multiply_convert_fusion.refs_0_ = bf16[1024,2048]{1,0:T(8,128)(2,1)S(1)} fusion(f32[1024,2048]{1,0:T(8,128)} %get-tuple-element.517, bf16[1024,1024]{1,0:T(8,128)(2,1)S(1)} %copy-done.59, bf16[2048,1024]{1,0:T(8,128)(2,1)S(1)} %turn.31.refs_4_), kind=kOutput, calls=%fused_computation.5 | convolution fusion | flops 4299161600 | bytes 18874368 | tf_op jit(solution)/shard_map/dot_general | solution.py:116
  192.4 4.1 %fusion.20.refs_1_.refs_2_ = bf16[1024,1024]{1,0:T(8,128)(2,1)S(1)} fusion(bf16[1024,1024]{1,0:T(8,128)(2,1)} %copy-done.66, bf16[1024,2048]{1,0:T(8,128)(2,1)S(1)} %multiply_convert_fusion.refs_0_), kind=kOutput, calls=%fused_computation.24 | convolution fusion | flops 2148532224 | bytes 6291456 | tf_op jit(solution)/shard_map/dot_general | solution.py:120
  201.5 7.2 %collective-permute-done.29.refs_1_ = bf16[512,1024]{1,0:T(8,128)(2,1)} collective-permute-done((bf16[512,1024]{1,0:T(8,128)(2,1)}, bf16[512,1024]{1,0:T(8,128)(2,1)}, u32[]{:S(2)}, u32[]{:S(2)}) %collective-permute-start.29) | collective-permute-done | bytes 1048608 | tf_op jit(solution)/shard_map/ppermute | solution.py:363
  213.6 3.3 fusion.28
  217.0 3.8 %norm_two_back.1 = (f32[512,1024]{1,0:T(8,128)S(1)}, bf16[512,1024]{1,0:T(8,128)(2,1)S(1)}, f32[1,1024]{1,0:T(1,128)S(1)}, f32[1,1024]{1,0:T(1,128)S(1)}) custom-call(bf16[1024,2048]{1,0:T(8,128)(2,1)S(1)} %multiply_convert_fusion.refs_0_, bf16[512,1024]{1,0:T(8,128)(2,1)S(1)} %collective-permute-done.33.refs_1_, f32[512,1024]{1,0:T(8,128)S(1)} %copy-done.29, ...), custom_call_target="tpu_custom_call" | custom-call | tf_op jit(solution)/shard_map/norm_two_back/pallas_call | solution.py:809
  220.8 4.6 %collective-permute-done.31.refs_3_ = bf16[256,1024]{1,0:T(8,128)(2,1)S(1)} collective-permute-done((bf16[256,1024]{1,0:T(8,128)(2,1)S(1)}, bf16[256,1024]{1,0:T(8,128)(2,1)S(1)}, u32[]{:S(2)}, u32[]{:S(2)}) %collective-permute-start.31) | collective-permute-done | bytes 524320 | tf_op jit(solution)/shard_map/ppermute | solution.py:370
  234.4 16.3 %attend_back.1.refs_0_ = bf16[1024,1536]{1,0:T(8,128)(2,1)S(1)} custom-call(s32[18]{0:T(128)S(1)} %copy-done.55, bf16[1024,1536]{1,0:T(8,128)(2,1)S(1)} %copy-done.12, bf16[1024,512]{1,0:T(8,128)(2,1)S(1)} %copy-done.10, bf16[1024,512]{1,0:T(8,128)(2,1)S(1)} %convolution_convert_fusion.3.grad, f32[8,1024]{1,0:T(8,128)S(1)} %broadcast_in_dim.182.seg, ...), custom_call_target="tpu_custom_call" | custom-call | flops 17179869184 | bytes 8388608 | tf_op jit(solution)/shard_map/attend_back/pallas_call | solution.py:330
  264.1 6.1 %collective-permute-done.42.refs_1_ = bf16[128,1024]{1,0:T(8,128)(2,1)S(1)} collective-permute-done((bf16[128,1024]{1,0:T(8,128)(2,1)S(1)}, bf16[128,1024]{1,0:T(8,128)(2,1)S(1)}, u32[]{:S(2)}, u32[]{:S(2)}) %collective-permute-start.42) | collective-permute-done | bytes 262176 | tf_op jit(solution)/shard_map/ppermute | solution.py:370
  270.1 4.8 %collective-permute-done.40.refs_4_ = bf16[384,1024]{1,0:T(8,128)(2,1)S(1)} collective-permute-done((bf16[384,1024]{1,0:T(8,128)(2,1)S(1)}, bf16[384,1024]{1,0:T(8,128)(2,1)S(1)}, u32[]{:S(2)}, u32[]{:S(2)}) %collective-permute-start.40) | collective-permute-done | bytes 786464 | tf_op jit(solution)/shard_map/ppermute | solution.py:370
  290.9 7.3 %collective-permute-done.43.refs_1_ = bf16[448,1024]{1,0:T(8,128)(2,1)S(1)} collective-permute-done((bf16[448,1024]{1,0:T(8,128)(2,1)S(1)}, bf16[448,1024]{1,0:T(8,128)(2,1)S(1)}, u32[]{:S(2)}, u32[]{:S(2)}) %collective-permute-start.43) | collective-permute-done | bytes 917536 | tf_op jit(solution)/shard_map/ppermute | solution.py:363
  306.1 5.2 %collective-permute-done.50.refs_3_ = bf16[64,1024]{1,0:T(8,128)(2,1)S(1)} collective-permute-done((bf16[64,1024]{1,0:T(8,128)(2,1)S(1)}, bf16[64,1024]{1,0:T(8,128)(2,1)S(1)}, u32[]{:S(2)}, u32[]{:S(2)}) %collective-permute-start.50) | collective-permute-done | bytes 131104 | tf_op jit(solution)/shard_map/ppermute | solution.py:370
  314.9 3.2 collective-permute-start.53
  322.0 3.8 %collective-permute-done.53.refs_3_.refs_1_ = bf16[96,1024]{1,0:T(8,128)(2,1)S(1)} collective-permute-done((bf16[96,1024]{1,0:T(8,128)(2,1)S(1)}, bf16[96,1024]{1,0:T(8,128)(2,1)S(1)}, u32[]{:S(2)}, u32[]{:S(2)}) %collective-permute-start.53) | collective-permute-done | bytes 196640 | tf_op jit(solution)/shard_map/ppermute | solution.py:370
  336.9 6.3 %collective-permute-done.56.refs_1_.refs_3_.refs_5_ = bf16[96,1024]{1,0:T(8,128)(2,1)S(1)} collective-permute-done((bf16[96,1024]{1,0:T(8,128)(2,1)S(1)}, bf16[96,1024]{1,0:T(8,128)(2,1)S(1)}, u32[]{:S(2)}, u32[]{:S(2)}) %collective-permute-start.56) | collective-permute-done | bytes 196640 | tf_op jit(solution)/shard_map/ppermute | solution.py:370
  (413 shorter events, 154.5 us)
Async XLA Ops:
  7.8 17.7 %collective-permute-start.2 = (bf16[144,1024]{1,0:T(8,128)(2,1)S(1)}, bf16[144,1024]{1,0:T(8,128)(2,1)S(1)}, u32[]{:S(2)}, u32[]{:S(2)}) collective-permute-start(bf16[144,1024]{1,0:T(8,128)(2,1)S(1)} %turn.21.refs_0_), channel_id=1, source_target_pairs={{0,16},{4,20},{8,24},{12,28},{16,0},{20,4},{24,8},{28,12},{1,17},{... | collective-permute-start | bytes 884744 | tf_op jit(solution)/shard_map/ppermute | solution.py:370
  13.4 14.9 %collective-permute-start.4 = (bf16[256,1024]{1,0:T(8,128)(2,1)S(1)}, bf16[256,1024]{1,0:T(8,128)(2,1)S(1)}, u32[]{:S(2)}, u32[]{:S(2)}) collective-permute-start(bf16[256,1024]{1,0:T(8,128)(2,1)S(1)} %get-tuple-element.778), channel_id=1, source_target_pairs={{0,2},{2,0},{1,3},{3,1},{4,6},{6,4},{5,7},{7,5},{8,10},{10,8},{9,1... | collective-permute-start | bytes 1572872 | tf_op jit(solution)/shard_map/ppermute | solution.py:363
  16.2 22.1 %collective-permute-start.5 = (bf16[256,1024]{1,0:T(8,128)(2,1)S(1)}, bf16[256,1024]{1,0:T(8,128)(2,1)S(1)}, u32[]{:S(2)}, u32[]{:S(2)}) collective-permute-start(bf16[256,1024]{1,0:T(8,128)(2,1)S(1)} %get-tuple-element.776), channel_id=1, source_target_pairs={{0,2},{2,0},{1,3},{3,1},{4,6},{6,4},{5,7},{7,5},{8,10},{10,8},{9,1... | collective-permute-start | bytes 1572872 | tf_op jit(solution)/shard_map/ppermute | solution.py:363
  41.9 17.3 %collective-permute-start.7 = (bf16[272,1024]{1,0:T(8,128)(2,1)}, bf16[272,1024]{1,0:T(8,128)(2,1)}, u32[]{:S(2)}, u32[]{:S(2)}) collective-permute-start(bf16[272,1024]{1,0:T(8,128)(2,1)} %get-tuple-element.411.refs_2_), channel_id=1, source_target_pairs={{0,2},{2,0},{1,3},{3,1},{4,6},{6,4},{5,7},{7,5},{8,10},{10,8},{9,1... | collective-permute-start | bytes 1671176 | tf_op jit(solution)/shard_map/ppermute | solution.py:363
  43.2 16.0 %collective-permute-start.6 = (bf16[288,1024]{1,0:T(8,128)(2,1)}, bf16[288,1024]{1,0:T(8,128)(2,1)}, u32[]{:S(2)}, u32[]{:S(2)}) collective-permute-start(bf16[288,1024]{1,0:T(8,128)(2,1)} %get-tuple-element.434.refs_0_.refs_4_), channel_id=1, source_target_pairs={{0,4},{4,0},{8,12},{12,8},{16,20},{20,16},{24,28},{28,24},{1,5},{5... | collective-permute-start | bytes 1769480 | tf_op jit(solution)/shard_map/ppermute | solution.py:370
  44.7 14.5 %collective-permute-start.8 = (bf16[128,1024]{1,0:T(8,128)(2,1)}, bf16[128,1024]{1,0:T(8,128)(2,1)}, u32[]{:S(2)}, u32[]{:S(2)}) collective-permute-start(bf16[128,1024]{1,0:T(8,128)(2,1)} %get-tuple-element.413.refs_4_), channel_id=1, source_target_pairs={{0,16},{4,20},{8,24},{12,28},{16,0},{20,4},{24,8},{28,12},{1,17},{... | collective-permute-start | bytes 786440 | tf_op jit(solution)/shard_map/ppermute | solution.py:370
  61.2 24.9 %collective-permute-start.10 = (bf16[528,1024]{1,0:T(8,128)(2,1)S(1)}, bf16[528,1024]{1,0:T(8,128)(2,1)S(1)}, u32[]{:S(2)}, u32[]{:S(2)}) collective-permute-start(bf16[528,1024]{1,0:T(8,128)(2,1)S(1)} %get-tuple-element.427.refs_2_), channel_id=1, source_target_pairs={{0,4},{4,0},{8,12},{12,8},{16,20},{20,16},{24,28},{28,24},{1,5},{5... | collective-permute-start | bytes 3244040 | tf_op jit(solution)/shard_map/ppermute | solution.py:370
  61.8 23.9 %collective-permute-start.9 = (bf16[512,1024]{1,0:T(8,128)(2,1)S(1)}, bf16[512,1024]{1,0:T(8,128)(2,1)S(1)}, u32[]{:S(2)}, u32[]{:S(2)}) collective-permute-start(bf16[512,1024]{1,0:T(8,128)(2,1)S(1)} %get-tuple-element.425.refs_0_), channel_id=1, source_target_pairs={{0,2},{2,0},{1,3},{3,1},{4,6},{6,4},{5,7},{7,5},{8,10},{10,8},{9,1... | collective-permute-start | bytes 3145736 | tf_op jit(solution)/shard_map/ppermute | solution.py:363
  62.3 16.6 %collective-permute-start.11 = (bf16[256,1024]{1,0:T(8,128)(2,1)S(1)}, bf16[256,1024]{1,0:T(8,128)(2,1)S(1)}, u32[]{:S(2)}, u32[]{:S(2)}) collective-permute-start(bf16[256,1024]{1,0:T(8,128)(2,1)S(1)} %get-tuple-element.430.refs_0_), channel_id=1, source_target_pairs={{0,8},{4,12},{8,0},{12,4},{16,24},{20,28},{24,16},{28,20},{1,9},{5... | collective-permute-start | bytes 1572872 | tf_op jit(solution)/shard_map/ppermute | solution.py:370
  63.1 14.8 %collective-permute-start.12 = (bf16[96,1024]{1,0:T(8,128)(2,1)S(1)}, bf16[96,1024]{1,0:T(8,128)(2,1)S(1)}, u32[]{:S(2)}, u32[]{:S(2)}) collective-permute-start(bf16[96,1024]{1,0:T(8,128)(2,1)S(1)} %get-tuple-element.432.refs_2_), channel_id=1, source_target_pairs={{0,16},{4,20},{8,24},{12,28},{16,0},{20,4},{24,8},{28,12},{1,17},{... | collective-permute-start | bytes 589832 | tf_op jit(solution)/shard_map/ppermute | solution.py:370
  96.8 14.3 %collective-permute-start.13 = (bf16[256,1024]{1,0:T(8,128)(2,1)S(1)}, bf16[256,1024]{1,0:T(8,128)(2,1)S(1)}, u32[]{:S(2)}, u32[]{:S(2)}) collective-permute-start(bf16[256,1024]{1,0:T(8,128)(2,1)S(1)} %get-tuple-element.452.refs_0_), channel_id=1, source_target_pairs={{0,4},{4,0},{8,12},{12,8},{16,20},{20,16},{24,28},{28,24},{1,5},{5... | collective-permute-start | bytes 1572872 | tf_op jit(solution)/shard_map/ppermute | solution.py:370
  97.9 16.8 %collective-permute-start.14 = (bf16[320,1024]{1,0:T(8,128)(2,1)S(1)}, bf16[320,1024]{1,0:T(8,128)(2,1)S(1)}, u32[]{:S(2)}, u32[]{:S(2)}) collective-permute-start(bf16[320,1024]{1,0:T(8,128)(2,1)S(1)} %get-tuple-element.454.refs_2_), channel_id=1, source_target_pairs={{0,2},{2,0},{1,3},{3,1},{4,6},{6,4},{5,7},{7,5},{8,10},{10,8},{9,1... | collective-permute-start | bytes 1966088 | tf_op jit(solution)/shard_map/ppermute | solution.py:363
  115.9 22.2 %collective-permute-start.21 = (bf16[512,1024]{1,0:T(8,128)(2,1)S(1)}, bf16[512,1024]{1,0:T(8,128)(2,1)S(1)}, u32[]{:S(2)}, u32[]{:S(2)}) collective-permute-start(bf16[512,1024]{1,0:T(8,128)(2,1)S(1)} %copy-done.5), channel_id=1, source_target_pairs={{0,1},{1,0},{2,3},{3,2},{4,5},{5,4},{6,7},{7,6},{8,9},{9,8},{10,11... | collective-permute-start | bytes 3145736 | tf_op jit(solution)/shard_map/ppermute | solution.py:359
  117.3 22.2 %collective-permute-start.19 = (bf16[128,1024]{1,0:T(8,128)(2,1)S(1)}, bf16[128,1024]{1,0:T(8,128)(2,1)S(1)}, u32[]{:S(2)}, u32[]{:S(2)}) collective-permute-start(bf16[128,1024]{1,0:T(8,128)(2,1)S(1)} %get-tuple-element.495.refs_4_), channel_id=1, source_target_pairs={{0,16},{4,20},{8,24},{12,28},{16,0},{20,4},{24,8},{28,12},{1,17},{... | collective-permute-start | bytes 786440 | tf_op jit(solution)/shard_map/ppermute | solution.py:370
  120.7 24.8 %collective-permute-start.17 = (bf16[512,1024]{1,0:T(8,128)(2,1)S(1)}, bf16[512,1024]{1,0:T(8,128)(2,1)S(1)}, u32[]{:S(2)}, u32[]{:S(2)}) collective-permute-start(bf16[512,1024]{1,0:T(8,128)(2,1)S(1)} %get-tuple-element.486.refs_0_), channel_id=1, source_target_pairs={{0,2},{2,0},{1,3},{3,1},{4,6},{6,4},{5,7},{7,5},{8,10},{10,8},{9,1... | collective-permute-start | bytes 3145736 | tf_op jit(solution)/shard_map/ppermute | solution.py:363
  121.2 24.5 %collective-permute-start.18 = (bf16[512,1024]{1,0:T(8,128)(2,1)S(1)}, bf16[512,1024]{1,0:T(8,128)(2,1)S(1)}, u32[]{:S(2)}, u32[]{:S(2)}) collective-permute-start(bf16[512,1024]{1,0:T(8,128)(2,1)S(1)} %get-tuple-element.488.refs_2_), channel_id=1, source_target_pairs={{0,4},{4,0},{8,12},{12,8},{16,20},{20,16},{24,28},{28,24},{1,5},{5... | collective-permute-start | bytes 3145736 | tf_op jit(solution)/shard_map/ppermute | solution.py:370
  159.7 17.5 %collective-permute-start.27 = (bf16[256,1024]{1,0:T(8,128)(2,1)S(1)}, bf16[256,1024]{1,0:T(8,128)(2,1)S(1)}, u32[]{:S(2)}, u32[]{:S(2)}) collective-permute-start(bf16[256,1024]{1,0:T(8,128)(2,1)S(1)} %get-tuple-element.508.refs_4_), channel_id=1, source_target_pairs={{0,8},{4,12},{8,0},{12,4},{16,24},{20,28},{24,16},{28,20},{1,9},{5... | collective-permute-start | bytes 1572872 | tf_op jit(solution)/shard_map/ppermute | solution.py:370
  159.8 20.0 %collective-permute-start.25 = (bf16[384,1024]{1,0:T(8,128)(2,1)S(1)}, bf16[384,1024]{1,0:T(8,128)(2,1)S(1)}, u32[]{:S(2)}, u32[]{:S(2)}) collective-permute-start(bf16[384,1024]{1,0:T(8,128)(2,1)S(1)} %get-tuple-element.504.refs_0_), channel_id=1, source_target_pairs={{0,2},{2,0},{1,3},{3,1},{4,6},{6,4},{5,7},{7,5},{8,10},{10,8},{9,1... | collective-permute-start | bytes 2359304 | tf_op jit(solution)/shard_map/ppermute | solution.py:363
  161.4 19.7 %collective-permute-start.26 = (bf16[384,1024]{1,0:T(8,128)(2,1)S(1)}, bf16[384,1024]{1,0:T(8,128)(2,1)S(1)}, u32[]{:S(2)}, u32[]{:S(2)}) collective-permute-start(bf16[384,1024]{1,0:T(8,128)(2,1)S(1)} %get-tuple-element.506.refs_2_), channel_id=1, source_target_pairs={{0,4},{4,0},{8,12},{12,8},{16,20},{20,16},{24,28},{28,24},{1,5},{5... | collective-permute-start | bytes 2359304 | tf_op jit(solution)/shard_map/ppermute | solution.py:370
  183.8 24.8 %collective-permute-start.29 = (bf16[512,1024]{1,0:T(8,128)(2,1)}, bf16[512,1024]{1,0:T(8,128)(2,1)}, u32[]{:S(2)}, u32[]{:S(2)}) collective-permute-start(bf16[512,1024]{1,0:T(8,128)(2,1)} %get-tuple-element.513), channel_id=1, source_target_pairs={{0,2},{2,0},{1,3},{3,1},{4,6},{6,4},{5,7},{7,5},{8,10},{10,8},{9,1... | collective-permute-start | bytes 3145736 | tf_op jit(solution)/shard_map/ppermute | solution.py:363
  184.4 24.6 %collective-permute-start.30 = (bf16[512,1024]{1,0:T(8,128)(2,1)}, bf16[512,1024]{1,0:T(8,128)(2,1)}, u32[]{:S(2)}, u32[]{:S(2)}) collective-permute-start(bf16[512,1024]{1,0:T(8,128)(2,1)} %get-tuple-element.514), channel_id=1, source_target_pairs={{0,4},{4,0},{8,12},{12,8},{16,20},{20,16},{24,28},{28,24},{1,5},{5... | collective-permute-start | bytes 3145736 | tf_op jit(solution)/shard_map/ppermute | solution.py:370
  211.0 14.4 %collective-permute-start.31 = (bf16[256,1024]{1,0:T(8,128)(2,1)S(1)}, bf16[256,1024]{1,0:T(8,128)(2,1)S(1)}, u32[]{:S(2)}, u32[]{:S(2)}) collective-permute-start(bf16[256,1024]{1,0:T(8,128)(2,1)S(1)} %get-tuple-element.534), channel_id=1, source_target_pairs={{0,4},{4,0},{8,12},{12,8},{16,20},{20,16},{24,28},{28,24},{1,5},{5... | collective-permute-start | bytes 1572872 | tf_op jit(solution)/shard_map/ppermute | solution.py:370
  227.2 24.0 %collective-permute-start.36 = (bf16[256,1024]{1,0:T(8,128)(2,1)S(1)}, bf16[256,1024]{1,0:T(8,128)(2,1)S(1)}, u32[]{:S(2)}, u32[]{:S(2)}) collective-permute-start(bf16[256,1024]{1,0:T(8,128)(2,1)S(1)} %get-tuple-element.564), channel_id=1, source_target_pairs={{0,8},{4,12},{8,0},{12,4},{16,24},{20,28},{24,16},{28,20},{1,9},{5... | collective-permute-start | bytes 1572872 | tf_op jit(solution)/shard_map/ppermute | solution.py:370
  228.6 25.3 %collective-permute-start.34 = (bf16[512,1024]{1,0:T(8,128)(2,1)S(1)}, bf16[512,1024]{1,0:T(8,128)(2,1)S(1)}, u32[]{:S(2)}, u32[]{:S(2)}) collective-permute-start(bf16[512,1024]{1,0:T(8,128)(2,1)S(1)} %get-tuple-element.561), channel_id=1, source_target_pairs={{0,2},{2,0},{1,3},{3,1},{4,6},{6,4},{5,7},{7,5},{8,10},{10,8},{9,1... | collective-permute-start | bytes 3145736 | tf_op jit(solution)/shard_map/ppermute | solution.py:363
  230.0 25.0 %collective-permute-start.35 = (bf16[512,1024]{1,0:T(8,128)(2,1)S(1)}, bf16[512,1024]{1,0:T(8,128)(2,1)S(1)}, u32[]{:S(2)}, u32[]{:S(2)}) collective-permute-start(bf16[512,1024]{1,0:T(8,128)(2,1)S(1)} %get-tuple-element.562), channel_id=1, source_target_pairs={{0,4},{4,0},{8,12},{12,8},{16,20},{20,16},{24,28},{28,24},{1,5},{5... | collective-permute-start | bytes 3145736 | tf_op jit(solution)/shard_map/ppermute | solution.py:370
  231.0 24.0 %collective-permute-start.38 = (bf16[512,1024]{1,0:T(8,128)(2,1)}, bf16[512,1024]{1,0:T(8,128)(2,1)S(1)}, u32[]{:S(2)}, u32[]{:S(2)}) collective-permute-start(bf16[512,1024]{1,0:T(8,128)(2,1)} %fusion.28), channel_id=1, source_target_pairs={{0,1},{1,0},{2,3},{3,2},{4,5},{5,4},{6,7},{7,6},{8,9},{9,8},{10,11... | collective-permute-start | bytes 3145736 | tf_op jit(solution)/shard_map/ppermute | solution.py:359
  233.9 16.8 %collective-permute-start.39 = (bf16[512,512]{1,0:T(8,128)(2,1)S(1)}, bf16[512,512]{1,0:T(8,128)(2,1)S(1)}, u32[]{:S(2)}, u32[]{:S(2)}) collective-permute-start(bf16[512,512]{1,0:T(8,128)(2,1)S(1)} %broadcast_select_fusion.2), channel_id=1, source_target_pairs={{0,1},{1,0},{2,3},{3,2},{4,5},{5,4},{6,7},{7,6},{8,9},{9,8},{10,11... | collective-permute-start | bytes 1572872 | tf_op jit(solution)/shard_map/ppermute | solution.py:359
  256.6 18.3 %collective-permute-start.40 = (bf16[384,1024]{1,0:T(8,128)(2,1)S(1)}, bf16[384,1024]{1,0:T(8,128)(2,1)S(1)}, u32[]{:S(2)}, u32[]{:S(2)}) collective-permute-start(bf16[384,1024]{1,0:T(8,128)(2,1)S(1)} %get-tuple-element.588), channel_id=1, source_target_pairs={{0,4},{4,0},{8,12},{12,8},{16,20},{20,16},{24,28},{28,24},{1,5},{5... | collective-permute-start | bytes 2359304 | tf_op jit(solution)/shard_map/ppermute | solution.py:370
  257.6 18.0 %collective-permute-start.41 = (bf16[384,1024]{1,0:T(8,128)(2,1)S(1)}, bf16[384,1024]{1,0:T(8,128)(2,1)S(1)}, u32[]{:S(2)}, u32[]{:S(2)}) collective-permute-start(bf16[384,1024]{1,0:T(8,128)(2,1)S(1)} %get-tuple-element.589), channel_id=1, source_target_pairs={{0,2},{2,0},{1,3},{3,1},{4,6},{6,4},{5,7},{7,5},{8,10},{10,8},{9,1... | collective-permute-start | bytes 2359304 | tf_op jit(solution)/shard_map/ppermute | solution.py:363
  278.6 19.6 %collective-permute-start.43 = (bf16[448,1024]{1,0:T(8,128)(2,1)S(1)}, bf16[448,1024]{1,0:T(8,128)(2,1)S(1)}, u32[]{:S(2)}, u32[]{:S(2)}) collective-permute-start(bf16[448,1024]{1,0:T(8,128)(2,1)S(1)} %get-tuple-element.612), channel_id=1, source_target_pairs={{0,2},{2,0},{1,3},{3,1},{4,6},{6,4},{5,7},{7,5},{8,10},{10,8},{9,1... | collective-permute-start | bytes 2752520 | tf_op jit(solution)/shard_map/ppermute | solution.py:363
  279.3 19.3 %collective-permute-start.44 = (bf16[448,1024]{1,0:T(8,128)(2,1)S(1)}, bf16[448,1024]{1,0:T(8,128)(2,1)S(1)}, u32[]{:S(2)}, u32[]{:S(2)}) collective-permute-start(bf16[448,1024]{1,0:T(8,128)(2,1)S(1)} %get-tuple-element.613), channel_id=1, source_target_pairs={{0,4},{4,0},{8,12},{12,8},{16,20},{20,16},{24,28},{28,24},{1,5},{5... | collective-permute-start | bytes 2752520 | tf_op jit(solution)/shard_map/ppermute | solution.py:370
  326.8 16.4 %collective-permute-start.58 = (bf16[256,1024]{1,0:T(8,128)(2,1)S(1)}, bf16[256,1024]{1,0:T(8,128)(2,1)}, u32[]{:S(2)}, u32[]{:S(2)}) collective-permute-start(bf16[256,1024]{1,0:T(8,128)(2,1)S(1)} %get-tuple-element.702), channel_id=1, source_target_pairs={{0,2},{2,0},{1,3},{3,1},{4,6},{6,4},{5,7},{7,5},{8,10},{10,8},{9,1... | collective-permute-start | bytes 1572872 | tf_op jit(solution)/shard_map/ppermute | solution.py:363
  (109 other events, 879.1 us)

commit v5 on v4

--- a/solution.py
+++ b/solution.py
@@ -1005,7 +1005,7 @@
 
     patches, cotangent = phase(
         bits,
-        [(gather_in, gather_vectors, len(far_bits()))],
+        [(gather_in, gather_vectors, len(far_bits())), *gather_rest],
         lambda *arrays: [to_rows(array) for array in arrays],
         patches,
         cotangent,
@@ -1067,7 +1067,7 @@
         return out_matrix, (hat_one * gain_one + shift_one).astype(BF16)
 
     out_matrix, normed_one = phase(
-        bits, [gather_up, (gather_down, len(far) - 1), *gather_rest], project, hat_one, out_columns
+        bits, [gather_up, (gather_down, len(far) - 1)], project, hat_one, out_columns
     )
 
     def matmul_rows(left, right, product, name):
@@ -1328,7 +1328,7 @@
         )
 
     scatters = [scatter_in, *scatter_out, scatter_up]
-    total = Total(narrow, [0, *ahead, 1])
+    total = Total(narrow, [0, far[-1], 1, *far[:-1]])
     phase(bits, [*scatters, total], None)
     core = own_c.astype(jnp.int32).reshape(1)
 

time: 357 us -> 354 us (level)
    ppermute x16, waiting for transfers between devices: 49.7 us -> 44.2 us  [swap_chip(): return lax.ppermute(array, 'sy', SWAP)]
    ppermute x30 -> x31, waiting for transfers between devices: 83.5 us -> 86.1 us  [swap_bit(): lax.ppermute(array, 'img', [(i, i ^ 1 << bit - 1) for i in range(count)])]
    ppermute x30 -> x31, starting transfers between devices: 46 us -> 45.8 us  [swap_bit(): lax.ppermute(array, 'img', [(i, i ^ 1 << bit - 1) for i in range(count)])]
  transfers between devices with their start and end apart: 62 -> 63, of which waited for: 37 -> 35; matrix products, arithmetic and copies ran while one was open for 19% -> 19% of each run, Pallas kernels for 15% -> 16%
where the time goes in v5:
time: 354 us; the launch traced here: 350 us
  waiting for transfers between devices  132 us (37%)
  Pallas kernels  70.3 us (20%)
  starting transfers between devices  63.7 us (18%)
  matrix products  51.3 us (14%)
  local copies, waits for them, and re-layouts  16.4 us (5%)
  other arithmetic  13.4 us (4%)
    ppermute x31, waiting for transfers between devices, swap_bit(): lax.ppermute(array, 'img', [(i, i ^ 1 << bit - 1) for i in range(count)])  86.1 us
    ppermute x31, starting transfers between devices, swap_bit(): lax.ppermute(array, 'img', [(i, i ^ 1 << bit - 1) for i in range(count)])  45.8 us
    ppermute x16, waiting for transfers between devices, swap_chip(): return lax.ppermute(array, 'sy', SWAP)  44.2 us
    pallas_call x21, Pallas kernels, run(): pl.pallas_call(kernel, name='turn', out_shape=tuple(self.shapes), in_spec...  21.9 us
    dot_general x9, matrix products, nn(): return jnp.dot(left, right, preferred_element_type=F32)  18.7 us
    dot_general x6, matrix products, tn(): lax.dot_general(left, right, (((0,), (0,)), ((), ())), preferred_element_...  17 us
    pallas_call x1, Pallas kernels, attention_back(): pl.pallas_call(functools.partial(attend_back_kernel, part * pairs, pairs,...  16.3 us
    pallas_call x6, Pallas kernels, by_rows(): pl.pallas_call(kernel, name=name, grid=(length // tile,), out_shape=[jax....  15.8 us
  transfers between devices with their start and end apart: 63, of which 35 were waited for; matrix products, arithmetic and copies ran while one was open for 19% of the time, Pallas kernels for 16%

profile of v5, /device:TPU:0, one launch (start us, length us, event | category | flops | bytes accessed | tf_op | source)
XLA Modules:
  0.0 349.6 jit_solution(18434034756402808825)
XLA Ops:
  7.9 4.1 %collective-permute-start.2 = (bf16[144,1024]{1,0:T(8,128)(2,1)S(1)}, bf16[144,1024]{1,0:T(8,128)(2,1)S(1)}, u32[]{:S(2)}, u32[]{:S(2)}) collective-permute-start(bf16[144,1024]{1,0:T(8,128)(2,1)S(1)} %get-tuple-element.390.refs_0_), channel_id=1, source_target_pairs={{0,16},{4,20},{8,24},{12,28},{16,0},{20,4},{24,8},{28,12},{1,17},{... | collective-permute-start | bytes 884744 | tf_op jit(solution)/shard_map/ppermute | solution.py:370
  16.9 8.7 %collective-permute-done.2.refs_1_ = bf16[144,1024]{1,0:T(8,128)(2,1)S(1)} collective-permute-done((bf16[144,1024]{1,0:T(8,128)(2,1)S(1)}, bf16[144,1024]{1,0:T(8,128)(2,1)S(1)}, u32[]{:S(2)}, u32[]{:S(2)}) %collective-permute-start.2) | collective-permute-done | bytes 294944 | tf_op jit(solution)/shard_map/ppermute | solution.py:370
  28.6 9.7 %collective-permute-done.6 = bf16[256,1024]{1,0:T(8,128)(2,1)S(1)} collective-permute-done((bf16[256,1024]{1,0:T(8,128)(2,1)S(1)}, bf16[256,1024]{1,0:T(8,128)(2,1)S(1)}, u32[]{:S(2)}, u32[]{:S(2)}) %collective-permute-start.6) | collective-permute-done | bytes 524320 | tf_op jit(solution)/shard_map/ppermute | solution.py:363
  50.3 3.3 first.4
  55.3 4.0 %collective-permute-done.9.refs_5_ = bf16[128,1024]{1,0:T(8,128)(2,1)} collective-permute-done((bf16[128,1024]{1,0:T(8,128)(2,1)}, bf16[128,1024]{1,0:T(8,128)(2,1)}, u32[]{:S(2)}, u32[]{:S(2)}) %collective-permute-start.9) | collective-permute-done | bytes 262176 | tf_op jit(solution)/shard_map/ppermute | solution.py:370
  65.4 3.4 collective-permute-start.13
  68.8 9.6 %collective-permute-done.13.refs_3_ = bf16[96,1024]{1,0:T(8,128)(2,1)S(1)} collective-permute-done((bf16[96,1024]{1,0:T(8,128)(2,1)S(1)}, bf16[96,1024]{1,0:T(8,128)(2,1)S(1)}, u32[]{:S(2)}, u32[]{:S(2)}) %collective-permute-start.13) | collective-permute-done | bytes 196640 | tf_op jit(solution)/shard_map/ppermute | solution.py:370
  79.1 6.7 %collective-permute-done.10.refs_1_ = bf16[512,1024]{1,0:T(8,128)(2,1)S(1)} collective-permute-done((bf16[512,1024]{1,0:T(8,128)(2,1)S(1)}, bf16[512,1024]{1,0:T(8,128)(2,1)S(1)}, u32[]{:S(2)}, u32[]{:S(2)}) %collective-permute-start.10) | collective-permute-done | bytes 1048608 | tf_op jit(solution)/shard_map/ppermute | solution.py:363
  99.4 4.4 %collective-permute-done.16.refs_1_ = bf16[192,1024]{1,0:T(8,128)(2,1)S(1)} collective-permute-done((bf16[192,1024]{1,0:T(8,128)(2,1)S(1)}, bf16[192,1024]{1,0:T(8,128)(2,1)S(1)}, u32[]{:S(2)}, u32[]{:S(2)}) %collective-permute-start.16) | collective-permute-done | bytes 393248 | tf_op jit(solution)/shard_map/ppermute | solution.py:370
  103.7 6.9 %collective-permute-done.14.refs_1_ = bf16[256,1024]{1,0:T(8,128)(2,1)S(1)} collective-permute-done((bf16[256,1024]{1,0:T(8,128)(2,1)S(1)}, bf16[256,1024]{1,0:T(8,128)(2,1)S(1)}, u32[]{:S(2)}, u32[]{:S(2)}) %collective-permute-start.14) | collective-permute-done | bytes 524320 | tf_op jit(solution)/shard_map/ppermute | solution.py:370
  114.8 3.4 collective-permute-start.20
  120.1 3.6 %add_convert_fusion.qkv = bf16[1024,1536]{1,0:T(8,128)(2,1)S(1)} fusion(bf16[1024,1024]{1,0:T(8,128)(2,1)S(1)} %constant_dynamic-update-slice_fusion, bf16[1024,1536]{1,0:T(8,128)(2,1)S(1)} %copy-done.14, f32[1536]{0:T(1024)S(1)} %maximum_reduce_fusion), kind=kOutput, calls=%fused_computation.8 | convolution fusion | flops 3224371200 | bytes 8394752 | tf_op jit(solution)/shard_map/dot_general | solution.py:124
  123.8 12.1 %attend.1 = (bf16[1024,512]{1,0:T(8,128)(2,1)S(1)}, f32[8,1024]{1,0:T(8,128)S(1)}) custom-call(s32[18]{0:T(128)S(1)} %pad_add_fusion.2.info, bf16[1024,1536]{1,0:T(8,128)(2,1)S(1)} %add_convert_fusion.qkv, f32[8,1024]{1,0:T(8,128)S(1)} %broadcast_in_dim.182.seg), custom_call_target="tpu_custom_call" | custom-call | tf_op jit(solution)/shard_map/attend/pallas_call | solution.py:288
  137.3 5.7 %collective-permute-done.18.refs_1_ = bf16[512,1024]{1,0:T(8,128)(2,1)S(1)} collective-permute-done((bf16[512,1024]{1,0:T(8,128)(2,1)S(1)}, bf16[512,1024]{1,0:T(8,128)(2,1)S(1)}, u32[]{:S(2)}, u32[]{:S(2)}) %collective-permute-start.18) | collective-permute-done | bytes 1048608 | tf_op jit(solution)/shard_map/ppermute | solution.py:363
  148.9 6.9 %collective-permute-done.23.refs_1_ = bf16[192,1024]{1,0:T(8,128)(2,1)S(1)} collective-permute-done((bf16[192,1024]{1,0:T(8,128)(2,1)S(1)}, bf16[192,1024]{1,0:T(8,128)(2,1)S(1)}, u32[]{:S(2)}, u32[]{:S(2)}) %collective-permute-start.23) | collective-permute-done | bytes 393248 | tf_op jit(solution)/shard_map/ppermute | solution.py:370
  160.3 9.1 %fusion.3 = (f32[1024,2048]{1,0:T(8,128)}, bf16[1024,2048]{1,0:T(8,128)(2,1)S(1)}) fusion(f32[2048]{0:T(1024)S(1)} %bitcast.132, bf16[1024,1024]{1,0:T(8,128)(2,1)S(1)} %constant_dynamic-update-slice_fusion.2, bf16[1024,2048]{1,0:T(8,128)(2,1)S(1)} %turn.29.refs_5_), kind=kOutput, calls=%fused_computation.4 | convolution fusion | flops 4318035968 | bytes 18882560 | tf_op jit(solution)/shard_map/dot_general | solution.py:124
  169.4 5.4 %convolution_convert_fusion.refs_0_ = bf16[2048,1024]{1,0:T(8,128)(2,1)S(1)} fusion(bf16[1024,2048]{1,0:T(8,128)(2,1)S(1)} %get-tuple-element.643.refs_0_, bf16[1024,1024]{1,0:T(8,128)(2,1)S(1)} %pad_maximum_fusion), kind=kOutput, calls=%fused_computation.9 | convolution fusion | flops 4297064448 | bytes 10485760 | tf_op jit(solution)/shard_map/dot_general | solution.py:120
  174.8 3.3 collective-permute-done.26.refs_1_
  183.8 7.0 %multiply_convert_fusion.refs_0_ = bf16[1024,2048]{1,0:T(8,128)(2,1)S(1)} fusion(f32[1024,2048]{1,0:T(8,128)} %get-tuple-element.529, bf16[1024,1024]{1,0:T(8,128)(2,1)S(1)} %copy-done.59, bf16[2048,1024]{1,0:T(8,128)(2,1)S(1)} %turn.31.refs_4_), kind=kOutput, calls=%fused_computation.5 | convolution fusion | flops 4299161600 | bytes 18874368 | tf_op jit(solution)/shard_map/dot_general | solution.py:116
  190.8 4.1 %fusion.20.refs_1_.refs_2_ = bf16[1024,1024]{1,0:T(8,128)(2,1)S(1)} fusion(bf16[1024,1024]{1,0:T(8,128)(2,1)} %copy-done.66, bf16[1024,2048]{1,0:T(8,128)(2,1)S(1)} %multiply_convert_fusion.refs_0_), kind=kOutput, calls=%fused_computation.24 | convolution fusion | flops 2148532224 | bytes 6291456 | tf_op jit(solution)/shard_map/dot_general | solution.py:120
  199.8 6.1 %collective-permute-done.30.refs_1_ = bf16[512,1024]{1,0:T(8,128)(2,1)} collective-permute-done((bf16[512,1024]{1,0:T(8,128)(2,1)}, bf16[512,1024]{1,0:T(8,128)(2,1)}, u32[]{:S(2)}, u32[]{:S(2)}) %collective-permute-start.30) | collective-permute-done | bytes 1048608 | tf_op jit(solution)/shard_map/ppermute | solution.py:363
  210.9 3.3 fusion.28
  214.3 3.8 %norm_two_back.1 = (f32[512,1024]{1,0:T(8,128)S(1)}, bf16[512,1024]{1,0:T(8,128)(2,1)S(1)}, f32[1,1024]{1,0:T(1,128)S(1)}, f32[1,1024]{1,0:T(1,128)S(1)}) custom-call(bf16[1024,2048]{1,0:T(8,128)(2,1)S(1)} %multiply_convert_fusion.refs_0_, bf16[512,1024]{1,0:T(8,128)(2,1)S(1)} %collective-permute-done.34.refs_1_, f32[512,1024]{1,0:T(8,128)S(1)} %copy-done.29, ...), custom_call_target="tpu_custom_call" | custom-call | tf_op jit(solution)/shard_map/norm_two_back/pallas_call | solution.py:809
  218.1 5.2 %collective-permute-done.32.refs_3_ = bf16[256,1024]{1,0:T(8,128)(2,1)S(1)} collective-permute-done((bf16[256,1024]{1,0:T(8,128)(2,1)S(1)}, bf16[256,1024]{1,0:T(8,128)(2,1)S(1)}, u32[]{:S(2)}, u32[]{:S(2)}) %collective-permute-start.32) | collective-permute-done | bytes 524320 | tf_op jit(solution)/shard_map/ppermute | solution.py:370
  232.0 16.3 %attend_back.1.refs_0_ = bf16[1024,1536]{1,0:T(8,128)(2,1)S(1)} custom-call(s32[18]{0:T(128)S(1)} %copy-done.55, bf16[1024,1536]{1,0:T(8,128)(2,1)S(1)} %copy-done.12, bf16[1024,512]{1,0:T(8,128)(2,1)S(1)} %copy-done.10, bf16[1024,512]{1,0:T(8,128)(2,1)S(1)} %convolution_convert_fusion.3.grad, f32[8,1024]{1,0:T(8,128)S(1)} %broadcast_in_dim.182.seg, ...), custom_call_target="tpu_custom_call" | custom-call | flops 17179869184 | bytes 8388608 | tf_op jit(solution)/shard_map/attend_back/pallas_call | solution.py:330
  261.8 5.8 %collective-permute-done.43.refs_1_ = bf16[128,1024]{1,0:T(8,128)(2,1)S(1)} collective-permute-done((bf16[128,1024]{1,0:T(8,128)(2,1)S(1)}, bf16[128,1024]{1,0:T(8,128)(2,1)S(1)}, u32[]{:S(2)}, u32[]{:S(2)}) %collective-permute-start.43) | collective-permute-done | bytes 262176 | tf_op jit(solution)/shard_map/ppermute | solution.py:370
  267.6 4.8 %collective-permute-done.41.refs_4_ = bf16[384,1024]{1,0:T(8,128)(2,1)S(1)} collective-permute-done((bf16[384,1024]{1,0:T(8,128)(2,1)S(1)}, bf16[384,1024]{1,0:T(8,128)(2,1)S(1)}, u32[]{:S(2)}, u32[]{:S(2)}) %collective-permute-start.41) | collective-permute-done | bytes 786464 | tf_op jit(solution)/shard_map/ppermute | solution.py:370
  288.9 6.7 %collective-permute-done.44.refs_1_ = bf16[448,1024]{1,0:T(8,128)(2,1)S(1)} collective-permute-done((bf16[448,1024]{1,0:T(8,128)(2,1)S(1)}, bf16[448,1024]{1,0:T(8,128)(2,1)S(1)}, u32[]{:S(2)}, u32[]{:S(2)}) %collective-permute-start.44) | collective-permute-done | bytes 917536 | tf_op jit(solution)/shard_map/ppermute | solution.py:363
  303.6 4.5 %collective-permute-done.51.refs_3_ = bf16[64,1024]{1,0:T(8,128)(2,1)S(1)} collective-permute-done((bf16[64,1024]{1,0:T(8,128)(2,1)S(1)}, bf16[64,1024]{1,0:T(8,128)(2,1)S(1)}, u32[]{:S(2)}, u32[]{:S(2)}) %collective-permute-start.51) | collective-permute-done | bytes 131104 | tf_op jit(solution)/shard_map/ppermute | solution.py:370
  319.7 5.9 %collective-permute-done.54.refs_3_.refs_1_ = bf16[96,1024]{1,0:T(8,128)(2,1)S(1)} collective-permute-done((bf16[96,1024]{1,0:T(8,128)(2,1)S(1)}, bf16[96,1024]{1,0:T(8,128)(2,1)S(1)}, u32[]{:S(2)}, u32[]{:S(2)}) %collective-permute-start.54) | collective-permute-done | bytes 196640 | tf_op jit(solution)/shard_map/ppermute | solution.py:370
  332.4 7.3 %collective-permute-done.57.refs_1_.refs_3_.refs_5_ = bf16[96,1024]{1,0:T(8,128)(2,1)S(1)} collective-permute-done((bf16[96,1024]{1,0:T(8,128)(2,1)S(1)}, bf16[96,1024]{1,0:T(8,128)(2,1)S(1)}, u32[]{:S(2)}, u32[]{:S(2)}) %collective-permute-start.57) | collective-permute-done | bytes 196640 | tf_op jit(solution)/shard_map/ppermute | solution.py:370
  342.7 3.7 %collective-permute-done.60 = bf16[64,1024]{1,0:T(8,128)(2,1)S(1)} collective-permute-done((bf16[64,1024]{1,0:T(8,128)(2,1)S(1)}, bf16[64,1024]{1,0:T(8,128)(2,1)S(1)}, u32[]{:S(2)}, u32[]{:S(2)}) %collective-permute-start.60) | collective-permute-done | bytes 131104 | tf_op jit(solution)/shard_map/ppermute | solution.py:370
  (415 shorter events, 152.0 us)
Async XLA Ops:
  7.9 17.6 %collective-permute-start.2 = (bf16[144,1024]{1,0:T(8,128)(2,1)S(1)}, bf16[144,1024]{1,0:T(8,128)(2,1)S(1)}, u32[]{:S(2)}, u32[]{:S(2)}) collective-permute-start(bf16[144,1024]{1,0:T(8,128)(2,1)S(1)} %get-tuple-element.390.refs_0_), channel_id=1, source_target_pairs={{0,16},{4,20},{8,24},{12,28},{16,0},{20,4},{24,8},{28,12},{1,17},{... | collective-permute-start | bytes 884744 | tf_op jit(solution)/shard_map/ppermute | solution.py:370
  13.4 15.1 %collective-permute-start.5 = (bf16[256,1024]{1,0:T(8,128)(2,1)S(1)}, bf16[256,1024]{1,0:T(8,128)(2,1)S(1)}, u32[]{:S(2)}, u32[]{:S(2)}) collective-permute-start(bf16[256,1024]{1,0:T(8,128)(2,1)S(1)} %get-tuple-element.790), channel_id=1, source_target_pairs={{0,2},{2,0},{1,3},{3,1},{4,6},{6,4},{5,7},{7,5},{8,10},{10,8},{9,1... | collective-permute-start | bytes 1572872 | tf_op jit(solution)/shard_map/ppermute | solution.py:363
  16.3 22.0 %collective-permute-start.6 = (bf16[256,1024]{1,0:T(8,128)(2,1)S(1)}, bf16[256,1024]{1,0:T(8,128)(2,1)S(1)}, u32[]{:S(2)}, u32[]{:S(2)}) collective-permute-start(bf16[256,1024]{1,0:T(8,128)(2,1)S(1)} %get-tuple-element.788), channel_id=1, source_target_pairs={{0,2},{2,0},{1,3},{3,1},{4,6},{6,4},{5,7},{7,5},{8,10},{10,8},{9,1... | collective-permute-start | bytes 1572872 | tf_op jit(solution)/shard_map/ppermute | solution.py:363
  26.1 14.1 %collective-permute-start.3 = (bf16[272,1024]{1,0:T(8,128)(2,1)S(1)}, bf16[272,1024]{1,0:T(8,128)(2,1)S(1)}, u32[]{:S(2)}, u32[]{:S(2)}) collective-permute-start(bf16[272,1024]{1,0:T(8,128)(2,1)S(1)} %turn.22.refs_0_), channel_id=1, source_target_pairs={{0,8},{4,12},{8,0},{12,4},{16,24},{20,28},{24,16},{28,20},{1,9},{5... | collective-permute-start | bytes 1671176 | tf_op jit(solution)/shard_map/ppermute | solution.py:370
  42.0 17.3 %collective-permute-start.7 = (bf16[256,1024]{1,0:T(8,128)(2,1)}, bf16[256,1024]{1,0:T(8,128)(2,1)}, u32[]{:S(2)}, u32[]{:S(2)}) collective-permute-start(bf16[256,1024]{1,0:T(8,128)(2,1)} %get-tuple-element.421.refs_0_), channel_id=1, source_target_pairs={{0,4},{4,0},{8,12},{12,8},{16,20},{20,16},{24,28},{28,24},{1,5},{5... | collective-permute-start | bytes 1572872 | tf_op jit(solution)/shard_map/ppermute | solution.py:370
  43.2 16.1 %collective-permute-start.8 = (bf16[336,1024]{1,0:T(8,128)(2,1)}, bf16[336,1024]{1,0:T(8,128)(2,1)}, u32[]{:S(2)}, u32[]{:S(2)}) collective-permute-start(bf16[336,1024]{1,0:T(8,128)(2,1)} %get-tuple-element.466.refs_2_.refs_4_), channel_id=1, source_target_pairs={{0,2},{2,0},{1,3},{3,1},{4,6},{6,4},{5,7},{7,5},{8,10},{10,8},{9,1... | collective-permute-start | bytes 2064392 | tf_op jit(solution)/shard_map/ppermute | solution.py:363
  44.8 14.5 %collective-permute-start.9 = (bf16[128,1024]{1,0:T(8,128)(2,1)}, bf16[128,1024]{1,0:T(8,128)(2,1)}, u32[]{:S(2)}, u32[]{:S(2)}) collective-permute-start(bf16[128,1024]{1,0:T(8,128)(2,1)} %get-tuple-element.425.refs_4_), channel_id=1, source_target_pairs={{0,16},{4,20},{8,24},{12,28},{16,0},{20,4},{24,8},{28,12},{1,17},{... | collective-permute-start | bytes 786440 | tf_op jit(solution)/shard_map/ppermute | solution.py:370
  61.3 24.9 %collective-permute-start.11 = (bf16[528,1024]{1,0:T(8,128)(2,1)S(1)}, bf16[528,1024]{1,0:T(8,128)(2,1)S(1)}, u32[]{:S(2)}, u32[]{:S(2)}) collective-permute-start(bf16[528,1024]{1,0:T(8,128)(2,1)S(1)} %get-tuple-element.439.refs_2_), channel_id=1, source_target_pairs={{0,4},{4,0},{8,12},{12,8},{16,20},{20,16},{24,28},{28,24},{1,5},{5... | collective-permute-start | bytes 3244040 | tf_op jit(solution)/shard_map/ppermute | solution.py:370
  62.1 23.7 %collective-permute-start.10 = (bf16[512,1024]{1,0:T(8,128)(2,1)S(1)}, bf16[512,1024]{1,0:T(8,128)(2,1)S(1)}, u32[]{:S(2)}, u32[]{:S(2)}) collective-permute-start(bf16[512,1024]{1,0:T(8,128)(2,1)S(1)} %get-tuple-element.437.refs_0_), channel_id=1, source_target_pairs={{0,2},{2,0},{1,3},{3,1},{4,6},{6,4},{5,7},{7,5},{8,10},{10,8},{9,1... | collective-permute-start | bytes 3145736 | tf_op jit(solution)/shard_map/ppermute | solution.py:363
  63.0 16.1 %collective-permute-start.12 = (bf16[256,1024]{1,0:T(8,128)(2,1)S(1)}, bf16[256,1024]{1,0:T(8,128)(2,1)S(1)}, u32[]{:S(2)}, u32[]{:S(2)}) collective-permute-start(bf16[256,1024]{1,0:T(8,128)(2,1)S(1)} %get-tuple-element.442.refs_0_), channel_id=1, source_target_pairs={{0,8},{4,12},{8,0},{12,4},{16,24},{20,28},{24,16},{28,20},{1,9},{5... | collective-permute-start | bytes 1572872 | tf_op jit(solution)/shard_map/ppermute | solution.py:370
  96.2 14.3 %collective-permute-start.14 = (bf16[256,1024]{1,0:T(8,128)(2,1)S(1)}, bf16[256,1024]{1,0:T(8,128)(2,1)S(1)}, u32[]{:S(2)}, u32[]{:S(2)}) collective-permute-start(bf16[256,1024]{1,0:T(8,128)(2,1)S(1)} %get-tuple-element.462.refs_0_), channel_id=1, source_target_pairs={{0,4},{4,0},{8,12},{12,8},{16,20},{20,16},{24,28},{28,24},{1,5},{5... | collective-permute-start | bytes 1572872 | tf_op jit(solution)/shard_map/ppermute | solution.py:370
  112.5 23.5 %collective-permute-start.22 = (bf16[512,1024]{1,0:T(8,128)(2,1)S(1)}, bf16[512,1024]{1,0:T(8,128)(2,1)S(1)}, u32[]{:S(2)}, u32[]{:S(2)}) collective-permute-start(bf16[512,1024]{1,0:T(8,128)(2,1)S(1)} %copy-done.5), channel_id=1, source_target_pairs={{0,1},{1,0},{2,3},{3,2},{4,5},{5,4},{6,7},{7,6},{8,9},{9,8},{10,11... | collective-permute-start | bytes 3145736 | tf_op jit(solution)/shard_map/ppermute | solution.py:359
  114.8 22.5 %collective-permute-start.20 = (bf16[128,1024]{1,0:T(8,128)(2,1)S(1)}, bf16[128,1024]{1,0:T(8,128)(2,1)S(1)}, u32[]{:S(2)}, u32[]{:S(2)}) collective-permute-start(bf16[128,1024]{1,0:T(8,128)(2,1)S(1)} %get-tuple-element.507.refs_4_), channel_id=1, source_target_pairs={{0,16},{4,20},{8,24},{12,28},{16,0},{20,4},{24,8},{28,12},{1,17},{... | collective-permute-start | bytes 786440 | tf_op jit(solution)/shard_map/ppermute | solution.py:370
  118.2 24.8 %collective-permute-start.18 = (bf16[512,1024]{1,0:T(8,128)(2,1)S(1)}, bf16[512,1024]{1,0:T(8,128)(2,1)S(1)}, u32[]{:S(2)}, u32[]{:S(2)}) collective-permute-start(bf16[512,1024]{1,0:T(8,128)(2,1)S(1)} %get-tuple-element.498.refs_0_), channel_id=1, source_target_pairs={{0,2},{2,0},{1,3},{3,1},{4,6},{6,4},{5,7},{7,5},{8,10},{10,8},{9,1... | collective-permute-start | bytes 3145736 | tf_op jit(solution)/shard_map/ppermute | solution.py:363
  119.1 24.5 %collective-permute-start.19 = (bf16[512,1024]{1,0:T(8,128)(2,1)S(1)}, bf16[512,1024]{1,0:T(8,128)(2,1)S(1)}, u32[]{:S(2)}, u32[]{:S(2)}) collective-permute-start(bf16[512,1024]{1,0:T(8,128)(2,1)S(1)} %get-tuple-element.500.refs_2_), channel_id=1, source_target_pairs={{0,4},{4,0},{8,12},{12,8},{16,20},{20,16},{24,28},{28,24},{1,5},{5... | collective-permute-start | bytes 3145736 | tf_op jit(solution)/shard_map/ppermute | solution.py:370
  157.5 17.3 %collective-permute-start.28 = (bf16[256,1024]{1,0:T(8,128)(2,1)S(1)}, bf16[256,1024]{1,0:T(8,128)(2,1)S(1)}, u32[]{:S(2)}, u32[]{:S(2)}) collective-permute-start(bf16[256,1024]{1,0:T(8,128)(2,1)S(1)} %get-tuple-element.520.refs_4_), channel_id=1, source_target_pairs={{0,8},{4,12},{8,0},{12,4},{16,24},{20,28},{24,16},{28,20},{1,9},{5... | collective-permute-start | bytes 1572872 | tf_op jit(solution)/shard_map/ppermute | solution.py:370
  158.5 19.7 %collective-permute-start.26 = (bf16[384,1024]{1,0:T(8,128)(2,1)S(1)}, bf16[384,1024]{1,0:T(8,128)(2,1)S(1)}, u32[]{:S(2)}, u32[]{:S(2)}) collective-permute-start(bf16[384,1024]{1,0:T(8,128)(2,1)S(1)} %get-tuple-element.516.refs_0_), channel_id=1, source_target_pairs={{0,2},{2,0},{1,3},{3,1},{4,6},{6,4},{5,7},{7,5},{8,10},{10,8},{9,1... | collective-permute-start | bytes 2359304 | tf_op jit(solution)/shard_map/ppermute | solution.py:363
  159.0 19.5 %collective-permute-start.27 = (bf16[384,1024]{1,0:T(8,128)(2,1)S(1)}, bf16[384,1024]{1,0:T(8,128)(2,1)S(1)}, u32[]{:S(2)}, u32[]{:S(2)}) collective-permute-start(bf16[384,1024]{1,0:T(8,128)(2,1)S(1)} %get-tuple-element.518.refs_2_), channel_id=1, source_target_pairs={{0,4},{4,0},{8,12},{12,8},{16,20},{20,16},{24,28},{28,24},{1,5},{5... | collective-permute-start | bytes 2359304 | tf_op jit(solution)/shard_map/ppermute | solution.py:370
  181.4 24.6 %collective-permute-start.30 = (bf16[512,1024]{1,0:T(8,128)(2,1)}, bf16[512,1024]{1,0:T(8,128)(2,1)}, u32[]{:S(2)}, u32[]{:S(2)}) collective-permute-start(bf16[512,1024]{1,0:T(8,128)(2,1)} %get-tuple-element.525), channel_id=1, source_target_pairs={{0,2},{2,0},{1,3},{3,1},{4,6},{6,4},{5,7},{7,5},{8,10},{10,8},{9,1... | collective-permute-start | bytes 3145736 | tf_op jit(solution)/shard_map/ppermute | solution.py:363
  182.7 24.2 %collective-permute-start.31 = (bf16[512,1024]{1,0:T(8,128)(2,1)}, bf16[512,1024]{1,0:T(8,128)(2,1)}, u32[]{:S(2)}, u32[]{:S(2)}) collective-permute-start(bf16[512,1024]{1,0:T(8,128)(2,1)} %get-tuple-element.526), channel_id=1, source_target_pairs={{0,4},{4,0},{8,12},{12,8},{16,20},{20,16},{24,28},{28,24},{1,5},{5... | collective-permute-start | bytes 3145736 | tf_op jit(solution)/shard_map/ppermute | solution.py:370
  208.9 14.4 %collective-permute-start.32 = (bf16[256,1024]{1,0:T(8,128)(2,1)S(1)}, bf16[256,1024]{1,0:T(8,128)(2,1)S(1)}, u32[]{:S(2)}, u32[]{:S(2)}) collective-permute-start(bf16[256,1024]{1,0:T(8,128)(2,1)S(1)} %get-tuple-element.546), channel_id=1, source_target_pairs={{0,4},{4,0},{8,12},{12,8},{16,20},{20,16},{24,28},{28,24},{1,5},{5... | collective-permute-start | bytes 1572872 | tf_op jit(solution)/shard_map/ppermute | solution.py:370
  210.1 14.1 %collective-permute-start.33 = (bf16[256,1024]{1,0:T(8,128)(2,1)S(1)}, bf16[256,1024]{1,0:T(8,128)(2,1)S(1)}, u32[]{:S(2)}, u32[]{:S(2)}) collective-permute-start(bf16[256,1024]{1,0:T(8,128)(2,1)S(1)} %get-tuple-element.547), channel_id=1, source_target_pairs={{0,2},{2,0},{1,3},{3,1},{4,6},{6,4},{5,7},{7,5},{8,10},{10,8},{9,1... | collective-permute-start | bytes 1572872 | tf_op jit(solution)/shard_map/ppermute | solution.py:363
  225.1 23.6 %collective-permute-start.37 = (bf16[256,1024]{1,0:T(8,128)(2,1)S(1)}, bf16[256,1024]{1,0:T(8,128)(2,1)S(1)}, u32[]{:S(2)}, u32[]{:S(2)}) collective-permute-start(bf16[256,1024]{1,0:T(8,128)(2,1)S(1)} %get-tuple-element.576), channel_id=1, source_target_pairs={{0,8},{4,12},{8,0},{12,4},{16,24},{20,28},{24,16},{28,20},{1,9},{5... | collective-permute-start | bytes 1572872 | tf_op jit(solution)/shard_map/ppermute | solution.py:370
  226.3 25.3 %collective-permute-start.35 = (bf16[512,1024]{1,0:T(8,128)(2,1)S(1)}, bf16[512,1024]{1,0:T(8,128)(2,1)S(1)}, u32[]{:S(2)}, u32[]{:S(2)}) collective-permute-start(bf16[512,1024]{1,0:T(8,128)(2,1)S(1)} %get-tuple-element.573), channel_id=1, source_target_pairs={{0,2},{2,0},{1,3},{3,1},{4,6},{6,4},{5,7},{7,5},{8,10},{10,8},{9,1... | collective-permute-start | bytes 3145736 | tf_op jit(solution)/shard_map/ppermute | solution.py:363
  227.5 25.0 %collective-permute-start.36 = (bf16[512,1024]{1,0:T(8,128)(2,1)S(1)}, bf16[512,1024]{1,0:T(8,128)(2,1)S(1)}, u32[]{:S(2)}, u32[]{:S(2)}) collective-permute-start(bf16[512,1024]{1,0:T(8,128)(2,1)S(1)} %get-tuple-element.574), channel_id=1, source_target_pairs={{0,4},{4,0},{8,12},{12,8},{16,20},{20,16},{24,28},{28,24},{1,5},{5... | collective-permute-start | bytes 3145736 | tf_op jit(solution)/shard_map/ppermute | solution.py:370
  228.5 24.0 %collective-permute-start.39 = (bf16[512,1024]{1,0:T(8,128)(2,1)}, bf16[512,1024]{1,0:T(8,128)(2,1)S(1)}, u32[]{:S(2)}, u32[]{:S(2)}) collective-permute-start(bf16[512,1024]{1,0:T(8,128)(2,1)} %fusion.28), channel_id=1, source_target_pairs={{0,1},{1,0},{2,3},{3,2},{4,5},{5,4},{6,7},{7,6},{8,9},{9,8},{10,11... | collective-permute-start | bytes 3145736 | tf_op jit(solution)/shard_map/ppermute | solution.py:359
  231.4 16.8 %collective-permute-start.40 = (bf16[512,512]{1,0:T(8,128)(2,1)S(1)}, bf16[512,512]{1,0:T(8,128)(2,1)S(1)}, u32[]{:S(2)}, u32[]{:S(2)}) collective-permute-start(bf16[512,512]{1,0:T(8,128)(2,1)S(1)} %broadcast_select_fusion.2), channel_id=1, source_target_pairs={{0,1},{1,0},{2,3},{3,2},{4,5},{5,4},{6,7},{7,6},{8,9},{9,8},{10,11... | collective-permute-start | bytes 1572872 | tf_op jit(solution)/shard_map/ppermute | solution.py:359
  254.2 18.3 %collective-permute-start.41 = (bf16[384,1024]{1,0:T(8,128)(2,1)S(1)}, bf16[384,1024]{1,0:T(8,128)(2,1)S(1)}, u32[]{:S(2)}, u32[]{:S(2)}) collective-permute-start(bf16[384,1024]{1,0:T(8,128)(2,1)S(1)} %get-tuple-element.600), channel_id=1, source_target_pairs={{0,4},{4,0},{8,12},{12,8},{16,20},{20,16},{24,28},{28,24},{1,5},{5... | collective-permute-start | bytes 2359304 | tf_op jit(solution)/shard_map/ppermute | solution.py:370
  255.1 18.0 %collective-permute-start.42 = (bf16[384,1024]{1,0:T(8,128)(2,1)S(1)}, bf16[384,1024]{1,0:T(8,128)(2,1)S(1)}, u32[]{:S(2)}, u32[]{:S(2)}) collective-permute-start(bf16[384,1024]{1,0:T(8,128)(2,1)S(1)} %get-tuple-element.601), channel_id=1, source_target_pairs={{0,2},{2,0},{1,3},{3,1},{4,6},{6,4},{5,7},{7,5},{8,10},{10,8},{9,1... | collective-permute-start | bytes 2359304 | tf_op jit(solution)/shard_map/ppermute | solution.py:363
  276.0 19.6 %collective-permute-start.44 = (bf16[448,1024]{1,0:T(8,128)(2,1)S(1)}, bf16[448,1024]{1,0:T(8,128)(2,1)S(1)}, u32[]{:S(2)}, u32[]{:S(2)}) collective-permute-start(bf16[448,1024]{1,0:T(8,128)(2,1)S(1)} %get-tuple-element.624), channel_id=1, source_target_pairs={{0,2},{2,0},{1,3},{3,1},{4,6},{6,4},{5,7},{7,5},{8,10},{10,8},{9,1... | collective-permute-start | bytes 2752520 | tf_op jit(solution)/shard_map/ppermute | solution.py:363
  277.2 19.3 %collective-permute-start.45 = (bf16[448,1024]{1,0:T(8,128)(2,1)S(1)}, bf16[448,1024]{1,0:T(8,128)(2,1)S(1)}, u32[]{:S(2)}, u32[]{:S(2)}) collective-permute-start(bf16[448,1024]{1,0:T(8,128)(2,1)S(1)} %get-tuple-element.625), channel_id=1, source_target_pairs={{0,4},{4,0},{8,12},{12,8},{16,20},{20,16},{24,28},{28,24},{1,5},{5... | collective-permute-start | bytes 2752520 | tf_op jit(solution)/shard_map/ppermute | solution.py:370
  310.8 14.8 %collective-permute-start.55 = (bf16[256,1024]{1,0:T(8,128)(2,1)S(1)}, bf16[256,1024]{1,0:T(8,128)(2,1)}, u32[]{:S(2)}, u32[]{:S(2)}) collective-permute-start(bf16[256,1024]{1,0:T(8,128)(2,1)S(1)} %get-tuple-element.684), channel_id=1, source_target_pairs={{0,2},{2,0},{1,3},{3,1},{4,6},{6,4},{5,7},{7,5},{8,10},{10,8},{9,1... | collective-permute-start | bytes 1572872 | tf_op jit(solution)/shard_map/ppermute | solution.py:363
  (110 other events, 866.9 us)

commit v6 on v5

--- a/solution.py
+++ b/solution.py
@@ -1328,7 +1328,8 @@
         )
 
     scatters = [scatter_in, *scatter_out, scatter_up]
-    total = Total(narrow, [0, far[-1], 1, *far[:-1]])
+    square = len(far) == 2
+    total = Total(narrow, [0, far[-1], *([] if square else [1, *far[:-1]])])
     phase(bits, [*scatters, total], None)
     core = own_c.astype(jnp.int32).reshape(1)
 
@@ -1418,15 +1419,29 @@
         mine = array[:local_len]
         return jnp.stack([pick(own_y, mine, other), pick(own_y, other, mine)], axis=0)
 
-    output = phase(bits, [*rest, send_grad], back_to_rows, output, send_output.result())
+    if square:
+        low = total.result().astype(BF16)
+        sides = [Rider(low, bit, 0, narrow_rows) for bit in (1, far[0])]
+        corner = 1 | (1 << (far[0] - 1))
+
+        def last_work(output, came, low):
+            across = lax.ppermute(low, "img", [(i, i ^ corner) for i in range(img_count)])
+            return back_to_rows(output, came), across
+
+        output, across = phase(
+            bits, [scatter_in, *scatter_out, *sides, send_grad], last_work, output, send_output.result(), low
+        )
+        near, far_side = (side.result().astype(F32) for side in sides)
+        narrow = (low.astype(F32) + near) + (far_side + across.astype(F32))
+    else:
+        output = phase(bits, [*rest, send_grad], back_to_rows, output, send_output.result())
     while scatter_in.left():
         phase(bits, rest, None)
-    while total.left() > 1:
-        phase(bits, [total], None)
-    if total.left():
+    while total.left():
         phase(bits, [total], None)
     input_grad = back_to_rows(grad_low, send_grad.result())
-    narrow = total.result()
+    if not square:
+        narrow = total.result()
     if paired:
 
         def in_rule(c):

time: 354 us -> 350 us (0.989)
  waiting for transfers between devices: 132 us -> 127 us
    ppermute x31, waiting for transfers between devices: 86.1 us -> 80.8 us  [swap_bit(): lax.ppermute(array, 'img', [(i, i ^ 1 << bit - 1) for i in range(count)])]
    pallas_call x21 -> x20, Pallas kernels: 21.9 us -> 21.3 us  [run(): pl.pallas_call(kernel, name='turn', out_shape=tuple(self.shapes), in_spec...]
  transfers between devices with their start and end apart: 63 -> 64, of which waited for: 35 -> 35; matrix products, arithmetic and copies ran while one was open for 19% -> 19% of each run, Pallas kernels for 16% -> 16%
where the time goes in v6:
time: 350 us; the launch traced here: 346 us
  waiting for transfers between devices  127 us (36%)
  Pallas kernels  69.7 us (20%)
  starting transfers between devices  67.1 us (19%)
  matrix products  51.3 us (15%)
  local copies, waits for them, and re-layouts  16.4 us (5%)
  other arithmetic  12.4 us (4%)
    ppermute x31, waiting for transfers between devices, swap_bit(): lax.ppermute(array, 'img', [(i, i ^ 1 << bit - 1) for i in range(count)])  80.8 us
    ppermute x31, starting transfers between devices, swap_bit(): lax.ppermute(array, 'img', [(i, i ^ 1 << bit - 1) for i in range(count)])  46.9 us
    ppermute x16, waiting for transfers between devices, swap_chip(): return lax.ppermute(array, 'sy', SWAP)  44.2 us
    pallas_call x20, Pallas kernels, run(): pl.pallas_call(kernel, name='turn', out_shape=tuple(self.shapes), in_spec...  21.3 us
    dot_general x9, matrix products, nn(): return jnp.dot(left, right, preferred_element_type=F32)  18.7 us
    dot_general x6, matrix products, tn(): lax.dot_general(left, right, (((0,), (0,)), ((), ())), preferred_element_...  17 us
    pallas_call x1, Pallas kernels, attention_back(): pl.pallas_call(functools.partial(attend_back_kernel, part * pairs, pairs,...  16.3 us
    pallas_call x6, Pallas kernels, by_rows(): pl.pallas_call(kernel, name=name, grid=(length // tile,), out_shape=[jax....  15.8 us
  transfers between devices with their start and end apart: 64, of which 35 were waited for; matrix products, arithmetic and copies ran while one was open for 19% of the time, Pallas kernels for 16%

profile of v6, /device:TPU:0, one launch (start us, length us, event | category | flops | bytes accessed | tf_op | source)
XLA Modules:
  0.0 346.2 jit_solution(12731655644621048605)
XLA Ops:
  7.9 4.1 %collective-permute-start.2 = (bf16[144,1024]{1,0:T(8,128)(2,1)S(1)}, bf16[144,1024]{1,0:T(8,128)(2,1)S(1)}, u32[]{:S(2)}, u32[]{:S(2)}) collective-permute-start(bf16[144,1024]{1,0:T(8,128)(2,1)S(1)} %get-tuple-element.385.refs_0_), channel_id=1, source_target_pairs={{0,16},{4,20},{8,24},{12,28},{16,0},{20,4},{24,8},{28,12},{1,17},{... | collective-permute-start | bytes 884744 | tf_op jit(solution)/shard_map/ppermute | solution.py:370
  16.9 8.7 %collective-permute-done.2.refs_1_ = bf16[144,1024]{1,0:T(8,128)(2,1)S(1)} collective-permute-done((bf16[144,1024]{1,0:T(8,128)(2,1)S(1)}, bf16[144,1024]{1,0:T(8,128)(2,1)S(1)}, u32[]{:S(2)}, u32[]{:S(2)}) %collective-permute-start.2) | collective-permute-done | bytes 294944 | tf_op jit(solution)/shard_map/ppermute | solution.py:370
  28.6 9.7 %collective-permute-done.6 = bf16[256,1024]{1,0:T(8,128)(2,1)S(1)} collective-permute-done((bf16[256,1024]{1,0:T(8,128)(2,1)S(1)}, bf16[256,1024]{1,0:T(8,128)(2,1)S(1)}, u32[]{:S(2)}, u32[]{:S(2)}) %collective-permute-start.6) | collective-permute-done | bytes 524320 | tf_op jit(solution)/shard_map/ppermute | solution.py:363
  44.8 3.2 collective-permute-start.9
  50.3 3.3 first.4
  55.3 4.0 %collective-permute-done.9.refs_5_ = bf16[128,1024]{1,0:T(8,128)(2,1)} collective-permute-done((bf16[128,1024]{1,0:T(8,128)(2,1)}, bf16[128,1024]{1,0:T(8,128)(2,1)}, u32[]{:S(2)}, u32[]{:S(2)}) %collective-permute-start.9) | collective-permute-done | bytes 262176 | tf_op jit(solution)/shard_map/ppermute | solution.py:370
  65.4 3.4 collective-permute-start.13
  68.8 9.6 %collective-permute-done.13.refs_3_ = bf16[96,1024]{1,0:T(8,128)(2,1)S(1)} collective-permute-done((bf16[96,1024]{1,0:T(8,128)(2,1)S(1)}, bf16[96,1024]{1,0:T(8,128)(2,1)S(1)}, u32[]{:S(2)}, u32[]{:S(2)}) %collective-permute-start.13) | collective-permute-done | bytes 196640 | tf_op jit(solution)/shard_map/ppermute | solution.py:370
  79.1 6.7 %collective-permute-done.10.refs_1_ = bf16[512,1024]{1,0:T(8,128)(2,1)S(1)} collective-permute-done((bf16[512,1024]{1,0:T(8,128)(2,1)S(1)}, bf16[512,1024]{1,0:T(8,128)(2,1)S(1)}, u32[]{:S(2)}, u32[]{:S(2)}) %collective-permute-start.10) | collective-permute-done | bytes 1048608 | tf_op jit(solution)/shard_map/ppermute | solution.py:363
  99.4 4.4 %collective-permute-done.16.refs_1_ = bf16[192,1024]{1,0:T(8,128)(2,1)S(1)} collective-permute-done((bf16[192,1024]{1,0:T(8,128)(2,1)S(1)}, bf16[192,1024]{1,0:T(8,128)(2,1)S(1)}, u32[]{:S(2)}, u32[]{:S(2)}) %collective-permute-start.16) | collective-permute-done | bytes 393248 | tf_op jit(solution)/shard_map/ppermute | solution.py:370
  103.7 6.9 %collective-permute-done.14.refs_1_ = bf16[256,1024]{1,0:T(8,128)(2,1)S(1)} collective-permute-done((bf16[256,1024]{1,0:T(8,128)(2,1)S(1)}, bf16[256,1024]{1,0:T(8,128)(2,1)S(1)}, u32[]{:S(2)}, u32[]{:S(2)}) %collective-permute-start.14) | collective-permute-done | bytes 524320 | tf_op jit(solution)/shard_map/ppermute | solution.py:370
  114.8 3.4 collective-permute-start.20
  120.1 3.6 %add_convert_fusion.qkv = bf16[1024,1536]{1,0:T(8,128)(2,1)S(1)} fusion(bf16[1024,1024]{1,0:T(8,128)(2,1)S(1)} %constant_dynamic-update-slice_fusion, bf16[1024,1536]{1,0:T(8,128)(2,1)S(1)} %copy-done.14, f32[1536]{0:T(1024)S(1)} %maximum_reduce_fusion), kind=kOutput, calls=%fused_computation.8 | convolution fusion | flops 3224371200 | bytes 8394752 | tf_op jit(solution)/shard_map/dot_general | solution.py:124
  123.8 12.1 %attend.1 = (bf16[1024,512]{1,0:T(8,128)(2,1)S(1)}, f32[8,1024]{1,0:T(8,128)S(1)}) custom-call(s32[18]{0:T(128)S(1)} %pad_add_fusion.2.info, bf16[1024,1536]{1,0:T(8,128)(2,1)S(1)} %add_convert_fusion.qkv, f32[8,1024]{1,0:T(8,128)S(1)} %broadcast_in_dim.182.seg), custom_call_target="tpu_custom_call" | custom-call | tf_op jit(solution)/shard_map/attend/pallas_call | solution.py:288
  137.3 5.7 %collective-permute-done.18.refs_1_ = bf16[512,1024]{1,0:T(8,128)(2,1)S(1)} collective-permute-done((bf16[512,1024]{1,0:T(8,128)(2,1)S(1)}, bf16[512,1024]{1,0:T(8,128)(2,1)S(1)}, u32[]{:S(2)}, u32[]{:S(2)}) %collective-permute-start.18) | collective-permute-done | bytes 1048608 | tf_op jit(solution)/shard_map/ppermute | solution.py:363
  148.9 6.9 %collective-permute-done.23.refs_1_ = bf16[192,1024]{1,0:T(8,128)(2,1)S(1)} collective-permute-done((bf16[192,1024]{1,0:T(8,128)(2,1)S(1)}, bf16[192,1024]{1,0:T(8,128)(2,1)S(1)}, u32[]{:S(2)}, u32[]{:S(2)}) %collective-permute-start.23) | collective-permute-done | bytes 393248 | tf_op jit(solution)/shard_map/ppermute | solution.py:370
  160.3 9.1 %fusion.3 = (f32[1024,2048]{1,0:T(8,128)}, bf16[1024,2048]{1,0:T(8,128)(2,1)S(1)}) fusion(f32[2048]{0:T(1024)S(1)} %bitcast.132, bf16[1024,1024]{1,0:T(8,128)(2,1)S(1)} %constant_dynamic-update-slice_fusion.2, bf16[1024,2048]{1,0:T(8,128)(2,1)S(1)} %turn.28.refs_5_), kind=kOutput, calls=%fused_computation.4 | convolution fusion | flops 4318035968 | bytes 18882560 | tf_op jit(solution)/shard_map/dot_general | solution.py:124
  169.4 5.4 %convolution_convert_fusion.refs_0_ = bf16[2048,1024]{1,0:T(8,128)(2,1)S(1)} fusion(bf16[1024,2048]{1,0:T(8,128)(2,1)S(1)} %get-tuple-element.638.refs_0_, bf16[1024,1024]{1,0:T(8,128)(2,1)S(1)} %pad_maximum_fusion), kind=kOutput, calls=%fused_computation.9 | convolution fusion | flops 4297064448 | bytes 10485760 | tf_op jit(solution)/shard_map/dot_general | solution.py:120
  174.8 3.3 collective-permute-done.26.refs_1_
  183.8 7.0 %multiply_convert_fusion.refs_0_ = bf16[1024,2048]{1,0:T(8,128)(2,1)S(1)} fusion(f32[1024,2048]{1,0:T(8,128)} %get-tuple-element.524, bf16[1024,1024]{1,0:T(8,128)(2,1)S(1)} %copy-done.59, bf16[2048,1024]{1,0:T(8,128)(2,1)S(1)} %turn.30.refs_4_), kind=kOutput, calls=%fused_computation.5 | convolution fusion | flops 4299161600 | bytes 18874368 | tf_op jit(solution)/shard_map/dot_general | solution.py:116
  190.8 4.1 %fusion.20.refs_1_.refs_2_ = bf16[1024,1024]{1,0:T(8,128)(2,1)S(1)} fusion(bf16[1024,1024]{1,0:T(8,128)(2,1)} %copy-done.66, bf16[1024,2048]{1,0:T(8,128)(2,1)S(1)} %multiply_convert_fusion.refs_0_), kind=kOutput, calls=%fused_computation.24 | convolution fusion | flops 2148532224 | bytes 6291456 | tf_op jit(solution)/shard_map/dot_general | solution.py:120
  199.8 6.1 %collective-permute-done.30.refs_1_ = bf16[512,1024]{1,0:T(8,128)(2,1)} collective-permute-done((bf16[512,1024]{1,0:T(8,128)(2,1)}, bf16[512,1024]{1,0:T(8,128)(2,1)}, u32[]{:S(2)}, u32[]{:S(2)}) %collective-permute-start.30) | collective-permute-done | bytes 1048608 | tf_op jit(solution)/shard_map/ppermute | solution.py:363
  210.9 3.3 fusion.28
  214.3 3.8 %norm_two_back.1 = (f32[512,1024]{1,0:T(8,128)S(1)}, bf16[512,1024]{1,0:T(8,128)(2,1)S(1)}, f32[1,1024]{1,0:T(1,128)S(1)}, f32[1,1024]{1,0:T(1,128)S(1)}) custom-call(bf16[1024,2048]{1,0:T(8,128)(2,1)S(1)} %multiply_convert_fusion.refs_0_, bf16[512,1024]{1,0:T(8,128)(2,1)S(1)} %collective-permute-done.34.refs_1_, f32[512,1024]{1,0:T(8,128)S(1)} %copy-done.29, ...), custom_call_target="tpu_custom_call" | custom-call | tf_op jit(solution)/shard_map/norm_two_back/pallas_call | solution.py:809
  218.1 5.2 %collective-permute-done.32.refs_3_ = bf16[256,1024]{1,0:T(8,128)(2,1)S(1)} collective-permute-done((bf16[256,1024]{1,0:T(8,128)(2,1)S(1)}, bf16[256,1024]{1,0:T(8,128)(2,1)S(1)}, u32[]{:S(2)}, u32[]{:S(2)}) %collective-permute-start.32) | collective-permute-done | bytes 524320 | tf_op jit(solution)/shard_map/ppermute | solution.py:370
  232.0 16.3 %attend_back.1.refs_0_ = bf16[1024,1536]{1,0:T(8,128)(2,1)S(1)} custom-call(s32[18]{0:T(128)S(1)} %copy-done.55, bf16[1024,1536]{1,0:T(8,128)(2,1)S(1)} %copy-done.12, bf16[1024,512]{1,0:T(8,128)(2,1)S(1)} %copy-done.10, bf16[1024,512]{1,0:T(8,128)(2,1)S(1)} %convolution_convert_fusion.3.grad, f32[8,1024]{1,0:T(8,128)S(1)} %broadcast_in_dim.182.seg, ...), custom_call_target="tpu_custom_call" | custom-call | flops 17179869184 | bytes 8388608 | tf_op jit(solution)/shard_map/attend_back/pallas_call | solution.py:330
  261.8 5.8 %collective-permute-done.43.refs_1_ = bf16[128,1024]{1,0:T(8,128)(2,1)S(1)} collective-permute-done((bf16[128,1024]{1,0:T(8,128)(2,1)S(1)}, bf16[128,1024]{1,0:T(8,128)(2,1)S(1)}, u32[]{:S(2)}, u32[]{:S(2)}) %collective-permute-start.43) | collective-permute-done | bytes 262176 | tf_op jit(solution)/shard_map/ppermute | solution.py:370
  267.6 4.8 %collective-permute-done.41.refs_4_ = bf16[384,1024]{1,0:T(8,128)(2,1)S(1)} collective-permute-done((bf16[384,1024]{1,0:T(8,128)(2,1)S(1)}, bf16[384,1024]{1,0:T(8,128)(2,1)S(1)}, u32[]{:S(2)}, u32[]{:S(2)}) %collective-permute-start.41) | collective-permute-done | bytes 786464 | tf_op jit(solution)/shard_map/ppermute | solution.py:370
  288.9 6.7 %collective-permute-done.44.refs_1_ = bf16[448,1024]{1,0:T(8,128)(2,1)S(1)} collective-permute-done((bf16[448,1024]{1,0:T(8,128)(2,1)S(1)}, bf16[448,1024]{1,0:T(8,128)(2,1)S(1)}, u32[]{:S(2)}, u32[]{:S(2)}) %collective-permute-start.44) | collective-permute-done | bytes 917536 | tf_op jit(solution)/shard_map/ppermute | solution.py:363
  303.6 4.5 %collective-permute-done.51.refs_3_ = bf16[64,1024]{1,0:T(8,128)(2,1)S(1)} collective-permute-done((bf16[64,1024]{1,0:T(8,128)(2,1)S(1)}, bf16[64,1024]{1,0:T(8,128)(2,1)S(1)}, u32[]{:S(2)}, u32[]{:S(2)}) %collective-permute-start.51) | collective-permute-done | bytes 131104 | tf_op jit(solution)/shard_map/ppermute | solution.py:370
  319.7 5.9 %collective-permute-done.54.refs_1_.refs_3_ = bf16[96,1024]{1,0:T(8,128)(2,1)S(1)} collective-permute-done((bf16[96,1024]{1,0:T(8,128)(2,1)S(1)}, bf16[96,1024]{1,0:T(8,128)(2,1)S(1)}, u32[]{:S(2)}, u32[]{:S(2)}) %collective-permute-start.54) | collective-permute-done | bytes 196640 | tf_op jit(solution)/shard_map/ppermute | solution.py:370
  336.1 3.2 collective-permute-done.59
  (417 shorter events, 153.3 us)
Async XLA Ops:
  7.9 17.6 %collective-permute-start.2 = (bf16[144,1024]{1,0:T(8,128)(2,1)S(1)}, bf16[144,1024]{1,0:T(8,128)(2,1)S(1)}, u32[]{:S(2)}, u32[]{:S(2)}) collective-permute-start(bf16[144,1024]{1,0:T(8,128)(2,1)S(1)} %get-tuple-element.385.refs_0_), channel_id=1, source_target_pairs={{0,16},{4,20},{8,24},{12,28},{16,0},{20,4},{24,8},{28,12},{1,17},{... | collective-permute-start | bytes 884744 | tf_op jit(solution)/shard_map/ppermute | solution.py:370
  13.4 15.1 %collective-permute-start.5 = (bf16[256,1024]{1,0:T(8,128)(2,1)S(1)}, bf16[256,1024]{1,0:T(8,128)(2,1)S(1)}, u32[]{:S(2)}, u32[]{:S(2)}) collective-permute-start(bf16[256,1024]{1,0:T(8,128)(2,1)S(1)} %get-tuple-element.780), channel_id=1, source_target_pairs={{0,2},{2,0},{1,3},{3,1},{4,6},{6,4},{5,7},{7,5},{8,10},{10,8},{9,1... | collective-permute-start | bytes 1572872 | tf_op jit(solution)/shard_map/ppermute | solution.py:363
  16.3 22.0 %collective-permute-start.6 = (bf16[256,1024]{1,0:T(8,128)(2,1)S(1)}, bf16[256,1024]{1,0:T(8,128)(2,1)S(1)}, u32[]{:S(2)}, u32[]{:S(2)}) collective-permute-start(bf16[256,1024]{1,0:T(8,128)(2,1)S(1)} %get-tuple-element.778), channel_id=1, source_target_pairs={{0,2},{2,0},{1,3},{3,1},{4,6},{6,4},{5,7},{7,5},{8,10},{10,8},{9,1... | collective-permute-start | bytes 1572872 | tf_op jit(solution)/shard_map/ppermute | solution.py:363
  26.1 14.1 %collective-permute-start.3 = (bf16[272,1024]{1,0:T(8,128)(2,1)S(1)}, bf16[272,1024]{1,0:T(8,128)(2,1)S(1)}, u32[]{:S(2)}, u32[]{:S(2)}) collective-permute-start(bf16[272,1024]{1,0:T(8,128)(2,1)S(1)} %turn.21.refs_0_), channel_id=1, source_target_pairs={{0,8},{4,12},{8,0},{12,4},{16,24},{20,28},{24,16},{28,20},{1,9},{5... | collective-permute-start | bytes 1671176 | tf_op jit(solution)/shard_map/ppermute | solution.py:370
  42.0 17.3 %collective-permute-start.7 = (bf16[256,1024]{1,0:T(8,128)(2,1)}, bf16[256,1024]{1,0:T(8,128)(2,1)}, u32[]{:S(2)}, u32[]{:S(2)}) collective-permute-start(bf16[256,1024]{1,0:T(8,128)(2,1)} %get-tuple-element.416.refs_0_), channel_id=1, source_target_pairs={{0,4},{4,0},{8,12},{12,8},{16,20},{20,16},{24,28},{28,24},{1,5},{5... | collective-permute-start | bytes 1572872 | tf_op jit(solution)/shard_map/ppermute | solution.py:370
  43.2 16.1 %collective-permute-start.8 = (bf16[336,1024]{1,0:T(8,128)(2,1)}, bf16[336,1024]{1,0:T(8,128)(2,1)}, u32[]{:S(2)}, u32[]{:S(2)}) collective-permute-start(bf16[336,1024]{1,0:T(8,128)(2,1)} %get-tuple-element.461.refs_2_.refs_4_), channel_id=1, source_target_pairs={{0,2},{2,0},{1,3},{3,1},{4,6},{6,4},{5,7},{7,5},{8,10},{10,8},{9,1... | collective-permute-start | bytes 2064392 | tf_op jit(solution)/shard_map/ppermute | solution.py:363
  44.8 14.5 %collective-permute-start.9 = (bf16[128,1024]{1,0:T(8,128)(2,1)}, bf16[128,1024]{1,0:T(8,128)(2,1)}, u32[]{:S(2)}, u32[]{:S(2)}) collective-permute-start(bf16[128,1024]{1,0:T(8,128)(2,1)} %get-tuple-element.420.refs_4_), channel_id=1, source_target_pairs={{0,16},{4,20},{8,24},{12,28},{16,0},{20,4},{24,8},{28,12},{1,17},{... | collective-permute-start | bytes 786440 | tf_op jit(solution)/shard_map/ppermute | solution.py:370
  61.3 24.9 %collective-permute-start.11 = (bf16[528,1024]{1,0:T(8,128)(2,1)S(1)}, bf16[528,1024]{1,0:T(8,128)(2,1)S(1)}, u32[]{:S(2)}, u32[]{:S(2)}) collective-permute-start(bf16[528,1024]{1,0:T(8,128)(2,1)S(1)} %get-tuple-element.434.refs_2_), channel_id=1, source_target_pairs={{0,4},{4,0},{8,12},{12,8},{16,20},{20,16},{24,28},{28,24},{1,5},{5... | collective-permute-start | bytes 3244040 | tf_op jit(solution)/shard_map/ppermute | solution.py:370
  62.1 23.7 %collective-permute-start.10 = (bf16[512,1024]{1,0:T(8,128)(2,1)S(1)}, bf16[512,1024]{1,0:T(8,128)(2,1)S(1)}, u32[]{:S(2)}, u32[]{:S(2)}) collective-permute-start(bf16[512,1024]{1,0:T(8,128)(2,1)S(1)} %get-tuple-element.432.refs_0_), channel_id=1, source_target_pairs={{0,2},{2,0},{1,3},{3,1},{4,6},{6,4},{5,7},{7,5},{8,10},{10,8},{9,1... | collective-permute-start | bytes 3145736 | tf_op jit(solution)/shard_map/ppermute | solution.py:363
  63.0 16.1 %collective-permute-start.12 = (bf16[256,1024]{1,0:T(8,128)(2,1)S(1)}, bf16[256,1024]{1,0:T(8,128)(2,1)S(1)}, u32[]{:S(2)}, u32[]{:S(2)}) collective-permute-start(bf16[256,1024]{1,0:T(8,128)(2,1)S(1)} %get-tuple-element.437.refs_0_), channel_id=1, source_target_pairs={{0,8},{4,12},{8,0},{12,4},{16,24},{20,28},{24,16},{28,20},{1,9},{5... | collective-permute-start | bytes 1572872 | tf_op jit(solution)/shard_map/ppermute | solution.py:370
  96.2 14.3 %collective-permute-start.14 = (bf16[256,1024]{1,0:T(8,128)(2,1)S(1)}, bf16[256,1024]{1,0:T(8,128)(2,1)S(1)}, u32[]{:S(2)}, u32[]{:S(2)}) collective-permute-start(bf16[256,1024]{1,0:T(8,128)(2,1)S(1)} %get-tuple-element.457.refs_0_), channel_id=1, source_target_pairs={{0,4},{4,0},{8,12},{12,8},{16,20},{20,16},{24,28},{28,24},{1,5},{5... | collective-permute-start | bytes 1572872 | tf_op jit(solution)/shard_map/ppermute | solution.py:370
  112.5 23.5 %collective-permute-start.22 = (bf16[512,1024]{1,0:T(8,128)(2,1)S(1)}, bf16[512,1024]{1,0:T(8,128)(2,1)S(1)}, u32[]{:S(2)}, u32[]{:S(2)}) collective-permute-start(bf16[512,1024]{1,0:T(8,128)(2,1)S(1)} %copy-done.5), channel_id=1, source_target_pairs={{0,1},{1,0},{2,3},{3,2},{4,5},{5,4},{6,7},{7,6},{8,9},{9,8},{10,11... | collective-permute-start | bytes 3145736 | tf_op jit(solution)/shard_map/ppermute | solution.py:359
  114.8 22.5 %collective-permute-start.20 = (bf16[128,1024]{1,0:T(8,128)(2,1)S(1)}, bf16[128,1024]{1,0:T(8,128)(2,1)S(1)}, u32[]{:S(2)}, u32[]{:S(2)}) collective-permute-start(bf16[128,1024]{1,0:T(8,128)(2,1)S(1)} %get-tuple-element.502.refs_4_), channel_id=1, source_target_pairs={{0,16},{4,20},{8,24},{12,28},{16,0},{20,4},{24,8},{28,12},{1,17},{... | collective-permute-start | bytes 786440 | tf_op jit(solution)/shard_map/ppermute | solution.py:370
  118.2 24.8 %collective-permute-start.18 = (bf16[512,1024]{1,0:T(8,128)(2,1)S(1)}, bf16[512,1024]{1,0:T(8,128)(2,1)S(1)}, u32[]{:S(2)}, u32[]{:S(2)}) collective-permute-start(bf16[512,1024]{1,0:T(8,128)(2,1)S(1)} %get-tuple-element.493.refs_0_), channel_id=1, source_target_pairs={{0,2},{2,0},{1,3},{3,1},{4,6},{6,4},{5,7},{7,5},{8,10},{10,8},{9,1... | collective-permute-start | bytes 3145736 | tf_op jit(solution)/shard_map/ppermute | solution.py:363
  119.1 24.5 %collective-permute-start.19 = (bf16[512,1024]{1,0:T(8,128)(2,1)S(1)}, bf16[512,1024]{1,0:T(8,128)(2,1)S(1)}, u32[]{:S(2)}, u32[]{:S(2)}) collective-permute-start(bf16[512,1024]{1,0:T(8,128)(2,1)S(1)} %get-tuple-element.495.refs_2_), channel_id=1, source_target_pairs={{0,4},{4,0},{8,12},{12,8},{16,20},{20,16},{24,28},{28,24},{1,5},{5... | collective-permute-start | bytes 3145736 | tf_op jit(solution)/shard_map/ppermute | solution.py:370
  157.5 17.3 %collective-permute-start.28 = (bf16[256,1024]{1,0:T(8,128)(2,1)S(1)}, bf16[256,1024]{1,0:T(8,128)(2,1)S(1)}, u32[]{:S(2)}, u32[]{:S(2)}) collective-permute-start(bf16[256,1024]{1,0:T(8,128)(2,1)S(1)} %get-tuple-element.515.refs_4_), channel_id=1, source_target_pairs={{0,8},{4,12},{8,0},{12,4},{16,24},{20,28},{24,16},{28,20},{1,9},{5... | collective-permute-start | bytes 1572872 | tf_op jit(solution)/shard_map/ppermute | solution.py:370
  158.5 19.7 %collective-permute-start.26 = (bf16[384,1024]{1,0:T(8,128)(2,1)S(1)}, bf16[384,1024]{1,0:T(8,128)(2,1)S(1)}, u32[]{:S(2)}, u32[]{:S(2)}) collective-permute-start(bf16[384,1024]{1,0:T(8,128)(2,1)S(1)} %get-tuple-element.511.refs_0_), channel_id=1, source_target_pairs={{0,2},{2,0},{1,3},{3,1},{4,6},{6,4},{5,7},{7,5},{8,10},{10,8},{9,1... | collective-permute-start | bytes 2359304 | tf_op jit(solution)/shard_map/ppermute | solution.py:363
  159.0 19.5 %collective-permute-start.27 = (bf16[384,1024]{1,0:T(8,128)(2,1)S(1)}, bf16[384,1024]{1,0:T(8,128)(2,1)S(1)}, u32[]{:S(2)}, u32[]{:S(2)}) collective-permute-start(bf16[384,1024]{1,0:T(8,128)(2,1)S(1)} %get-tuple-element.513.refs_2_), channel_id=1, source_target_pairs={{0,4},{4,0},{8,12},{12,8},{16,20},{20,16},{24,28},{28,24},{1,5},{5... | collective-permute-start | bytes 2359304 | tf_op jit(solution)/shard_map/ppermute | solution.py:370
  181.4 24.6 %collective-permute-start.30 = (bf16[512,1024]{1,0:T(8,128)(2,1)}, bf16[512,1024]{1,0:T(8,128)(2,1)}, u32[]{:S(2)}, u32[]{:S(2)}) collective-permute-start(bf16[512,1024]{1,0:T(8,128)(2,1)} %get-tuple-element.520), channel_id=1, source_target_pairs={{0,2},{2,0},{1,3},{3,1},{4,6},{6,4},{5,7},{7,5},{8,10},{10,8},{9,1... | collective-permute-start | bytes 3145736 | tf_op jit(solution)/shard_map/ppermute | solution.py:363
  182.7 24.2 %collective-permute-start.31 = (bf16[512,1024]{1,0:T(8,128)(2,1)}, bf16[512,1024]{1,0:T(8,128)(2,1)}, u32[]{:S(2)}, u32[]{:S(2)}) collective-permute-start(bf16[512,1024]{1,0:T(8,128)(2,1)} %get-tuple-element.521), channel_id=1, source_target_pairs={{0,4},{4,0},{8,12},{12,8},{16,20},{20,16},{24,28},{28,24},{1,5},{5... | collective-permute-start | bytes 3145736 | tf_op jit(solution)/shard_map/ppermute | solution.py:370
  208.9 14.4 %collective-permute-start.32 = (bf16[256,1024]{1,0:T(8,128)(2,1)S(1)}, bf16[256,1024]{1,0:T(8,128)(2,1)S(1)}, u32[]{:S(2)}, u32[]{:S(2)}) collective-permute-start(bf16[256,1024]{1,0:T(8,128)(2,1)S(1)} %get-tuple-element.541), channel_id=1, source_target_pairs={{0,4},{4,0},{8,12},{12,8},{16,20},{20,16},{24,28},{28,24},{1,5},{5... | collective-permute-start | bytes 1572872 | tf_op jit(solution)/shard_map/ppermute | solution.py:370
  225.1 23.6 %collective-permute-start.37 = (bf16[256,1024]{1,0:T(8,128)(2,1)S(1)}, bf16[256,1024]{1,0:T(8,128)(2,1)S(1)}, u32[]{:S(2)}, u32[]{:S(2)}) collective-permute-start(bf16[256,1024]{1,0:T(8,128)(2,1)S(1)} %get-tuple-element.571), channel_id=1, source_target_pairs={{0,8},{4,12},{8,0},{12,4},{16,24},{20,28},{24,16},{28,20},{1,9},{5... | collective-permute-start | bytes 1572872 | tf_op jit(solution)/shard_map/ppermute | solution.py:370
  226.3 25.3 %collective-permute-start.35 = (bf16[512,1024]{1,0:T(8,128)(2,1)S(1)}, bf16[512,1024]{1,0:T(8,128)(2,1)S(1)}, u32[]{:S(2)}, u32[]{:S(2)}) collective-permute-start(bf16[512,1024]{1,0:T(8,128)(2,1)S(1)} %get-tuple-element.568), channel_id=1, source_target_pairs={{0,2},{2,0},{1,3},{3,1},{4,6},{6,4},{5,7},{7,5},{8,10},{10,8},{9,1... | collective-permute-start | bytes 3145736 | tf_op jit(solution)/shard_map/ppermute | solution.py:363
  227.5 25.0 %collective-permute-start.36 = (bf16[512,1024]{1,0:T(8,128)(2,1)S(1)}, bf16[512,1024]{1,0:T(8,128)(2,1)S(1)}, u32[]{:S(2)}, u32[]{:S(2)}) collective-permute-start(bf16[512,1024]{1,0:T(8,128)(2,1)S(1)} %get-tuple-element.569), channel_id=1, source_target_pairs={{0,4},{4,0},{8,12},{12,8},{16,20},{20,16},{24,28},{28,24},{1,5},{5... | collective-permute-start | bytes 3145736 | tf_op jit(solution)/shard_map/ppermute | solution.py:370
  228.5 24.0 %collective-permute-start.39 = (bf16[512,1024]{1,0:T(8,128)(2,1)}, bf16[512,1024]{1,0:T(8,128)(2,1)S(1)}, u32[]{:S(2)}, u32[]{:S(2)}) collective-permute-start(bf16[512,1024]{1,0:T(8,128)(2,1)} %fusion.28), channel_id=1, source_target_pairs={{0,1},{1,0},{2,3},{3,2},{4,5},{5,4},{6,7},{7,6},{8,9},{9,8},{10,11... | collective-permute-start | bytes 3145736 | tf_op jit(solution)/shard_map/ppermute | solution.py:359
  231.4 16.8 %collective-permute-start.40 = (bf16[512,512]{1,0:T(8,128)(2,1)S(1)}, bf16[512,512]{1,0:T(8,128)(2,1)S(1)}, u32[]{:S(2)}, u32[]{:S(2)}) collective-permute-start(bf16[512,512]{1,0:T(8,128)(2,1)S(1)} %broadcast_select_fusion.2), channel_id=1, source_target_pairs={{0,1},{1,0},{2,3},{3,2},{4,5},{5,4},{6,7},{7,6},{8,9},{9,8},{10,11... | collective-permute-start | bytes 1572872 | tf_op jit(solution)/shard_map/ppermute | solution.py:359
  254.2 18.3 %collective-permute-start.41 = (bf16[384,1024]{1,0:T(8,128)(2,1)S(1)}, bf16[384,1024]{1,0:T(8,128)(2,1)S(1)}, u32[]{:S(2)}, u32[]{:S(2)}) collective-permute-start(bf16[384,1024]{1,0:T(8,128)(2,1)S(1)} %get-tuple-element.595), channel_id=1, source_target_pairs={{0,4},{4,0},{8,12},{12,8},{16,20},{20,16},{24,28},{28,24},{1,5},{5... | collective-permute-start | bytes 2359304 | tf_op jit(solution)/shard_map/ppermute | solution.py:370
  255.1 18.0 %collective-permute-start.42 = (bf16[384,1024]{1,0:T(8,128)(2,1)S(1)}, bf16[384,1024]{1,0:T(8,128)(2,1)S(1)}, u32[]{:S(2)}, u32[]{:S(2)}) collective-permute-start(bf16[384,1024]{1,0:T(8,128)(2,1)S(1)} %get-tuple-element.596), channel_id=1, source_target_pairs={{0,2},{2,0},{1,3},{3,1},{4,6},{6,4},{5,7},{7,5},{8,10},{10,8},{9,1... | collective-permute-start | bytes 2359304 | tf_op jit(solution)/shard_map/ppermute | solution.py:363
  276.0 19.6 %collective-permute-start.44 = (bf16[448,1024]{1,0:T(8,128)(2,1)S(1)}, bf16[448,1024]{1,0:T(8,128)(2,1)S(1)}, u32[]{:S(2)}, u32[]{:S(2)}) collective-permute-start(bf16[448,1024]{1,0:T(8,128)(2,1)S(1)} %get-tuple-element.619), channel_id=1, source_target_pairs={{0,2},{2,0},{1,3},{3,1},{4,6},{6,4},{5,7},{7,5},{8,10},{10,8},{9,1... | collective-permute-start | bytes 2752520 | tf_op jit(solution)/shard_map/ppermute | solution.py:363
  277.2 19.3 %collective-permute-start.45 = (bf16[448,1024]{1,0:T(8,128)(2,1)S(1)}, bf16[448,1024]{1,0:T(8,128)(2,1)S(1)}, u32[]{:S(2)}, u32[]{:S(2)}) collective-permute-start(bf16[448,1024]{1,0:T(8,128)(2,1)S(1)} %get-tuple-element.620), channel_id=1, source_target_pairs={{0,4},{4,0},{8,12},{12,8},{16,20},{20,16},{24,28},{28,24},{1,5},{5... | collective-permute-start | bytes 2752520 | tf_op jit(solution)/shard_map/ppermute | solution.py:370
  310.8 14.8 %collective-permute-start.55 = (bf16[256,1024]{1,0:T(8,128)(2,1)S(1)}, bf16[256,1024]{1,0:T(8,128)(2,1)}, u32[]{:S(2)}, u32[]{:S(2)}) collective-permute-start(bf16[256,1024]{1,0:T(8,128)(2,1)S(1)} %get-tuple-element.679), channel_id=1, source_target_pairs={{0,2},{2,0},{1,3},{3,1},{4,6},{6,4},{5,7},{7,5},{8,10},{10,8},{9,1... | collective-permute-start | bytes 1572872 | tf_op jit(solution)/shard_map/ppermute | solution.py:363
  326.3 15.4 %collective-permute-start.60 = (bf16[256,1024]{1,0:T(8,128)(2,1)S(1)}, bf16[256,1024]{1,0:T(8,128)(2,1)S(1)}, u32[]{:S(2)}, u32[]{:S(2)}) collective-permute-start(bf16[256,1024]{1,0:T(8,128)(2,1)S(1)} %get-tuple-element.708), channel_id=1, source_target_pairs={{0,2},{2,0},{1,3},{3,1},{4,6},{6,4},{5,7},{7,5},{8,10},{10,8},{9,1... | collective-permute-start | bytes 1572872 | tf_op jit(solution)/shard_map/ppermute | solution.py:363
  (111 other events, 849.7 us)

commit v7 on v6

--- a/solution.py
+++ b/solution.py
@@ -1076,12 +1076,17 @@
     def attend(normed_one, in_matrix, out_matrix, grad_own):
         normed_one = with_core(normed_one)
         qkv = (nn(normed_one, in_matrix) + bias_qkv).astype(BF16)
+        for move in gather_rest:
+            old = move.arrays()
+            new, qkv = fence(old, qkv)
+            move.relabel(lambda array, table=list(zip(old, new)): next(b for a, b in table if a is array))
+            swap_rows([move], bits)
         mixed, log_sum = attention(qkv, seg, info, per, head_size)
         away = matmul_rows(mixed, out_matrix, nn, "out_away")
         return normed_one, qkv, mixed, log_sum, away, with_core(grad_own)
 
     normed_one, qkv, mixed, log_sum, out_away, grad_last = phase(
-        bits, [gather_up, *gather_rest], attend, normed_one, in_matrix, out_matrix, grad_own
+        bits, [gather_up], attend, normed_one, in_matrix, out_matrix, grad_own, also=gather_rest
     )
 
     def project_out(stream, mixed, out_away, out_matrix):

time: 350 us -> 348 us (level)
  waiting for transfers between devices: 127 us -> 121 us
  Pallas kernels: 69.7 us -> 74.1 us
    ppermute x16, waiting for transfers between devices: 44.2 us -> 36.5 us  [swap_chip(): return lax.ppermute(array, 'sy', SWAP)]
    pallas_call x20 -> x21, Pallas kernels: 21.3 us -> 22.7 us  [run(): pl.pallas_call(kernel, name='turn', out_shape=tuple(self.shapes), in_spec...]
  transfers between devices with their start and end apart: 64 -> 64, of which waited for: 35 -> 33; matrix products, arithmetic and copies ran while one was open for 19% -> 19% of each run, Pallas kernels for 16% -> 17%
where the time goes in v7:
time: 348 us; the launch traced here: 344 us
  waiting for transfers between devices  121 us (35%)
  Pallas kernels  74.1 us (21%)
  starting transfers between devices  65.7 us (19%)
  matrix products  51.4 us (15%)
  local copies, waits for them, and re-layouts  16.4 us (5%)
  other arithmetic  12.4 us (4%)
    ppermute x31, waiting for transfers between devices, swap_bit(): lax.ppermute(array, 'img', [(i, i ^ 1 << bit - 1) for i in range(count)])  83.2 us
    ppermute x31, starting transfers between devices, swap_bit(): lax.ppermute(array, 'img', [(i, i ^ 1 << bit - 1) for i in range(count)])  46.3 us
    ppermute x16, waiting for transfers between devices, swap_chip(): return lax.ppermute(array, 'sy', SWAP)  36.5 us
    pallas_call x21, Pallas kernels, run(): pl.pallas_call(kernel, name='turn', out_shape=tuple(self.shapes), in_spec...  22.7 us
    dot_general x9, matrix products, nn(): return jnp.dot(left, right, preferred_element_type=F32)  18.7 us
    pallas_call x1, Pallas kernels, attention_back(): pl.pallas_call(functools.partial(attend_back_kernel, part * pairs, pairs,...  18 us
    dot_general x6, matrix products, tn(): lax.dot_general(left, right, (((0,), (0,)), ((), ())), preferred_element_...  17 us
    pallas_call x6, Pallas kernels, by_rows(): pl.pallas_call(kernel, name=name, grid=(length // tile,), out_shape=[jax....  15.8 us
  transfers between devices with their start and end apart: 64, of which 33 were waited for; matrix products, arithmetic and copies ran while one was open for 19% of the time, Pallas kernels for 17%

profile of v7, /device:TPU:0, one launch (start us, length us, event | category | flops | bytes accessed | tf_op | source)
XLA Modules:
  0.0 343.8 jit_solution(15812317969545016529)
XLA Ops:
  7.9 4.1 %collective-permute-start.2 = (bf16[144,1024]{1,0:T(8,128)(2,1)S(1)}, bf16[144,1024]{1,0:T(8,128)(2,1)S(1)}, u32[]{:S(2)}, u32[]{:S(2)}) collective-permute-start(bf16[144,1024]{1,0:T(8,128)(2,1)S(1)} %get-tuple-element.387.refs_0_), channel_id=1, source_target_pairs={{0,16},{4,20},{8,24},{12,28},{16,0},{20,4},{24,8},{28,12},{1,17},{... | collective-permute-start | bytes 884744 | tf_op jit(solution)/shard_map/ppermute | solution.py:370
  16.9 8.7 %collective-permute-done.2.refs_1_ = bf16[144,1024]{1,0:T(8,128)(2,1)S(1)} collective-permute-done((bf16[144,1024]{1,0:T(8,128)(2,1)S(1)}, bf16[144,1024]{1,0:T(8,128)(2,1)S(1)}, u32[]{:S(2)}, u32[]{:S(2)}) %collective-permute-start.2) | collective-permute-done | bytes 294944 | tf_op jit(solution)/shard_map/ppermute | solution.py:370
  28.6 9.7 %collective-permute-done.6 = bf16[256,1024]{1,0:T(8,128)(2,1)S(1)} collective-permute-done((bf16[256,1024]{1,0:T(8,128)(2,1)S(1)}, bf16[256,1024]{1,0:T(8,128)(2,1)S(1)}, u32[]{:S(2)}, u32[]{:S(2)}) %collective-permute-start.6) | collective-permute-done | bytes 524320 | tf_op jit(solution)/shard_map/ppermute | solution.py:363
  44.8 3.2 collective-permute-start.9
  50.3 3.3 first.4
  55.3 4.0 %collective-permute-done.9.refs_5_ = bf16[128,1024]{1,0:T(8,128)(2,1)} collective-permute-done((bf16[128,1024]{1,0:T(8,128)(2,1)}, bf16[128,1024]{1,0:T(8,128)(2,1)}, u32[]{:S(2)}, u32[]{:S(2)}) %collective-permute-start.9) | collective-permute-done | bytes 262176 | tf_op jit(solution)/shard_map/ppermute | solution.py:370
  65.4 3.4 collective-permute-start.13
  68.8 9.6 %collective-permute-done.13.refs_3_ = bf16[96,1024]{1,0:T(8,128)(2,1)S(1)} collective-permute-done((bf16[96,1024]{1,0:T(8,128)(2,1)S(1)}, bf16[96,1024]{1,0:T(8,128)(2,1)S(1)}, u32[]{:S(2)}, u32[]{:S(2)}) %collective-permute-start.13) | collective-permute-done | bytes 196640 | tf_op jit(solution)/shard_map/ppermute | solution.py:370
  79.1 6.7 %collective-permute-done.10.refs_1_ = bf16[512,1024]{1,0:T(8,128)(2,1)S(1)} collective-permute-done((bf16[512,1024]{1,0:T(8,128)(2,1)S(1)}, bf16[512,1024]{1,0:T(8,128)(2,1)S(1)}, u32[]{:S(2)}, u32[]{:S(2)}) %collective-permute-start.10) | collective-permute-done | bytes 1048608 | tf_op jit(solution)/shard_map/ppermute | solution.py:363
  99.4 4.4 %collective-permute-done.16.refs_1_ = bf16[192,1024]{1,0:T(8,128)(2,1)S(1)} collective-permute-done((bf16[192,1024]{1,0:T(8,128)(2,1)S(1)}, bf16[192,1024]{1,0:T(8,128)(2,1)S(1)}, u32[]{:S(2)}, u32[]{:S(2)}) %collective-permute-start.16) | collective-permute-done | bytes 393248 | tf_op jit(solution)/shard_map/ppermute | solution.py:370
  103.7 6.9 %collective-permute-done.14.refs_1_ = bf16[256,1024]{1,0:T(8,128)(2,1)S(1)} collective-permute-done((bf16[256,1024]{1,0:T(8,128)(2,1)S(1)}, bf16[256,1024]{1,0:T(8,128)(2,1)S(1)}, u32[]{:S(2)}, u32[]{:S(2)}) %collective-permute-start.14) | collective-permute-done | bytes 524320 | tf_op jit(solution)/shard_map/ppermute | solution.py:370
  115.8 3.6 %add_convert_fusion.qkv = bf16[1024,1536]{1,0:T(8,128)(2,1)S(1)} fusion(bf16[1024,1024]{1,0:T(8,128)(2,1)S(1)} %constant_dynamic-update-slice_fusion, bf16[1024,1536]{1,0:T(8,128)(2,1)S(1)} %copy-done.14, f32[1536]{0:T(1024)S(1)} %maximum_reduce_fusion), kind=kOutput, calls=%fused_computation.8 | convolution fusion | flops 3224371200 | bytes 8394752 | tf_op jit(solution)/shard_map/dot_general | solution.py:124
  121.9 3.4 %collective-permute-start.21 = (bf16[128,1024]{1,0:T(8,128)(2,1)S(1)}, bf16[128,1024]{1,0:T(8,128)(2,1)S(1)}, u32[]{:S(2)}, u32[]{:S(2)}) collective-permute-start(bf16[128,1024]{1,0:T(8,128)(2,1)S(1)} %turn.28.refs_4_), channel_id=1, source_target_pairs={{0,16},{4,20},{8,24},{12,28},{16,0},{20,4},{24,8},{28,12},{1,17},{... | collective-permute-start | bytes 786440 | tf_op jit(solution)/shard_map/ppermute | solution.py:370
  125.3 13.4 %attend.1 = (bf16[1024,512]{1,0:T(8,128)(2,1)S(1)}, f32[8,1024]{1,0:T(8,128)S(1)}) custom-call(s32[18]{0:T(128)S(1)} %pad_add_fusion.2.info, bf16[1024,1536]{1,0:T(8,128)(2,1)S(1)} %add_convert_fusion.qkv, f32[8,1024]{1,0:T(8,128)S(1)} %broadcast_in_dim.182.seg), custom_call_target="tpu_custom_call" | custom-call | tf_op jit(solution)/shard_map/attend/pallas_call | solution.py:288
  145.0 7.4 %collective-permute-done.23.refs_1_ = bf16[192,1024]{1,0:T(8,128)(2,1)S(1)} collective-permute-done((bf16[192,1024]{1,0:T(8,128)(2,1)S(1)}, bf16[192,1024]{1,0:T(8,128)(2,1)S(1)}, u32[]{:S(2)}, u32[]{:S(2)}) %collective-permute-start.23) | collective-permute-done | bytes 393248 | tf_op jit(solution)/shard_map/ppermute | solution.py:370
  156.5 9.1 %fusion.3 = (f32[1024,2048]{1,0:T(8,128)}, bf16[1024,2048]{1,0:T(8,128)(2,1)S(1)}) fusion(f32[2048]{0:T(1024)S(1)} %bitcast.132, bf16[1024,1024]{1,0:T(8,128)(2,1)S(1)} %constant_dynamic-update-slice_fusion.2, bf16[1024,2048]{1,0:T(8,128)(2,1)S(1)} %turn.30.refs_5_), kind=kOutput, calls=%fused_computation.4 | convolution fusion | flops 4318035968 | bytes 18882560 | tf_op jit(solution)/shard_map/dot_general | solution.py:124
  165.6 5.4 %convolution_convert_fusion.refs_0_ = bf16[2048,1024]{1,0:T(8,128)(2,1)S(1)} fusion(bf16[1024,2048]{1,0:T(8,128)(2,1)S(1)} %get-tuple-element.642.refs_0_, bf16[1024,1024]{1,0:T(8,128)(2,1)S(1)} %pad_maximum_fusion), kind=kOutput, calls=%fused_computation.9 | convolution fusion | flops 4297064448 | bytes 10485760 | tf_op jit(solution)/shard_map/dot_general | solution.py:120
  179.8 7.0 %multiply_convert_fusion.refs_0_ = bf16[1024,2048]{1,0:T(8,128)(2,1)S(1)} fusion(f32[1024,2048]{1,0:T(8,128)} %get-tuple-element.528, bf16[1024,1024]{1,0:T(8,128)(2,1)S(1)} %copy-done.59, bf16[2048,1024]{1,0:T(8,128)(2,1)S(1)} %turn.32.refs_4_), kind=kOutput, calls=%fused_computation.5 | convolution fusion | flops 4299161600 | bytes 18874368 | tf_op jit(solution)/shard_map/dot_general | solution.py:116
  186.8 4.1 %fusion.20.refs_1_.refs_2_ = bf16[1024,1024]{1,0:T(8,128)(2,1)S(1)} fusion(bf16[1024,1024]{1,0:T(8,128)(2,1)} %copy-done.66, bf16[1024,2048]{1,0:T(8,128)(2,1)S(1)} %multiply_convert_fusion.refs_0_), kind=kOutput, calls=%fused_computation.24 | convolution fusion | flops 2148532224 | bytes 6291456 | tf_op jit(solution)/shard_map/dot_general | solution.py:120
  195.8 6.0 %collective-permute-done.30.refs_1_ = bf16[512,1024]{1,0:T(8,128)(2,1)} collective-permute-done((bf16[512,1024]{1,0:T(8,128)(2,1)}, bf16[512,1024]{1,0:T(8,128)(2,1)}, u32[]{:S(2)}, u32[]{:S(2)}) %collective-permute-start.30) | collective-permute-done | bytes 1048608 | tf_op jit(solution)/shard_map/ppermute | solution.py:363
  207.1 3.3 fusion.28
  210.4 3.8 %norm_two_back.1 = (f32[512,1024]{1,0:T(8,128)S(1)}, bf16[512,1024]{1,0:T(8,128)(2,1)S(1)}, f32[1,1024]{1,0:T(1,128)S(1)}, f32[1,1024]{1,0:T(1,128)S(1)}) custom-call(bf16[1024,2048]{1,0:T(8,128)(2,1)S(1)} %multiply_convert_fusion.refs_0_, bf16[512,1024]{1,0:T(8,128)(2,1)S(1)} %collective-permute-done.34.refs_1_, f32[512,1024]{1,0:T(8,128)S(1)} %copy-done.29, ...), custom_call_target="tpu_custom_call" | custom-call | tf_op jit(solution)/shard_map/norm_two_back/pallas_call | solution.py:809
  214.2 4.7 %collective-permute-done.32.refs_3_ = bf16[256,1024]{1,0:T(8,128)(2,1)S(1)} collective-permute-done((bf16[256,1024]{1,0:T(8,128)(2,1)S(1)}, bf16[256,1024]{1,0:T(8,128)(2,1)S(1)}, u32[]{:S(2)}, u32[]{:S(2)}) %collective-permute-start.32) | collective-permute-done | bytes 524320 | tf_op jit(solution)/shard_map/ppermute | solution.py:370
  228.0 18.0 %attend_back.1.refs_0_ = bf16[1024,1536]{1,0:T(8,128)(2,1)S(1)} custom-call(s32[18]{0:T(128)S(1)} %copy-done.55, bf16[1024,1536]{1,0:T(8,128)(2,1)S(1)} %copy-done.12, bf16[1024,512]{1,0:T(8,128)(2,1)S(1)} %copy-done.10, bf16[1024,512]{1,0:T(8,128)(2,1)S(1)} %convolution_convert_fusion.3.grad, f32[8,1024]{1,0:T(8,128)S(1)} %broadcast_in_dim.182.seg, ...), custom_call_target="tpu_custom_call" | custom-call | flops 17179869184 | bytes 8388608 | tf_op jit(solution)/shard_map/attend_back/pallas_call | solution.py:330
  249.7 3.4 collective-permute-start.43
  260.8 3.5 %collective-permute-done.43.refs_1_ = bf16[128,1024]{1,0:T(8,128)(2,1)S(1)} collective-permute-done((bf16[128,1024]{1,0:T(8,128)(2,1)S(1)}, bf16[128,1024]{1,0:T(8,128)(2,1)S(1)}, u32[]{:S(2)}, u32[]{:S(2)}) %collective-permute-start.43) | collective-permute-done | bytes 262176 | tf_op jit(solution)/shard_map/ppermute | solution.py:370
  264.3 7.1 %collective-permute-done.41.refs_4_ = bf16[384,1024]{1,0:T(8,128)(2,1)S(1)} collective-permute-done((bf16[384,1024]{1,0:T(8,128)(2,1)S(1)}, bf16[384,1024]{1,0:T(8,128)(2,1)S(1)}, u32[]{:S(2)}, u32[]{:S(2)}) %collective-permute-start.41) | collective-permute-done | bytes 786464 | tf_op jit(solution)/shard_map/ppermute | solution.py:370
  284.9 2.9 output.1.refs_5_
  287.8 6.7 %collective-permute-done.44.refs_1_ = bf16[448,1024]{1,0:T(8,128)(2,1)S(1)} collective-permute-done((bf16[448,1024]{1,0:T(8,128)(2,1)S(1)}, bf16[448,1024]{1,0:T(8,128)(2,1)S(1)}, u32[]{:S(2)}, u32[]{:S(2)}) %collective-permute-start.44) | collective-permute-done | bytes 917536 | tf_op jit(solution)/shard_map/ppermute | solution.py:363
  300.7 4.8 %collective-permute-done.51.refs_3_ = bf16[64,1024]{1,0:T(8,128)(2,1)S(1)} collective-permute-done((bf16[64,1024]{1,0:T(8,128)(2,1)S(1)}, bf16[64,1024]{1,0:T(8,128)(2,1)S(1)}, u32[]{:S(2)}, u32[]{:S(2)}) %collective-permute-start.51) | collective-permute-done | bytes 131104 | tf_op jit(solution)/shard_map/ppermute | solution.py:370
  305.4 3.5 %collective-permute-done.52.refs_1_.refs_3_ = bf16[128,1024]{1,0:T(8,128)(2,1)S(1)} collective-permute-done((bf16[128,1024]{1,0:T(8,128)(2,1)S(1)}, bf16[128,1024]{1,0:T(8,128)(2,1)S(1)}, u32[]{:S(2)}, u32[]{:S(2)}) %collective-permute-start.52) | collective-permute-done | bytes 262176 | tf_op jit(solution)/shard_map/ppermute | solution.py:370
  316.9 6.8 %collective-permute-done.54.refs_1_.refs_3_ = bf16[96,1024]{1,0:T(8,128)(2,1)S(1)} collective-permute-done((bf16[96,1024]{1,0:T(8,128)(2,1)S(1)}, bf16[96,1024]{1,0:T(8,128)(2,1)S(1)}, u32[]{:S(2)}, u32[]{:S(2)}) %collective-permute-start.54) | collective-permute-done | bytes 196640 | tf_op jit(solution)/shard_map/ppermute | solution.py:370
  (418 shorter events, 149.2 us)
Async XLA Ops:
  7.9 17.6 %collective-permute-start.2 = (bf16[144,1024]{1,0:T(8,128)(2,1)S(1)}, bf16[144,1024]{1,0:T(8,128)(2,1)S(1)}, u32[]{:S(2)}, u32[]{:S(2)}) collective-permute-start(bf16[144,1024]{1,0:T(8,128)(2,1)S(1)} %get-tuple-element.387.refs_0_), channel_id=1, source_target_pairs={{0,16},{4,20},{8,24},{12,28},{16,0},{20,4},{24,8},{28,12},{1,17},{... | collective-permute-start | bytes 884744 | tf_op jit(solution)/shard_map/ppermute | solution.py:370
  13.4 15.1 %collective-permute-start.5 = (bf16[256,1024]{1,0:T(8,128)(2,1)S(1)}, bf16[256,1024]{1,0:T(8,128)(2,1)S(1)}, u32[]{:S(2)}, u32[]{:S(2)}) collective-permute-start(bf16[256,1024]{1,0:T(8,128)(2,1)S(1)} %get-tuple-element.784), channel_id=1, source_target_pairs={{0,2},{2,0},{1,3},{3,1},{4,6},{6,4},{5,7},{7,5},{8,10},{10,8},{9,1... | collective-permute-start | bytes 1572872 | tf_op jit(solution)/shard_map/ppermute | solution.py:363
  16.3 22.0 %collective-permute-start.6 = (bf16[256,1024]{1,0:T(8,128)(2,1)S(1)}, bf16[256,1024]{1,0:T(8,128)(2,1)S(1)}, u32[]{:S(2)}, u32[]{:S(2)}) collective-permute-start(bf16[256,1024]{1,0:T(8,128)(2,1)S(1)} %get-tuple-element.782), channel_id=1, source_target_pairs={{0,2},{2,0},{1,3},{3,1},{4,6},{6,4},{5,7},{7,5},{8,10},{10,8},{9,1... | collective-permute-start | bytes 1572872 | tf_op jit(solution)/shard_map/ppermute | solution.py:363
  26.1 14.1 %collective-permute-start.3 = (bf16[272,1024]{1,0:T(8,128)(2,1)S(1)}, bf16[272,1024]{1,0:T(8,128)(2,1)S(1)}, u32[]{:S(2)}, u32[]{:S(2)}) collective-permute-start(bf16[272,1024]{1,0:T(8,128)(2,1)S(1)} %turn.22.refs_0_), channel_id=1, source_target_pairs={{0,8},{4,12},{8,0},{12,4},{16,24},{20,28},{24,16},{28,20},{1,9},{5... | collective-permute-start | bytes 1671176 | tf_op jit(solution)/shard_map/ppermute | solution.py:370
  42.0 17.3 %collective-permute-start.7 = (bf16[256,1024]{1,0:T(8,128)(2,1)}, bf16[256,1024]{1,0:T(8,128)(2,1)}, u32[]{:S(2)}, u32[]{:S(2)}) collective-permute-start(bf16[256,1024]{1,0:T(8,128)(2,1)} %get-tuple-element.418.refs_0_), channel_id=1, source_target_pairs={{0,4},{4,0},{8,12},{12,8},{16,20},{20,16},{24,28},{28,24},{1,5},{5... | collective-permute-start | bytes 1572872 | tf_op jit(solution)/shard_map/ppermute | solution.py:370
  43.2 16.1 %collective-permute-start.8 = (bf16[336,1024]{1,0:T(8,128)(2,1)}, bf16[336,1024]{1,0:T(8,128)(2,1)}, u32[]{:S(2)}, u32[]{:S(2)}) collective-permute-start(bf16[336,1024]{1,0:T(8,128)(2,1)} %get-tuple-element.469.refs_2_.refs_0_), channel_id=1, source_target_pairs={{0,2},{2,0},{1,3},{3,1},{4,6},{6,4},{5,7},{7,5},{8,10},{10,8},{9,1... | collective-permute-start | bytes 2064392 | tf_op jit(solution)/shard_map/ppermute | solution.py:363
  44.8 14.5 %collective-permute-start.9 = (bf16[128,1024]{1,0:T(8,128)(2,1)}, bf16[128,1024]{1,0:T(8,128)(2,1)}, u32[]{:S(2)}, u32[]{:S(2)}) collective-permute-start(bf16[128,1024]{1,0:T(8,128)(2,1)} %get-tuple-element.422.refs_4_), channel_id=1, source_target_pairs={{0,16},{4,20},{8,24},{12,28},{16,0},{20,4},{24,8},{28,12},{1,17},{... | collective-permute-start | bytes 786440 | tf_op jit(solution)/shard_map/ppermute | solution.py:370
  61.3 24.9 %collective-permute-start.11 = (bf16[528,1024]{1,0:T(8,128)(2,1)S(1)}, bf16[528,1024]{1,0:T(8,128)(2,1)S(1)}, u32[]{:S(2)}, u32[]{:S(2)}) collective-permute-start(bf16[528,1024]{1,0:T(8,128)(2,1)S(1)} %get-tuple-element.436.refs_2_), channel_id=1, source_target_pairs={{0,4},{4,0},{8,12},{12,8},{16,20},{20,16},{24,28},{28,24},{1,5},{5... | collective-permute-start | bytes 3244040 | tf_op jit(solution)/shard_map/ppermute | solution.py:370
  62.1 23.7 %collective-permute-start.10 = (bf16[512,1024]{1,0:T(8,128)(2,1)S(1)}, bf16[512,1024]{1,0:T(8,128)(2,1)S(1)}, u32[]{:S(2)}, u32[]{:S(2)}) collective-permute-start(bf16[512,1024]{1,0:T(8,128)(2,1)S(1)} %get-tuple-element.434.refs_0_), channel_id=1, source_target_pairs={{0,2},{2,0},{1,3},{3,1},{4,6},{6,4},{5,7},{7,5},{8,10},{10,8},{9,1... | collective-permute-start | bytes 3145736 | tf_op jit(solution)/shard_map/ppermute | solution.py:363
  63.0 16.1 %collective-permute-start.12 = (bf16[256,1024]{1,0:T(8,128)(2,1)S(1)}, bf16[256,1024]{1,0:T(8,128)(2,1)S(1)}, u32[]{:S(2)}, u32[]{:S(2)}) collective-permute-start(bf16[256,1024]{1,0:T(8,128)(2,1)S(1)} %get-tuple-element.439.refs_0_), channel_id=1, source_target_pairs={{0,8},{4,12},{8,0},{12,4},{16,24},{20,28},{24,16},{28,20},{1,9},{5... | collective-permute-start | bytes 1572872 | tf_op jit(solution)/shard_map/ppermute | solution.py:370
  96.2 14.3 %collective-permute-start.14 = (bf16[256,1024]{1,0:T(8,128)(2,1)S(1)}, bf16[256,1024]{1,0:T(8,128)(2,1)S(1)}, u32[]{:S(2)}, u32[]{:S(2)}) collective-permute-start(bf16[256,1024]{1,0:T(8,128)(2,1)S(1)} %get-tuple-element.459.refs_0_), channel_id=1, source_target_pairs={{0,4},{4,0},{8,12},{12,8},{16,20},{20,16},{24,28},{28,24},{1,5},{5... | collective-permute-start | bytes 1572872 | tf_op jit(solution)/shard_map/ppermute | solution.py:370
  112.5 26.2 %collective-permute-start.22 = (bf16[512,1024]{1,0:T(8,128)(2,1)S(1)}, bf16[512,1024]{1,0:T(8,128)(2,1)S(1)}, u32[]{:S(2)}, u32[]{:S(2)}) collective-permute-start(bf16[512,1024]{1,0:T(8,128)(2,1)S(1)} %copy-done.5), channel_id=1, source_target_pairs={{0,1},{1,0},{2,3},{3,2},{4,5},{5,4},{6,7},{7,6},{8,9},{9,8},{10,11... | collective-permute-start | bytes 3145736 | tf_op jit(solution)/shard_map/ppermute | solution.py:359
  113.9 26.2 %collective-permute-start.18 = (bf16[512,1024]{1,0:T(8,128)(2,1)S(1)}, bf16[512,1024]{1,0:T(8,128)(2,1)S(1)}, u32[]{:S(2)}, u32[]{:S(2)}) collective-permute-start(bf16[512,1024]{1,0:T(8,128)(2,1)S(1)} %get-tuple-element.497.refs_0_), channel_id=1, source_target_pairs={{0,2},{2,0},{1,3},{3,1},{4,6},{6,4},{5,7},{7,5},{8,10},{10,8},{9,1... | collective-permute-start | bytes 3145736 | tf_op jit(solution)/shard_map/ppermute | solution.py:363
  114.7 25.3 %collective-permute-start.19 = (bf16[512,1024]{1,0:T(8,128)(2,1)S(1)}, bf16[512,1024]{1,0:T(8,128)(2,1)S(1)}, u32[]{:S(2)}, u32[]{:S(2)}) collective-permute-start(bf16[512,1024]{1,0:T(8,128)(2,1)S(1)} %get-tuple-element.499.refs_2_), channel_id=1, source_target_pairs={{0,4},{4,0},{8,12},{12,8},{16,20},{20,16},{24,28},{28,24},{1,5},{5... | collective-permute-start | bytes 3145736 | tf_op jit(solution)/shard_map/ppermute | solution.py:370
  121.9 18.2 %collective-permute-start.21 = (bf16[128,1024]{1,0:T(8,128)(2,1)S(1)}, bf16[128,1024]{1,0:T(8,128)(2,1)S(1)}, u32[]{:S(2)}, u32[]{:S(2)}) collective-permute-start(bf16[128,1024]{1,0:T(8,128)(2,1)S(1)} %turn.28.refs_4_), channel_id=1, source_target_pairs={{0,16},{4,20},{8,24},{12,28},{16,0},{20,4},{24,8},{28,12},{1,17},{... | collective-permute-start | bytes 786440 | tf_op jit(solution)/shard_map/ppermute | solution.py:370
  153.5 17.5 %collective-permute-start.28 = (bf16[256,1024]{1,0:T(8,128)(2,1)S(1)}, bf16[256,1024]{1,0:T(8,128)(2,1)S(1)}, u32[]{:S(2)}, u32[]{:S(2)}) collective-permute-start(bf16[256,1024]{1,0:T(8,128)(2,1)S(1)} %get-tuple-element.519.refs_4_), channel_id=1, source_target_pairs={{0,8},{4,12},{8,0},{12,4},{16,24},{20,28},{24,16},{28,20},{1,9},{5... | collective-permute-start | bytes 1572872 | tf_op jit(solution)/shard_map/ppermute | solution.py:370
  153.9 19.7 %collective-permute-start.26 = (bf16[384,1024]{1,0:T(8,128)(2,1)S(1)}, bf16[384,1024]{1,0:T(8,128)(2,1)S(1)}, u32[]{:S(2)}, u32[]{:S(2)}) collective-permute-start(bf16[384,1024]{1,0:T(8,128)(2,1)S(1)} %get-tuple-element.515.refs_0_), channel_id=1, source_target_pairs={{0,2},{2,0},{1,3},{3,1},{4,6},{6,4},{5,7},{7,5},{8,10},{10,8},{9,1... | collective-permute-start | bytes 2359304 | tf_op jit(solution)/shard_map/ppermute | solution.py:363
  155.2 19.4 %collective-permute-start.27 = (bf16[384,1024]{1,0:T(8,128)(2,1)S(1)}, bf16[384,1024]{1,0:T(8,128)(2,1)S(1)}, u32[]{:S(2)}, u32[]{:S(2)}) collective-permute-start(bf16[384,1024]{1,0:T(8,128)(2,1)S(1)} %get-tuple-element.517.refs_2_), channel_id=1, source_target_pairs={{0,4},{4,0},{8,12},{12,8},{16,20},{20,16},{24,28},{28,24},{1,5},{5... | collective-permute-start | bytes 2359304 | tf_op jit(solution)/shard_map/ppermute | solution.py:370
  177.4 24.4 %collective-permute-start.30 = (bf16[512,1024]{1,0:T(8,128)(2,1)}, bf16[512,1024]{1,0:T(8,128)(2,1)}, u32[]{:S(2)}, u32[]{:S(2)}) collective-permute-start(bf16[512,1024]{1,0:T(8,128)(2,1)} %get-tuple-element.524), channel_id=1, source_target_pairs={{0,2},{2,0},{1,3},{3,1},{4,6},{6,4},{5,7},{7,5},{8,10},{10,8},{9,1... | collective-permute-start | bytes 3145736 | tf_op jit(solution)/shard_map/ppermute | solution.py:363
  178.1 24.4 %collective-permute-start.31 = (bf16[512,1024]{1,0:T(8,128)(2,1)}, bf16[512,1024]{1,0:T(8,128)(2,1)}, u32[]{:S(2)}, u32[]{:S(2)}) collective-permute-start(bf16[512,1024]{1,0:T(8,128)(2,1)} %get-tuple-element.525), channel_id=1, source_target_pairs={{0,4},{4,0},{8,12},{12,8},{16,20},{20,16},{24,28},{28,24},{1,5},{5... | collective-permute-start | bytes 3145736 | tf_op jit(solution)/shard_map/ppermute | solution.py:370
  204.6 14.4 %collective-permute-start.32 = (bf16[256,1024]{1,0:T(8,128)(2,1)S(1)}, bf16[256,1024]{1,0:T(8,128)(2,1)S(1)}, u32[]{:S(2)}, u32[]{:S(2)}) collective-permute-start(bf16[256,1024]{1,0:T(8,128)(2,1)S(1)} %get-tuple-element.545), channel_id=1, source_target_pairs={{0,4},{4,0},{8,12},{12,8},{16,20},{20,16},{24,28},{28,24},{1,5},{5... | collective-permute-start | bytes 1572872 | tf_op jit(solution)/shard_map/ppermute | solution.py:370
  221.5 25.0 %collective-permute-start.37 = (bf16[256,1024]{1,0:T(8,128)(2,1)S(1)}, bf16[256,1024]{1,0:T(8,128)(2,1)S(1)}, u32[]{:S(2)}, u32[]{:S(2)}) collective-permute-start(bf16[256,1024]{1,0:T(8,128)(2,1)S(1)} %get-tuple-element.575), channel_id=1, source_target_pairs={{0,8},{4,12},{8,0},{12,4},{16,24},{20,28},{24,16},{28,20},{1,9},{5... | collective-permute-start | bytes 1572872 | tf_op jit(solution)/shard_map/ppermute | solution.py:370
  222.9 25.3 %collective-permute-start.35 = (bf16[512,1024]{1,0:T(8,128)(2,1)S(1)}, bf16[512,1024]{1,0:T(8,128)(2,1)S(1)}, u32[]{:S(2)}, u32[]{:S(2)}) collective-permute-start(bf16[512,1024]{1,0:T(8,128)(2,1)S(1)} %get-tuple-element.572), channel_id=1, source_target_pairs={{0,2},{2,0},{1,3},{3,1},{4,6},{6,4},{5,7},{7,5},{8,10},{10,8},{9,1... | collective-permute-start | bytes 3145736 | tf_op jit(solution)/shard_map/ppermute | solution.py:363
  223.5 25.0 %collective-permute-start.36 = (bf16[512,1024]{1,0:T(8,128)(2,1)S(1)}, bf16[512,1024]{1,0:T(8,128)(2,1)S(1)}, u32[]{:S(2)}, u32[]{:S(2)}) collective-permute-start(bf16[512,1024]{1,0:T(8,128)(2,1)S(1)} %get-tuple-element.573), channel_id=1, source_target_pairs={{0,4},{4,0},{8,12},{12,8},{16,20},{20,16},{24,28},{28,24},{1,5},{5... | collective-permute-start | bytes 3145736 | tf_op jit(solution)/shard_map/ppermute | solution.py:370
  224.5 24.0 %collective-permute-start.39 = (bf16[512,1024]{1,0:T(8,128)(2,1)}, bf16[512,1024]{1,0:T(8,128)(2,1)S(1)}, u32[]{:S(2)}, u32[]{:S(2)}) collective-permute-start(bf16[512,1024]{1,0:T(8,128)(2,1)} %fusion.28), channel_id=1, source_target_pairs={{0,1},{1,0},{2,3},{3,2},{4,5},{5,4},{6,7},{7,6},{8,9},{9,8},{10,11... | collective-permute-start | bytes 3145736 | tf_op jit(solution)/shard_map/ppermute | solution.py:359
  227.4 18.6 %collective-permute-start.40 = (bf16[512,512]{1,0:T(8,128)(2,1)S(1)}, bf16[512,512]{1,0:T(8,128)(2,1)S(1)}, u32[]{:S(2)}, u32[]{:S(2)}) collective-permute-start(bf16[512,512]{1,0:T(8,128)(2,1)S(1)} %broadcast_select_fusion.2), channel_id=1, source_target_pairs={{0,1},{1,0},{2,3},{3,2},{4,5},{5,4},{6,7},{7,6},{8,9},{9,8},{10,11... | collective-permute-start | bytes 1572872 | tf_op jit(solution)/shard_map/ppermute | solution.py:359
  249.7 14.6 %collective-permute-start.43 = (bf16[128,1024]{1,0:T(8,128)(2,1)S(1)}, bf16[128,1024]{1,0:T(8,128)(2,1)S(1)}, u32[]{:S(2)}, u32[]{:S(2)}) collective-permute-start(bf16[128,1024]{1,0:T(8,128)(2,1)S(1)} %get-tuple-element.601), channel_id=1, source_target_pairs={{0,16},{4,20},{8,24},{12,28},{16,0},{20,4},{24,8},{28,12},{1,17},{... | collective-permute-start | bytes 786440 | tf_op jit(solution)/shard_map/ppermute | solution.py:370
  253.1 18.3 %collective-permute-start.41 = (bf16[384,1024]{1,0:T(8,128)(2,1)S(1)}, bf16[384,1024]{1,0:T(8,128)(2,1)S(1)}, u32[]{:S(2)}, u32[]{:S(2)}) collective-permute-start(bf16[384,1024]{1,0:T(8,128)(2,1)S(1)} %get-tuple-element.599), channel_id=1, source_target_pairs={{0,4},{4,0},{8,12},{12,8},{16,20},{20,16},{24,28},{28,24},{1,5},{5... | collective-permute-start | bytes 2359304 | tf_op jit(solution)/shard_map/ppermute | solution.py:370
  254.1 18.0 %collective-permute-start.42 = (bf16[384,1024]{1,0:T(8,128)(2,1)S(1)}, bf16[384,1024]{1,0:T(8,128)(2,1)S(1)}, u32[]{:S(2)}, u32[]{:S(2)}) collective-permute-start(bf16[384,1024]{1,0:T(8,128)(2,1)S(1)} %get-tuple-element.600), channel_id=1, source_target_pairs={{0,2},{2,0},{1,3},{3,1},{4,6},{6,4},{5,7},{7,5},{8,10},{10,8},{9,1... | collective-permute-start | bytes 2359304 | tf_op jit(solution)/shard_map/ppermute | solution.py:363
  275.0 19.6 %collective-permute-start.44 = (bf16[448,1024]{1,0:T(8,128)(2,1)S(1)}, bf16[448,1024]{1,0:T(8,128)(2,1)S(1)}, u32[]{:S(2)}, u32[]{:S(2)}) collective-permute-start(bf16[448,1024]{1,0:T(8,128)(2,1)S(1)} %get-tuple-element.623), channel_id=1, source_target_pairs={{0,2},{2,0},{1,3},{3,1},{4,6},{6,4},{5,7},{7,5},{8,10},{10,8},{9,1... | collective-permute-start | bytes 2752520 | tf_op jit(solution)/shard_map/ppermute | solution.py:363
  276.2 19.3 %collective-permute-start.45 = (bf16[448,1024]{1,0:T(8,128)(2,1)S(1)}, bf16[448,1024]{1,0:T(8,128)(2,1)S(1)}, u32[]{:S(2)}, u32[]{:S(2)}) collective-permute-start(bf16[448,1024]{1,0:T(8,128)(2,1)S(1)} %get-tuple-element.624), channel_id=1, source_target_pairs={{0,4},{4,0},{8,12},{12,8},{16,20},{20,16},{24,28},{28,24},{1,5},{5... | collective-permute-start | bytes 2752520 | tf_op jit(solution)/shard_map/ppermute | solution.py:370
  324.4 14.9 %collective-permute-start.60 = (bf16[256,1024]{1,0:T(8,128)(2,1)S(1)}, bf16[256,1024]{1,0:T(8,128)(2,1)S(1)}, u32[]{:S(2)}, u32[]{:S(2)}) collective-permute-start(bf16[256,1024]{1,0:T(8,128)(2,1)S(1)} %get-tuple-element.712), channel_id=1, source_target_pairs={{0,2},{2,0},{1,3},{3,1},{4,6},{6,4},{5,7},{7,5},{8,10},{10,8},{9,1... | collective-permute-start | bytes 1572872 | tf_op jit(solution)/shard_map/ppermute | solution.py:363
  (111 other events, 820.1 us)

commit v8 on v7

--- a/solution.py
+++ b/solution.py
@@ -1434,7 +1434,7 @@
             return back_to_rows(output, came), across
 
         output, across = phase(
-            bits, [scatter_in, *scatter_out, *sides, send_grad], last_work, output, send_output.result(), low
+            bits, [send_grad, scatter_in, *scatter_out, *sides], last_work, output, send_output.result(), low
         )
         near, far_side = (side.result().astype(F32) for side in sides)
         narrow = (low.astype(F32) + near) + (far_side + across.astype(F32))

time: 348 us -> 348 us (level)
  transfers between devices with their start and end apart: 64 -> 64, of which waited for: 33 -> 35; matrix products, arithmetic and copies ran while one was open for 19% -> 19% of each run, Pallas kernels for 17% -> 16%
where the time goes in v8:
time: 348 us; the launch traced here: 344 us
  waiting for transfers between devices  123 us (35%)
  Pallas kernels  71.1 us (20%)
  starting transfers between devices  66.5 us (19%)
  matrix products  51.4 us (15%)
  local copies, waits for them, and re-layouts  16.4 us (5%)
  other arithmetic  12.4 us (4%)
    ppermute x31, waiting for transfers between devices, swap_bit(): lax.ppermute(array, 'img', [(i, i ^ 1 << bit - 1) for i in range(count)])  83.6 us
    ppermute x31, starting transfers between devices, swap_bit(): lax.ppermute(array, 'img', [(i, i ^ 1 << bit - 1) for i in range(count)])  46.4 us
    ppermute x16, waiting for transfers between devices, swap_chip(): return lax.ppermute(array, 'sy', SWAP)  38.3 us
    pallas_call x21, Pallas kernels, run(): pl.pallas_call(kernel, name='turn', out_shape=tuple(self.shapes), in_spec...  22.7 us
    dot_general x9, matrix products, nn(): return jnp.dot(left, right, preferred_element_type=F32)  18.7 us
    dot_general x6, matrix products, tn(): lax.dot_general(left, right, (((0,), (0,)), ((), ())), preferred_element_...  17 us
    pallas_call x1, Pallas kernels, attention_back(): pl.pallas_call(functools.partial(attend_back_kernel, part * pairs, pairs,...  16.3 us
    ppermute x16, starting transfers between devices, swap_chip(): return lax.ppermute(array, 'sy', SWAP)  16.1 us
  transfers between devices with their start and end apart: 64, of which 35 were waited for; matrix products, arithmetic and copies ran while one was open for 19% of the time, Pallas kernels for 16%

profile of v8, /device:TPU:0, one launch (start us, length us, event | category | flops | bytes accessed | tf_op | source)
XLA Modules:
  0.0 343.8 jit_solution(11685914243764204846)
XLA Ops:
  7.9 4.1 %collective-permute-start.2 = (bf16[144,1024]{1,0:T(8,128)(2,1)S(1)}, bf16[144,1024]{1,0:T(8,128)(2,1)S(1)}, u32[]{:S(2)}, u32[]{:S(2)}) collective-permute-start(bf16[144,1024]{1,0:T(8,128)(2,1)S(1)} %get-tuple-element.387.refs_0_), channel_id=1, source_target_pairs={{0,16},{4,20},{8,24},{12,28},{16,0},{20,4},{24,8},{28,12},{1,17},{... | collective-permute-start | bytes 884744 | tf_op jit(solution)/shard_map/ppermute | solution.py:370
  16.9 8.7 %collective-permute-done.2.refs_1_ = bf16[144,1024]{1,0:T(8,128)(2,1)S(1)} collective-permute-done((bf16[144,1024]{1,0:T(8,128)(2,1)S(1)}, bf16[144,1024]{1,0:T(8,128)(2,1)S(1)}, u32[]{:S(2)}, u32[]{:S(2)}) %collective-permute-start.2) | collective-permute-done | bytes 294944 | tf_op jit(solution)/shard_map/ppermute | solution.py:370
  28.6 9.7 %collective-permute-done.6 = bf16[256,1024]{1,0:T(8,128)(2,1)S(1)} collective-permute-done((bf16[256,1024]{1,0:T(8,128)(2,1)S(1)}, bf16[256,1024]{1,0:T(8,128)(2,1)S(1)}, u32[]{:S(2)}, u32[]{:S(2)}) %collective-permute-start.6) | collective-permute-done | bytes 524320 | tf_op jit(solution)/shard_map/ppermute | solution.py:363
  44.8 3.2 collective-permute-start.9
  50.3 3.3 first.4
  55.3 4.0 %collective-permute-done.9.refs_5_ = bf16[128,1024]{1,0:T(8,128)(2,1)} collective-permute-done((bf16[128,1024]{1,0:T(8,128)(2,1)}, bf16[128,1024]{1,0:T(8,128)(2,1)}, u32[]{:S(2)}, u32[]{:S(2)}) %collective-permute-start.9) | collective-permute-done | bytes 262176 | tf_op jit(solution)/shard_map/ppermute | solution.py:370
  65.4 3.4 collective-permute-start.13
  68.8 9.6 %collective-permute-done.13.refs_3_ = bf16[96,1024]{1,0:T(8,128)(2,1)S(1)} collective-permute-done((bf16[96,1024]{1,0:T(8,128)(2,1)S(1)}, bf16[96,1024]{1,0:T(8,128)(2,1)S(1)}, u32[]{:S(2)}, u32[]{:S(2)}) %collective-permute-start.13) | collective-permute-done | bytes 196640 | tf_op jit(solution)/shard_map/ppermute | solution.py:370
  79.1 6.7 %collective-permute-done.10.refs_1_ = bf16[512,1024]{1,0:T(8,128)(2,1)S(1)} collective-permute-done((bf16[512,1024]{1,0:T(8,128)(2,1)S(1)}, bf16[512,1024]{1,0:T(8,128)(2,1)S(1)}, u32[]{:S(2)}, u32[]{:S(2)}) %collective-permute-start.10) | collective-permute-done | bytes 1048608 | tf_op jit(solution)/shard_map/ppermute | solution.py:363
  99.4 4.4 %collective-permute-done.16.refs_1_ = bf16[192,1024]{1,0:T(8,128)(2,1)S(1)} collective-permute-done((bf16[192,1024]{1,0:T(8,128)(2,1)S(1)}, bf16[192,1024]{1,0:T(8,128)(2,1)S(1)}, u32[]{:S(2)}, u32[]{:S(2)}) %collective-permute-start.16) | collective-permute-done | bytes 393248 | tf_op jit(solution)/shard_map/ppermute | solution.py:370
  103.7 6.9 %collective-permute-done.14.refs_1_ = bf16[256,1024]{1,0:T(8,128)(2,1)S(1)} collective-permute-done((bf16[256,1024]{1,0:T(8,128)(2,1)S(1)}, bf16[256,1024]{1,0:T(8,128)(2,1)S(1)}, u32[]{:S(2)}, u32[]{:S(2)}) %collective-permute-start.14) | collective-permute-done | bytes 524320 | tf_op jit(solution)/shard_map/ppermute | solution.py:370
  115.8 3.6 %add_convert_fusion.qkv = bf16[1024,1536]{1,0:T(8,128)(2,1)S(1)} fusion(bf16[1024,1024]{1,0:T(8,128)(2,1)S(1)} %constant_dynamic-update-slice_fusion, bf16[1024,1536]{1,0:T(8,128)(2,1)S(1)} %copy-done.14, f32[1536]{0:T(1024)S(1)} %maximum_reduce_fusion), kind=kOutput, calls=%fused_computation.8 | convolution fusion | flops 3224371200 | bytes 8394752 | tf_op jit(solution)/shard_map/dot_general | solution.py:124
  121.9 3.4 %collective-permute-start.21 = (bf16[128,1024]{1,0:T(8,128)(2,1)S(1)}, bf16[128,1024]{1,0:T(8,128)(2,1)S(1)}, u32[]{:S(2)}, u32[]{:S(2)}) collective-permute-start(bf16[128,1024]{1,0:T(8,128)(2,1)S(1)} %turn.28.refs_4_), channel_id=1, source_target_pairs={{0,16},{4,20},{8,24},{12,28},{16,0},{20,4},{24,8},{28,12},{1,17},{... | collective-permute-start | bytes 786440 | tf_op jit(solution)/shard_map/ppermute | solution.py:370
  125.3 12.1 %attend.1 = (bf16[1024,512]{1,0:T(8,128)(2,1)S(1)}, f32[8,1024]{1,0:T(8,128)S(1)}) custom-call(s32[18]{0:T(128)S(1)} %pad_add_fusion.2.info, bf16[1024,1536]{1,0:T(8,128)(2,1)S(1)} %add_convert_fusion.qkv, f32[8,1024]{1,0:T(8,128)S(1)} %broadcast_in_dim.182.seg), custom_call_target="tpu_custom_call" | custom-call | tf_op jit(solution)/shard_map/attend/pallas_call | solution.py:288
  145.0 6.8 %collective-permute-done.23.refs_1_ = bf16[192,1024]{1,0:T(8,128)(2,1)S(1)} collective-permute-done((bf16[192,1024]{1,0:T(8,128)(2,1)S(1)}, bf16[192,1024]{1,0:T(8,128)(2,1)S(1)}, u32[]{:S(2)}, u32[]{:S(2)}) %collective-permute-start.23) | collective-permute-done | bytes 393248 | tf_op jit(solution)/shard_map/ppermute | solution.py:370
  156.5 9.1 %fusion.3 = (f32[1024,2048]{1,0:T(8,128)}, bf16[1024,2048]{1,0:T(8,128)(2,1)S(1)}) fusion(f32[2048]{0:T(1024)S(1)} %bitcast.132, bf16[1024,1024]{1,0:T(8,128)(2,1)S(1)} %constant_dynamic-update-slice_fusion.2, bf16[1024,2048]{1,0:T(8,128)(2,1)S(1)} %turn.30.refs_5_), kind=kOutput, calls=%fused_computation.4 | convolution fusion | flops 4318035968 | bytes 18882560 | tf_op jit(solution)/shard_map/dot_general | solution.py:124
  165.6 5.4 %convolution_convert_fusion.refs_0_ = bf16[2048,1024]{1,0:T(8,128)(2,1)S(1)} fusion(bf16[1024,2048]{1,0:T(8,128)(2,1)S(1)} %get-tuple-element.642.refs_0_, bf16[1024,1024]{1,0:T(8,128)(2,1)S(1)} %pad_maximum_fusion), kind=kOutput, calls=%fused_computation.9 | convolution fusion | flops 4297064448 | bytes 10485760 | tf_op jit(solution)/shard_map/dot_general | solution.py:120
  179.7 7.0 %multiply_convert_fusion.refs_0_ = bf16[1024,2048]{1,0:T(8,128)(2,1)S(1)} fusion(f32[1024,2048]{1,0:T(8,128)} %get-tuple-element.528, bf16[1024,1024]{1,0:T(8,128)(2,1)S(1)} %copy-done.59, bf16[2048,1024]{1,0:T(8,128)(2,1)S(1)} %turn.32.refs_4_), kind=kOutput, calls=%fused_computation.5 | convolution fusion | flops 4299161600 | bytes 18874368 | tf_op jit(solution)/shard_map/dot_general | solution.py:116
  186.8 4.1 %fusion.20.refs_1_.refs_2_ = bf16[1024,1024]{1,0:T(8,128)(2,1)S(1)} fusion(bf16[1024,1024]{1,0:T(8,128)(2,1)} %copy-done.66, bf16[1024,2048]{1,0:T(8,128)(2,1)S(1)} %multiply_convert_fusion.refs_0_), kind=kOutput, calls=%fused_computation.24 | convolution fusion | flops 2148532224 | bytes 6291456 | tf_op jit(solution)/shard_map/dot_general | solution.py:120
  195.8 6.1 %collective-permute-done.30.refs_1_ = bf16[512,1024]{1,0:T(8,128)(2,1)} collective-permute-done((bf16[512,1024]{1,0:T(8,128)(2,1)}, bf16[512,1024]{1,0:T(8,128)(2,1)}, u32[]{:S(2)}, u32[]{:S(2)}) %collective-permute-start.30) | collective-permute-done | bytes 1048608 | tf_op jit(solution)/shard_map/ppermute | solution.py:363
  206.8 3.3 fusion.28
  210.2 3.8 %norm_two_back.1 = (f32[512,1024]{1,0:T(8,128)S(1)}, bf16[512,1024]{1,0:T(8,128)(2,1)S(1)}, f32[1,1024]{1,0:T(1,128)S(1)}, f32[1,1024]{1,0:T(1,128)S(1)}) custom-call(bf16[1024,2048]{1,0:T(8,128)(2,1)S(1)} %multiply_convert_fusion.refs_0_, bf16[512,1024]{1,0:T(8,128)(2,1)S(1)} %collective-permute-done.34.refs_1_, f32[512,1024]{1,0:T(8,128)S(1)} %copy-done.29, ...), custom_call_target="tpu_custom_call" | custom-call | tf_op jit(solution)/shard_map/norm_two_back/pallas_call | solution.py:809
  214.0 4.9 %collective-permute-done.32.refs_3_ = bf16[256,1024]{1,0:T(8,128)(2,1)S(1)} collective-permute-done((bf16[256,1024]{1,0:T(8,128)(2,1)S(1)}, bf16[256,1024]{1,0:T(8,128)(2,1)S(1)}, u32[]{:S(2)}, u32[]{:S(2)}) %collective-permute-start.32) | collective-permute-done | bytes 524320 | tf_op jit(solution)/shard_map/ppermute | solution.py:370
  228.0 16.3 %attend_back.1.refs_0_ = bf16[1024,1536]{1,0:T(8,128)(2,1)S(1)} custom-call(s32[18]{0:T(128)S(1)} %copy-done.55, bf16[1024,1536]{1,0:T(8,128)(2,1)S(1)} %copy-done.12, bf16[1024,512]{1,0:T(8,128)(2,1)S(1)} %copy-done.10, bf16[1024,512]{1,0:T(8,128)(2,1)S(1)} %convolution_convert_fusion.3.grad, f32[8,1024]{1,0:T(8,128)S(1)} %broadcast_in_dim.182.seg, ...), custom_call_target="tpu_custom_call" | custom-call | flops 17179869184 | bytes 8388608 | tf_op jit(solution)/shard_map/attend_back/pallas_call | solution.py:330
  249.7 3.4 %collective-permute-start.43 = (bf16[128,1024]{1,0:T(8,128)(2,1)S(1)}, bf16[128,1024]{1,0:T(8,128)(2,1)S(1)}, u32[]{:S(2)}, u32[]{:S(2)}) collective-permute-start(bf16[128,1024]{1,0:T(8,128)(2,1)S(1)} %get-tuple-element.601), channel_id=1, source_target_pairs={{0,16},{4,20},{8,24},{12,28},{16,0},{20,4},{24,8},{28,12},{1,17},{... | collective-permute-start | bytes 786440 | tf_op jit(solution)/shard_map/ppermute | solution.py:370
  260.8 3.5 %collective-permute-done.43.refs_1_ = bf16[128,1024]{1,0:T(8,128)(2,1)S(1)} collective-permute-done((bf16[128,1024]{1,0:T(8,128)(2,1)S(1)}, bf16[128,1024]{1,0:T(8,128)(2,1)S(1)}, u32[]{:S(2)}, u32[]{:S(2)}) %collective-permute-start.43) | collective-permute-done | bytes 262176 | tf_op jit(solution)/shard_map/ppermute | solution.py:370
  264.3 7.1 %collective-permute-done.41.refs_4_ = bf16[384,1024]{1,0:T(8,128)(2,1)S(1)} collective-permute-done((bf16[384,1024]{1,0:T(8,128)(2,1)S(1)}, bf16[384,1024]{1,0:T(8,128)(2,1)S(1)}, u32[]{:S(2)}, u32[]{:S(2)}) %collective-permute-start.41) | collective-permute-done | bytes 786464 | tf_op jit(solution)/shard_map/ppermute | solution.py:370
  284.9 2.9 output.1.refs_5_
  287.8 6.7 %collective-permute-done.44.refs_1_ = bf16[448,1024]{1,0:T(8,128)(2,1)S(1)} collective-permute-done((bf16[448,1024]{1,0:T(8,128)(2,1)S(1)}, bf16[448,1024]{1,0:T(8,128)(2,1)S(1)}, u32[]{:S(2)}, u32[]{:S(2)}) %collective-permute-start.44) | collective-permute-done | bytes 917536 | tf_op jit(solution)/shard_map/ppermute | solution.py:363
  300.7 4.8 %collective-permute-done.51.refs_3_ = bf16[64,1024]{1,0:T(8,128)(2,1)S(1)} collective-permute-done((bf16[64,1024]{1,0:T(8,128)(2,1)S(1)}, bf16[64,1024]{1,0:T(8,128)(2,1)S(1)}, u32[]{:S(2)}, u32[]{:S(2)}) %collective-permute-start.51) | collective-permute-done | bytes 131104 | tf_op jit(solution)/shard_map/ppermute | solution.py:370
  305.4 3.5 %collective-permute-done.52.refs_1_.refs_3_ = bf16[128,1024]{1,0:T(8,128)(2,1)S(1)} collective-permute-done((bf16[128,1024]{1,0:T(8,128)(2,1)S(1)}, bf16[128,1024]{1,0:T(8,128)(2,1)S(1)}, u32[]{:S(2)}, u32[]{:S(2)}) %collective-permute-start.52) | collective-permute-done | bytes 262176 | tf_op jit(solution)/shard_map/ppermute | solution.py:370
  317.0 6.7 %collective-permute-done.54.refs_1_.refs_3_ = bf16[96,1024]{1,0:T(8,128)(2,1)S(1)} collective-permute-done((bf16[96,1024]{1,0:T(8,128)(2,1)S(1)}, bf16[96,1024]{1,0:T(8,128)(2,1)S(1)}, u32[]{:S(2)}, u32[]{:S(2)}) %collective-permute-start.54) | collective-permute-done | bytes 196640 | tf_op jit(solution)/shard_map/ppermute | solution.py:370
  (418 shorter events, 152.7 us)
Async XLA Ops:
  7.9 17.6 %collective-permute-start.2 = (bf16[144,1024]{1,0:T(8,128)(2,1)S(1)}, bf16[144,1024]{1,0:T(8,128)(2,1)S(1)}, u32[]{:S(2)}, u32[]{:S(2)}) collective-permute-start(bf16[144,1024]{1,0:T(8,128)(2,1)S(1)} %get-tuple-element.387.refs_0_), channel_id=1, source_target_pairs={{0,16},{4,20},{8,24},{12,28},{16,0},{20,4},{24,8},{28,12},{1,17},{... | collective-permute-start | bytes 884744 | tf_op jit(solution)/shard_map/ppermute | solution.py:370
  13.4 15.1 %collective-permute-start.5 = (bf16[256,1024]{1,0:T(8,128)(2,1)S(1)}, bf16[256,1024]{1,0:T(8,128)(2,1)S(1)}, u32[]{:S(2)}, u32[]{:S(2)}) collective-permute-start(bf16[256,1024]{1,0:T(8,128)(2,1)S(1)} %get-tuple-element.784), channel_id=1, source_target_pairs={{0,2},{2,0},{1,3},{3,1},{4,6},{6,4},{5,7},{7,5},{8,10},{10,8},{9,1... | collective-permute-start | bytes 1572872 | tf_op jit(solution)/shard_map/ppermute | solution.py:363
  16.3 22.0 %collective-permute-start.6 = (bf16[256,1024]{1,0:T(8,128)(2,1)S(1)}, bf16[256,1024]{1,0:T(8,128)(2,1)S(1)}, u32[]{:S(2)}, u32[]{:S(2)}) collective-permute-start(bf16[256,1024]{1,0:T(8,128)(2,1)S(1)} %get-tuple-element.782), channel_id=1, source_target_pairs={{0,2},{2,0},{1,3},{3,1},{4,6},{6,4},{5,7},{7,5},{8,10},{10,8},{9,1... | collective-permute-start | bytes 1572872 | tf_op jit(solution)/shard_map/ppermute | solution.py:363
  26.1 14.1 %collective-permute-start.3 = (bf16[272,1024]{1,0:T(8,128)(2,1)S(1)}, bf16[272,1024]{1,0:T(8,128)(2,1)S(1)}, u32[]{:S(2)}, u32[]{:S(2)}) collective-permute-start(bf16[272,1024]{1,0:T(8,128)(2,1)S(1)} %turn.22.refs_0_), channel_id=1, source_target_pairs={{0,8},{4,12},{8,0},{12,4},{16,24},{20,28},{24,16},{28,20},{1,9},{5... | collective-permute-start | bytes 1671176 | tf_op jit(solution)/shard_map/ppermute | solution.py:370
  42.0 17.3 %collective-permute-start.7 = (bf16[256,1024]{1,0:T(8,128)(2,1)}, bf16[256,1024]{1,0:T(8,128)(2,1)}, u32[]{:S(2)}, u32[]{:S(2)}) collective-permute-start(bf16[256,1024]{1,0:T(8,128)(2,1)} %get-tuple-element.418.refs_0_), channel_id=1, source_target_pairs={{0,4},{4,0},{8,12},{12,8},{16,20},{20,16},{24,28},{28,24},{1,5},{5... | collective-permute-start | bytes 1572872 | tf_op jit(solution)/shard_map/ppermute | solution.py:370
  43.2 16.1 %collective-permute-start.8 = (bf16[336,1024]{1,0:T(8,128)(2,1)}, bf16[336,1024]{1,0:T(8,128)(2,1)}, u32[]{:S(2)}, u32[]{:S(2)}) collective-permute-start(bf16[336,1024]{1,0:T(8,128)(2,1)} %get-tuple-element.469.refs_2_.refs_0_), channel_id=1, source_target_pairs={{0,2},{2,0},{1,3},{3,1},{4,6},{6,4},{5,7},{7,5},{8,10},{10,8},{9,1... | collective-permute-start | bytes 2064392 | tf_op jit(solution)/shard_map/ppermute | solution.py:363
  44.8 14.5 %collective-permute-start.9 = (bf16[128,1024]{1,0:T(8,128)(2,1)}, bf16[128,1024]{1,0:T(8,128)(2,1)}, u32[]{:S(2)}, u32[]{:S(2)}) collective-permute-start(bf16[128,1024]{1,0:T(8,128)(2,1)} %get-tuple-element.422.refs_4_), channel_id=1, source_target_pairs={{0,16},{4,20},{8,24},{12,28},{16,0},{20,4},{24,8},{28,12},{1,17},{... | collective-permute-start | bytes 786440 | tf_op jit(solution)/shard_map/ppermute | solution.py:370
  61.3 24.9 %collective-permute-start.11 = (bf16[528,1024]{1,0:T(8,128)(2,1)S(1)}, bf16[528,1024]{1,0:T(8,128)(2,1)S(1)}, u32[]{:S(2)}, u32[]{:S(2)}) collective-permute-start(bf16[528,1024]{1,0:T(8,128)(2,1)S(1)} %get-tuple-element.436.refs_2_), channel_id=1, source_target_pairs={{0,4},{4,0},{8,12},{12,8},{16,20},{20,16},{24,28},{28,24},{1,5},{5... | collective-permute-start | bytes 3244040 | tf_op jit(solution)/shard_map/ppermute | solution.py:370
  62.1 23.7 %collective-permute-start.10 = (bf16[512,1024]{1,0:T(8,128)(2,1)S(1)}, bf16[512,1024]{1,0:T(8,128)(2,1)S(1)}, u32[]{:S(2)}, u32[]{:S(2)}) collective-permute-start(bf16[512,1024]{1,0:T(8,128)(2,1)S(1)} %get-tuple-element.434.refs_0_), channel_id=1, source_target_pairs={{0,2},{2,0},{1,3},{3,1},{4,6},{6,4},{5,7},{7,5},{8,10},{10,8},{9,1... | collective-permute-start | bytes 3145736 | tf_op jit(solution)/shard_map/ppermute | solution.py:363
  63.0 16.1 %collective-permute-start.12 = (bf16[256,1024]{1,0:T(8,128)(2,1)S(1)}, bf16[256,1024]{1,0:T(8,128)(2,1)S(1)}, u32[]{:S(2)}, u32[]{:S(2)}) collective-permute-start(bf16[256,1024]{1,0:T(8,128)(2,1)S(1)} %get-tuple-element.439.refs_0_), channel_id=1, source_target_pairs={{0,8},{4,12},{8,0},{12,4},{16,24},{20,28},{24,16},{28,20},{1,9},{5... | collective-permute-start | bytes 1572872 | tf_op jit(solution)/shard_map/ppermute | solution.py:370
  96.2 14.3 %collective-permute-start.14 = (bf16[256,1024]{1,0:T(8,128)(2,1)S(1)}, bf16[256,1024]{1,0:T(8,128)(2,1)S(1)}, u32[]{:S(2)}, u32[]{:S(2)}) collective-permute-start(bf16[256,1024]{1,0:T(8,128)(2,1)S(1)} %get-tuple-element.459.refs_0_), channel_id=1, source_target_pairs={{0,4},{4,0},{8,12},{12,8},{16,20},{20,16},{24,28},{28,24},{1,5},{5... | collective-permute-start | bytes 1572872 | tf_op jit(solution)/shard_map/ppermute | solution.py:370
  112.5 24.9 %collective-permute-start.22 = (bf16[512,1024]{1,0:T(8,128)(2,1)S(1)}, bf16[512,1024]{1,0:T(8,128)(2,1)S(1)}, u32[]{:S(2)}, u32[]{:S(2)}) collective-permute-start(bf16[512,1024]{1,0:T(8,128)(2,1)S(1)} %copy-done.5), channel_id=1, source_target_pairs={{0,1},{1,0},{2,3},{3,2},{4,5},{5,4},{6,7},{7,6},{8,9},{9,8},{10,11... | collective-permute-start | bytes 3145736 | tf_op jit(solution)/shard_map/ppermute | solution.py:359
  113.9 25.1 %collective-permute-start.18 = (bf16[512,1024]{1,0:T(8,128)(2,1)S(1)}, bf16[512,1024]{1,0:T(8,128)(2,1)S(1)}, u32[]{:S(2)}, u32[]{:S(2)}) collective-permute-start(bf16[512,1024]{1,0:T(8,128)(2,1)S(1)} %get-tuple-element.497.refs_0_), channel_id=1, source_target_pairs={{0,2},{2,0},{1,3},{3,1},{4,6},{6,4},{5,7},{7,5},{8,10},{10,8},{9,1... | collective-permute-start | bytes 3145736 | tf_op jit(solution)/shard_map/ppermute | solution.py:363
  114.7 24.8 %collective-permute-start.19 = (bf16[512,1024]{1,0:T(8,128)(2,1)S(1)}, bf16[512,1024]{1,0:T(8,128)(2,1)S(1)}, u32[]{:S(2)}, u32[]{:S(2)}) collective-permute-start(bf16[512,1024]{1,0:T(8,128)(2,1)S(1)} %get-tuple-element.499.refs_2_), channel_id=1, source_target_pairs={{0,4},{4,0},{8,12},{12,8},{16,20},{20,16},{24,28},{28,24},{1,5},{5... | collective-permute-start | bytes 3145736 | tf_op jit(solution)/shard_map/ppermute | solution.py:370
  121.9 17.7 %collective-permute-start.21 = (bf16[128,1024]{1,0:T(8,128)(2,1)S(1)}, bf16[128,1024]{1,0:T(8,128)(2,1)S(1)}, u32[]{:S(2)}, u32[]{:S(2)}) collective-permute-start(bf16[128,1024]{1,0:T(8,128)(2,1)S(1)} %turn.28.refs_4_), channel_id=1, source_target_pairs={{0,16},{4,20},{8,24},{12,28},{16,0},{20,4},{24,8},{28,12},{1,17},{... | collective-permute-start | bytes 786440 | tf_op jit(solution)/shard_map/ppermute | solution.py:370
  153.5 17.5 %collective-permute-start.28 = (bf16[256,1024]{1,0:T(8,128)(2,1)S(1)}, bf16[256,1024]{1,0:T(8,128)(2,1)S(1)}, u32[]{:S(2)}, u32[]{:S(2)}) collective-permute-start(bf16[256,1024]{1,0:T(8,128)(2,1)S(1)} %get-tuple-element.519.refs_4_), channel_id=1, source_target_pairs={{0,8},{4,12},{8,0},{12,4},{16,24},{20,28},{24,16},{28,20},{1,9},{5... | collective-permute-start | bytes 1572872 | tf_op jit(solution)/shard_map/ppermute | solution.py:370
  153.9 19.8 %collective-permute-start.26 = (bf16[384,1024]{1,0:T(8,128)(2,1)S(1)}, bf16[384,1024]{1,0:T(8,128)(2,1)S(1)}, u32[]{:S(2)}, u32[]{:S(2)}) collective-permute-start(bf16[384,1024]{1,0:T(8,128)(2,1)S(1)} %get-tuple-element.515.refs_0_), channel_id=1, source_target_pairs={{0,2},{2,0},{1,3},{3,1},{4,6},{6,4},{5,7},{7,5},{8,10},{10,8},{9,1... | collective-permute-start | bytes 2359304 | tf_op jit(solution)/shard_map/ppermute | solution.py:363
  155.2 19.4 %collective-permute-start.27 = (bf16[384,1024]{1,0:T(8,128)(2,1)S(1)}, bf16[384,1024]{1,0:T(8,128)(2,1)S(1)}, u32[]{:S(2)}, u32[]{:S(2)}) collective-permute-start(bf16[384,1024]{1,0:T(8,128)(2,1)S(1)} %get-tuple-element.517.refs_2_), channel_id=1, source_target_pairs={{0,4},{4,0},{8,12},{12,8},{16,20},{20,16},{24,28},{28,24},{1,5},{5... | collective-permute-start | bytes 2359304 | tf_op jit(solution)/shard_map/ppermute | solution.py:370
  177.4 24.4 %collective-permute-start.30 = (bf16[512,1024]{1,0:T(8,128)(2,1)}, bf16[512,1024]{1,0:T(8,128)(2,1)}, u32[]{:S(2)}, u32[]{:S(2)}) collective-permute-start(bf16[512,1024]{1,0:T(8,128)(2,1)} %get-tuple-element.524), channel_id=1, source_target_pairs={{0,2},{2,0},{1,3},{3,1},{4,6},{6,4},{5,7},{7,5},{8,10},{10,8},{9,1... | collective-permute-start | bytes 3145736 | tf_op jit(solution)/shard_map/ppermute | solution.py:363
  178.2 24.3 %collective-permute-start.31 = (bf16[512,1024]{1,0:T(8,128)(2,1)}, bf16[512,1024]{1,0:T(8,128)(2,1)}, u32[]{:S(2)}, u32[]{:S(2)}) collective-permute-start(bf16[512,1024]{1,0:T(8,128)(2,1)} %get-tuple-element.525), channel_id=1, source_target_pairs={{0,4},{4,0},{8,12},{12,8},{16,20},{20,16},{24,28},{28,24},{1,5},{5... | collective-permute-start | bytes 3145736 | tf_op jit(solution)/shard_map/ppermute | solution.py:370
  204.5 14.4 %collective-permute-start.32 = (bf16[256,1024]{1,0:T(8,128)(2,1)S(1)}, bf16[256,1024]{1,0:T(8,128)(2,1)S(1)}, u32[]{:S(2)}, u32[]{:S(2)}) collective-permute-start(bf16[256,1024]{1,0:T(8,128)(2,1)S(1)} %get-tuple-element.545), channel_id=1, source_target_pairs={{0,4},{4,0},{8,12},{12,8},{16,20},{20,16},{24,28},{28,24},{1,5},{5... | collective-permute-start | bytes 1572872 | tf_op jit(solution)/shard_map/ppermute | solution.py:370
  221.1 23.6 %collective-permute-start.37 = (bf16[256,1024]{1,0:T(8,128)(2,1)S(1)}, bf16[256,1024]{1,0:T(8,128)(2,1)S(1)}, u32[]{:S(2)}, u32[]{:S(2)}) collective-permute-start(bf16[256,1024]{1,0:T(8,128)(2,1)S(1)} %get-tuple-element.575), channel_id=1, source_target_pairs={{0,8},{4,12},{8,0},{12,4},{16,24},{20,28},{24,16},{28,20},{1,9},{5... | collective-permute-start | bytes 1572872 | tf_op jit(solution)/shard_map/ppermute | solution.py:370
  222.3 25.3 %collective-permute-start.35 = (bf16[512,1024]{1,0:T(8,128)(2,1)S(1)}, bf16[512,1024]{1,0:T(8,128)(2,1)S(1)}, u32[]{:S(2)}, u32[]{:S(2)}) collective-permute-start(bf16[512,1024]{1,0:T(8,128)(2,1)S(1)} %get-tuple-element.572), channel_id=1, source_target_pairs={{0,2},{2,0},{1,3},{3,1},{4,6},{6,4},{5,7},{7,5},{8,10},{10,8},{9,1... | collective-permute-start | bytes 3145736 | tf_op jit(solution)/shard_map/ppermute | solution.py:363
  223.5 25.0 %collective-permute-start.36 = (bf16[512,1024]{1,0:T(8,128)(2,1)S(1)}, bf16[512,1024]{1,0:T(8,128)(2,1)S(1)}, u32[]{:S(2)}, u32[]{:S(2)}) collective-permute-start(bf16[512,1024]{1,0:T(8,128)(2,1)S(1)} %get-tuple-element.573), channel_id=1, source_target_pairs={{0,4},{4,0},{8,12},{12,8},{16,20},{20,16},{24,28},{28,24},{1,5},{5... | collective-permute-start | bytes 3145736 | tf_op jit(solution)/shard_map/ppermute | solution.py:370
  224.5 24.0 %collective-permute-start.39 = (bf16[512,1024]{1,0:T(8,128)(2,1)}, bf16[512,1024]{1,0:T(8,128)(2,1)S(1)}, u32[]{:S(2)}, u32[]{:S(2)}) collective-permute-start(bf16[512,1024]{1,0:T(8,128)(2,1)} %fusion.28), channel_id=1, source_target_pairs={{0,1},{1,0},{2,3},{3,2},{4,5},{5,4},{6,7},{7,6},{8,9},{9,8},{10,11... | collective-permute-start | bytes 3145736 | tf_op jit(solution)/shard_map/ppermute | solution.py:359
  227.4 16.9 %collective-permute-start.40 = (bf16[512,512]{1,0:T(8,128)(2,1)S(1)}, bf16[512,512]{1,0:T(8,128)(2,1)S(1)}, u32[]{:S(2)}, u32[]{:S(2)}) collective-permute-start(bf16[512,512]{1,0:T(8,128)(2,1)S(1)} %broadcast_select_fusion.2), channel_id=1, source_target_pairs={{0,1},{1,0},{2,3},{3,2},{4,5},{5,4},{6,7},{7,6},{8,9},{9,8},{10,11... | collective-permute-start | bytes 1572872 | tf_op jit(solution)/shard_map/ppermute | solution.py:359
  249.7 14.6 %collective-permute-start.43 = (bf16[128,1024]{1,0:T(8,128)(2,1)S(1)}, bf16[128,1024]{1,0:T(8,128)(2,1)S(1)}, u32[]{:S(2)}, u32[]{:S(2)}) collective-permute-start(bf16[128,1024]{1,0:T(8,128)(2,1)S(1)} %get-tuple-element.601), channel_id=1, source_target_pairs={{0,16},{4,20},{8,24},{12,28},{16,0},{20,4},{24,8},{28,12},{1,17},{... | collective-permute-start | bytes 786440 | tf_op jit(solution)/shard_map/ppermute | solution.py:370
  253.1 18.3 %collective-permute-start.41 = (bf16[384,1024]{1,0:T(8,128)(2,1)S(1)}, bf16[384,1024]{1,0:T(8,128)(2,1)S(1)}, u32[]{:S(2)}, u32[]{:S(2)}) collective-permute-start(bf16[384,1024]{1,0:T(8,128)(2,1)S(1)} %get-tuple-element.599), channel_id=1, source_target_pairs={{0,4},{4,0},{8,12},{12,8},{16,20},{20,16},{24,28},{28,24},{1,5},{5... | collective-permute-start | bytes 2359304 | tf_op jit(solution)/shard_map/ppermute | solution.py:370
  254.1 18.0 %collective-permute-start.42 = (bf16[384,1024]{1,0:T(8,128)(2,1)S(1)}, bf16[384,1024]{1,0:T(8,128)(2,1)S(1)}, u32[]{:S(2)}, u32[]{:S(2)}) collective-permute-start(bf16[384,1024]{1,0:T(8,128)(2,1)S(1)} %get-tuple-element.600), channel_id=1, source_target_pairs={{0,2},{2,0},{1,3},{3,1},{4,6},{6,4},{5,7},{7,5},{8,10},{10,8},{9,1... | collective-permute-start | bytes 2359304 | tf_op jit(solution)/shard_map/ppermute | solution.py:363
  275.0 19.6 %collective-permute-start.44 = (bf16[448,1024]{1,0:T(8,128)(2,1)S(1)}, bf16[448,1024]{1,0:T(8,128)(2,1)S(1)}, u32[]{:S(2)}, u32[]{:S(2)}) collective-permute-start(bf16[448,1024]{1,0:T(8,128)(2,1)S(1)} %get-tuple-element.623), channel_id=1, source_target_pairs={{0,2},{2,0},{1,3},{3,1},{4,6},{6,4},{5,7},{7,5},{8,10},{10,8},{9,1... | collective-permute-start | bytes 2752520 | tf_op jit(solution)/shard_map/ppermute | solution.py:363
  276.2 19.3 %collective-permute-start.45 = (bf16[448,1024]{1,0:T(8,128)(2,1)S(1)}, bf16[448,1024]{1,0:T(8,128)(2,1)S(1)}, u32[]{:S(2)}, u32[]{:S(2)}) collective-permute-start(bf16[448,1024]{1,0:T(8,128)(2,1)S(1)} %get-tuple-element.624), channel_id=1, source_target_pairs={{0,4},{4,0},{8,12},{12,8},{16,20},{20,16},{24,28},{28,24},{1,5},{5... | collective-permute-start | bytes 2752520 | tf_op jit(solution)/shard_map/ppermute | solution.py:370
  324.4 14.9 %collective-permute-start.57 = (bf16[256,1024]{1,0:T(8,128)(2,1)S(1)}, bf16[256,1024]{1,0:T(8,128)(2,1)S(1)}, u32[]{:S(2)}, u32[]{:S(2)}) collective-permute-start(bf16[256,1024]{1,0:T(8,128)(2,1)S(1)} %get-tuple-element.708), channel_id=1, source_target_pairs={{0,2},{2,0},{1,3},{3,1},{4,6},{6,4},{5,7},{7,5},{8,10},{10,8},{9,1... | collective-permute-start | bytes 1572872 | tf_op jit(solution)/shard_map/ppermute | solution.py:363
  (111 other events, 823.4 us)
